TPU v7x, 32 devices: a whole 2x2x4 slice. The times are simulated.
32 devices in a mesh: dp: 4 (over y, x), fsdp: 8 (over z, core).
Axes of the slice: x: 2, y: 2, z: 4, core: 2. Of those that a mesh axis runs over, the one named last changes fastest.
Arguments:
- tokens: bfloat16 [32768, 512], P(('dp', 'fsdp')), may hold values from -6 to 6
- encoded: bfloat16 [32768, 512], P(('dp', 'fsdp')), may hold values from -6 to 6
- cotangent: bfloat16 [32768, 512], P(('dp', 'fsdp')), may hold values from -6 to 6
- target_ids: int32 [32, 1024], P(('dp', 'fsdp')), may hold values from 0 to 9, never falling along the last dimension, each value on 1 to 200 neighbouring positions
- source_ids: int32 [32, 1024], P(('dp', 'fsdp')), may hold values from 0 to 9, never falling along the last dimension, each value on 1 to 200 neighbouring positions
- qkv_master: float32 [6, 512, 512], P(None, ('dp', 'fsdp')), may hold values from -0.25 to 0.25
- qkv_first: float32 [6, 512, 512], P(None, ('dp', 'fsdp')), may hold values from -16 to 16
- qkv_second: float32 [6, 512, 512], P(None, ('dp', 'fsdp')), may hold values from 0 to 100, as said below
- out_master: float32 [2, 512, 512], P(None, ('dp', 'fsdp')), may hold values from -1.75 to 1.75
- out_first: float32 [2, 512, 512], P(None, ('dp', 'fsdp')), may hold values from -16 to 16
- out_second: float32 [2, 512, 512], P(None, ('dp', 'fsdp')), may hold values from 0 to 100, as said below
- ffn_in_master: float32 [512, 2048], P(('dp', 'fsdp')), may hold values from -0.25 to 0.25
- ffn_in_first: float32 [512, 2048], P(('dp', 'fsdp')), may hold values from -16 to 16
- ffn_in_second: float32 [512, 2048], P(('dp', 'fsdp')), may hold values from 0 to 100, as said below
- ffn_out_master: float32 [2048, 512], P(('dp', 'fsdp')), may hold values from -0.125 to 0.125
- ffn_out_first: float32 [2048, 512], P(('dp', 'fsdp')), may hold values from -16 to 16
- ffn_out_second: float32 [2048, 512], P(('dp', 'fsdp')), may hold values from 0 to 100, as said below
- vector_master: float32 [17, 512], P(None, ('dp', 'fsdp')), may hold values from -3 to 3
- vector_first: float32 [17, 512], P(None, ('dp', 'fsdp')), may hold values from -16 to 16
- vector_second: float32 [17, 512], P(None, ('dp', 'fsdp')), may hold values from 0 to 120, as said below
Outputs:
- layer_out: bfloat16 [32768, 512], P(('dp', 'fsdp'))
- tokens_grad: float32 [32768, 512], P(('dp', 'fsdp'))
- encoded_grad: float32 [32768, 512], P(('dp', 'fsdp'))
- qkv_first_new: float32 [6, 512, 512], P(None, ('dp', 'fsdp'))
- qkv_second_new: float32 [6, 512, 512], P(None, ('dp', 'fsdp'))
- qkv_master_new: float32 [6, 512, 512], P(None, ('dp', 'fsdp'))
- qkv_copy: bfloat16 [6, 512, 512], P(None, ('dp', 'fsdp'))
- out_first_new: float32 [2, 512, 512], P(None, ('dp', 'fsdp'))
- out_second_new: float32 [2, 512, 512], P(None, ('dp', 'fsdp'))
- out_master_new: float32 [2, 512, 512], P(None, ('dp', 'fsdp'))
- out_copy: bfloat16 [2, 512, 512], P(None, ('dp', 'fsdp'))
- ffn_in_first_new: float32 [512, 2048], P(('dp', 'fsdp'))
- ffn_in_second_new: float32 [512, 2048], P(('dp', 'fsdp'))
- ffn_in_master_new: float32 [512, 2048], P(('dp', 'fsdp'))
- ffn_in_copy: bfloat16 [512, 2048], P(('dp', 'fsdp'))
- ffn_out_first_new: float32 [2048, 512], P(('dp', 'fsdp'))
- ffn_out_second_new: float32 [2048, 512], P(('dp', 'fsdp'))
- ffn_out_master_new: float32 [2048, 512], P(('dp', 'fsdp'))
- ffn_out_copy: bfloat16 [2048, 512], P(('dp', 'fsdp'))
- vector_first_new: float32 [17, 512], P(None, ('dp', 'fsdp'))
- vector_second_new: float32 [17, 512], P(None, ('dp', 'fsdp'))
- vector_master_new: float32 [17, 512], P(None, ('dp', 'fsdp'))
- vector_copy: bfloat16 [17, 512], P(None, ('dp', 'fsdp'))
Inputs may be any that keep to these rules, and one draw needn't show every extreme that they name: `target_ids`: in each row (one group) ids never fall and every id of 0 to 9 occurs, in a run of 1 to 200 positions; one run has exactly 200. `source_ids`: in each row (one group) ids never fall and every id of 0 to 9 occurs, in a run of 1 to 200 positions; one run has exactly 200. `qkv_second`: positive. `out_second`: positive. `ffn_in_second`: positive. `ffn_out_second`: positive. `vector_second`: positive.
All inputs are finite; a program needn't handle non-finite values.
Results may differ from a plain program's by a relative error of at most 0.02.
The roundings to bfloat16 on the way count: a program that leaves them out, or rounds other values in their place, can miss the bound.
Values may be sent and summed in bfloat16 or wider, within the bound.
No kernel may reach another device: no remote copies, remote signals or barrier semaphores. Data moves between devices by JAX's collectives and lax.ppermute only.
A program may use at most 192 MiB of HBM per device.

v0:
```python
import math

import jax
import jax.numpy as jnp
from jax import lax
from jax.sharding import PartitionSpec as P

HEADS = 8
STEP = 5


norm_eps = 1e-05
beta_first = 0.5
beta_second = 0.5
adam_eps = 1e-08
weight_decay = 0.01
mask_fill = -1000000000.0


def matmul(left, right):
    return jnp.dot(left, right, preferred_element_type=jnp.float32)


def product_left(left, right):
    return lax.dot_general(
        left, right, (((0,), (0,)), ((), ())), preferred_element_type=jnp.float32
    )


def product_right(left, right):
    return lax.dot_general(
        left, right, (((1,), (1,)), ((), ())), preferred_element_type=jnp.float32
    )


def column_sums(values):
    return jnp.sum(values.astype(jnp.float32), axis=0)


def gelu_unit(values):
    return jax.nn.gelu(values, approximate=True)


def layer_norm(values, gain, shift):
    center = values - jnp.mean(values, axis=-1, keepdims=True)
    spread = jnp.mean(center * center, axis=-1, keepdims=True)
    return center * lax.rsqrt(spread + norm_eps) * (1.0 + gain) + shift


def block_scores(query_heads, key_heads, id_block, col_ids, factor):
    scores = (
        jnp.einsum("thd,shd->hts", query_heads, key_heads, preferred_element_type=jnp.float32)
        * factor
    )
    same_mask = (id_block[:, None] == col_ids[None, :])[None]
    return jnp.where(same_mask, scores, mask_fill)


def attend_forward(queries, key_rows, value_rows, row_ids, col_ids):
    total_rows = queries.shape[0]
    block_rows = min(512, total_rows)
    block_count = total_rows // block_rows
    head_width = queries.shape[1] // HEADS
    factor = 1.0 / math.sqrt(head_width)
    key_heads = key_rows.reshape(-1, HEADS, head_width)
    value_heads = value_rows.reshape(-1, HEADS, head_width)

    def block_step(pieces):
        query_block, id_block = pieces
        query_heads = query_block.reshape(block_rows, HEADS, head_width)
        scores = block_scores(query_heads, key_heads, id_block, col_ids, factor)
        largest = jnp.max(scores, axis=-1, keepdims=True)
        expo_values = jnp.exp(scores - largest)
        totals = jnp.sum(expo_values, axis=-1, keepdims=True)
        probs_low = (expo_values / totals).astype(jnp.bfloat16)
        mixed = jnp.einsum(
            "hts,shd->thd", probs_low, value_heads, preferred_element_type=jnp.float32
        )
        log_sums = (largest + jnp.log(totals))[..., 0]
        return (mixed.reshape(block_rows, -1), log_sums)

    mixed_blocks, log_sums = lax.map(
        block_step,
        (queries.reshape(block_count, block_rows, -1), row_ids.reshape(block_count, block_rows)),
    )
    return (mixed_blocks.reshape(total_rows, -1), log_sums)


def attend_backward(queries, key_rows, value_rows, row_ids, col_ids, log_sums, grad_mixed):
    total_rows = queries.shape[0]
    key_count = key_rows.shape[0]
    block_rows = min(512, total_rows)
    block_count = total_rows // block_rows
    head_width = queries.shape[1] // HEADS
    factor = 1.0 / math.sqrt(head_width)
    key_heads = key_rows.reshape(-1, HEADS, head_width)
    value_heads = value_rows.reshape(-1, HEADS, head_width)

    def block_step(carry, pieces):
        grad_keys, grad_values = carry
        query_block, id_block, sum_block, grad_block = pieces
        query_heads = query_block.reshape(block_rows, HEADS, head_width)
        grad_heads = grad_block.reshape(block_rows, HEADS, head_width)
        scores = block_scores(query_heads, key_heads, id_block, col_ids, factor)
        probs = jnp.exp(scores - sum_block[..., None])
        probs_low = probs.astype(jnp.bfloat16)
        grad_values = grad_values + jnp.einsum(
            "hts,thd->shd", probs_low, grad_heads, preferred_element_type=jnp.float32
        )
        grad_probs = jnp.einsum(
            "thd,shd->hts", grad_heads, value_heads, preferred_element_type=jnp.float32
        )
        inner = jnp.sum(probs * grad_probs, axis=-1, keepdims=True)
        grad_scores = (probs * (grad_probs - inner)).astype(jnp.bfloat16)
        grad_query = (
            jnp.einsum("hts,shd->thd", grad_scores, key_heads, preferred_element_type=jnp.float32)
            * factor
        )
        grad_keys = (
            grad_keys
            + jnp.einsum(
                "hts,thd->shd", grad_scores, query_heads, preferred_element_type=jnp.float32
            )
            * factor
        )
        return ((grad_keys, grad_values), grad_query.reshape(block_rows, -1))

    start = (
        jnp.zeros((key_count, HEADS, head_width), jnp.float32),
        jnp.zeros((key_count, HEADS, head_width), jnp.float32),
    )
    carried, grad_queries = lax.scan(
        block_step,
        start,
        (
            queries.reshape(block_count, block_rows, -1),
            row_ids.reshape(block_count, block_rows),
            log_sums,
            grad_mixed.reshape(block_count, block_rows, -1),
        ),
    )
    grad_keys, grad_values = carried
    return (
        grad_queries.reshape(total_rows, -1),
        grad_keys.reshape(key_count, -1),
        grad_values.reshape(key_count, -1),
    )


def adamw(master, grad, first, second, rate):
    first_new = beta_first * first + (1.0 - beta_first) * grad
    second_new = beta_second * second + (1.0 - beta_second) * grad * grad
    first_hat = first_new / (1.0 - beta_first**STEP)
    second_hat = second_new / (1.0 - beta_second**STEP)
    master_new = master - rate * (
        first_hat / (jnp.sqrt(second_hat) + adam_eps) + weight_decay * master
    )
    return (first_new, second_new, master_new, master_new.astype(jnp.bfloat16))


def body(
    tokens,
    encoded,
    cotangent,
    target_ids,
    source_ids,
    qkv_master,
    qkv_first,
    qkv_second,
    out_master,
    out_first,
    out_second,
    ffn_in_master,
    ffn_in_first,
    ffn_in_second,
    ffn_out_master,
    ffn_out_first,
    ffn_out_second,
    vector_master,
    vector_first,
    vector_second,
):
    low_qkv = qkv_master.astype(jnp.bfloat16)
    low_out = out_master.astype(jnp.bfloat16)
    low_ffn_in = ffn_in_master.astype(jnp.bfloat16)
    low_ffn_out = ffn_out_master.astype(jnp.bfloat16)
    low_vector = vector_master.astype(jnp.bfloat16)
    forward_set = (
        lax.all_gather(low_qkv, ("dp", "fsdp"), axis=1, tiled=True),
        lax.all_gather(low_out, ("dp", "fsdp"), axis=1, tiled=True),
        lax.all_gather(low_ffn_in, ("dp", "fsdp"), axis=0, tiled=True),
        lax.all_gather(low_ffn_out, ("dp", "fsdp"), axis=0, tiled=True),
        lax.all_gather(low_vector, ("dp", "fsdp"), axis=1, tiled=True),
    )
    qkv_full, out_full, ffn_in_full, ffn_out_full, vector_full = forward_set
    vectors = vector_full.astype(jnp.float32)
    model_width = vectors.shape[1]
    ffn_bias = vectors[13:].reshape(-1)
    row_ids = target_ids[0]
    source_row = source_ids[0]
    inputs = tokens.astype(jnp.float32)
    queries = (matmul(tokens, qkv_full[0]) + vectors[0]).astype(jnp.bfloat16)
    key_rows = matmul(tokens, qkv_full[1]).astype(jnp.bfloat16)
    value_rows = (matmul(tokens, qkv_full[2]) + vectors[1]).astype(jnp.bfloat16)
    mixed_raw, self_sums = attend_forward(queries, key_rows, value_rows, row_ids, row_ids)
    mixed = mixed_raw.astype(jnp.bfloat16)
    first_sum = inputs + matmul(mixed, out_full[0]) + vectors[2]
    first_norm, first_back = jax.vjp(layer_norm, first_sum, vectors[7], vectors[10])
    first_low = first_norm.astype(jnp.bfloat16)
    cross_queries = (matmul(first_low, qkv_full[3]) + vectors[3]).astype(jnp.bfloat16)
    cross_keys = matmul(encoded, qkv_full[4]).astype(jnp.bfloat16)
    cross_values = (matmul(encoded, qkv_full[5]) + vectors[4]).astype(jnp.bfloat16)
    cross_raw, cross_sums = attend_forward(
        cross_queries, cross_keys, cross_values, row_ids, source_row
    )
    cross_mixed = cross_raw.astype(jnp.bfloat16)
    second_sum = first_norm + matmul(cross_mixed, out_full[1]) + vectors[5]
    second_norm, second_back = jax.vjp(layer_norm, second_sum, vectors[8], vectors[11])
    second_low = second_norm.astype(jnp.bfloat16)
    hidden_pre = matmul(second_low, ffn_in_full) + ffn_bias
    hidden_value, gelu_back = jax.vjp(gelu_unit, hidden_pre)
    hidden = hidden_value.astype(jnp.bfloat16)
    third_sum = second_norm + matmul(hidden, ffn_out_full) + vectors[6]
    layer_value, third_back = jax.vjp(layer_norm, third_sum, vectors[9], vectors[12])
    layer_out = layer_value.astype(jnp.bfloat16)
    qkv_back, out_back, ffn_in_back, ffn_out_back = (
        lax.all_gather(low_qkv, ("dp", "fsdp"), axis=1, tiled=True),
        lax.all_gather(low_out, ("dp", "fsdp"), axis=1, tiled=True),
        lax.all_gather(low_ffn_in, ("dp", "fsdp"), axis=0, tiled=True),
        lax.all_gather(low_ffn_out, ("dp", "fsdp"), axis=0, tiled=True),
    )
    grad_third, grad_gain_three, grad_shift_three = third_back(cotangent.astype(jnp.float32))
    grad_ffn = grad_third.astype(jnp.bfloat16)
    grad_ffn_out = product_left(hidden, grad_ffn)
    grad_bias_two = column_sums(grad_ffn)
    grad_hidden = product_right(grad_ffn, ffn_out_back)
    grad_pre = gelu_back(grad_hidden)[0].astype(jnp.bfloat16)
    grad_ffn_in = product_left(second_low, grad_pre)
    grad_bias_one = column_sums(grad_pre)
    grad_second = grad_third + product_right(grad_pre, ffn_in_back)
    grad_second_sum, grad_gain_two, grad_shift_two = second_back(grad_second)
    grad_cross_out = grad_second_sum.astype(jnp.bfloat16)
    grad_weight_cross_out = product_left(cross_mixed, grad_cross_out)
    grad_bias_cross_out = column_sums(grad_cross_out)
    grad_cross_mixed = product_right(grad_cross_out, out_back[1]).astype(jnp.bfloat16)
    cross_query_grad, cross_key_grad, cross_value_grad = attend_backward(
        cross_queries, cross_keys, cross_values, row_ids, source_row, cross_sums, grad_cross_mixed
    )
    cross_query_low = cross_query_grad.astype(jnp.bfloat16)
    cross_key_low = cross_key_grad.astype(jnp.bfloat16)
    cross_value_low = cross_value_grad.astype(jnp.bfloat16)
    grad_weight_cross_query = product_left(first_low, cross_query_low)
    grad_weight_cross_key = product_left(encoded, cross_key_low)
    grad_weight_cross_value = product_left(encoded, cross_value_low)
    grad_bias_cross_query = column_sums(cross_query_low)
    grad_bias_cross_value = column_sums(cross_value_low)
    encoded_grad = product_right(cross_key_low, qkv_back[4]) + product_right(
        cross_value_low, qkv_back[5]
    )
    grad_first = grad_second_sum + product_right(cross_query_low, qkv_back[3])
    grad_first_sum, grad_gain_one, grad_shift_one = first_back(grad_first)
    grad_self_out = grad_first_sum.astype(jnp.bfloat16)
    grad_weight_self_out = product_left(mixed, grad_self_out)
    grad_bias_self_out = column_sums(grad_self_out)
    grad_mixed = product_right(grad_self_out, out_back[0]).astype(jnp.bfloat16)
    self_query_grad, self_key_grad, self_value_grad = attend_backward(
        queries, key_rows, value_rows, row_ids, row_ids, self_sums, grad_mixed
    )
    self_query_low = self_query_grad.astype(jnp.bfloat16)
    self_key_low = self_key_grad.astype(jnp.bfloat16)
    self_value_low = self_value_grad.astype(jnp.bfloat16)
    grad_weight_query = product_left(tokens, self_query_low)
    grad_weight_key = product_left(tokens, self_key_low)
    grad_weight_value = product_left(tokens, self_value_low)
    grad_bias_query = column_sums(self_query_low)
    grad_bias_value = column_sums(self_value_low)
    tokens_grad = (
        grad_first_sum
        + product_right(self_query_low, qkv_back[0])
        + product_right(self_key_low, qkv_back[1])
        + product_right(self_value_low, qkv_back[2])
    )
    grad_qkv = jnp.stack(
        [
            grad_weight_query,
            grad_weight_key,
            grad_weight_value,
            grad_weight_cross_query,
            grad_weight_cross_key,
            grad_weight_cross_value,
        ]
    )
    grad_out = jnp.stack([grad_weight_self_out, grad_weight_cross_out])
    small_rows = jnp.stack(
        [
            grad_bias_query,
            grad_bias_value,
            grad_bias_self_out,
            grad_bias_cross_query,
            grad_bias_cross_value,
            grad_bias_cross_out,
            grad_bias_two,
            grad_gain_one,
            grad_gain_two,
            grad_gain_three,
            grad_shift_one,
            grad_shift_two,
            grad_shift_three,
        ]
    )
    grad_vector = jnp.concatenate([small_rows, grad_bias_one.reshape(-1, model_width)], axis=0)
    summed_qkv, summed_out, summed_ffn_in, summed_ffn_out, summed_vector = (
        lax.psum_scatter(grad_qkv, ("dp", "fsdp"), scatter_dimension=1, tiled=True),
        lax.psum_scatter(grad_out, ("dp", "fsdp"), scatter_dimension=1, tiled=True),
        lax.psum_scatter(grad_ffn_in, ("dp", "fsdp"), scatter_dimension=0, tiled=True),
        lax.psum_scatter(grad_ffn_out, ("dp", "fsdp"), scatter_dimension=0, tiled=True),
        lax.psum_scatter(grad_vector, ("dp", "fsdp"), scatter_dimension=1, tiled=True),
    )
    total_tokens = tokens.shape[0] * lax.axis_size("dp") * lax.axis_size("fsdp")
    grad_scale = 1.0 / math.sqrt(total_tokens)
    qkv_first_new, qkv_second_new, qkv_master_new, qkv_copy = adamw(
        qkv_master, summed_qkv * grad_scale, qkv_first, qkv_second, 0.04
    )
    out_first_new, out_second_new, out_master_new, out_copy = adamw(
        out_master, summed_out * grad_scale, out_first, out_second, 0.3
    )
    ffn_in_first_new, ffn_in_second_new, ffn_in_master_new, ffn_in_copy = adamw(
        ffn_in_master, summed_ffn_in * grad_scale, ffn_in_first, ffn_in_second, 0.04
    )
    ffn_out_first_new, ffn_out_second_new, ffn_out_master_new, ffn_out_copy = adamw(
        ffn_out_master, summed_ffn_out * grad_scale, ffn_out_first, ffn_out_second, 0.02
    )
    vector_first_new, vector_second_new, vector_master_new, vector_copy = adamw(
        vector_master, summed_vector * grad_scale, vector_first, vector_second, 0.35
    )
    return (
        layer_out,
        tokens_grad,
        encoded_grad,
        qkv_first_new,
        qkv_second_new,
        qkv_master_new,
        qkv_copy,
        out_first_new,
        out_second_new,
        out_master_new,
        out_copy,
        ffn_in_first_new,
        ffn_in_second_new,
        ffn_in_master_new,
        ffn_in_copy,
        ffn_out_first_new,
        ffn_out_second_new,
        ffn_out_master_new,
        ffn_out_copy,
        vector_first_new,
        vector_second_new,
        vector_master_new,
        vector_copy,
    )


def solution(mesh):
    return jax.shard_map(
        body,
        mesh=mesh,
        in_specs=(
            P(("dp", "fsdp"), None),
            P(("dp", "fsdp"), None),
            P(("dp", "fsdp"), None),
            P(("dp", "fsdp"), None),
            P(("dp", "fsdp"), None),
            P(None, ("dp", "fsdp"), None),
            P(None, ("dp", "fsdp"), None),
            P(None, ("dp", "fsdp"), None),
            P(None, ("dp", "fsdp"), None),
            P(None, ("dp", "fsdp"), None),
            P(None, ("dp", "fsdp"), None),
            P(("dp", "fsdp"), None),
            P(("dp", "fsdp"), None),
            P(("dp", "fsdp"), None),
            P(("dp", "fsdp"), None),
            P(("dp", "fsdp"), None),
            P(("dp", "fsdp"), None),
            P(None, ("dp", "fsdp")),
            P(None, ("dp", "fsdp")),
            P(None, ("dp", "fsdp")),
        ),
        out_specs=(
            P(("dp", "fsdp"), None),
            P(("dp", "fsdp"), None),
            P(("dp", "fsdp"), None),
            P(None, ("dp", "fsdp"), None),
            P(None, ("dp", "fsdp"), None),
            P(None, ("dp", "fsdp"), None),
            P(None, ("dp", "fsdp"), None),
            P(None, ("dp", "fsdp"), None),
            P(None, ("dp", "fsdp"), None),
            P(None, ("dp", "fsdp"), None),
            P(None, ("dp", "fsdp"), None),
            P(("dp", "fsdp"), None),
            P(("dp", "fsdp"), None),
            P(("dp", "fsdp"), None),
            P(("dp", "fsdp"), None),
            P(("dp", "fsdp"), None),
            P(("dp", "fsdp"), None),
            P(("dp", "fsdp"), None),
            P(("dp", "fsdp"), None),
            P(None, ("dp", "fsdp")),
            P(None, ("dp", "fsdp")),
            P(None, ("dp", "fsdp")),
            P(None, ("dp", "fsdp")),
        ),
        check_vma=False,
    )
```

profile of v0, /device:TPU:0, one launch (start us, length us, event | category | flops | bytes accessed | tf_op | source)
XLA Modules:
  0.0 1220.4 jit_solution(13486432953612517785)
XLA Ops:
  14.5 44.0 %all_gather.20 = bf16[17,512]{0,1:T(8,128)(2,1)S(1)} all-gather(bf16[17,16]{0,1:T(8,128)(2,1)S(1)} %convert_element_type.195), channel_id=1, replica_groups=mesh['dp'=4,'fsdp'=8] {'dp','fsdp'}, dimensions={1}, use_global_device_ids=true | all-gather | bytes 17952 | tf_op jit(solution)/shard_map/all_gather | solution.py:193
  66.0 7.7 all-gather.5.cloned.1.call-done
  82.1 38.1 %while.54 = (s32[]{:T(128)}, bf16[2,512,512]{2,1,0:T(8,128)(2,1)}, f32[2,8,512]{2,1,0:T(8,128)}, s32[2,512]{1,0:T(2,128)S(1)}, s32[1,1024]{1,0:T(1,128)S(1)}, /*...) while((s32[]{:T(128)}, bf16[2,512,512]{2,1,0:T(8,128)(2,1)}, ...), condition=%wide.region_3.4_spmd, body=%wide.region_0.3_spmd.sunk | while | flops 1124593664 | bytes 58861684 | solution.py:82
  86.6 4.2 fusion.171
  90.8 5.8 fusion.172
  105.6 4.2 fusion.171
  109.9 5.8 fusion.172
  120.2 9.8 all-gather.7.cloned.1.call-done
  142.6 33.1 %while.55 = (s32[]{:T(128)}, bf16[2,512,512]{2,1,0:T(8,128)(2,1)S(1)}, f32[2,8,512]{2,1,0:T(8,128)S(1)}, s32[2,512]{1,0:T(2,128)S(1)}, s32[1,1024]{1,0:T(1,128)S...) while((s32[]{:T(128)}, ...), condition=%wide.region_9.10_spmd, body=%wide.region_6.9_spmd.sunk | while | flops 1124593664 | bytes 58861684 | solution.py:82
  144.1 4.7 fusion.176
  148.8 4.2 fusion.177
  153.0 5.8 fusion.178
  160.6 4.7 fusion.176
  165.3 4.2 fusion.177
  169.6 5.8 fusion.178
  180.2 8.8 all-gather.9.cloned.1.call-done
  189.0 9.5 multiply_convert_fusion.2
  198.5 49.3 %all-gather.11.cloned.1.call-done = bf16[2048,512]{1,0:T(8,128)(2,1)} async-done(((bf16[64,512]{1,0:T(8,128)(2,1)}), bf16[2048,512]{1,0:T(8,128)(2,1)}) %all-gather.11.cloned.1.call-update) | async-done | bytes 2097168 | tf_op jit(solution)/shard_map/all_gather | solution.py:192
  247.8 6.2 fusion.65
  259.6 9.1 convert_reduce_fusion
  269.4 7.7 multiply_reduce_fusion.2
  284.3 102.2 %while.56 = (s32[]{:T(128)}, f32[1024,8,64]{0,2,1:T(8,128)}, f32[1024,8,64]{0,2,1:T(8,128)}, bf16[2,512,512]{2,1,0:T(8,128)(2,1)}, bf16[2,512,512]{1,2,0:T(8,128...) while((s32[]{:T(128)}, f32[1024,8,64]{0,2,1:T(8,128)}, ...), condition=%wide.region_20.21_spmd.clone, body=%wide.region_18.20_spmd.clone.sunk | while | flops 2725769216 | bytes 201156976 | solution.py:132
  290.2 3.8 fusion.189
  294.0 11.9 multiply_reduce_fusion.11
  305.8 9.4 multiply_convert_fusion.5
  315.2 8.9 bitcast_add_fusion.9
  324.1 4.8 convolution_multiply_fusion.4
  341.0 3.8 fusion.189
  344.7 11.9 multiply_reduce_fusion.11
  356.6 9.4 multiply_convert_fusion.5
  366.0 9.5 bitcast_add_fusion.9
  375.4 4.8 convolution_multiply_fusion.4
  388.6 4.7 multiply_reduce_fusion.3
  400.5 100.4 %while.57 = (s32[]{:T(128)}, f32[1024,8,64]{0,2,1:T(8,128)}, f32[1024,8,64]{0,2,1:T(8,128)}, bf16[2,512,512]{2,1,0:T(8,128)(2,1)}, bf16[2,512,512]{1,2,0:T(8,128...) while((s32[]{:T(128)}, f32[1024,8,64]{0,2,1:T(8,128)}, ...), condition=%wide.region_25.26_spmd.clone, body=%wide.region_23.25_spmd.clone.sunk | while | flops 2725769216 | bytes 209283440 | solution.py:132
  410.9 11.9 multiply_reduce_fusion.12
  422.7 9.4 multiply_convert_fusion.6
  432.1 8.8 bitcast_add_fusion.11
  460.6 11.9 multiply_reduce_fusion.12
  472.4 9.4 multiply_convert_fusion.6
  481.8 9.4 bitcast_add_fusion.11
  512.4 6.6 fusion.68
  520.5 6.7 fusion.48
  542.8 9.7 copy.171
  568.2 73.6 %reduce-scatter.16.cloned.1.call-done = f32[16,17]{1,0:T(8,128)} async-done(((f32[512,17]{1,0:T(8,128)}), f32[16,17]{1,0:T(8,128)}) %reduce-scatter.16.cloned.1.call-update) | async-done | bytes 1104
  643.1 134.7 %reduce-scatter.10.cloned.1.call-done = f32[2,16,512]{2,1,0:T(8,128)} async-done(((f32[2,512,512]{2,1,0:T(8,128)}), f32[2,16,512]{2,1,0:T(8,128)}) %reduce-scatter.10.cloned.1.call-update) | async-done | bytes 65552 | tf_op jit(solution)/shard_map/reduce_scatter | solution.py:314
  779.3 139.5 %reduce-scatter.14.cloned.1.call-done = f32[64,512]{1,0:T(8,128)} async-done(((f32[2048,512]{1,0:T(8,128)}), f32[64,512]{1,0:T(8,128)}) %reduce-scatter.14.cloned.1.call-update) | async-done | bytes 131088 | tf_op jit(solution)/shard_map/reduce_scatter | solution.py:316
  920.5 140.1 %reduce-scatter.12.cloned.1.call-done = f32[16,2048]{1,0:T(8,128)} async-done(((f32[512,2048]{1,0:T(8,128)}), f32[16,2048]{1,0:T(8,128)}) %reduce-scatter.12.cloned.1.call-update) | async-done | bytes 131088 | tf_op jit(solution)/shard_map/reduce_scatter | solution.py:315
  1062.3 149.4 %reduce-scatter.8.cloned.1.call-done = f32[6,16,512]{2,0,1:T(8,128)} async-done(((f32[6,512,512]{2,0,1:T(8,128)}), f32[6,16,512]{2,0,1:T(8,128)}) %reduce-scatter.8.cloned.1.call-update) | async-done | bytes 196624 | tf_op jit(solution)/shard_map/reduce_scatter | solution.py:313
  (439 shorter events, 199.0 us)
Async XLA Ops:
  7.2 129.7 %copy-start = (bf16[1024,512]{1,0:T(8,128)(2,1)S(1)}, bf16[1024,512]{1,0:T(8,128)(2,1)}, u32[]{:S(2)}) copy-start(bf16[1024,512]{1,0:T(8,128)(2,1)} %param.29) | copy-start | bytes 3145732
  7.2 52.0 %copy-start.51 = (s32[1,1024]{1,0:T(1,128)S(1)}, s32[1,1024]{1,0:T(1,128)}, u32[]{:S(2)}) copy-start(s32[1,1024]{1,0:T(1,128)} %param.31) | copy-start | bytes 12292
  7.2 66.4 %all-gather.5.cloned.1.call-start = ((), (), s32[]{:S(2)}) async-start(), calls=%async_computation.5 | async-start | bytes 3244032 | tf_op jit(solution)/shard_map/all_gather | solution.py:189
  8.9 121.0 %all-gather.7.cloned.1.call-start = ((), (), s32[]{:S(2)}) async-start(), calls=%async_computation.6 | async-start | bytes 1081344 | tf_op jit(solution)/shard_map/all_gather | solution.py:190
  10.5 178.5 %all-gather.9.cloned.1.call-start = ((), (), s32[]{:S(2)}) async-start(), calls=%async_computation.7 | async-start | bytes 2162688 | tf_op jit(solution)/shard_map/all_gather | solution.py:191
  12.1 235.7 %all-gather.11.cloned.1.call-start = ((), (), s32[]{:S(2)}) async-start(), calls=%async_computation.8 | async-start | bytes 2162688 | tf_op jit(solution)/shard_map/all_gather | solution.py:192
  13.7 628.0 %reduce-scatter.16.cloned.1.call-start = ((), (), s32[]{:S(2)}) async-start(), calls=%async_computation.13 | async-start | bytes 270336
  82.1 47.9 %copy-start.112 = (f32[512]{0:T(512)S(1)}, f32[512]{0:T(512)}, u32[]{:S(2)}) copy-start(f32[512]{0:T(512)} %get-tuple-element.574) | copy-start | bytes 6148
  120.2 12.3 %copy-start.12 = (bf16[1024,8,64]{0,2,1:T(8,128)(2,1)}, bf16[1024,8,64]{0,2,1:T(8,128)(2,1)S(1)}, u32[]{:S(2)}) copy-start(bf16[1024,8,64]{0,2,1:T(8,128)(2,1)S(1)} %get-tuple-element.1099) | copy-start | bytes 3145732
  120.2 12.3 %copy-start.14 = (bf16[1024,8,64]{0,2,1:T(8,128)(2,1)}, bf16[1024,8,64]{0,2,1:T(8,128)(2,1)S(1)}, u32[]{:S(2)}) copy-start(bf16[1024,8,64]{0,2,1:T(8,128)(2,1)S(1)} %get-tuple-element.1100) | copy-start | bytes 3145732
  142.5 34.1 %copy-start.66 = (f32[1024]{0:T(1024)S(1)}, f32[1024]{0:T(1024)}, u32[]{:S(2)}) copy-start(f32[1024]{0:T(1024)} %copy-done.65) | copy-start | bytes 12292
  142.6 34.1 %copy-start.75 = (f32[1024]{0:T(1024)S(1)}, f32[1024]{0:T(1024)}, u32[]{:S(2)}) copy-start(f32[1024]{0:T(1024)} %copy-done.74) | copy-start | bytes 12292
  142.6 34.1 %copy-start.84 = (f32[512]{0:T(512)S(1)}, f32[512]{0:T(512)}, u32[]{:S(2)}) copy-start(f32[512]{0:T(512)} %get-tuple-element.573) | copy-start | bytes 6148
  142.6 34.1 %copy-start.104 = (f32[512]{0:T(512)S(1)}, f32[512]{0:T(512)}, u32[]{:S(2)}) copy-start(f32[512]{0:T(512)} %get-tuple-element.572) | copy-start | bytes 6148
  142.6 34.1 %copy-start.109 = (f32[512]{0:T(512)S(1)}, f32[512]{0:T(512)}, u32[]{:S(2)}) copy-start(f32[512]{0:T(512)} %get-tuple-element.569) | copy-start | bytes 6148
  179.8 18.7 %copy-start.26 = (f32[1024,512]{0,1:T(8,128)}, f32[1024,512]{0,1:T(8,128)S(1)}, u32[]{:S(2)}) copy-start(f32[1024,512]{0,1:T(8,128)S(1)} %get-tuple-element.701) | copy-start | bytes 6291460
  179.8 97.3 %copy-start.78 = (f32[1024]{0:T(1024)}, f32[1024]{0:T(1024)S(1)}, u32[]{:S(2)}) copy-start(f32[1024]{0:T(1024)S(1)} %broadcast_multiply_fusion.1) | copy-start | bytes 12292
  180.2 96.9 %copy-start.87 = (f32[1024]{0:T(1024)}, f32[1024]{0:T(1024)S(1)}, u32[]{:S(2)}) copy-start(f32[1024]{0:T(1024)S(1)} %fusion.46) | copy-start | bytes 12292
  189.0 58.8 %copy-start.108 = (f32[512]{0:T(512)S(1)}, f32[512]{0:T(512)}, u32[]{:S(2)}) copy-start(f32[512]{0:T(512)} %get-tuple-element.566) | copy-start | bytes 6148
  247.8 11.8 copy-start.118
  284.3 104.3 %copy-start.67 = (f32[1024]{0:T(1024)S(1)}, f32[1024]{0:T(1024)}, u32[]{:S(2)}) copy-start(f32[1024]{0:T(1024)} %copy-done.65) | copy-start | bytes 12292
  305.8 9.4 copy-start.3
  356.6 9.4 copy-start.3
  366.0 9.5 copy-start.1
  422.7 9.4 copy-start.4
  472.4 9.4 copy-start.4
  481.8 9.4 copy-start.2
  481.8 9.4 copy-start.13
  509.4 268.4 %reduce-scatter.10.cloned.1.call-start = ((), (), s32[]{:S(2)}) async-start(), calls=%async_computation.10 | async-start | bytes 2162688 | tf_op jit(solution)/shard_map/reduce_scatter | solution.py:314
  511.2 407.6 %reduce-scatter.14.cloned.1.call-start = ((), (), s32[]{:S(2)}) async-start(), calls=%async_computation.12 | async-start | bytes 4325376 | tf_op jit(solution)/shard_map/reduce_scatter | solution.py:316
  519.0 541.6 %reduce-scatter.12.cloned.1.call-start = ((), (), s32[]{:S(2)}) async-start(), calls=%async_computation.11 | async-start | bytes 4325376 | tf_op jit(solution)/shard_map/reduce_scatter | solution.py:315
  527.2 684.5 %reduce-scatter.8.cloned.1.call-start = ((), (), s32[]{:S(2)}) async-start(), calls=%async_computation.9 | async-start | bytes 8650752 | tf_op jit(solution)/shard_map/reduce_scatter | solution.py:313
  529.2 10.1 copy-start.29
  564.8 77.0 %copy-start.81 = (f32[17,16]{0,1:T(8,128)S(1)}, f32[17,16]{0,1:T(8,128)}, u32[]{:S(2)}) copy-start(f32[17,16]{0,1:T(8,128)} %param.45) | copy-start | bytes 3268
  564.8 77.0 %copy-start.92 = (f32[17,16]{0,1:T(8,128)S(1)}, f32[17,16]{0,1:T(8,128)}, u32[]{:S(2)}) copy-start(f32[17,16]{0,1:T(8,128)} %param.47) | copy-start | bytes 3268
  564.8 77.0 %copy-start.93 = (f32[17,16]{0,1:T(8,128)S(1)}, f32[17,16]{0,1:T(8,128)}, u32[]{:S(2)}) copy-start(f32[17,16]{0,1:T(8,128)} %param.46) | copy-start | bytes 3268
  564.8 213.0 %copy-start.56 = (f32[2,16,512]{2,1,0:T(8,128)S(1)}, f32[2,16,512]{2,1,0:T(8,128)}, u32[]{:S(2)}) copy-start(f32[2,16,512]{2,1,0:T(8,128)} %param.36) | copy-start | bytes 196612
  564.8 213.0 %copy-start.63 = (f32[2,16,512]{2,1,0:T(8,128)S(1)}, f32[2,16,512]{2,1,0:T(8,128)}, u32[]{:S(2)}) copy-start(f32[2,16,512]{2,1,0:T(8,128)} %param.38) | copy-start | bytes 196612
  564.8 213.0 %copy-start.64 = (f32[2,16,512]{2,1,0:T(8,128)S(1)}, f32[2,16,512]{2,1,0:T(8,128)}, u32[]{:S(2)}) copy-start(f32[2,16,512]{2,1,0:T(8,128)} %param.37) | copy-start | bytes 196612
  564.8 354.0 %copy-start.49 = (f32[64,512]{1,0:T(8,128)S(1)}, f32[64,512]{1,0:T(8,128)}, u32[]{:S(2)}) copy-start(f32[64,512]{1,0:T(8,128)} %param.42) | copy-start | bytes 393220
  564.8 353.9 %copy-start.59 = (f32[64,512]{1,0:T(8,128)S(1)}, f32[64,512]{1,0:T(8,128)}, u32[]{:S(2)}) copy-start(f32[64,512]{1,0:T(8,128)} %param.44) | copy-start | bytes 393220
  564.8 353.9 %copy-start.60 = (f32[64,512]{1,0:T(8,128)S(1)}, f32[64,512]{1,0:T(8,128)}, u32[]{:S(2)}) copy-start(f32[64,512]{1,0:T(8,128)} %param.43) | copy-start | bytes 393220
  564.9 495.7 %copy-start.50 = (f32[16,2048]{1,0:T(8,128)S(1)}, f32[16,2048]{1,0:T(8,128)}, u32[]{:S(2)}) copy-start(f32[16,2048]{1,0:T(8,128)} %param.39) | copy-start | bytes 393220
  564.9 495.7 %copy-start.61 = (f32[16,2048]{1,0:T(8,128)S(1)}, f32[16,2048]{1,0:T(8,128)}, u32[]{:S(2)}) copy-start(f32[16,2048]{1,0:T(8,128)} %param.41) | copy-start | bytes 393220
  564.9 495.7 %copy-start.62 = (f32[16,2048]{1,0:T(8,128)S(1)}, f32[16,2048]{1,0:T(8,128)}, u32[]{:S(2)}) copy-start(f32[16,2048]{1,0:T(8,128)} %param.40) | copy-start | bytes 393220
  568.2 643.5 %copy-start.48 = (f32[6,16,512]{2,1,0:T(8,128)S(1)}, f32[6,16,512]{2,1,0:T(8,128)}, u32[]{:S(2)}) copy-start(f32[6,16,512]{2,1,0:T(8,128)} %param.33) | copy-start | bytes 589828
  568.2 643.5 %copy-start.57 = (f32[6,16,512]{2,1,0:T(8,128)S(1)}, f32[6,16,512]{2,1,0:T(8,128)}, u32[]{:S(2)}) copy-start(f32[6,16,512]{2,1,0:T(8,128)} %param.35) | copy-start | bytes 589828
  568.2 643.5 %copy-start.58 = (f32[6,16,512]{2,1,0:T(8,128)S(1)}, f32[6,16,512]{2,1,0:T(8,128)}, u32[]{:S(2)}) copy-start(f32[6,16,512]{2,1,0:T(8,128)} %param.34) | copy-start | bytes 589828
  (94 other events, 334.0 us)
Sparse Core Ops, SparseCore 0:
  11.7 61.9 all-gather.4
  77.3 52.6 all-gather.6
  133.5 55.4 all-gather.8
  192.4 55.3 all-gather.10
  509.5 132.2 reduce-scatter.15
  644.0 133.7 reduce-scatter.9
  780.0 138.6 reduce-scatter.13
  921.0 139.5 reduce-scatter.11
  1062.9 148.7 reduce-scatter.7
where the time goes:
time: 1230 us; the launch traced here: 1220 us
  waiting for transfers between devices  713 us (58%)
  matrix products  259 us (21%)
  other arithmetic  102 us (8%)
  local copies, waits for them, and re-layouts  86.4 us (7%)
  blocking collectives  44 us (4%)
  between operations  15.2 us (1%)
    reduce_scatter x1, waiting for transfers between devices, body(): lax.psum_scatter(grad_qkv, ('dp', 'fsdp'), scatter_dimension=1, tiled=True)  149 us
    reduce_scatter x1, waiting for transfers between devices, body(): lax.psum_scatter(grad_ffn_in, ('dp', 'fsdp'), scatter_dimension=0, tiled=...  140 us
    reduce_scatter x1, waiting for transfers between devices, body(): lax.psum_scatter(grad_ffn_out, ('dp', 'fsdp'), scatter_dimension=0, tiled...  139 us
    reduce_scatter x1, waiting for transfers between devices, body(): lax.psum_scatter(grad_out, ('dp', 'fsdp'), scatter_dimension=1, tiled=True)  135 us
    unnamed x10, waiting for transfers between devices  73.7 us
    dot_general x8, matrix products, block_scores(): jnp.einsum('thd,shd->hts', query_heads, key_heads, preferred_element_type...  62.8 us
    all_gather x1, waiting for transfers between devices, body(): lax.all_gather(low_ffn_out, ('dp', 'fsdp'), axis=0, tiled=True)  49.3 us
    all_gather x1, blocking collectives, body(): lax.all_gather(low_vector, ('dp', 'fsdp'), axis=1, tiled=True)  44 us
  transfers between devices with their start and end apart: 9, of which 9 were waited for; matrix products, arithmetic and copies ran while one was open for 14% of the time, Pallas kernels for 0%

commit v1 on v0

--- a/solution.py
+++ b/solution.py
@@ -156,6 +156,58 @@
         first_hat / (jnp.sqrt(second_hat) + adam_eps) + weight_decay * master
     )
     return (first_new, second_new, master_new, master_new.astype(jnp.bfloat16))
+
+
+AXES = ("dp", "fsdp")
+
+
+def exchange(values, offset):
+    count = lax.axis_size("dp") * lax.axis_size("fsdp")
+    return lax.ppermute(values, AXES, [(i, i ^ offset) for i in range(count)])
+
+
+def gather_pieces(piece):
+    dp_count, fsdp_count = lax.axis_size("dp"), lax.axis_size("fsdp")
+    depth = fsdp_count // 2
+    stack = jnp.stack([piece] + [exchange(piece, 2 * k) for k in range(1, depth)])
+    near = [stack] + [exchange(stack, fsdp_count * k) for k in range(1, dp_count)]
+    far = [exchange(item, 1) for item in near]
+    return near, far
+
+
+def own_index():
+    return lax.axis_index("dp") * lax.axis_size("fsdp") + lax.axis_index("fsdp")
+
+
+def ordered(near, far):
+    count = lax.axis_size("dp") * lax.axis_size("fsdp")
+    both = jnp.stack([jnp.stack(near), jnp.stack(far)], axis=2)
+    flat = both.reshape((count,) + both.shape[3:])
+    return flat[jnp.arange(count) ^ own_index()]
+
+
+def pick(values, index, axis):
+    return lax.dynamic_index_in_dim(values, index, axis, keepdims=False)
+
+
+def scatter_sum(grad):
+    dp_count, fsdp_count = lax.axis_size("dp"), lax.axis_size("fsdp")
+    depth = fsdp_count // 2
+    place_dp, place_fsdp = lax.axis_index("dp"), lax.axis_index("fsdp")
+    core, layer = place_fsdp % 2, place_fsdp // 2
+    low = jnp.bfloat16
+    grad = grad.reshape((dp_count, depth, 2) + grad.shape[1:])
+    received = exchange(pick(grad, 1 - core, 2).astype(low), 1)
+    pair = pick(grad, core, 2).astype(jnp.float32) + received.astype(jnp.float32)
+    square = pick(pair, place_dp, 0)
+    for k in range(1, dp_count):
+        part = exchange(pick(pair, place_dp ^ k, 0).astype(low), fsdp_count * k)
+        square = square + part.astype(jnp.float32)
+    total = pick(square, layer, 0)
+    for k in range(1, depth):
+        part = exchange(pick(square, layer ^ k, 0).astype(low), 2 * k)
+        total = total + part.astype(jnp.float32)
+    return total
 
 
 def body(
@@ -185,14 +237,39 @@
     low_ffn_in = ffn_in_master.astype(jnp.bfloat16)
     low_ffn_out = ffn_out_master.astype(jnp.bfloat16)
     low_vector = vector_master.astype(jnp.bfloat16)
-    forward_set = (
-        lax.all_gather(low_qkv, ("dp", "fsdp"), axis=1, tiled=True),
-        lax.all_gather(low_out, ("dp", "fsdp"), axis=1, tiled=True),
-        lax.all_gather(low_ffn_in, ("dp", "fsdp"), axis=0, tiled=True),
-        lax.all_gather(low_ffn_out, ("dp", "fsdp"), axis=0, tiled=True),
-        lax.all_gather(low_vector, ("dp", "fsdp"), axis=1, tiled=True),
-    )
-    qkv_full, out_full, ffn_in_full, ffn_out_full, vector_full = forward_set
+    width = tokens.shape[1]
+    count = lax.axis_size("dp") * lax.axis_size("fsdp")
+    rows = width // count
+    vector_count = low_vector.shape[0]
+    vector_row = jnp.pad(low_vector.reshape(1, -1), ((0, 7), (0, width - low_vector.size)))
+    first_set = ordered(
+        *gather_pieces(jnp.concatenate([low_qkv[:3].reshape(-1, width), vector_row]))
+    )
+    second_set = ordered(
+        *gather_pieces(
+            jnp.concatenate([low_qkv[3:].reshape(-1, width), low_out.reshape(-1, width)])
+        )
+    )
+    in_piece = low_ffn_in.reshape(rows, -1, width).transpose(1, 0, 2).reshape(-1, width)
+    third_set = ordered(*gather_pieces(jnp.concatenate([in_piece, low_ffn_out])))
+
+    def whole(part):
+        return part.reshape(count, -1, rows, width).transpose(1, 0, 2, 3).reshape(-1, width, width)
+
+    qkv_full = [*whole(first_set[:, : 3 * rows]), *whole(second_set[:, : 3 * rows])]
+    out_full = whole(second_set[:, 3 * rows :])
+    in_rows = in_piece.shape[0]
+    ffn_in_full = (
+        third_set[:, :in_rows].reshape(count, -1, rows, width).transpose(0, 2, 1, 3)
+    ).reshape(width, -1)
+    ffn_out_full = third_set[:, in_rows:].reshape(-1, width)
+    vector_full = (
+        first_set[:, 3 * rows, : low_vector.size]
+        .reshape(count, vector_count, -1)
+        .transpose(1, 0, 2)
+        .reshape(vector_count, width)
+    )
+    qkv_back, out_back, ffn_in_back, ffn_out_back = qkv_full, out_full, ffn_in_full, ffn_out_full
     vectors = vector_full.astype(jnp.float32)
     model_width = vectors.shape[1]
     ffn_bias = vectors[13:].reshape(-1)
@@ -223,12 +300,6 @@
     third_sum = second_norm + matmul(hidden, ffn_out_full) + vectors[6]
     layer_value, third_back = jax.vjp(layer_norm, third_sum, vectors[9], vectors[12])
     layer_out = layer_value.astype(jnp.bfloat16)
-    qkv_back, out_back, ffn_in_back, ffn_out_back = (
-        lax.all_gather(low_qkv, ("dp", "fsdp"), axis=1, tiled=True),
-        lax.all_gather(low_out, ("dp", "fsdp"), axis=1, tiled=True),
-        lax.all_gather(low_ffn_in, ("dp", "fsdp"), axis=0, tiled=True),
-        lax.all_gather(low_ffn_out, ("dp", "fsdp"), axis=0, tiled=True),
-    )
     grad_third, grad_gain_three, grad_shift_three = third_back(cotangent.astype(jnp.float32))
     grad_ffn = grad_third.astype(jnp.bfloat16)
     grad_ffn_out = product_left(hidden, grad_ffn)
@@ -280,17 +351,6 @@
         + product_right(self_key_low, qkv_back[1])
         + product_right(self_value_low, qkv_back[2])
     )
-    grad_qkv = jnp.stack(
-        [
-            grad_weight_query,
-            grad_weight_key,
-            grad_weight_value,
-            grad_weight_cross_query,
-            grad_weight_cross_key,
-            grad_weight_cross_value,
-        ]
-    )
-    grad_out = jnp.stack([grad_weight_self_out, grad_weight_cross_out])
     small_rows = jnp.stack(
         [
             grad_bias_query,
@@ -309,13 +369,41 @@
         ]
     )
     grad_vector = jnp.concatenate([small_rows, grad_bias_one.reshape(-1, model_width)], axis=0)
-    summed_qkv, summed_out, summed_ffn_in, summed_ffn_out, summed_vector = (
-        lax.psum_scatter(grad_qkv, ("dp", "fsdp"), scatter_dimension=1, tiled=True),
-        lax.psum_scatter(grad_out, ("dp", "fsdp"), scatter_dimension=1, tiled=True),
-        lax.psum_scatter(grad_ffn_in, ("dp", "fsdp"), scatter_dimension=0, tiled=True),
-        lax.psum_scatter(grad_ffn_out, ("dp", "fsdp"), scatter_dimension=0, tiled=True),
-        lax.psum_scatter(grad_vector, ("dp", "fsdp"), scatter_dimension=1, tiled=True),
-    )
+
+    def split(parts):
+        return jnp.concatenate([part.reshape(count, -1, width) for part in parts], axis=1)
+
+    in_split = grad_ffn_in.reshape(count, rows, -1, width).transpose(0, 2, 1, 3)
+    ffn_total = scatter_sum(split([in_split, grad_ffn_out]))
+    cross_total = scatter_sum(
+        split(
+            [
+                grad_weight_cross_query,
+                grad_weight_cross_key,
+                grad_weight_cross_value,
+                grad_weight_cross_out,
+            ]
+        )
+    )
+    vector_split = grad_vector.reshape(vector_count, count, -1).transpose(1, 0, 2).reshape(count, -1)
+    vector_split = jnp.pad(vector_split, ((0, 0), (0, width - vector_split.shape[1])))
+    self_total = scatter_sum(
+        split(
+            [
+                grad_weight_query,
+                grad_weight_key,
+                grad_weight_value,
+                grad_weight_self_out,
+                vector_split[:, None],
+            ]
+        )
+    )
+    summed_qkv = jnp.concatenate([self_total[: 3 * rows], cross_total[: 3 * rows]])
+    summed_qkv = summed_qkv.reshape(6, rows, width)
+    summed_out = jnp.stack([self_total[3 * rows : 4 * rows], cross_total[3 * rows :]])
+    summed_ffn_in = ffn_total[:in_rows].reshape(-1, rows, width).transpose(1, 0, 2).reshape(rows, -1)
+    summed_ffn_out = ffn_total[in_rows:]
+    summed_vector = self_total[4 * rows, : low_vector.size].reshape(vector_count, -1)
     total_tokens = tokens.shape[0] * lax.axis_size("dp") * lax.axis_size("fsdp")
     grad_scale = 1.0 / math.sqrt(total_tokens)
     qkv_first_new, qkv_second_new, qkv_master_new, qkv_copy = adamw(

time: 1230 us -> 648 us (0.53)
  waiting for transfers between devices: 713 us -> 65.3 us
  starting transfers between devices: 0.55 us -> 58.4 us
  local copies, waits for them, and re-layouts: 86.4 us -> 143 us
  blocking collectives: 44 us -> 0 us
  other arithmetic: 102 us -> 120 us
  between operations: 15.2 us -> 2.59 us
    reduce_scatter x4 -> x0, waiting for transfers between devices: 564 us -> none  [the longest x1 149 us: body(): lax.psum_scatter(grad_qkv, ('dp', 'fsdp'), scatter_dimension=1, tiled=True)]
    all_gather x4 -> x0, waiting for transfers between devices: 75.6 us -> none  [the longest x1 49.3 us: body(): lax.all_gather(low_ffn_out, ('dp', 'fsdp'), axis=0, tiled=True)]
    unnamed x10 -> x0, waiting for transfers between devices: 73.7 us -> none
    ppermute x0 -> x51, waiting for transfers between devices: none -> 65.3 us  [exchange(): return lax.ppermute(values, AXES, [(i, i ^ offset) for i in range(count)])]
    ppermute x0 -> x51, starting transfers between devices: none -> 58.4 us  [exchange(): return lax.ppermute(values, AXES, [(i, i ^ offset) for i in range(count)])]
    all_gather x1 -> x0, blocking collectives: 44 us -> none  [body(): lax.all_gather(low_vector, ('dp', 'fsdp'), axis=1, tiled=True)]
    unnamed x217 -> x286, local copies, waits for them, and re-layouts: 18.8 us -> 43 us
    dot_general x4, matrix products: 7.25 us -> 27.7 us  [block_step(): jnp.einsum('hts,thd->shd', grad_scores, query_heads, preferred_element_ty...]
  transfers between devices with their start and end apart: 9 -> 51, of which waited for: 9 -> 16; matrix products, arithmetic and copies ran while one was open for 14% -> 28% of each run, Pallas kernels for 0% -> 0%
where the time goes in v1:
time: 648 us; the launch traced here: 639 us
  matrix products  248 us (38%)
  local copies, waits for them, and re-layouts  143 us (22%)
  other arithmetic  120 us (19%)
  waiting for transfers between devices  65.3 us (10%)
  starting transfers between devices  58.4 us (9%)
    ppermute x51, waiting for transfers between devices, exchange(): return lax.ppermute(values, AXES, [(i, i ^ offset) for i in range(count)])  65.3 us
    dot_general x8, matrix products, block_scores(): jnp.einsum('thd,shd->hts', query_heads, key_heads, preferred_element_type...  62.7 us
    ppermute x51, starting transfers between devices, exchange(): return lax.ppermute(values, AXES, [(i, i ^ offset) for i in range(count)])  58.4 us
    unnamed x286, local copies, waits for them, and re-layouts  43 us
    convert_element_type x4, other arithmetic, block_step(): grad_scores = (probs * (grad_probs - inner)).astype(jnp.bfloat16)  37.4 us
    dot_general x4, matrix products, block_step(): jnp.einsum('hts,thd->shd', probs_low, grad_heads, preferred_element_type=...  36.3 us
    dot_general x4, matrix products, block_step(): jnp.einsum('hts,thd->shd', grad_scores, query_heads, preferred_element_ty...  27.7 us
    dot_general x10, matrix products, product_right(): lax.dot_general(left, right, (((1,), (1,)), ((), ())), preferred_element_...  27.6 us
  transfers between devices with their start and end apart: 51, of which 16 were waited for; matrix products, arithmetic and copies ran while one was open for 28% of the time, Pallas kernels for 0%

profile of v1, /device:TPU:0, one launch (start us, length us, event | category | flops | bytes accessed | tf_op | source)
XLA Modules:
  0.0 638.9 jit_solution(14093318753890361648)
XLA Ops:
  44.5 13.0 %collective-permute-done.4 = bf16[4,56,512]{2,1,0:T(8,128)(2,1)S(1)} collective-permute-done((bf16[4,56,512]{2,1,0:T(8,128)(2,1)S(1)}, bf16[4,56,512]{2,1,0:T(8,128)(2,1)S(1)}, u32[]{:S(2)}, u32[]{:S(2)}) %collective-permute-start.4) | collective-permute-done | bytes 229408 | tf_op jit(solution)/shard_map/ppermute | solution.py:166
  77.1 9.8 %collective-permute-done.24 = bf16[4,128,512]{2,1,0:T(8,128)(2,1)} collective-permute-done((bf16[4,128,512]{2,1,0:T(8,128)(2,1)}, bf16[4,128,512]{2,1,0:T(8,128)(2,1)}, u32[]{:S(2)}, u32[]{:S(2)}) %collective-permute-start.24) | collective-permute-done | bytes 524320 | tf_op jit(solution)/shard_map/ppermute | solution.py:166
  88.1 37.5 %while.54 = (s32[]{:T(128)}, bf16[2,512,512]{2,1,0:T(8,128)(2,1)}, f32[2,8,512]{2,1,0:T(8,128)S(1)}, s32[2,512]{1,0:T(2,128)S(1)}, s32[1,1024]{1,0:T(1,128)S(1)}...) while((s32[]{:T(128)}, bf16[2,512,512]{2,1,0:T(8,128)(2,1)}, ...), condition=%wide.region_3.4_spmd, body=%wide.region_0.3_spmd.sunk | while | flops 1124593664 | bytes 58862184 | solution.py:82
  93.1 4.2 fusion.236
  97.4 5.8 fusion.237
  111.6 4.2 fusion.236
  115.9 5.8 fusion.237
  142.2 4.1 gather_fusion.1
  160.5 32.6 %while.55 = (s32[]{:T(128)}, bf16[2,512,512]{2,1,0:T(8,128)(2,1)}, f32[2,8,512]{2,1,0:T(8,128)S(1)}, s32[2,512]{1,0:T(2,128)S(1)}, s32[1,1024]{1,0:T(1,128)S(1)}...) while((s32[]{:T(128)}, bf16[2,512,512]{2,1,0:T(8,128)(2,1)}, ...), condition=%wide.region_9.10_spmd, body=%wide.region_6.9_spmd.sunk | while | flops 1124593664 | bytes 58862184 | solution.py:82
  161.0 4.7 fusion.241
  165.7 4.2 fusion.242
  170.0 5.8 fusion.243
  177.3 4.7 fusion.241
  182.0 4.2 fusion.242
  186.2 5.8 fusion.243
  193.2 4.4 fusion.104
  206.5 5.2 gather_fusion.2
  217.8 4.8 multiply_convert_fusion.2
  231.4 8.6 %convert_reduce_fusion = (f32[2048]{0:T(1024)}, bf16[1024,2048]{1,0:T(8,128)(2,1)S(1)}) fusion(f32[1024,2048]{1,0:T(8,128)S(1)} %get-tuple-element.873, f32[2048]{0:T(1024)S(1)} %copy-done.128, bf16[1024,512]{0,1:T(8,128)(2,1)S(1)} %get-tuple-element.785, bf16[2048,512]{1,0:T(8,128)(2,1)S(1)} %bitcast.555), kind=kOutput, calls=%fused_computation.70 | convolution fusion | flops 2195716096 | bytes 15745024 | tf_op jit(solution)/shard_map/dot_general | solution.py:31
  240.1 4.0 multiply_reduce_fusion.2
  244.1 4.4 fusion.86
  248.5 4.5 fusion.116
  257.8 105.8 %while.56 = (s32[]{:T(128)}, f32[1024,8,64]{0,2,1:T(8,128)}, f32[1024,8,64]{0,2,1:T(8,128)}, bf16[2,512,512]{2,1,0:T(8,128)(2,1)}, bf16[2,512,512]{1,2,0:T(8,128...) while((s32[]{:T(128)}, f32[1024,8,64]{0,2,1:T(8,128)}, ...), condition=%wide.region_20.21_spmd.clone, body=%wide.region_18.20_spmd.clone.sunk | while | flops 2725769216 | bytes 190671696 | solution.py:132
  268.6 11.8 %multiply_reduce_fusion.13 = (f32[8,512]{1,0:T(8,128)}, f32[8,512,1024]{2,1,0:T(8,128)}) fusion(f32[8,512,1024]{2,1,0:T(8,128)S(1)} %fusion.254, f32[8,512]{1,0:T(8,128)} %dynamic-slice_bitcast_fusion.4, bf16[512,8,64]{0,2,1:T(8,128)(2,1)} %bitcast.498, bf16[1024,8,64]{0,2,1:T(8,128)(2,1)} %get-tuple-element.1215, ...), kind=kOutput, calls=%fused_computation.30.clone.1 | convolution fusion | flops 557838336 | bytes 35684352 | tf_op jit(solution)/shard_map/while/body/eval_jaxpr/thd,shd->hts/dot_general | solution.py:52
  280.5 9.3 %multiply_convert_fusion.5 = bf16[8,512,1024]{2,1,0:T(8,128)(2,1)} fusion(f32[8,512,1024]{2,1,0:T(8,128)} %get-tuple-element.1113, f32[8,512,1024]{2,1,0:T(8,128)S(1)} %fusion.254, f32[8,512]{1,0:T(8,128)} %get-tuple-element.1114), kind=kLoop, calls=%fused_computation.29.clone.1 | loop fusion | flops 12582912 | bytes 41959424 | tf_op jit(solution)/shard_map/while/body/eval_jaxpr/convert_element_type | solution.py:114
  289.8 6.6 %bitcast_add_fusion.16 = f32[1024,8,64]{0,2,1:T(8,128)} fusion(f32[1024,8,64]{0,2,1:T(8,128)} %get-tuple-element.1196, bf16[512,8,64]{0,2,1:T(8,128)(2,1)} %bitcast.499, bf16[8,512,1024]{2,1,0:T(8,128)(2,1)} %multiply_convert_fusion.5, pred[]{:T(512)S(6)} %compare.19), kind=kOutput, calls=%fused_computation.35.clone.1 | convolution fusion | flops 538443776 | bytes 13107201 | tf_op jit(solution)/shard_map/while/body/eval_jaxpr/hts,thd->shd/dot_general | solution.py:121
  301.4 8.8 %bitcast_add_fusion.17 = f32[1024,8,64]{0,2,1:T(8,128)} fusion(f32[1024,8,64]{0,2,1:T(8,128)} %get-tuple-element.1197, bf16[512,8,64]{0,2,1:T(8,128)(2,1)S(1)} %bitcast.495, f32[8,512,1024]{2,1,0:T(8,128)} %get-tuple-element.1113, pred[]{:T(512)S(6)} %compare.19), kind=kOutput, calls=%fused_computation.34.clone.1 | convolution fusion | flops 542113792 | bytes 21495808 | tf_op jit(solution)/shard_map/while/body/eval_jaxpr/hts,thd->shd/dot_general | solution.py:107
  320.9 11.8 %multiply_reduce_fusion.13 = (f32[8,512]{1,0:T(8,128)}, f32[8,512,1024]{2,1,0:T(8,128)}) fusion(f32[8,512,1024]{2,1,0:T(8,128)S(1)} %fusion.254, f32[8,512]{1,0:T(8,128)} %dynamic-slice_bitcast_fusion.4, bf16[512,8,64]{0,2,1:T(8,128)(2,1)} %bitcast.498, bf16[1024,8,64]{0,2,1:T(8,128)(2,1)} %get-tuple-element.1215, ...), kind=kOutput, calls=%fused_computation.30.clone.1 | convolution fusion | flops 557838336 | bytes 35684352 | tf_op jit(solution)/shard_map/while/body/eval_jaxpr/thd,shd->hts/dot_general | solution.py:52
  332.7 9.3 %multiply_convert_fusion.5 = bf16[8,512,1024]{2,1,0:T(8,128)(2,1)} fusion(f32[8,512,1024]{2,1,0:T(8,128)} %get-tuple-element.1113, f32[8,512,1024]{2,1,0:T(8,128)S(1)} %fusion.254, f32[8,512]{1,0:T(8,128)} %get-tuple-element.1114), kind=kLoop, calls=%fused_computation.29.clone.1 | loop fusion | flops 12582912 | bytes 41959424 | tf_op jit(solution)/shard_map/while/body/eval_jaxpr/convert_element_type | solution.py:114
  342.0 7.2 %bitcast_add_fusion.16 = f32[1024,8,64]{0,2,1:T(8,128)} fusion(f32[1024,8,64]{0,2,1:T(8,128)} %get-tuple-element.1196, bf16[512,8,64]{0,2,1:T(8,128)(2,1)} %bitcast.499, bf16[8,512,1024]{2,1,0:T(8,128)(2,1)} %multiply_convert_fusion.5, pred[]{:T(512)S(6)} %compare.19), kind=kOutput, calls=%fused_computation.35.clone.1 | convolution fusion | flops 538443776 | bytes 13107201 | tf_op jit(solution)/shard_map/while/body/eval_jaxpr/hts,thd->shd/dot_general | solution.py:121
  354.2 9.4 %bitcast_add_fusion.17 = f32[1024,8,64]{0,2,1:T(8,128)} fusion(f32[1024,8,64]{0,2,1:T(8,128)} %get-tuple-element.1197, bf16[512,8,64]{0,2,1:T(8,128)(2,1)S(1)} %bitcast.495, f32[8,512,1024]{2,1,0:T(8,128)} %get-tuple-element.1113, pred[]{:T(512)S(6)} %compare.19), kind=kOutput, calls=%fused_computation.34.clone.1 | convolution fusion | flops 542113792 | bytes 21495808 | tf_op jit(solution)/shard_map/while/body/eval_jaxpr/hts,thd->shd/dot_general | solution.py:107
  365.6 4.7 multiply_reduce_fusion.3
  374.2 97.6 %while.57 = (s32[]{:T(128)}, f32[1024,8,64]{0,2,1:T(8,128)}, f32[1024,8,64]{0,2,1:T(8,128)}, bf16[2,512,512]{2,1,0:T(8,128)(2,1)}, bf16[2,512,512]{1,2,0:T(8,128...) while((s32[]{:T(128)}, f32[1024,8,64]{0,2,1:T(8,128)}, ...), condition=%wide.region_25.26_spmd.clone, body=%wide.region_23.25_spmd.clone.sunk | while | flops 2725769216 | bytes 198929264 | solution.py:132
  382.0 11.8 %multiply_reduce_fusion.14 = (f32[8,512]{1,0:T(8,128)}, f32[8,512,1024]{2,1,0:T(8,128)}) fusion(f32[8,512,1024]{2,1,0:T(8,128)S(1)} %fusion.265, f32[8,512]{1,0:T(8,128)} %dynamic-slice_bitcast_fusion.5, bf16[512,8,64]{0,2,1:T(8,128)(2,1)} %bitcast.500, bf16[1024,8,64]{0,2,1:T(8,128)(2,1)} %get-tuple-element.1254, ...), kind=kOutput, calls=%fused_computation.44.clone.1 | convolution fusion | flops 557838336 | bytes 35684352 | tf_op jit(solution)/shard_map/while/body/eval_jaxpr/thd,shd->hts/dot_general | solution.py:52
  393.9 9.3 %multiply_convert_fusion.6 = bf16[8,512,1024]{2,1,0:T(8,128)(2,1)} fusion(f32[8,512,1024]{2,1,0:T(8,128)} %get-tuple-element.1126, f32[8,512,1024]{2,1,0:T(8,128)S(1)} %fusion.265, f32[8,512]{1,0:T(8,128)} %get-tuple-element.1127), kind=kLoop, calls=%fused_computation.43.clone.1 | loop fusion | flops 12582912 | bytes 41959424 | tf_op jit(solution)/shard_map/while/body/eval_jaxpr/convert_element_type | solution.py:114
  403.2 6.6 %bitcast_add_fusion.18 = f32[1024,8,64]{0,2,1:T(8,128)} fusion(f32[1024,8,64]{0,2,1:T(8,128)} %get-tuple-element.1235, bf16[512,8,64]{0,2,1:T(8,128)(2,1)} %bitcast.501, bf16[8,512,1024]{2,1,0:T(8,128)(2,1)} %multiply_convert_fusion.6, pred[]{:T(512)S(6)} %compare.20), kind=kOutput, calls=%fused_computation.49.clone.1 | convolution fusion | flops 538443776 | bytes 13107201 | tf_op jit(solution)/shard_map/while/body/eval_jaxpr/hts,thd->shd/dot_general | solution.py:121
  413.6 8.8 %bitcast_add_fusion.19 = f32[1024,8,64]{0,2,1:T(8,128)} fusion(f32[1024,8,64]{0,2,1:T(8,128)} %get-tuple-element.1236, bf16[512,8,64]{0,2,1:T(8,128)(2,1)S(1)} %bitcast.497, f32[8,512,1024]{2,1,0:T(8,128)} %get-tuple-element.1126, pred[]{:T(512)S(6)} %compare.20), kind=kOutput, calls=%fused_computation.48.clone.1 | convolution fusion | flops 542113792 | bytes 21495808 | tf_op jit(solution)/shard_map/while/body/eval_jaxpr/hts,thd->shd/dot_general | solution.py:107
  430.0 11.8 %multiply_reduce_fusion.14 = (f32[8,512]{1,0:T(8,128)}, f32[8,512,1024]{2,1,0:T(8,128)}) fusion(f32[8,512,1024]{2,1,0:T(8,128)S(1)} %fusion.265, f32[8,512]{1,0:T(8,128)} %dynamic-slice_bitcast_fusion.5, bf16[512,8,64]{0,2,1:T(8,128)(2,1)} %bitcast.500, bf16[1024,8,64]{0,2,1:T(8,128)(2,1)} %get-tuple-element.1254, ...), kind=kOutput, calls=%fused_computation.44.clone.1 | convolution fusion | flops 557838336 | bytes 35684352 | tf_op jit(solution)/shard_map/while/body/eval_jaxpr/thd,shd->hts/dot_general | solution.py:52
  441.8 9.3 %multiply_convert_fusion.6 = bf16[8,512,1024]{2,1,0:T(8,128)(2,1)} fusion(f32[8,512,1024]{2,1,0:T(8,128)} %get-tuple-element.1126, f32[8,512,1024]{2,1,0:T(8,128)S(1)} %fusion.265, f32[8,512]{1,0:T(8,128)} %get-tuple-element.1127), kind=kLoop, calls=%fused_computation.43.clone.1 | loop fusion | flops 12582912 | bytes 41959424 | tf_op jit(solution)/shard_map/while/body/eval_jaxpr/convert_element_type | solution.py:114
  451.1 7.2 %bitcast_add_fusion.18 = f32[1024,8,64]{0,2,1:T(8,128)} fusion(f32[1024,8,64]{0,2,1:T(8,128)} %get-tuple-element.1235, bf16[512,8,64]{0,2,1:T(8,128)(2,1)} %bitcast.501, bf16[8,512,1024]{2,1,0:T(8,128)(2,1)} %multiply_convert_fusion.6, pred[]{:T(512)S(6)} %compare.20), kind=kOutput, calls=%fused_computation.49.clone.1 | convolution fusion | flops 538443776 | bytes 13107201 | tf_op jit(solution)/shard_map/while/body/eval_jaxpr/hts,thd->shd/dot_general | solution.py:121
  462.1 9.3 %bitcast_add_fusion.19 = f32[1024,8,64]{0,2,1:T(8,128)} fusion(f32[1024,8,64]{0,2,1:T(8,128)} %get-tuple-element.1236, bf16[512,8,64]{0,2,1:T(8,128)(2,1)S(1)} %bitcast.497, f32[8,512,1024]{2,1,0:T(8,128)} %get-tuple-element.1126, pred[]{:T(512)S(6)} %compare.20), kind=kOutput, calls=%fused_computation.48.clone.1 | convolution fusion | flops 542113792 | bytes 21495808 | tf_op jit(solution)/shard_map/while/body/eval_jaxpr/hts,thd->shd/dot_general | solution.py:107
  513.9 6.2 reshape.662
  520.1 4.1 copy.363
  560.9 3.9 collective-permute-done.39
  572.6 3.9 collective-permute-done.32
  578.3 4.1 collective-permute-start.35
  611.1 9.1 %collective-permute-done.46 = bf16[4,128,512]{2,1,0:T(8,128)(2,1)} collective-permute-done((bf16[4,128,512]{2,1,0:T(8,128)(2,1)S(1)}, bf16[4,128,512]{2,1,0:T(8,128)(2,1)}, u32[]{:S(2)}, u32[]{:S(2)}) %collective-permute-start.46) | collective-permute-done | bytes 524320 | tf_op jit(solution)/shard_map/ppermute | solution.py:166
  629.1 7.8 %collective-permute-done.49 = bf16[128,512]{1,0:T(8,128)(2,1)S(1)} collective-permute-done((bf16[128,512]{1,0:T(8,128)(2,1)S(1)}, bf16[128,512]{1,0:T(8,128)(2,1)S(1)}, u32[]{:S(2)}, u32[]{:S(2)}) %collective-permute-start.49) | collective-permute-done | bytes 131104 | tf_op jit(solution)/shard_map/ppermute | solution.py:166
  (691 shorter events, 329.9 us)
Async XLA Ops:
  3.4 20.6 %collective-permute-start = (bf16[56,512]{1,0:T(8,128)(2,1)}, bf16[56,512]{1,0:T(8,128)(2,1)}, u32[]{:S(2)}, u32[]{:S(2)}) collective-permute-start(bf16[56,512]{1,0:T(8,128)(2,1)} %get-tuple-element.865), channel_id=1, source_target_pairs={{0,2},{1,3},{2,0},{3,1},{4,6},{5,7},{6,4},{7,5},{8,10},{9,11},{10,... | collective-permute-start | bytes 172040 | tf_op jit(solution)/shard_map/ppermute | solution.py:166
  6.4 17.6 %collective-permute-start.1 = (bf16[56,512]{1,0:T(8,128)(2,1)}, bf16[56,512]{1,0:T(8,128)(2,1)}, u32[]{:S(2)}, u32[]{:S(2)}) collective-permute-start(bf16[56,512]{1,0:T(8,128)(2,1)} %get-tuple-element.865), channel_id=1, source_target_pairs={{0,4},{1,5},{2,6},{3,7},{4,0},{5,1},{6,2},{7,3},{8,12},{9,13},{10,... | collective-permute-start | bytes 172040 | tf_op jit(solution)/shard_map/ppermute | solution.py:166
  9.0 15.6 %collective-permute-start.2 = (bf16[56,512]{1,0:T(8,128)(2,1)}, bf16[56,512]{1,0:T(8,128)(2,1)}, u32[]{:S(2)}, u32[]{:S(2)}) collective-permute-start(bf16[56,512]{1,0:T(8,128)(2,1)} %get-tuple-element.865), channel_id=1, source_target_pairs={{0,6},{1,7},{2,4},{3,5},{4,2},{5,3},{6,0},{7,1},{8,14},{9,15},{10,... | collective-permute-start | bytes 172040 | tf_op jit(solution)/shard_map/ppermute | solution.py:166
  10.5 18.8 %collective-permute-start.10 = (bf16[80,512]{1,0:T(8,128)(2,1)}, bf16[80,512]{1,0:T(8,128)(2,1)S(1)}, u32[]{:S(2)}, u32[]{:S(2)}) collective-permute-start(bf16[80,512]{1,0:T(8,128)(2,1)} %get-tuple-element.863), channel_id=1, source_target_pairs={{0,2},{1,3},{2,0},{3,1},{4,6},{5,7},{6,4},{7,5},{8,10},{9,11},{10,... | collective-permute-start | bytes 245768 | tf_op jit(solution)/shard_map/ppermute | solution.py:166
  11.4 18.1 %collective-permute-start.11 = (bf16[80,512]{1,0:T(8,128)(2,1)}, bf16[80,512]{1,0:T(8,128)(2,1)}, u32[]{:S(2)}, u32[]{:S(2)}) collective-permute-start(bf16[80,512]{1,0:T(8,128)(2,1)} %get-tuple-element.863), channel_id=1, source_target_pairs={{0,4},{1,5},{2,6},{3,7},{4,0},{5,1},{6,2},{7,3},{8,12},{9,13},{10,... | collective-permute-start | bytes 245768 | tf_op jit(solution)/shard_map/ppermute | solution.py:166
  24.0 7.5 %collective-permute-start.12 = (bf16[80,512]{1,0:T(8,128)(2,1)}, bf16[80,512]{1,0:T(8,128)(2,1)S(1)}, u32[]{:S(2)}, u32[]{:S(2)}) collective-permute-start(bf16[80,512]{1,0:T(8,128)(2,1)} %get-tuple-element.863), channel_id=1, source_target_pairs={{0,6},{1,7},{2,4},{3,5},{4,2},{5,3},{6,0},{7,1},{8,14},{9,15},{10,... | collective-permute-start | bytes 245768 | tf_op jit(solution)/shard_map/ppermute | solution.py:166
  24.0 10.6 %collective-permute-start.20 = (bf16[128,512]{1,0:T(8,128)(2,1)S(1)}, bf16[128,512]{1,0:T(8,128)(2,1)S(1)}, u32[]{:S(2)}, u32[]{:S(2)}) collective-permute-start(bf16[128,512]{1,0:T(8,128)(2,1)S(1)} %copy-done.85), channel_id=1, source_target_pairs={{0,2},{1,3},{2,0},{3,1},{4,6},{5,7},{6,4},{7,5},{8,10},{9,11},{10,... | collective-permute-start | bytes 393224 | tf_op jit(solution)/shard_map/ppermute | solution.py:166
  24.5 14.4 %collective-permute-start.21 = (bf16[128,512]{1,0:T(8,128)(2,1)S(1)}, bf16[128,512]{1,0:T(8,128)(2,1)S(1)}, u32[]{:S(2)}, u32[]{:S(2)}) collective-permute-start(bf16[128,512]{1,0:T(8,128)(2,1)S(1)} %copy-done.85), channel_id=1, source_target_pairs={{0,4},{1,5},{2,6},{3,7},{4,0},{5,1},{6,2},{7,3},{8,12},{9,13},{10,... | collective-permute-start | bytes 393224 | tf_op jit(solution)/shard_map/ppermute | solution.py:166
  29.3 11.2 %collective-permute-start.22 = (bf16[128,512]{1,0:T(8,128)(2,1)S(1)}, bf16[128,512]{1,0:T(8,128)(2,1)S(1)}, u32[]{:S(2)}, u32[]{:S(2)}) collective-permute-start(bf16[128,512]{1,0:T(8,128)(2,1)S(1)} %copy-done.85), channel_id=1, source_target_pairs={{0,6},{1,7},{2,4},{3,5},{4,2},{5,3},{6,0},{7,1},{8,14},{9,15},{10,... | collective-permute-start | bytes 393224 | tf_op jit(solution)/shard_map/ppermute | solution.py:166
  29.4 12.5 %collective-permute-start.3 = (bf16[4,56,512]{2,1,0:T(8,128)(2,1)S(1)}, bf16[4,56,512]{2,1,0:T(8,128)(2,1)S(1)}, u32[]{:S(2)}, u32[]{:S(2)}) collective-permute-start(bf16[4,56,512]{2,1,0:T(8,128)(2,1)S(1)} %get-tuple-element.842), channel_id=1, source_target_pairs={{0,8},{1,9},{2,10},{3,11},{4,12},{5,13},{6,14},{7,15},{8,0},{9,1},... | collective-permute-start | bytes 688136 | tf_op jit(solution)/shard_map/ppermute | solution.py:166
  33.1 24.8 %collective-permute-start.13 = (bf16[4,80,512]{2,1,0:T(8,128)(2,1)}, bf16[4,80,512]{2,1,0:T(8,128)(2,1)}, u32[]{:S(2)}, u32[]{:S(2)}) collective-permute-start(bf16[4,80,512]{2,1,0:T(8,128)(2,1)} %get-tuple-element.838), channel_id=1, source_target_pairs={{0,8},{1,9},{2,10},{3,11},{4,12},{5,13},{6,14},{7,15},{8,0},{9,1},... | collective-permute-start | bytes 983048 | tf_op jit(solution)/shard_map/ppermute | solution.py:166
  34.6 23.4 %collective-permute-start.14 = (bf16[4,80,512]{2,1,0:T(8,128)(2,1)}, bf16[4,80,512]{2,1,0:T(8,128)(2,1)}, u32[]{:S(2)}, u32[]{:S(2)}) collective-permute-start(bf16[4,80,512]{2,1,0:T(8,128)(2,1)} %get-tuple-element.838), channel_id=1, source_target_pairs={{0,16},{1,17},{2,18},{3,19},{4,20},{5,21},{6,22},{7,23},{8,24},{9,... | collective-permute-start | bytes 983048 | tf_op jit(solution)/shard_map/ppermute | solution.py:166
  38.9 18.5 %collective-permute-start.4 = (bf16[4,56,512]{2,1,0:T(8,128)(2,1)S(1)}, bf16[4,56,512]{2,1,0:T(8,128)(2,1)S(1)}, u32[]{:S(2)}, u32[]{:S(2)}) collective-permute-start(bf16[4,56,512]{2,1,0:T(8,128)(2,1)S(1)} %get-tuple-element.842), channel_id=1, source_target_pairs={{0,16},{1,17},{2,18},{3,19},{4,20},{5,21},{6,22},{7,23},{8,24},{9,... | collective-permute-start | bytes 688136 | tf_op jit(solution)/shard_map/ppermute | solution.py:166
  40.5 17.0 %collective-permute-start.5 = (bf16[4,56,512]{2,1,0:T(8,128)(2,1)S(1)}, bf16[4,56,512]{2,1,0:T(8,128)(2,1)S(1)}, u32[]{:S(2)}, u32[]{:S(2)}) collective-permute-start(bf16[4,56,512]{2,1,0:T(8,128)(2,1)S(1)} %get-tuple-element.842), channel_id=1, source_target_pairs={{0,24},{1,25},{2,26},{3,27},{4,28},{5,29},{6,30},{7,31},{8,16},{9,... | collective-permute-start | bytes 688136 | tf_op jit(solution)/shard_map/ppermute | solution.py:166
  41.9 16.7 %collective-permute-start.15 = (bf16[4,80,512]{2,1,0:T(8,128)(2,1)}, bf16[4,80,512]{2,1,0:T(8,128)(2,1)}, u32[]{:S(2)}, u32[]{:S(2)}) collective-permute-start(bf16[4,80,512]{2,1,0:T(8,128)(2,1)} %get-tuple-element.838), channel_id=1, source_target_pairs={{0,24},{1,25},{2,26},{3,27},{4,28},{5,29},{6,30},{7,31},{8,16},{9,... | collective-permute-start | bytes 983048 | tf_op jit(solution)/shard_map/ppermute | solution.py:166
  57.9 6.0 collective-permute-start.8
  58.0 6.6 %collective-permute-start.9 = (bf16[4,56,512]{2,1,0:T(8,128)(2,1)S(1)}, bf16[4,56,512]{2,1,0:T(8,128)(2,1)S(1)}, u32[]{:S(2)}, u32[]{:S(2)}) collective-permute-start(bf16[4,56,512]{2,1,0:T(8,128)(2,1)S(1)} %collective-permute-done.5), channel_id=1, source_target_pairs={{0,1},{1,0},{2,3},{3,2},{4,5},{5,4},{6,7},{7,6},{8,9},{9,8},{10,11... | collective-permute-start | bytes 688136 | tf_op jit(solution)/shard_map/ppermute | solution.py:166
  58.6 79.7 %collective-permute-start.16 = (bf16[4,80,512]{2,1,0:T(8,128)(2,1)}, bf16[4,80,512]{2,1,0:T(8,128)(2,1)}, u32[]{:S(2)}, u32[]{:S(2)}) collective-permute-start(bf16[4,80,512]{2,1,0:T(8,128)(2,1)} %get-tuple-element.838), channel_id=1, source_target_pairs={{0,1},{1,0},{2,3},{3,2},{4,5},{5,4},{6,7},{7,6},{8,9},{9,8},{10,11... | collective-permute-start | bytes 983048 | tf_op jit(solution)/shard_map/ppermute | solution.py:166
  61.1 15.4 %collective-permute-start.23 = (bf16[4,128,512]{2,1,0:T(8,128)(2,1)}, bf16[4,128,512]{2,1,0:T(8,128)(2,1)}, u32[]{:S(2)}, u32[]{:S(2)}) collective-permute-start(bf16[4,128,512]{2,1,0:T(8,128)(2,1)} %get-tuple-element.836), channel_id=1, source_target_pairs={{0,8},{1,9},{2,10},{3,11},{4,12},{5,13},{6,14},{7,15},{8,0},{9,1},... | collective-permute-start | bytes 1572872 | tf_op jit(solution)/shard_map/ppermute | solution.py:166
  62.4 24.6 %collective-permute-start.24 = (bf16[4,128,512]{2,1,0:T(8,128)(2,1)}, bf16[4,128,512]{2,1,0:T(8,128)(2,1)}, u32[]{:S(2)}, u32[]{:S(2)}) collective-permute-start(bf16[4,128,512]{2,1,0:T(8,128)(2,1)} %get-tuple-element.836), channel_id=1, source_target_pairs={{0,16},{1,17},{2,18},{3,19},{4,20},{5,21},{6,22},{7,23},{8,24},{9,... | collective-permute-start | bytes 1572872 | tf_op jit(solution)/shard_map/ppermute | solution.py:166
  63.9 70.8 %collective-permute-start.25 = (bf16[4,128,512]{2,1,0:T(8,128)(2,1)}, bf16[4,128,512]{2,1,0:T(8,128)(2,1)}, u32[]{:S(2)}, u32[]{:S(2)}) collective-permute-start(bf16[4,128,512]{2,1,0:T(8,128)(2,1)} %get-tuple-element.836), channel_id=1, source_target_pairs={{0,24},{1,25},{2,26},{3,27},{4,28},{5,29},{6,30},{7,31},{8,16},{9,... | collective-permute-start | bytes 1572872 | tf_op jit(solution)/shard_map/ppermute | solution.py:166
  64.6 73.8 %collective-permute-start.17 = (bf16[4,80,512]{2,1,0:T(8,128)(2,1)}, bf16[4,80,512]{2,1,0:T(8,128)(2,1)}, u32[]{:S(2)}, u32[]{:S(2)}) collective-permute-start(bf16[4,80,512]{2,1,0:T(8,128)(2,1)} %collective-permute-done.13), channel_id=1, source_target_pairs={{0,1},{1,0},{2,3},{3,2},{4,5},{5,4},{6,7},{7,6},{8,9},{9,8},{10,11... | collective-permute-start | bytes 983048 | tf_op jit(solution)/shard_map/ppermute | solution.py:166
  76.6 62.3 %collective-permute-start.18 = (bf16[4,80,512]{2,1,0:T(8,128)(2,1)}, bf16[4,80,512]{2,1,0:T(8,128)(2,1)}, u32[]{:S(2)}, u32[]{:S(2)}) collective-permute-start(bf16[4,80,512]{2,1,0:T(8,128)(2,1)} %collective-permute-done.14), channel_id=1, source_target_pairs={{0,1},{1,0},{2,3},{3,2},{4,5},{5,4},{6,7},{7,6},{8,9},{9,8},{10,11... | collective-permute-start | bytes 983048 | tf_op jit(solution)/shard_map/ppermute | solution.py:166
  86.9 52.1 %collective-permute-start.19 = (bf16[4,80,512]{2,1,0:T(8,128)(2,1)}, bf16[4,80,512]{2,1,0:T(8,128)(2,1)}, u32[]{:S(2)}, u32[]{:S(2)}) collective-permute-start(bf16[4,80,512]{2,1,0:T(8,128)(2,1)} %collective-permute-done.15), channel_id=1, source_target_pairs={{0,1},{1,0},{2,3},{3,2},{4,5},{5,4},{6,7},{7,6},{8,9},{9,8},{10,11... | collective-permute-start | bytes 983048 | tf_op jit(solution)/shard_map/ppermute | solution.py:166
  134.7 67.2 %collective-permute-start.26 = (bf16[4,128,512]{2,1,0:T(8,128)(2,1)}, bf16[4,128,512]{2,1,0:T(8,128)(2,1)}, u32[]{:S(2)}, u32[]{:S(2)}) collective-permute-start(bf16[4,128,512]{2,1,0:T(8,128)(2,1)} %get-tuple-element.836), channel_id=1, source_target_pairs={{0,1},{1,0},{2,3},{3,2},{4,5},{5,4},{6,7},{7,6},{8,9},{9,8},{10,11... | collective-permute-start | bytes 1572872 | tf_op jit(solution)/shard_map/ppermute | solution.py:166
  138.3 63.5 %collective-permute-start.27 = (bf16[4,128,512]{2,1,0:T(8,128)(2,1)}, bf16[4,128,512]{2,1,0:T(8,128)(2,1)}, u32[]{:S(2)}, u32[]{:S(2)}) collective-permute-start(bf16[4,128,512]{2,1,0:T(8,128)(2,1)} %collective-permute-done.23), channel_id=1, source_target_pairs={{0,1},{1,0},{2,3},{3,2},{4,5},{5,4},{6,7},{7,6},{8,9},{9,8},{10,11... | collective-permute-start | bytes 1572872 | tf_op jit(solution)/shard_map/ppermute | solution.py:166
  138.4 63.5 %collective-permute-start.28 = (bf16[4,128,512]{2,1,0:T(8,128)(2,1)}, bf16[4,128,512]{2,1,0:T(8,128)(2,1)}, u32[]{:S(2)}, u32[]{:S(2)}) collective-permute-start(bf16[4,128,512]{2,1,0:T(8,128)(2,1)} %collective-permute-done.24), channel_id=1, source_target_pairs={{0,1},{1,0},{2,3},{3,2},{4,5},{5,4},{6,7},{7,6},{8,9},{9,8},{10,11... | collective-permute-start | bytes 1572872 | tf_op jit(solution)/shard_map/ppermute | solution.py:166
  138.9 63.0 %collective-permute-start.29 = (bf16[4,128,512]{2,1,0:T(8,128)(2,1)}, bf16[4,128,512]{2,1,0:T(8,128)(2,1)}, u32[]{:S(2)}, u32[]{:S(2)}) collective-permute-start(bf16[4,128,512]{2,1,0:T(8,128)(2,1)} %collective-permute-done.25), channel_id=1, source_target_pairs={{0,1},{1,0},{2,3},{3,2},{4,5},{5,4},{6,7},{7,6},{8,9},{9,8},{10,11... | collective-permute-start | bytes 1572872 | tf_op jit(solution)/shard_map/ppermute | solution.py:166
  513.5 39.7 %collective-permute-start.30 = (bf16[4,4,65,512]{3,1,2,0:T(4,128)(2,1)}, bf16[4,4,65,512]{3,1,2,0:T(4,128)(2,1)}, u32[]{:S(2)}, u32[]{:S(2)}) collective-permute-start(bf16[4,4,65,512]{3,1,2,0:T(4,128)(2,1)} %copy.359), channel_id=1, source_target_pairs={{0,1},{1,0},{2,3},{3,2},{4,5},{5,4},{6,7},{7,6},{8,9},{9,8},{10,11... | collective-permute-start | bytes 3194888 | tf_op jit(solution)/shard_map/ppermute | solution.py:166
  527.0 62.5 %collective-permute-start.44 = (bf16[4,4,128,512]{3,2,1,0:T(8,128)(2,1)}, bf16[4,4,128,512]{3,2,1,0:T(8,128)(2,1)}, u32[]{:S(2)}, u32[]{:S(2)}) collective-permute-start(bf16[4,4,128,512]{3,2,1,0:T(8,128)(2,1)} %fusion.34), channel_id=1, source_target_pairs={{0,1},{1,0},{2,3},{3,2},{4,5},{5,4},{6,7},{7,6},{8,9},{9,8},{10,11... | collective-permute-start | bytes 6291464 | tf_op jit(solution)/shard_map/ppermute | solution.py:166
  536.5 10.1 %collective-permute-start.37 = (bf16[4,4,64,512]{3,2,1,0:T(8,128)(2,1)}, bf16[4,4,64,512]{3,2,1,0:T(8,128)(2,1)}, u32[]{:S(2)}, u32[]{:S(2)}) collective-permute-start(bf16[4,4,64,512]{3,2,1,0:T(8,128)(2,1)} %fusion.38), channel_id=1, source_target_pairs={{0,1},{1,0},{2,3},{3,2},{4,5},{5,4},{6,7},{7,6},{8,9},{9,8},{10,11... | collective-permute-start | bytes 3145736 | tf_op jit(solution)/shard_map/ppermute | solution.py:166
  549.2 9.2 %collective-permute-start.38 = (bf16[4,64,512]{2,1,0:T(8,128)(2,1)S(1)}, bf16[4,64,512]{2,1,0:T(8,128)(2,1)S(1)}, u32[]{:S(2)}, u32[]{:S(2)}) collective-permute-start(bf16[4,64,512]{2,1,0:T(8,128)(2,1)S(1)} %get-tuple-element.815), channel_id=1, source_target_pairs={{0,8},{1,9},{2,10},{3,11},{4,12},{5,13},{6,14},{7,15},{8,0},{9,1},... | collective-permute-start | bytes 786440 | tf_op jit(solution)/shard_map/ppermute | solution.py:166
  550.1 14.8 %collective-permute-start.39 = (bf16[4,64,512]{2,1,0:T(8,128)(2,1)S(1)}, bf16[4,64,512]{2,1,0:T(8,128)(2,1)S(1)}, u32[]{:S(2)}, u32[]{:S(2)}) collective-permute-start(bf16[4,64,512]{2,1,0:T(8,128)(2,1)S(1)} %get-tuple-element.817), channel_id=1, source_target_pairs={{0,16},{1,17},{2,18},{3,19},{4,20},{5,21},{6,22},{7,23},{8,24},{9,... | collective-permute-start | bytes 786440 | tf_op jit(solution)/shard_map/ppermute | solution.py:166
  552.5 15.5 %collective-permute-start.40 = (bf16[4,64,512]{2,1,0:T(8,128)(2,1)S(1)}, bf16[4,64,512]{2,1,0:T(8,128)(2,1)S(1)}, u32[]{:S(2)}, u32[]{:S(2)}) collective-permute-start(bf16[4,64,512]{2,1,0:T(8,128)(2,1)S(1)} %get-tuple-element.816), channel_id=1, source_target_pairs={{0,24},{1,25},{2,26},{3,27},{4,28},{5,29},{6,30},{7,31},{8,16},{9,... | collective-permute-start | bytes 786440 | tf_op jit(solution)/shard_map/ppermute | solution.py:166
  555.8 14.7 %collective-permute-start.31 = (bf16[4,65,512]{2,1,0:T(8,128)(2,1)S(1)}, bf16[4,65,512]{2,1,0:T(8,128)(2,1)S(1)}, u32[]{:S(2)}, u32[]{:S(2)}) collective-permute-start(bf16[4,65,512]{2,1,0:T(8,128)(2,1)S(1)} %get-tuple-element.811), channel_id=1, source_target_pairs={{0,8},{1,9},{2,10},{3,11},{4,12},{5,13},{6,14},{7,15},{8,0},{9,1},... | collective-permute-start | bytes 798728 | tf_op jit(solution)/shard_map/ppermute | solution.py:166
  558.4 18.0 %collective-permute-start.32 = (bf16[4,65,512]{2,1,0:T(8,128)(2,1)S(1)}, bf16[4,65,512]{2,1,0:T(8,128)(2,1)S(1)}, u32[]{:S(2)}, u32[]{:S(2)}) collective-permute-start(bf16[4,65,512]{2,1,0:T(8,128)(2,1)S(1)} %get-tuple-element.813), channel_id=1, source_target_pairs={{0,16},{1,17},{2,18},{3,19},{4,20},{5,21},{6,22},{7,23},{8,24},{9,... | collective-permute-start | bytes 798728 | tf_op jit(solution)/shard_map/ppermute | solution.py:166
  564.9 13.0 %collective-permute-start.33 = (bf16[4,65,512]{2,1,0:T(8,128)(2,1)S(1)}, bf16[4,65,512]{2,1,0:T(8,128)(2,1)S(1)}, u32[]{:S(2)}, u32[]{:S(2)}) collective-permute-start(bf16[4,65,512]{2,1,0:T(8,128)(2,1)S(1)} %get-tuple-element.812), channel_id=1, source_target_pairs={{0,24},{1,25},{2,26},{3,27},{4,28},{5,29},{6,30},{7,31},{8,16},{9,... | collective-permute-start | bytes 798728 | tf_op jit(solution)/shard_map/ppermute | solution.py:166
  568.3 10.1 %collective-permute-start.41 = (bf16[64,512]{1,0:T(8,128)(2,1)S(1)}, bf16[64,512]{1,0:T(8,128)(2,1)S(1)}, u32[]{:S(2)}, u32[]{:S(2)}) collective-permute-start(bf16[64,512]{1,0:T(8,128)(2,1)S(1)} %get-tuple-element.832), channel_id=1, source_target_pairs={{0,2},{1,3},{2,0},{3,1},{4,6},{5,7},{6,4},{7,5},{8,10},{9,11},{10,... | collective-permute-start | bytes 196616 | tf_op jit(solution)/shard_map/ppermute | solution.py:166
  570.4 12.0 %collective-permute-start.42 = (bf16[64,512]{1,0:T(8,128)(2,1)S(1)}, bf16[64,512]{1,0:T(8,128)(2,1)S(1)}, u32[]{:S(2)}, u32[]{:S(2)}) collective-permute-start(bf16[64,512]{1,0:T(8,128)(2,1)S(1)} %get-tuple-element.834), channel_id=1, source_target_pairs={{0,4},{1,5},{2,6},{3,7},{4,0},{5,1},{6,2},{7,3},{8,12},{9,13},{10,... | collective-permute-start | bytes 196616 | tf_op jit(solution)/shard_map/ppermute | solution.py:166
  576.4 6.6 %collective-permute-start.43 = (bf16[64,512]{1,0:T(8,128)(2,1)S(1)}, bf16[64,512]{1,0:T(8,128)(2,1)S(1)}, u32[]{:S(2)}, u32[]{:S(2)}) collective-permute-start(bf16[64,512]{1,0:T(8,128)(2,1)S(1)} %get-tuple-element.833), channel_id=1, source_target_pairs={{0,6},{1,7},{2,4},{3,5},{4,2},{5,3},{6,0},{7,1},{8,14},{9,15},{10,... | collective-permute-start | bytes 196616 | tf_op jit(solution)/shard_map/ppermute | solution.py:166
  578.3 9.1 %collective-permute-start.35 = (bf16[65,512]{1,0:T(8,128)(2,1)S(1)}, bf16[65,512]{1,0:T(8,128)(2,1)S(1)}, u32[]{:S(2)}, u32[]{:S(2)}) collective-permute-start(bf16[65,512]{1,0:T(8,128)(2,1)S(1)} %get-tuple-element.831), channel_id=1, source_target_pairs={{0,4},{1,5},{2,6},{3,7},{4,0},{5,1},{6,2},{7,3},{8,12},{9,13},{10,... | collective-permute-start | bytes 199688 | tf_op jit(solution)/shard_map/ppermute | solution.py:166
  582.4 6.3 collective-permute-start.36
  595.3 15.8 %collective-permute-start.45 = (bf16[4,128,512]{2,1,0:T(8,128)(2,1)S(1)}, bf16[4,128,512]{2,1,0:T(8,128)(2,1)}, u32[]{:S(2)}, u32[]{:S(2)}) collective-permute-start(bf16[4,128,512]{2,1,0:T(8,128)(2,1)S(1)} %get-tuple-element.806), channel_id=1, source_target_pairs={{0,8},{1,9},{2,10},{3,11},{4,12},{5,13},{6,14},{7,15},{8,0},{9,1},... | collective-permute-start | bytes 1572872 | tf_op jit(solution)/shard_map/ppermute | solution.py:166
  598.2 22.0 %collective-permute-start.46 = (bf16[4,128,512]{2,1,0:T(8,128)(2,1)S(1)}, bf16[4,128,512]{2,1,0:T(8,128)(2,1)}, u32[]{:S(2)}, u32[]{:S(2)}) collective-permute-start(bf16[4,128,512]{2,1,0:T(8,128)(2,1)S(1)} %get-tuple-element.808), channel_id=1, source_target_pairs={{0,16},{1,17},{2,18},{3,19},{4,20},{5,21},{6,22},{7,23},{8,24},{9,... | collective-permute-start | bytes 1572872 | tf_op jit(solution)/shard_map/ppermute | solution.py:166
  598.7 21.5 %collective-permute-start.47 = (bf16[4,128,512]{2,1,0:T(8,128)(2,1)S(1)}, bf16[4,128,512]{2,1,0:T(8,128)(2,1)}, u32[]{:S(2)}, u32[]{:S(2)}) collective-permute-start(bf16[4,128,512]{2,1,0:T(8,128)(2,1)S(1)} %get-tuple-element.807), channel_id=1, source_target_pairs={{0,24},{1,25},{2,26},{3,27},{4,28},{5,29},{6,30},{7,31},{8,16},{9,... | collective-permute-start | bytes 1572872 | tf_op jit(solution)/shard_map/ppermute | solution.py:166
  622.3 6.8 %collective-permute-start.48 = (bf16[128,512]{1,0:T(8,128)(2,1)S(1)}, bf16[128,512]{1,0:T(8,128)(2,1)S(1)}, u32[]{:S(2)}, u32[]{:S(2)}) collective-permute-start(bf16[128,512]{1,0:T(8,128)(2,1)S(1)} %get-tuple-element.824), channel_id=1, source_target_pairs={{0,2},{1,3},{2,0},{3,1},{4,6},{5,7},{6,4},{7,5},{8,10},{9,11},{10,... | collective-permute-start | bytes 393224 | tf_op jit(solution)/shard_map/ppermute | solution.py:166
  625.2 11.7 %collective-permute-start.49 = (bf16[128,512]{1,0:T(8,128)(2,1)S(1)}, bf16[128,512]{1,0:T(8,128)(2,1)S(1)}, u32[]{:S(2)}, u32[]{:S(2)}) collective-permute-start(bf16[128,512]{1,0:T(8,128)(2,1)S(1)} %get-tuple-element.826), channel_id=1, source_target_pairs={{0,4},{1,5},{2,6},{3,7},{4,0},{5,1},{6,2},{7,3},{8,12},{9,13},{10,... | collective-permute-start | bytes 393224 | tf_op jit(solution)/shard_map/ppermute | solution.py:166
  627.0 9.9 %collective-permute-start.50 = (bf16[128,512]{1,0:T(8,128)(2,1)S(1)}, bf16[128,512]{1,0:T(8,128)(2,1)S(1)}, u32[]{:S(2)}, u32[]{:S(2)}) collective-permute-start(bf16[128,512]{1,0:T(8,128)(2,1)S(1)} %get-tuple-element.825), channel_id=1, source_target_pairs={{0,6},{1,7},{2,4},{3,5},{4,2},{5,3},{6,0},{7,1},{8,14},{9,15},{10,... | collective-permute-start | bytes 393224 | tf_op jit(solution)/shard_map/ppermute | solution.py:166
  (160 other events, 1746.4 us)

commit v2 on v1

v2 whole, which is shorter than its diff:
```python
import math

import jax
import jax.numpy as jnp
from jax import lax
from jax.experimental import pallas as pl
from jax.experimental.pallas import tpu as pltpu
from jax.sharding import PartitionSpec as P

HEADS = 8
STEP = 5

SEGMENTS = 10

norm_eps = 1e-05
beta_first = 0.5
beta_second = 0.5
adam_eps = 1e-08
weight_decay = 0.01
mask_fill = -1000000000.0
LOW = jnp.bfloat16
FULL = jnp.float32


def dot_nn(left, right):
    return lax.dot_general(left, right, (((1,), (0,)), ((), ())), preferred_element_type=FULL)


def dot_nt(left, right):
    return lax.dot_general(left, right, (((1,), (1,)), ((), ())), preferred_element_type=FULL)


def head_masks(width, group, factor):
    lane = lax.broadcasted_iota(jnp.int32, (1, group * width), 1) // width
    return [jnp.where(lane == h, factor, 0.0).astype(LOW) for h in range(group)]


def window(start, size, total):
    return pl.multiple_of(jnp.minimum(start // 16 * 16, total - size), 16)


def inside(base, size, begin, end):
    place = lax.broadcasted_iota(jnp.int32, (size, 1), 0) + base
    return (place >= begin) & (place < end)


def attend_forward(row_starts, col_starts, q_ref, k_ref, v_ref, out_ref, sums_ref):
    total, model = q_ref.shape
    width = model // HEADS
    group = 256 // width
    span = 256
    scales = head_masks(width, group, 1.0 / math.sqrt(width))

    def segment(s, carry):
        row_begin, row_end = row_starts[s], row_starts[s + 1]
        col_begin, col_end = col_starts[s], col_starts[s + 1]
        row_base, col_base = window(row_begin, span, total), window(col_begin, span, total)
        rows, cols = pl.ds(row_base, span), pl.ds(col_base, span)
        row_mask = inside(row_base, span, row_begin, row_end)
        col_mask = inside(col_base, span, col_begin, col_end)
        for g in range(HEADS // group):
            lanes = slice(g * 256, (g + 1) * 256)
            query, keys, values = q_ref[rows, lanes], k_ref[cols, lanes], v_ref[cols, lanes]
            stacked = jnp.concatenate([query * scale for scale in scales], axis=0)
            scores = jnp.where(col_mask, dot_nt(keys, stacked), mask_fill)
            largest = jnp.max(scores, axis=0, keepdims=True)
            expo = jnp.exp(scores - largest)
            totals = jnp.sum(expo, axis=0, keepdims=True)
            sums_ref[s, g] = largest + jnp.log(totals)
            probs = (expo * (1.0 / totals)).astype(LOW)
            turned = values.T
            parts = [
                dot_nn(turned[h * width : (h + 1) * width], probs[:, h * span : (h + 1) * span])
                for h in range(group)
            ]
            mixed = jnp.concatenate(parts, axis=0).T
            old = out_ref[rows, lanes].astype(FULL)
            out_ref[rows, lanes] = jnp.where(row_mask, mixed, old).astype(LOW)
        return carry

    lax.fori_loop(0, SEGMENTS, segment, 0)


def attend_backward(
    row_starts, col_starts, q_ref, k_ref, v_ref, grad_ref, sums_ref, dq_ref, dk_ref, dv_ref
):
    total, model = q_ref.shape
    width = model // HEADS
    group = 256 // width
    span = 256
    factor = 1.0 / math.sqrt(width)
    scales = head_masks(width, group, factor)
    picks = head_masks(width, group, 1.0)

    def segment(s, carry):
        row_begin, row_end = row_starts[s], row_starts[s + 1]
        col_begin, col_end = col_starts[s], col_starts[s + 1]
        row_base, col_base = window(row_begin, span, total), window(col_begin, span, total)
        rows, cols = pl.ds(row_base, span), pl.ds(col_base, span)
        row_mask = inside(row_base, span, row_begin, row_end)
        col_mask = inside(col_base, span, col_begin, col_end)
        for g in range(HEADS // group):
            lanes = slice(g * 256, (g + 1) * 256)
            query, keys, values = q_ref[rows, lanes], k_ref[cols, lanes], v_ref[cols, lanes]
            grad = jnp.where(row_mask, grad_ref[rows, lanes].astype(FULL), 0.0).astype(LOW)
            stacked = jnp.concatenate([query * scale for scale in scales], axis=0)
            grads = jnp.concatenate([grad * item for item in picks], axis=0)
            scores = jnp.where(col_mask, dot_nt(keys, stacked), mask_fill)
            probs = jnp.exp(scores - sums_ref[s, g])
            grad_values = dot_nn(probs.astype(LOW), grads)
            weighted = probs * dot_nt(values, grads)
            inner = jnp.sum(weighted, axis=0, keepdims=True)
            grad_scores = (weighted - probs * inner).astype(LOW)
            grad_keys = dot_nn(grad_scores, stacked)
            turned = keys.T
            parts = [
                dot_nn(
                    turned[h * width : (h + 1) * width], grad_scores[:, h * span : (h + 1) * span]
                )
                for h in range(group)
            ]
            grad_query = jnp.concatenate(parts, axis=0).T * factor
            for ref, place, mask, value in (
                (dq_ref, rows, row_mask, grad_query),
                (dk_ref, cols, col_mask, grad_keys),
                (dv_ref, cols, col_mask, grad_values),
            ):
                old = ref[place, lanes].astype(FULL)
                ref[place, lanes] = jnp.where(mask, value, old).astype(LOW)
        return carry

    lax.fori_loop(0, SEGMENTS, segment, 0)


def normalize(values):
    center = values - jnp.mean(values, axis=-1, keepdims=True)
    inverse = lax.rsqrt(jnp.mean(center * center, axis=-1, keepdims=True) + norm_eps)
    return center * inverse, inverse


def normalize_back(grad, gain, unit, inverse):
    scaled = grad * (1.0 + gain)
    mean = jnp.mean(scaled, axis=-1, keepdims=True)
    along = jnp.mean(scaled * unit, axis=-1, keepdims=True)
    return (scaled - mean - unit * along) * inverse


def column_sum(values):
    return jnp.sum(values.astype(FULL), axis=0, keepdims=True)


STEP_ROWS = 256


def row_steps(total, step):
    def run(i, carry):
        step(pl.ds(pl.multiple_of(i * STEP_ROWS, STEP_ROWS), STEP_ROWS))
        return carry

    lax.fori_loop(0, total // STEP_ROWS, run, 0)


def self_forward_kernel(
    row_starts, tokens, weights, vectors, queries, keys, values, mixed, sums
):
    def project(rows):
        block = tokens[rows, :]
        queries[rows, :] = (dot_nn(block, weights[0]) + vectors[0:1, :]).astype(LOW)
        keys[rows, :] = dot_nn(block, weights[1]).astype(LOW)
        values[rows, :] = (dot_nn(block, weights[2]) + vectors[1:2, :]).astype(LOW)

    row_steps(tokens.shape[0], project)
    attend_forward(row_starts, row_starts, queries, keys, values, mixed, sums)


def cross_forward_kernel(
    row_starts, col_starts, tokens, encoded, mixed, weights, out_weights, vectors,
    unit_one, inverse_one, first_low, queries, keys, values, cross_mixed, sums, unit_two, inverse_two,
):
    def project(rows):
        block = encoded[rows, :]
        keys[rows, :] = dot_nn(block, weights[1]).astype(LOW)
        values[rows, :] = (dot_nn(block, weights[2]) + vectors[4:5, :]).astype(LOW)
        summed = tokens[rows, :].astype(FULL) + dot_nn(mixed[rows, :], out_weights[0])
        unit, inverse = normalize(summed + vectors[2:3, :])
        unit_one[rows, :] = unit
        inverse_one[rows, :] = inverse
        low = (unit * (1.0 + vectors[7:8, :]) + vectors[10:11, :]).astype(LOW)
        first_low[rows, :] = low
        queries[rows, :] = (dot_nn(low, weights[0]) + vectors[3:4, :]).astype(LOW)

    total = tokens.shape[0]
    row_steps(total, project)
    attend_forward(row_starts, col_starts, queries, keys, values, cross_mixed, sums)

    def finish(rows):
        first = unit_one[rows, :] * (1.0 + vectors[7:8, :]) + vectors[10:11, :]
        summed = first + dot_nn(cross_mixed[rows, :], out_weights[1]) + vectors[5:6, :]
        unit, inverse = normalize(summed)
        unit_two[rows, :] = unit
        inverse_two[rows, :] = inverse

    row_steps(total, finish)


gelu_scale = math.sqrt(2.0 / math.pi)
gelu_cubic = 0.044715


def ffn_kernel(
    unit_two, inverse_two, cotangent, first_weights, second_weights, cross_out, vectors, bias,
    layer_out, second_low, hidden, grad_ffn, grad_pre, grad_sum, grad_out, grad_mixed, sums, bias_sums,
    slopes,
):
    step = pl.program_id(0)

    @pl.when(step == 0)
    def _():
        sums[...] = jnp.zeros_like(sums)
        bias_sums[...] = jnp.zeros_like(bias_sums)

    unit = unit_two[...]
    second = unit * (1.0 + vectors[8:9, :]) + vectors[11:12, :]
    low = second.astype(LOW)
    second_low[...] = low
    model = low.shape[1]
    pieces = first_weights.shape[1] // model
    total = second + vectors[6:7, :]
    for j in range(pieces):
        lanes = slice(j * model, (j + 1) * model)
        pre = dot_nn(low, first_weights[:, lanes]) + bias[:, lanes]
        square = pre * pre
        bend = jnp.tanh(gelu_scale * pre * (1.0 + gelu_cubic * square))
        half = 0.5 * (1.0 + bend)
        value = (pre * half).astype(LOW)
        hidden[:, lanes] = value
        inner = gelu_scale * (1.0 + 3.0 * gelu_cubic * square)
        slopes[:, lanes] = half + 0.5 * pre * (1.0 - bend * bend) * inner
        total = total + dot_nn(value, second_weights[lanes, :])
    unit_three, inverse_three = normalize(total)
    layer_out[...] = (unit_three * (1.0 + vectors[9:10, :]) + vectors[12:13, :]).astype(LOW)
    upper = cotangent[...].astype(FULL)
    third = normalize_back(upper, vectors[9:10, :], unit_three, inverse_three)
    third_low = third.astype(LOW)
    grad_ffn[...] = third_low
    sums[0:1, :] += column_sum(third_low)
    sums[1:2, :] += column_sum(upper * unit_three)
    sums[2:3, :] += column_sum(upper)
    below = third
    for j in range(pieces):
        lanes = slice(j * model, (j + 1) * model)
        pre = (dot_nt(third_low, second_weights[lanes, :]) * slopes[:, lanes]).astype(LOW)
        grad_pre[:, lanes] = pre
        bias_sums[0:1, lanes] += column_sum(pre)
        below = below + dot_nt(pre, first_weights[:, lanes])
    sums[3:4, :] += column_sum(below * unit)
    sums[4:5, :] += column_sum(below)
    second_sum = normalize_back(below, vectors[8:9, :], unit, inverse_two[...])
    grad_sum[...] = second_sum
    out_low = second_sum.astype(LOW)
    grad_out[...] = out_low
    sums[5:6, :] += column_sum(out_low)
    grad_mixed[...] = dot_nt(out_low, cross_out[...]).astype(LOW)


def cross_backward_kernel(
    row_starts, col_starts, queries, keys, values, grad_mixed_in, sums_in, weights, self_out, vectors,
    grad_sum, unit_one, inverse_one,
    dq, dk, dv, encoded_grad, first_sum, self_low, grad_mixed, sums,
):
    attend_backward(
        row_starts, col_starts, queries, keys, values, grad_mixed_in, sums_in, dq, dk, dv
    )
    sums[...] = jnp.zeros_like(sums)

    def finish(rows):
        query, key, value = dq[rows, :], dk[rows, :], dv[rows, :]
        sums[0:1, :] += column_sum(query)
        sums[1:2, :] += column_sum(value)
        encoded_grad[rows, :] = dot_nt(key, weights[1]) + dot_nt(value, weights[2])
        upper = grad_sum[rows, :] + dot_nt(query, weights[0])
        unit = unit_one[rows, :]
        sums[2:3, :] += column_sum(upper * unit)
        sums[3:4, :] += column_sum(upper)
        below = normalize_back(upper, vectors[7:8, :], unit, inverse_one[rows, :])
        first_sum[rows, :] = below
        low = below.astype(LOW)
        self_low[rows, :] = low
        sums[4:5, :] += column_sum(low)
        grad_mixed[rows, :] = dot_nt(low, self_out[...]).astype(LOW)

    row_steps(queries.shape[0], finish)


def self_backward_kernel(
    row_starts, queries, keys, values, grad_mixed, sums_in, weights, first_sum,
    dq, dk, dv, tokens_grad, sums,
):
    attend_backward(
        row_starts, row_starts, queries, keys, values, grad_mixed, sums_in, dq, dk, dv
    )
    sums[...] = jnp.zeros_like(sums)

    def finish(rows):
        query, key, value = dq[rows, :], dk[rows, :], dv[rows, :]
        sums[0:1, :] += column_sum(query)
        sums[1:2, :] += column_sum(value)
        below = first_sum[rows, :] + dot_nt(query, weights[0])
        tokens_grad[rows, :] = below + dot_nt(key, weights[1]) + dot_nt(value, weights[2])

    row_steps(queries.shape[0], finish)


PARAMS = pltpu.CompilerParams(vmem_limit_bytes=56 << 20)


def call(kernel, name, scalars, arrays, outs, flops, expo):
    specs = [pl.BlockSpec(memory_space=pltpu.SMEM)] * len(scalars)
    specs += [pl.BlockSpec(memory_space=pltpu.VMEM)] * len(arrays)
    shapes = [jax.ShapeDtypeStruct(*item) for item in outs]
    moved = sum(item.size * item.dtype.itemsize for item in [*arrays, *shapes])
    return pl.pallas_call(
        kernel,
        out_shape=shapes,
        in_specs=specs,
        out_specs=[pl.BlockSpec(memory_space=pltpu.VMEM)] * len(outs),
        compiler_params=PARAMS,
        cost_estimate=pl.CostEstimate(flops=flops, transcendentals=expo, bytes_accessed=moved),
        name=name,
    )(*scalars, *arrays)


def local_step(tokens, encoded, cotangent, row_starts, col_starts, qkv, out, ffn_in, ffn_out, vectors):
    total, model = tokens.shape
    hidden_width = ffn_in.shape[1]
    bias = vectors[13:].reshape(1, -1)
    wide = ((total, model), LOW)
    tall = ((total, model), FULL)
    thin = ((total, 1), FULL)
    groups = HEADS * (model // HEADS) // 256
    log_sums = ((SEGMENTS, groups, 1, 1024), FULL)
    small = ((8, model), FULL)
    unit_flops = 2 * total * model * model
    attend_flops = 2 * SEGMENTS * HEADS * 256 * 256 * 256
    queries, keys, values, mixed, self_sums = call(
        self_forward_kernel, "self_forward", [row_starts], [tokens, qkv[:3], vectors],
        [wide, wide, wide, wide, log_sums], 3 * unit_flops + 2 * attend_flops, 0,
    )
    (
        unit_one, inverse_one, first_low, cross_queries, cross_keys, cross_values,
        cross_mixed, cross_sums, unit_two, inverse_two,
    ) = call(
        cross_forward_kernel, "cross_forward", [row_starts, col_starts],
        [tokens, encoded, mixed, qkv[3:], out, vectors],
        [tall, thin, wide, wide, wide, wide, wide, log_sums, tall, thin],
        5 * unit_flops + 2 * attend_flops, 0,
    )
    steps = total // STEP_ROWS
    block = pl.BlockSpec((STEP_ROWS, model), lambda i: (i, 0))
    block_wide = pl.BlockSpec((STEP_ROWS, hidden_width), lambda i: (i, 0))
    block_thin = pl.BlockSpec((STEP_ROWS, 1), lambda i: (i, 0))

    def fixed(shape):
        return pl.BlockSpec(shape, lambda i: (0,) * len(shape))

    hid = ((total, hidden_width), LOW)
    (
        layer_out, second_low, hidden, grad_ffn, grad_pre, grad_sum, grad_cross_out,
        grad_cross_mixed, ffn_sums, bias_sums,
    ) = pl.pallas_call(
        ffn_kernel,
        grid=(steps,),
        out_shape=[
            jax.ShapeDtypeStruct(*item)
            for item in (wide, wide, hid, wide, hid, tall, wide, wide, small, ((8, hidden_width), FULL))
        ],
        in_specs=[
            block, block_thin, block, fixed(ffn_in.shape), fixed(ffn_out.shape),
            fixed((model, model)), fixed(vectors.shape), fixed(bias.shape),
        ],
        out_specs=[
            block, block, block_wide, block, block_wide, block, block, block,
            fixed((8, model)), fixed((8, hidden_width)),
        ],
        scratch_shapes=[pltpu.VMEM((STEP_ROWS, hidden_width), FULL)],
        compiler_params=PARAMS,
        cost_estimate=pl.CostEstimate(
            flops=17 * unit_flops, transcendentals=total * hidden_width, bytes_accessed=24 << 20
        ),
        name="ffn",
    )(unit_two, inverse_two, cotangent, ffn_in, ffn_out, out[1], vectors, bias)
    (
        cross_dq, cross_dk, cross_dv, encoded_grad, first_sum, grad_self_out, grad_mixed, cross_vec,
    ) = call(
        cross_backward_kernel, "cross_backward", [row_starts, col_starts],
        [
            cross_queries, cross_keys, cross_values, grad_cross_mixed, cross_sums, qkv[3:], out[0],
            vectors, grad_sum, unit_one, inverse_one,
        ],
        [wide, wide, wide, tall, tall, wide, wide, small], 4 * unit_flops + 5 * attend_flops, 0,
    )
    self_dq, self_dk, self_dv, tokens_grad, self_vec = call(
        self_backward_kernel, "self_backward", [row_starts],
        [queries, keys, values, grad_mixed, self_sums, qkv[:3], first_sum],
        [wide, wide, wide, tall, small], 3 * unit_flops + 5 * attend_flops, 0,
    )

    def weight_grad(left, right):
        return lax.dot_general(
            left, right, (((0,), (0,)), ((), ())), preferred_element_type=FULL
        )

    grads = dict(
        ffn_out=weight_grad(hidden, grad_ffn),
        ffn_in=weight_grad(second_low, grad_pre),
        cross_out=weight_grad(cross_mixed, grad_cross_out),
        cross_query=weight_grad(first_low, cross_dq),
        cross_key=weight_grad(encoded, cross_dk),
        cross_value=weight_grad(encoded, cross_dv),
        self_out=weight_grad(mixed, grad_self_out),
        query=weight_grad(tokens, self_dq),
        key=weight_grad(tokens, self_dk),
        value=weight_grad(tokens, self_dv),
    )
    small_rows = [
        self_vec[0:2], cross_vec[4:5], cross_vec[0:2], ffn_sums[5:6], ffn_sums[0:1],
        cross_vec[2:3], ffn_sums[3:4], ffn_sums[1:2], cross_vec[3:4], ffn_sums[4:5], ffn_sums[2:3],
    ]
    grads["vector"] = jnp.concatenate(small_rows + [bias_sums[0].reshape(-1, model)], axis=0)
    return layer_out, tokens_grad, encoded_grad, grads


def segment_starts(ids):
    marks = jnp.arange(SEGMENTS + 1, dtype=ids.dtype)
    return jnp.sum((ids[None, :] < marks[:, None]).astype(jnp.int32), axis=1)


def adamw(master, grad, first, second, rate):
    first_new = beta_first * first + (1.0 - beta_first) * grad
    second_new = beta_second * second + (1.0 - beta_second) * grad * grad
    first_hat = first_new / (1.0 - beta_first**STEP)
    second_hat = second_new / (1.0 - beta_second**STEP)
    master_new = master - rate * (
        first_hat / (jnp.sqrt(second_hat) + adam_eps) + weight_decay * master
    )
    return (first_new, second_new, master_new, master_new.astype(jnp.bfloat16))


AXES = ("dp", "fsdp")


def exchange(values, offset):
    count = lax.axis_size("dp") * lax.axis_size("fsdp")
    return lax.ppermute(values, AXES, [(i, i ^ offset) for i in range(count)])


def gather_pieces(piece):
    dp_count, fsdp_count = lax.axis_size("dp"), lax.axis_size("fsdp")
    depth = fsdp_count // 2
    stack = jnp.stack([piece] + [exchange(piece, 2 * k) for k in range(1, depth)])
    near = [stack] + [exchange(stack, fsdp_count * k) for k in range(1, dp_count)]
    far = [exchange(item, 1) for item in near]
    return near, far


def own_index():
    return lax.axis_index("dp") * lax.axis_size("fsdp") + lax.axis_index("fsdp")


def ordered(near, far):
    count = lax.axis_size("dp") * lax.axis_size("fsdp")
    both = jnp.stack([jnp.stack(near), jnp.stack(far)], axis=2)
    flat = both.reshape((count,) + both.shape[3:])
    return flat[jnp.arange(count) ^ own_index()]


def pick(values, index, axis):
    return lax.dynamic_index_in_dim(values, index, axis, keepdims=False)


def scatter_sum(grad):
    dp_count, fsdp_count = lax.axis_size("dp"), lax.axis_size("fsdp")
    depth = fsdp_count // 2
    place_dp, place_fsdp = lax.axis_index("dp"), lax.axis_index("fsdp")
    core, layer = place_fsdp % 2, place_fsdp // 2
    low = jnp.bfloat16
    grad = grad.reshape((dp_count, depth, 2) + grad.shape[1:])
    received = exchange(pick(grad, 1 - core, 2).astype(low), 1)
    pair = pick(grad, core, 2).astype(jnp.float32) + received.astype(jnp.float32)
    square = pick(pair, place_dp, 0)
    for k in range(1, dp_count):
        part = exchange(pick(pair, place_dp ^ k, 0).astype(low), fsdp_count * k)
        square = square + part.astype(jnp.float32)
    total = pick(square, layer, 0)
    for k in range(1, depth):
        part = exchange(pick(square, layer ^ k, 0).astype(low), 2 * k)
        total = total + part.astype(jnp.float32)
    return total


def body(
    tokens,
    encoded,
    cotangent,
    target_ids,
    source_ids,
    qkv_master,
    qkv_first,
    qkv_second,
    out_master,
    out_first,
    out_second,
    ffn_in_master,
    ffn_in_first,
    ffn_in_second,
    ffn_out_master,
    ffn_out_first,
    ffn_out_second,
    vector_master,
    vector_first,
    vector_second,
):
    low_qkv = qkv_master.astype(jnp.bfloat16)
    low_out = out_master.astype(jnp.bfloat16)
    low_ffn_in = ffn_in_master.astype(jnp.bfloat16)
    low_ffn_out = ffn_out_master.astype(jnp.bfloat16)
    low_vector = vector_master.astype(jnp.bfloat16)
    width = tokens.shape[1]
    count = lax.axis_size("dp") * lax.axis_size("fsdp")
    rows = width // count
    vector_count = low_vector.shape[0]
    vector_row = jnp.pad(low_vector.reshape(1, -1), ((0, 7), (0, width - low_vector.size)))
    first_set = ordered(
        *gather_pieces(jnp.concatenate([low_qkv[:3].reshape(-1, width), vector_row]))
    )
    second_set = ordered(
        *gather_pieces(
            jnp.concatenate([low_qkv[3:].reshape(-1, width), low_out.reshape(-1, width)])
        )
    )
    in_piece = low_ffn_in.reshape(rows, -1, width).transpose(1, 0, 2).reshape(-1, width)
    third_set = ordered(*gather_pieces(jnp.concatenate([in_piece, low_ffn_out])))

    def whole(part):
        return part.reshape(count, -1, rows, width).transpose(1, 0, 2, 3).reshape(-1, width, width)

    qkv_full = [*whole(first_set[:, : 3 * rows]), *whole(second_set[:, : 3 * rows])]
    out_full = whole(second_set[:, 3 * rows :])
    in_rows = in_piece.shape[0]
    ffn_in_full = (
        third_set[:, :in_rows].reshape(count, -1, rows, width).transpose(0, 2, 1, 3)
    ).reshape(width, -1)
    ffn_out_full = third_set[:, in_rows:].reshape(-1, width)
    vector_full = (
        first_set[:, 3 * rows, : low_vector.size]
        .reshape(count, vector_count, -1)
        .transpose(1, 0, 2)
        .reshape(vector_count, width)
    )
    vectors = vector_full.astype(jnp.float32)
    layer_out, tokens_grad, encoded_grad, grads = local_step(
        tokens,
        encoded,
        cotangent,
        segment_starts(target_ids[0]),
        segment_starts(source_ids[0]),
        jnp.stack(qkv_full),
        out_full,
        ffn_in_full,
        ffn_out_full,
        vectors,
    )

    def split(parts):
        return jnp.concatenate([part.reshape(count, -1, width) for part in parts], axis=1)

    in_split = grads["ffn_in"].reshape(count, rows, -1, width).transpose(0, 2, 1, 3)
    ffn_total = scatter_sum(split([in_split, grads["ffn_out"]]))
    cross_total = scatter_sum(
        split(
            [
                grads["cross_query"],
                grads["cross_key"],
                grads["cross_value"],
                grads["cross_out"],
            ]
        )
    )
    vector_split = grads["vector"].reshape(vector_count, count, -1).transpose(1, 0, 2).reshape(count, -1)
    vector_split = jnp.pad(vector_split, ((0, 0), (0, width - vector_split.shape[1])))
    self_total = scatter_sum(
        split(
            [
                grads["query"],
                grads["key"],
                grads["value"],
                grads["self_out"],
                vector_split[:, None],
            ]
        )
    )
    summed_qkv = jnp.concatenate([self_total[: 3 * rows], cross_total[: 3 * rows]])
    summed_qkv = summed_qkv.reshape(6, rows, width)
    summed_out = jnp.stack([self_total[3 * rows : 4 * rows], cross_total[3 * rows :]])
    summed_ffn_in = ffn_total[:in_rows].reshape(-1, rows, width).transpose(1, 0, 2).reshape(rows, -1)
    summed_ffn_out = ffn_total[in_rows:]
    summed_vector = self_total[4 * rows, : low_vector.size].reshape(vector_count, -1)
    total_tokens = tokens.shape[0] * lax.axis_size("dp") * lax.axis_size("fsdp")
    grad_scale = 1.0 / math.sqrt(total_tokens)
    qkv_first_new, qkv_second_new, qkv_master_new, qkv_copy = adamw(
        qkv_master, summed_qkv * grad_scale, qkv_first, qkv_second, 0.04
    )
    out_first_new, out_second_new, out_master_new, out_copy = adamw(
        out_master, summed_out * grad_scale, out_first, out_second, 0.3
    )
    ffn_in_first_new, ffn_in_second_new, ffn_in_master_new, ffn_in_copy = adamw(
        ffn_in_master, summed_ffn_in * grad_scale, ffn_in_first, ffn_in_second, 0.04
    )
    ffn_out_first_new, ffn_out_second_new, ffn_out_master_new, ffn_out_copy = adamw(
        ffn_out_master, summed_ffn_out * grad_scale, ffn_out_first, ffn_out_second, 0.02
    )
    vector_first_new, vector_second_new, vector_master_new, vector_copy = adamw(
        vector_master, summed_vector * grad_scale, vector_first, vector_second, 0.35
    )
    return (
        layer_out,
        tokens_grad,
        encoded_grad,
        qkv_first_new,
        qkv_second_new,
        qkv_master_new,
        qkv_copy,
        out_first_new,
        out_second_new,
        out_master_new,
        out_copy,
        ffn_in_first_new,
        ffn_in_second_new,
        ffn_in_master_new,
        ffn_in_copy,
        ffn_out_first_new,
        ffn_out_second_new,
        ffn_out_master_new,
        ffn_out_copy,
        vector_first_new,
        vector_second_new,
        vector_master_new,
        vector_copy,
    )


def solution(mesh):
    return jax.shard_map(
        body,
        mesh=mesh,
        in_specs=(
            P(("dp", "fsdp"), None),
            P(("dp", "fsdp"), None),
            P(("dp", "fsdp"), None),
            P(("dp", "fsdp"), None),
            P(("dp", "fsdp"), None),
            P(None, ("dp", "fsdp"), None),
            P(None, ("dp", "fsdp"), None),
            P(None, ("dp", "fsdp"), None),
            P(None, ("dp", "fsdp"), None),
            P(None, ("dp", "fsdp"), None),
            P(None, ("dp", "fsdp"), None),
            P(("dp", "fsdp"), None),
            P(("dp", "fsdp"), None),
            P(("dp", "fsdp"), None),
            P(("dp", "fsdp"), None),
            P(("dp", "fsdp"), None),
            P(("dp", "fsdp"), None),
            P(None, ("dp", "fsdp")),
            P(None, ("dp", "fsdp")),
            P(None, ("dp", "fsdp")),
        ),
        out_specs=(
            P(("dp", "fsdp"), None),
            P(("dp", "fsdp"), None),
            P(("dp", "fsdp"), None),
            P(None, ("dp", "fsdp"), None),
            P(None, ("dp", "fsdp"), None),
            P(None, ("dp", "fsdp"), None),
            P(None, ("dp", "fsdp"), None),
            P(None, ("dp", "fsdp"), None),
            P(None, ("dp", "fsdp"), None),
            P(None, ("dp", "fsdp"), None),
            P(None, ("dp", "fsdp"), None),
            P(("dp", "fsdp"), None),
            P(("dp", "fsdp"), None),
            P(("dp", "fsdp"), None),
            P(("dp", "fsdp"), None),
            P(("dp", "fsdp"), None),
            P(("dp", "fsdp"), None),
            P(("dp", "fsdp"), None),
            P(("dp", "fsdp"), None),
            P(None, ("dp", "fsdp")),
            P(None, ("dp", "fsdp")),
            P(None, ("dp", "fsdp")),
            P(None, ("dp", "fsdp")),
        ),
        check_vma=False,
    )
```

time: 648 us -> 375 us (0.58)
  matrix products: 248 us -> 17.5 us
  Pallas kernels: 0 us -> 122 us
  other arithmetic: 120 us -> 35.2 us
  local copies, waits for them, and re-layouts: 143 us -> 60 us
  waiting for transfers between devices: 65.3 us -> 76.6 us
    dot_general x58 -> x10, matrix products: 248 us -> 17.5 us  [weight_grad(): lax.dot_general(left, right, (((0,), (0,)), ((), ())), preferred_element_...]
    pallas_call x0 -> x5, Pallas kernels: none -> 122 us  [the longest x4 100 us: call(): pl.pallas_call(kernel, out_shape=shapes, in_specs=specs, out_specs=[pl.Bl...]
    convert_element_type x7 -> x0, other arithmetic: 38 us -> none  [the longest x4 37.4 us: block_step(): grad_scores = (probs * (grad_probs - inner)).astype(jnp.bfloat16)]
    reduce_sum x17 -> x1, other arithmetic: 33.5 us -> 0.65 us  [segment_starts(): return jnp.sum((ids[None, :] < marks[:, None]).astype(jnp.int32), axis=1)]
    unnamed x286 -> x116, local copies, waits for them, and re-layouts: 43 us -> 20.4 us
    dynamic_slice x24 -> x1, local copies, waits for them, and re-layouts: 15 us -> 0.37 us  [pick(): return lax.dynamic_index_in_dim(values, index, axis, keepdims=False)]
    dynamic_update_slice x16 -> x0, local copies, waits for them, and re-layouts: 14.2 us -> none  [attend_forward(): lax.map(block_step, (queries.reshape(block_count, block_rows, -1), row_id...]
    ppermute x51, waiting for transfers between devices: 65.3 us -> 76.6 us  [exchange(): return lax.ppermute(values, AXES, [(i, i ^ offset) for i in range(count)])]
  transfers between devices with their start and end apart: 51 -> 51, of which waited for: 16 -> 18; matrix products, arithmetic and copies ran while one was open for 28% -> 17% of each run, Pallas kernels for 0% -> 12%
where the time goes in v2:
time: 375 us; the launch traced here: 370 us
  Pallas kernels  122 us (33%)
  waiting for transfers between devices  76.6 us (20%)
  local copies, waits for them, and re-layouts  60 us (16%)
  starting transfers between devices  56.4 us (15%)
  other arithmetic  35.2 us (9%)
  matrix products  17.5 us (5%)
    pallas_call x4, Pallas kernels, call(): pl.pallas_call(kernel, out_shape=shapes, in_specs=specs, out_specs=[pl.Bl...  100 us
    ppermute x51, waiting for transfers between devices, exchange(): return lax.ppermute(values, AXES, [(i, i ^ offset) for i in range(count)])  76.6 us
    ppermute x51, starting transfers between devices, exchange(): return lax.ppermute(values, AXES, [(i, i ^ offset) for i in range(count)])  56.4 us
    pallas_call x1, Pallas kernels, local_step(): pl.pallas_call(ffn_kernel, grid=(steps,), out_shape=[jax.ShapeDtypeStruct...  21.9 us
    unnamed x116, local copies, waits for them, and re-layouts  20.4 us
    dot_general x10, matrix products, weight_grad(): lax.dot_general(left, right, (((0,), (0,)), ((), ())), preferred_element_...  17.5 us
    another operation x12, other arithmetic, ordered(): both = jnp.stack([jnp.stack(near), jnp.stack(far)], axis=2)  12.1 us
    reshape x2, local copies, waits for them, and re-layouts, body(): grads['ffn_in'].reshape(count, rows, -1, width).transpose(0, 2, 1, 3)  10.1 us
  transfers between devices with their start and end apart: 51, of which 18 were waited for; matrix products, arithmetic and copies ran while one was open for 17% of the time, Pallas kernels for 12%

profile of v2, /device:TPU:0, one launch (start us, length us, event | category | flops | bytes accessed | tf_op | source)
XLA Modules:
  0.0 369.9 jit_solution(10040871253334656224)
XLA Ops:
  2.6 4.1 %collective-permute-start.1 = (bf16[56,512]{1,0:T(8,128)(2,1)S(1)}, bf16[56,512]{1,0:T(8,128)(2,1)S(1)}, u32[]{:S(2)}, u32[]{:S(2)}) collective-permute-start(bf16[56,512]{1,0:T(8,128)(2,1)S(1)} %get-tuple-element.313), channel_id=1, source_target_pairs={{0,4},{1,5},{2,6},{3,7},{4,0},{5,1},{6,2},{7,3},{8,12},{9,13},{10,... | collective-permute-start | bytes 172040 | tf_op jit(solution)/shard_map/ppermute | solution.py:454
  9.1 2.0 collective-permute-start.11
  11.1 2.5 collective-permute-start.10
  20.6 2.9 collective-permute-start.20
  23.7 2.6 collective-permute-start.5
  27.1 2.4 collective-permute-start.15
  29.5 4.1 %collective-permute-done.21 = bf16[128,512]{1,0:T(8,128)(2,1)S(1)} collective-permute-done((bf16[128,512]{1,0:T(8,128)(2,1)S(1)}, bf16[128,512]{1,0:T(8,128)(2,1)S(1)}, u32[]{:S(2)}, u32[]{:S(2)}) %collective-permute-start.21) | collective-permute-done | bytes 131104 | tf_op jit(solution)/shard_map/ppermute | solution.py:454
  37.8 11.6 %collective-permute-done.4 = bf16[4,56,512]{2,1,0:T(8,128)(2,1)S(1)} collective-permute-done((bf16[4,56,512]{2,1,0:T(8,128)(2,1)S(1)}, bf16[4,56,512]{2,1,0:T(8,128)(2,1)S(1)}, u32[]{:S(2)}, u32[]{:S(2)}) %collective-permute-start.4) | collective-permute-done | bytes 229408 | tf_op jit(solution)/shard_map/ppermute | solution.py:454
  50.7 2.2 maximum_bitcast_fusion.2
  56.7 1.9 gather_fusion
  62.4 6.2 %collective-permute-done.25 = bf16[4,128,512]{2,1,0:T(8,128)(2,1)} collective-permute-done((bf16[4,128,512]{2,1,0:T(8,128)(2,1)S(1)}, bf16[4,128,512]{2,1,0:T(8,128)(2,1)}, u32[]{:S(2)}, u32[]{:S(2)}) %collective-permute-start.25) | collective-permute-done | bytes 524320 | tf_op jit(solution)/shard_map/ppermute | solution.py:454
  68.6 10.7 %collective-permute-done.24 = bf16[4,128,512]{2,1,0:T(8,128)(2,1)} collective-permute-done((bf16[4,128,512]{2,1,0:T(8,128)(2,1)S(1)}, bf16[4,128,512]{2,1,0:T(8,128)(2,1)}, u32[]{:S(2)}, u32[]{:S(2)}) %collective-permute-start.24) | collective-permute-done | bytes 524320 | tf_op jit(solution)/shard_map/ppermute | solution.py:454
  79.4 18.9 %self_forward.1 = (bf16[1024,512]{1,0:T(8,128)(2,1)}, bf16[1024,512]{1,0:T(8,128)(2,1)}, bf16[1024,512]{1,0:T(8,128)(2,1)}, bf16[1024,512]{1,0:T(8,128)(2,1)}, f32[10,2,1,1024]{3,2,1,0:T(1,128)}) custom-call(s32[11]{0:T(128)} %get-tuple-element.315.row_starts, bf16[1024,512]{1,0:T(8,128)(2,1)} %tokens.3, bf16[3,512,512]{2,1,0:T(8,128)(2,1)} %pad_maximum_fusion.4.weights, ...), custom_call_target="tpu_custom_call" | custom-call | flops 6979321856 | bytes 6932480 | tf_op jit(solution)/shard_map/self_forward/pallas_call | solution.py:322
  99.5 2.9 maximum_bitcast_fusion
  104.6 2.3 gather_fusion.1
  111.7 25.9 %cross_forward.1 = (f32[1024,512]{1,0:T(8,128)}, f32[1024,1]{1,0:T(8,128)}, bf16[1024,512]{1,0:T(8,128)(2,1)}, bf16[1024,512]{1,0:T(8,128)(2,1)}, bf16[1024,512]...) custom-call(s32[11]{0:T(128)} %get-tuple-element.315.row_starts, ...), custom_call_target="tpu_custom_call" | custom-call | flops 8053063680 | bytes 15329280 | tf_op jit(solution)/shard_map/cross_forward/pallas_call | solution.py:322
  137.7 1.9 maximum_bitcast_fusion.1
  139.9 2.3 pad_maximum_fusion
  142.2 5.1 %gather_fusion.2 = bf16[32,128,512]{2,1,0:T(8,128)(2,1)} fusion(bf16[32,128,512]{2,1,0:T(8,128)(2,1)} %bitcast.260, s32[1024]{0:T(1024)S(1)} %pad_clamp_fusion), kind=kCustom, calls=%fused_computation.2 | custom fusion | bytes 8388736 | tf_op jit(solution)/shard_map/gather | solution.py:474
  147.2 3.9 %fusion.54 = (bf16[32,64,512]{2,1,0:T(8,128)(2,1)}, bf16[32,64,512]{2,1,0:T(8,128)(2,1)S(1)}) fusion(bf16[32,128,512]{2,1,0:T(8,128)(2,1)} %gather_fusion.2), kind=kLoop, calls=%fused_computation.167 | loop fusion | bytes 8388608 | tf_op jit(solution)/shard_map/slice | solution.py:553
  151.2 2.0 copy.234
  153.2 1.9 copy.268
  155.1 21.9 %ffn.1 = (bf16[1024,512]{1,0:T(8,128)(2,1)}, bf16[1024,512]{1,0:T(8,128)(2,1)}, bf16[1024,2048]{1,0:T(8,128)(2,1)}, bf16[1024,512]{1,0:T(8,128)(2,1)}, bf16[1024...) custom-call(f32[1024,512]{1,0:T(8,128)} %get-tuple-element.62.unit_t, ...), custom_call_target="tpu_custom_call" | custom-call | flops 9126805504 | bytes 25165824 | tf_op jit(solution)/shard_map/ffn/pallas_call | solution.py:370
  177.0 29.5 %cross_backward.1 = (bf16[1024,512]{1,0:T(8,128)(2,1)}, bf16[1024,512]{1,0:T(8,128)(2,1)}, bf16[1024,512]{1,0:T(8,128)(2,1)}, f32[1024,512]{1,0:T(8,128)}, f32[1...) custom-call(s32[11]{0:T(128)} %get-tuple-element.315.row_starts, ...), custom_call_target="tpu_custom_call" | custom-call | flops 15569256448 | bytes 20060160 | tf_op jit(solution)/shard_map/cross_backward/pallas_call | solution.py:322
  209.6 2.0 fusion.62
  211.5 26.1 %self_backward.1 = (bf16[1024,512]{1,0:T(8,128)(2,1)}, bf16[1024,512]{1,0:T(8,128)(2,1)}, bf16[1024,512]{1,0:T(8,128)(2,1)}, f32[1024,512]{1,0:T(8,128)}, f32[8,512]{1,0:T(8,128)}) custom-call(s32[11]{0:T(128)} %get-tuple-element.315.row_starts, bf16[1024,512]{1,0:T(8,128)(2,1)} %get-tuple-element.65.queries, bf16[1024,512]{1,0:T(8,128)(2,1)} %get-tuple-element.66.keys, ...), custom_call_target="tpu_custom_call" | custom-call | flops 15032385536 | bytes 13205504 | tf_op jit(solution)/shard_map/self_backward/pallas_call | solution.py:322
  239.2 2.1 fusion.59
  257.2 4.4 %fusion.67 = f32[512,2048]{1,0:T(8,128)} fusion(bf16[1024,512]{1,0:T(8,128)(2,1)S(1)} %copy-done.9, bf16[1024,2048]{1,0:T(8,128)(2,1)S(1)} %copy-done.5), kind=kOutput, calls=%fused_computation.180 | convolution fusion | flops 2147483648 | bytes 9437184 | tf_op jit(solution)/shard_map/dot_general | solution.py:409
  261.6 4.6 %fusion.68 = f32[2048,512]{1,0:T(8,128)} fusion(bf16[1024,2048]{1,0:T(8,128)(2,1)S(1)} %copy-done.42, bf16[1024,512]{1,0:T(8,128)(2,1)S(1)} %copy-done.43), kind=kOutput, calls=%fused_computation.181 | convolution fusion | flops 2147483648 | bytes 9437184 | tf_op jit(solution)/shard_map/dot_general | solution.py:409
  266.2 6.0 %reshape.244 = f32[32,16,4,512]{3,2,1,0:T(4,128)} reshape(f32[512,2048]{1,0:T(8,128)} %fusion.67) | data formatting | bytes 8388608 | tf_op jit(solution)/shard_map/reshape | solution.py:577
  272.2 4.1 %copy.249 = f32[32,16,4,512]{3,1,2,0:T(8,128)S(1)} copy(f32[32,16,4,512]{3,2,1,0:T(4,128)} %reshape.244) | data formatting | bytes 8388608 | tf_op jit(solution)/shard_map/reshape | solution.py:577
  286.5 2.0 bitcast_add_fusion
  289.6 2.5 collective-permute-done.38
  293.9 4.2 %collective-permute-done.40 = bf16[4,64,512]{2,1,0:T(8,128)(2,1)S(1)} collective-permute-done((bf16[4,64,512]{2,1,0:T(8,128)(2,1)S(1)}, bf16[4,64,512]{2,1,0:T(8,128)(2,1)S(1)}, u32[]{:S(2)}, u32[]{:S(2)}) %collective-permute-start.40) | collective-permute-done | bytes 262176 | tf_op jit(solution)/shard_map/ppermute | solution.py:454
  300.3 3.8 %collective-permute-done.31 = bf16[4,65,512]{2,1,0:T(8,128)(2,1)S(1)} collective-permute-done((bf16[4,65,512]{2,1,0:T(8,128)(2,1)S(1)}, bf16[4,65,512]{2,1,0:T(8,128)(2,1)S(1)}, u32[]{:S(2)}, u32[]{:S(2)}) %collective-permute-start.31) | collective-permute-done | bytes 266272 | tf_op jit(solution)/shard_map/ppermute | solution.py:454
  304.1 3.5 collective-permute-start.43
  307.6 2.7 collective-permute-done.33
  312.4 2.0 collective-permute-start.34
  316.9 3.7 %collective-permute-done.36 = bf16[65,512]{1,0:T(8,128)(2,1)S(1)} collective-permute-done((bf16[65,512]{1,0:T(8,128)(2,1)S(1)}, bf16[65,512]{1,0:T(8,128)(2,1)S(1)}, u32[]{:S(2)}, u32[]{:S(2)}) %collective-permute-start.36) | collective-permute-done | bytes 66592 | tf_op jit(solution)/shard_map/ppermute | solution.py:454
  320.6 1.9 collective-permute-done.35
  323.4 2.9 fusion.4
  326.3 2.0 copy-done.4
  335.9 7.6 %collective-permute-done.45 = bf16[4,128,512]{2,1,0:T(8,128)(2,1)S(1)} collective-permute-done((bf16[4,128,512]{2,1,0:T(8,128)(2,1)S(1)}, bf16[4,128,512]{2,1,0:T(8,128)(2,1)S(1)}, u32[]{:S(2)}, u32[]{:S(2)}) %collective-permute-start.45) | collective-permute-done | bytes 524320 | tf_op jit(solution)/shard_map/ppermute | solution.py:454
  343.5 7.5 %collective-permute-done.47 = bf16[4,128,512]{2,1,0:T(8,128)(2,1)} collective-permute-done((bf16[4,128,512]{2,1,0:T(8,128)(2,1)S(1)}, bf16[4,128,512]{2,1,0:T(8,128)(2,1)}, u32[]{:S(2)}, u32[]{:S(2)}) %collective-permute-start.47) | collective-permute-done | bytes 524320 | tf_op jit(solution)/shard_map/ppermute | solution.py:454
  354.3 2.2 collective-permute-start.48
  356.5 2.6 collective-permute-start.50
  360.7 2.9 collective-permute-done.50
  363.5 4.3 %collective-permute-done.49 = bf16[128,512]{1,0:T(8,128)(2,1)S(1)} collective-permute-done((bf16[128,512]{1,0:T(8,128)(2,1)S(1)}, bf16[128,512]{1,0:T(8,128)(2,1)S(1)}, u32[]{:S(2)}, u32[]{:S(2)}) %collective-permute-start.49) | collective-permute-done | bytes 131104 | tf_op jit(solution)/shard_map/ppermute | solution.py:454
  (296 shorter events, 88.7 us)
Async XLA Ops:
  2.6 16.5 %collective-permute-start.1 = (bf16[56,512]{1,0:T(8,128)(2,1)S(1)}, bf16[56,512]{1,0:T(8,128)(2,1)S(1)}, u32[]{:S(2)}, u32[]{:S(2)}) collective-permute-start(bf16[56,512]{1,0:T(8,128)(2,1)S(1)} %get-tuple-element.313), channel_id=1, source_target_pairs={{0,4},{1,5},{2,6},{3,7},{4,0},{5,1},{6,2},{7,3},{8,12},{9,13},{10,... | collective-permute-start | bytes 172040 | tf_op jit(solution)/shard_map/ppermute | solution.py:454
  6.7 12.4 %collective-permute-start = (bf16[56,512]{1,0:T(8,128)(2,1)S(1)}, bf16[56,512]{1,0:T(8,128)(2,1)S(1)}, u32[]{:S(2)}, u32[]{:S(2)}) collective-permute-start(bf16[56,512]{1,0:T(8,128)(2,1)S(1)} %get-tuple-element.313), channel_id=1, source_target_pairs={{0,2},{1,3},{2,0},{3,1},{4,6},{5,7},{6,4},{7,5},{8,10},{9,11},{10,... | collective-permute-start | bytes 172040 | tf_op jit(solution)/shard_map/ppermute | solution.py:454
  8.2 12.3 %collective-permute-start.2 = (bf16[56,512]{1,0:T(8,128)(2,1)S(1)}, bf16[56,512]{1,0:T(8,128)(2,1)S(1)}, u32[]{:S(2)}, u32[]{:S(2)}) collective-permute-start(bf16[56,512]{1,0:T(8,128)(2,1)S(1)} %get-tuple-element.313), channel_id=1, source_target_pairs={{0,6},{1,7},{2,4},{3,5},{4,2},{5,3},{6,0},{7,1},{8,14},{9,15},{10,... | collective-permute-start | bytes 172040 | tf_op jit(solution)/shard_map/ppermute | solution.py:454
  9.1 14.4 %collective-permute-start.11 = (bf16[80,512]{1,0:T(8,128)(2,1)S(1)}, bf16[80,512]{1,0:T(8,128)(2,1)S(1)}, u32[]{:S(2)}, u32[]{:S(2)}) collective-permute-start(bf16[80,512]{1,0:T(8,128)(2,1)S(1)} %get-tuple-element.311), channel_id=1, source_target_pairs={{0,4},{1,5},{2,6},{3,7},{4,0},{5,1},{6,2},{7,3},{8,12},{9,13},{10,... | collective-permute-start | bytes 245768 | tf_op jit(solution)/shard_map/ppermute | solution.py:454
  11.1 12.6 %collective-permute-start.10 = (bf16[80,512]{1,0:T(8,128)(2,1)S(1)}, bf16[80,512]{1,0:T(8,128)(2,1)S(1)}, u32[]{:S(2)}, u32[]{:S(2)}) collective-permute-start(bf16[80,512]{1,0:T(8,128)(2,1)S(1)} %get-tuple-element.311), channel_id=1, source_target_pairs={{0,2},{1,3},{2,0},{3,1},{4,6},{5,7},{6,4},{7,5},{8,10},{9,11},{10,... | collective-permute-start | bytes 245768 | tf_op jit(solution)/shard_map/ppermute | solution.py:454
  19.1 7.2 %collective-permute-start.12 = (bf16[80,512]{1,0:T(8,128)(2,1)S(1)}, bf16[80,512]{1,0:T(8,128)(2,1)S(1)}, u32[]{:S(2)}, u32[]{:S(2)}) collective-permute-start(bf16[80,512]{1,0:T(8,128)(2,1)S(1)} %get-tuple-element.311), channel_id=1, source_target_pairs={{0,6},{1,7},{2,4},{3,5},{4,2},{5,3},{6,0},{7,1},{8,14},{9,15},{10,... | collective-permute-start | bytes 245768 | tf_op jit(solution)/shard_map/ppermute | solution.py:454
  19.1 14.5 %collective-permute-start.21 = (bf16[128,512]{1,0:T(8,128)(2,1)S(1)}, bf16[128,512]{1,0:T(8,128)(2,1)S(1)}, u32[]{:S(2)}, u32[]{:S(2)}) collective-permute-start(bf16[128,512]{1,0:T(8,128)(2,1)S(1)} %get-tuple-element.307), channel_id=1, source_target_pairs={{0,4},{1,5},{2,6},{3,7},{4,0},{5,1},{6,2},{7,3},{8,12},{9,13},{10,... | collective-permute-start | bytes 393224 | tf_op jit(solution)/shard_map/ppermute | solution.py:454
  20.6 14.5 %collective-permute-start.20 = (bf16[128,512]{1,0:T(8,128)(2,1)S(1)}, bf16[128,512]{1,0:T(8,128)(2,1)S(1)}, u32[]{:S(2)}, u32[]{:S(2)}) collective-permute-start(bf16[128,512]{1,0:T(8,128)(2,1)S(1)} %get-tuple-element.307), channel_id=1, source_target_pairs={{0,2},{1,3},{2,0},{3,1},{4,6},{5,7},{6,4},{7,5},{8,10},{9,11},{10,... | collective-permute-start | bytes 393224 | tf_op jit(solution)/shard_map/ppermute | solution.py:454
  23.5 12.1 %collective-permute-start.22 = (bf16[128,512]{1,0:T(8,128)(2,1)S(1)}, bf16[128,512]{1,0:T(8,128)(2,1)S(1)}, u32[]{:S(2)}, u32[]{:S(2)}) collective-permute-start(bf16[128,512]{1,0:T(8,128)(2,1)S(1)} %get-tuple-element.307), channel_id=1, source_target_pairs={{0,6},{1,7},{2,4},{3,5},{4,2},{5,3},{6,0},{7,1},{8,14},{9,15},{10,... | collective-permute-start | bytes 393224 | tf_op jit(solution)/shard_map/ppermute | solution.py:454
  23.7 13.5 %collective-permute-start.5 = (bf16[4,56,512]{2,1,0:T(8,128)(2,1)S(1)}, bf16[4,56,512]{2,1,0:T(8,128)(2,1)S(1)}, u32[]{:S(2)}, u32[]{:S(2)}) collective-permute-start(bf16[4,56,512]{2,1,0:T(8,128)(2,1)S(1)} %get-tuple-element.303), channel_id=1, source_target_pairs={{0,24},{1,25},{2,26},{3,27},{4,28},{5,29},{6,30},{7,31},{8,16},{9,... | collective-permute-start | bytes 688136 | tf_op jit(solution)/shard_map/ppermute | solution.py:454
  27.1 22.8 %collective-permute-start.15 = (bf16[4,80,512]{2,1,0:T(8,128)(2,1)}, bf16[4,80,512]{2,1,0:T(8,128)(2,1)}, u32[]{:S(2)}, u32[]{:S(2)}) collective-permute-start(bf16[4,80,512]{2,1,0:T(8,128)(2,1)} %get-tuple-element.299), channel_id=1, source_target_pairs={{0,24},{1,25},{2,26},{3,27},{4,28},{5,29},{6,30},{7,31},{8,16},{9,... | collective-permute-start | bytes 983048 | tf_op jit(solution)/shard_map/ppermute | solution.py:454
  33.6 16.4 %collective-permute-start.14 = (bf16[4,80,512]{2,1,0:T(8,128)(2,1)}, bf16[4,80,512]{2,1,0:T(8,128)(2,1)S(1)}, u32[]{:S(2)}, u32[]{:S(2)}) collective-permute-start(bf16[4,80,512]{2,1,0:T(8,128)(2,1)} %get-tuple-element.299), channel_id=1, source_target_pairs={{0,16},{1,17},{2,18},{3,19},{4,20},{5,21},{6,22},{7,23},{8,24},{9,... | collective-permute-start | bytes 983048 | tf_op jit(solution)/shard_map/ppermute | solution.py:454
  35.1 14.3 %collective-permute-start.4 = (bf16[4,56,512]{2,1,0:T(8,128)(2,1)S(1)}, bf16[4,56,512]{2,1,0:T(8,128)(2,1)S(1)}, u32[]{:S(2)}, u32[]{:S(2)}) collective-permute-start(bf16[4,56,512]{2,1,0:T(8,128)(2,1)S(1)} %get-tuple-element.303), channel_id=1, source_target_pairs={{0,16},{1,17},{2,18},{3,19},{4,20},{5,21},{6,22},{7,23},{8,24},{9,... | collective-permute-start | bytes 688136 | tf_op jit(solution)/shard_map/ppermute | solution.py:454
  35.6 13.7 %collective-permute-start.3 = (bf16[4,56,512]{2,1,0:T(8,128)(2,1)S(1)}, bf16[4,56,512]{2,1,0:T(8,128)(2,1)S(1)}, u32[]{:S(2)}, u32[]{:S(2)}) collective-permute-start(bf16[4,56,512]{2,1,0:T(8,128)(2,1)S(1)} %get-tuple-element.303), channel_id=1, source_target_pairs={{0,8},{1,9},{2,10},{3,11},{4,12},{5,13},{6,14},{7,15},{8,0},{9,1},... | collective-permute-start | bytes 688136 | tf_op jit(solution)/shard_map/ppermute | solution.py:454
  37.1 13.4 %collective-permute-start.13 = (bf16[4,80,512]{2,1,0:T(8,128)(2,1)}, bf16[4,80,512]{2,1,0:T(8,128)(2,1)S(1)}, u32[]{:S(2)}, u32[]{:S(2)}) collective-permute-start(bf16[4,80,512]{2,1,0:T(8,128)(2,1)} %get-tuple-element.299), channel_id=1, source_target_pairs={{0,8},{1,9},{2,10},{3,11},{4,12},{5,13},{6,14},{7,15},{8,0},{9,1},... | collective-permute-start | bytes 983048 | tf_op jit(solution)/shard_map/ppermute | solution.py:454
  49.4 5.3 %collective-permute-start.9 = (bf16[4,56,512]{2,1,0:T(8,128)(2,1)S(1)}, bf16[4,56,512]{2,1,0:T(8,128)(2,1)S(1)}, u32[]{:S(2)}, u32[]{:S(2)}) collective-permute-start(bf16[4,56,512]{2,1,0:T(8,128)(2,1)S(1)} %collective-permute-done.5), channel_id=1, source_target_pairs={{0,1},{1,0},{2,3},{3,2},{4,5},{5,4},{6,7},{7,6},{8,9},{9,8},{10,11... | collective-permute-start | bytes 688136 | tf_op jit(solution)/shard_map/ppermute | solution.py:454
  49.9 6.4 %collective-permute-start.7 = (bf16[4,56,512]{2,1,0:T(8,128)(2,1)S(1)}, bf16[4,56,512]{2,1,0:T(8,128)(2,1)S(1)}, u32[]{:S(2)}, u32[]{:S(2)}) collective-permute-start(bf16[4,56,512]{2,1,0:T(8,128)(2,1)S(1)} %collective-permute-done.3), channel_id=1, source_target_pairs={{0,1},{1,0},{2,3},{3,2},{4,5},{5,4},{6,7},{7,6},{8,9},{9,8},{10,11... | collective-permute-start | bytes 688136 | tf_op jit(solution)/shard_map/ppermute | solution.py:454
  50.5 51.9 %collective-permute-start.16 = (bf16[4,80,512]{2,1,0:T(8,128)(2,1)}, bf16[4,80,512]{2,1,0:T(8,128)(2,1)}, u32[]{:S(2)}, u32[]{:S(2)}) collective-permute-start(bf16[4,80,512]{2,1,0:T(8,128)(2,1)} %get-tuple-element.299), channel_id=1, source_target_pairs={{0,1},{1,0},{2,3},{3,2},{4,5},{5,4},{6,7},{7,6},{8,9},{9,8},{10,11... | collective-permute-start | bytes 983048 | tf_op jit(solution)/shard_map/ppermute | solution.py:454
  52.9 15.8 %collective-permute-start.25 = (bf16[4,128,512]{2,1,0:T(8,128)(2,1)S(1)}, bf16[4,128,512]{2,1,0:T(8,128)(2,1)}, u32[]{:S(2)}, u32[]{:S(2)}) collective-permute-start(bf16[4,128,512]{2,1,0:T(8,128)(2,1)S(1)} %get-tuple-element.297), channel_id=1, source_target_pairs={{0,24},{1,25},{2,26},{3,27},{4,28},{5,29},{6,30},{7,31},{8,16},{9,... | collective-permute-start | bytes 1572872 | tf_op jit(solution)/shard_map/ppermute | solution.py:454
  54.6 24.7 %collective-permute-start.24 = (bf16[4,128,512]{2,1,0:T(8,128)(2,1)S(1)}, bf16[4,128,512]{2,1,0:T(8,128)(2,1)}, u32[]{:S(2)}, u32[]{:S(2)}) collective-permute-start(bf16[4,128,512]{2,1,0:T(8,128)(2,1)S(1)} %get-tuple-element.297), channel_id=1, source_target_pairs={{0,16},{1,17},{2,18},{3,19},{4,20},{5,21},{6,22},{7,23},{8,24},{9,... | collective-permute-start | bytes 1572872 | tf_op jit(solution)/shard_map/ppermute | solution.py:454
  55.1 44.0 %collective-permute-start.23 = (bf16[4,128,512]{2,1,0:T(8,128)(2,1)S(1)}, bf16[4,128,512]{2,1,0:T(8,128)(2,1)}, u32[]{:S(2)}, u32[]{:S(2)}) collective-permute-start(bf16[4,128,512]{2,1,0:T(8,128)(2,1)S(1)} %get-tuple-element.297), channel_id=1, source_target_pairs={{0,8},{1,9},{2,10},{3,11},{4,12},{5,13},{6,14},{7,15},{8,0},{9,1},... | collective-permute-start | bytes 1572872 | tf_op jit(solution)/shard_map/ppermute | solution.py:454
  56.4 46.2 %collective-permute-start.19 = (bf16[4,80,512]{2,1,0:T(8,128)(2,1)}, bf16[4,80,512]{2,1,0:T(8,128)(2,1)}, u32[]{:S(2)}, u32[]{:S(2)}) collective-permute-start(bf16[4,80,512]{2,1,0:T(8,128)(2,1)} %collective-permute-done.15), channel_id=1, source_target_pairs={{0,1},{1,0},{2,3},{3,2},{4,5},{5,4},{6,7},{7,6},{8,9},{9,8},{10,11... | collective-permute-start | bytes 983048 | tf_op jit(solution)/shard_map/ppermute | solution.py:454
  68.6 34.3 %collective-permute-start.18 = (bf16[4,80,512]{2,1,0:T(8,128)(2,1)S(1)}, bf16[4,80,512]{2,1,0:T(8,128)(2,1)S(1)}, u32[]{:S(2)}, u32[]{:S(2)}) collective-permute-start(bf16[4,80,512]{2,1,0:T(8,128)(2,1)S(1)} %collective-permute-done.14), channel_id=1, source_target_pairs={{0,1},{1,0},{2,3},{3,2},{4,5},{5,4},{6,7},{7,6},{8,9},{9,8},{10,11... | collective-permute-start | bytes 983048 | tf_op jit(solution)/shard_map/ppermute | solution.py:454
  79.4 23.7 %collective-permute-start.17 = (bf16[4,80,512]{2,1,0:T(8,128)(2,1)S(1)}, bf16[4,80,512]{2,1,0:T(8,128)(2,1)S(1)}, u32[]{:S(2)}, u32[]{:S(2)}) collective-permute-start(bf16[4,80,512]{2,1,0:T(8,128)(2,1)S(1)} %copy-done.14), channel_id=1, source_target_pairs={{0,1},{1,0},{2,3},{3,2},{4,5},{5,4},{6,7},{7,6},{8,9},{9,8},{10,11... | collective-permute-start | bytes 983048 | tf_op jit(solution)/shard_map/ppermute | solution.py:454
  99.1 38.5 %collective-permute-start.26 = (bf16[4,128,512]{2,1,0:T(8,128)(2,1)S(1)}, bf16[4,128,512]{2,1,0:T(8,128)(2,1)}, u32[]{:S(2)}, u32[]{:S(2)}) collective-permute-start(bf16[4,128,512]{2,1,0:T(8,128)(2,1)S(1)} %get-tuple-element.297), channel_id=1, source_target_pairs={{0,1},{1,0},{2,3},{3,2},{4,5},{5,4},{6,7},{7,6},{8,9},{9,8},{10,11... | collective-permute-start | bytes 1572872 | tf_op jit(solution)/shard_map/ppermute | solution.py:454
  102.4 35.2 %collective-permute-start.29 = (bf16[4,128,512]{2,1,0:T(8,128)(2,1)}, bf16[4,128,512]{2,1,0:T(8,128)(2,1)}, u32[]{:S(2)}, u32[]{:S(2)}) collective-permute-start(bf16[4,128,512]{2,1,0:T(8,128)(2,1)} %collective-permute-done.25), channel_id=1, source_target_pairs={{0,1},{1,0},{2,3},{3,2},{4,5},{5,4},{6,7},{7,6},{8,9},{9,8},{10,11... | collective-permute-start | bytes 1572872 | tf_op jit(solution)/shard_map/ppermute | solution.py:454
  102.6 35.1 %collective-permute-start.28 = (bf16[4,128,512]{2,1,0:T(8,128)(2,1)}, bf16[4,128,512]{2,1,0:T(8,128)(2,1)}, u32[]{:S(2)}, u32[]{:S(2)}) collective-permute-start(bf16[4,128,512]{2,1,0:T(8,128)(2,1)} %collective-permute-done.24), channel_id=1, source_target_pairs={{0,1},{1,0},{2,3},{3,2},{4,5},{5,4},{6,7},{7,6},{8,9},{9,8},{10,11... | collective-permute-start | bytes 1572872 | tf_op jit(solution)/shard_map/ppermute | solution.py:454
  102.9 34.7 %collective-permute-start.27 = (bf16[4,128,512]{2,1,0:T(8,128)(2,1)}, bf16[4,128,512]{2,1,0:T(8,128)(2,1)}, u32[]{:S(2)}, u32[]{:S(2)}) collective-permute-start(bf16[4,128,512]{2,1,0:T(8,128)(2,1)} %collective-permute-done.23), channel_id=1, source_target_pairs={{0,1},{1,0},{2,3},{3,2},{4,5},{5,4},{6,7},{7,6},{8,9},{9,8},{10,11... | collective-permute-start | bytes 1572872 | tf_op jit(solution)/shard_map/ppermute | solution.py:454
  251.2 28.4 %collective-permute-start.37 = (bf16[4,4,64,512]{3,2,1,0:T(8,128)(2,1)}, bf16[4,4,64,512]{3,2,1,0:T(8,128)(2,1)}, u32[]{:S(2)}, u32[]{:S(2)}) collective-permute-start(bf16[4,4,64,512]{3,2,1,0:T(8,128)(2,1)} %fusion.7), channel_id=1, source_target_pairs={{0,1},{1,0},{2,3},{3,2},{4,5},{5,4},{6,7},{7,6},{8,9},{9,8},{10,11... | collective-permute-start | bytes 3145736 | tf_op jit(solution)/shard_map/ppermute | solution.py:454
  255.0 31.5 %collective-permute-start.30 = (bf16[4,4,65,512]{3,1,2,0:T(4,128)(2,1)S(1)}, bf16[4,4,65,512]{3,1,2,0:T(4,128)(2,1)}, u32[]{:S(2)}, u32[]{:S(2)}) collective-permute-start(bf16[4,4,65,512]{3,1,2,0:T(4,128)(2,1)S(1)} %fusion.6), channel_id=1, source_target_pairs={{0,1},{1,0},{2,3},{3,2},{4,5},{5,4},{6,7},{7,6},{8,9},{9,8},{10,11... | collective-permute-start | bytes 3194888 | tf_op jit(solution)/shard_map/ppermute | solution.py:454
  279.0 44.4 %collective-permute-start.44 = (bf16[4,4,128,512]{3,2,1,0:T(8,128)(2,1)}, bf16[4,4,128,512]{3,2,1,0:T(8,128)(2,1)S(1)}, u32[]{:S(2)}, u32[]{:S(2)}) collective-permute-start(bf16[4,4,128,512]{3,2,1,0:T(8,128)(2,1)} %fusion.5), channel_id=1, source_target_pairs={{0,1},{1,0},{2,3},{3,2},{4,5},{5,4},{6,7},{7,6},{8,9},{9,8},{10,11... | collective-permute-start | bytes 6291464 | tf_op jit(solution)/shard_map/ppermute | solution.py:454
  282.9 9.2 %collective-permute-start.38 = (bf16[4,64,512]{2,1,0:T(8,128)(2,1)S(1)}, bf16[4,64,512]{2,1,0:T(8,128)(2,1)S(1)}, u32[]{:S(2)}, u32[]{:S(2)}) collective-permute-start(bf16[4,64,512]{2,1,0:T(8,128)(2,1)S(1)} %get-tuple-element.276), channel_id=1, source_target_pairs={{0,8},{1,9},{2,10},{3,11},{4,12},{5,13},{6,14},{7,15},{8,0},{9,1},... | collective-permute-start | bytes 786440 | tf_op jit(solution)/shard_map/ppermute | solution.py:454
  283.9 14.3 %collective-permute-start.40 = (bf16[4,64,512]{2,1,0:T(8,128)(2,1)S(1)}, bf16[4,64,512]{2,1,0:T(8,128)(2,1)S(1)}, u32[]{:S(2)}, u32[]{:S(2)}) collective-permute-start(bf16[4,64,512]{2,1,0:T(8,128)(2,1)S(1)} %get-tuple-element.277), channel_id=1, source_target_pairs={{0,24},{1,25},{2,26},{3,27},{4,28},{5,29},{6,30},{7,31},{8,16},{9,... | collective-permute-start | bytes 786440 | tf_op jit(solution)/shard_map/ppermute | solution.py:454
  285.4 13.9 %collective-permute-start.39 = (bf16[4,64,512]{2,1,0:T(8,128)(2,1)S(1)}, bf16[4,64,512]{2,1,0:T(8,128)(2,1)S(1)}, u32[]{:S(2)}, u32[]{:S(2)}) collective-permute-start(bf16[4,64,512]{2,1,0:T(8,128)(2,1)S(1)} %get-tuple-element.278), channel_id=1, source_target_pairs={{0,16},{1,17},{2,18},{3,19},{4,20},{5,21},{6,22},{7,23},{8,24},{9,... | collective-permute-start | bytes 786440 | tf_op jit(solution)/shard_map/ppermute | solution.py:454
  288.7 15.4 %collective-permute-start.31 = (bf16[4,65,512]{2,1,0:T(8,128)(2,1)S(1)}, bf16[4,65,512]{2,1,0:T(8,128)(2,1)S(1)}, u32[]{:S(2)}, u32[]{:S(2)}) collective-permute-start(bf16[4,65,512]{2,1,0:T(8,128)(2,1)S(1)} %get-tuple-element.273), channel_id=1, source_target_pairs={{0,8},{1,9},{2,10},{3,11},{4,12},{5,13},{6,14},{7,15},{8,0},{9,1},... | collective-permute-start | bytes 798728 | tf_op jit(solution)/shard_map/ppermute | solution.py:454
  292.1 18.1 %collective-permute-start.33 = (bf16[4,65,512]{2,1,0:T(8,128)(2,1)S(1)}, bf16[4,65,512]{2,1,0:T(8,128)(2,1)S(1)}, u32[]{:S(2)}, u32[]{:S(2)}) collective-permute-start(bf16[4,65,512]{2,1,0:T(8,128)(2,1)S(1)} %get-tuple-element.274), channel_id=1, source_target_pairs={{0,24},{1,25},{2,26},{3,27},{4,28},{5,29},{6,30},{7,31},{8,16},{9,... | collective-permute-start | bytes 798728 | tf_op jit(solution)/shard_map/ppermute | solution.py:454
  298.1 14.1 %collective-permute-start.32 = (bf16[4,65,512]{2,1,0:T(8,128)(2,1)S(1)}, bf16[4,65,512]{2,1,0:T(8,128)(2,1)S(1)}, u32[]{:S(2)}, u32[]{:S(2)}) collective-permute-start(bf16[4,65,512]{2,1,0:T(8,128)(2,1)S(1)} %get-tuple-element.275), channel_id=1, source_target_pairs={{0,16},{1,17},{2,18},{3,19},{4,20},{5,21},{6,22},{7,23},{8,24},{9,... | collective-permute-start | bytes 798728 | tf_op jit(solution)/shard_map/ppermute | solution.py:454
  299.5 14.9 %collective-permute-start.41 = (bf16[64,512]{1,0:T(8,128)(2,1)S(1)}, bf16[64,512]{1,0:T(8,128)(2,1)S(1)}, u32[]{:S(2)}, u32[]{:S(2)}) collective-permute-start(bf16[64,512]{1,0:T(8,128)(2,1)S(1)} %get-tuple-element.293), channel_id=1, source_target_pairs={{0,2},{1,3},{2,0},{3,1},{4,6},{5,7},{6,4},{7,5},{8,10},{9,11},{10,... | collective-permute-start | bytes 196616 | tf_op jit(solution)/shard_map/ppermute | solution.py:454
  304.1 11.8 %collective-permute-start.43 = (bf16[64,512]{1,0:T(8,128)(2,1)S(1)}, bf16[64,512]{1,0:T(8,128)(2,1)S(1)}, u32[]{:S(2)}, u32[]{:S(2)}) collective-permute-start(bf16[64,512]{1,0:T(8,128)(2,1)S(1)} %get-tuple-element.294), channel_id=1, source_target_pairs={{0,6},{1,7},{2,4},{3,5},{4,2},{5,3},{6,0},{7,1},{8,14},{9,15},{10,... | collective-permute-start | bytes 196616 | tf_op jit(solution)/shard_map/ppermute | solution.py:454
  310.2 6.2 %collective-permute-start.42 = (bf16[64,512]{1,0:T(8,128)(2,1)S(1)}, bf16[64,512]{1,0:T(8,128)(2,1)S(1)}, u32[]{:S(2)}, u32[]{:S(2)}) collective-permute-start(bf16[64,512]{1,0:T(8,128)(2,1)S(1)} %get-tuple-element.295), channel_id=1, source_target_pairs={{0,4},{1,5},{2,6},{3,7},{4,0},{5,1},{6,2},{7,3},{8,12},{9,13},{10,... | collective-permute-start | bytes 196616 | tf_op jit(solution)/shard_map/ppermute | solution.py:454
  314.4 6.2 %collective-permute-start.36 = (bf16[65,512]{1,0:T(8,128)(2,1)S(1)}, bf16[65,512]{1,0:T(8,128)(2,1)S(1)}, u32[]{:S(2)}, u32[]{:S(2)}) collective-permute-start(bf16[65,512]{1,0:T(8,128)(2,1)S(1)} %get-tuple-element.291), channel_id=1, source_target_pairs={{0,6},{1,7},{2,4},{3,5},{4,2},{5,3},{6,0},{7,1},{8,14},{9,15},{10,... | collective-permute-start | bytes 199688 | tf_op jit(solution)/shard_map/ppermute | solution.py:454
  315.9 6.6 %collective-permute-start.35 = (bf16[65,512]{1,0:T(8,128)(2,1)S(1)}, bf16[65,512]{1,0:T(8,128)(2,1)S(1)}, u32[]{:S(2)}, u32[]{:S(2)}) collective-permute-start(bf16[65,512]{1,0:T(8,128)(2,1)S(1)} %get-tuple-element.292), channel_id=1, source_target_pairs={{0,4},{1,5},{2,6},{3,7},{4,0},{5,1},{6,2},{7,3},{8,12},{9,13},{10,... | collective-permute-start | bytes 199688 | tf_op jit(solution)/shard_map/ppermute | solution.py:454
  328.6 14.9 %collective-permute-start.45 = (bf16[4,128,512]{2,1,0:T(8,128)(2,1)S(1)}, bf16[4,128,512]{2,1,0:T(8,128)(2,1)S(1)}, u32[]{:S(2)}, u32[]{:S(2)}) collective-permute-start(bf16[4,128,512]{2,1,0:T(8,128)(2,1)S(1)} %get-tuple-element.268), channel_id=1, source_target_pairs={{0,8},{1,9},{2,10},{3,11},{4,12},{5,13},{6,14},{7,15},{8,0},{9,1},... | collective-permute-start | bytes 1572872 | tf_op jit(solution)/shard_map/ppermute | solution.py:454
  330.3 20.7 %collective-permute-start.47 = (bf16[4,128,512]{2,1,0:T(8,128)(2,1)S(1)}, bf16[4,128,512]{2,1,0:T(8,128)(2,1)}, u32[]{:S(2)}, u32[]{:S(2)}) collective-permute-start(bf16[4,128,512]{2,1,0:T(8,128)(2,1)S(1)} %get-tuple-element.269), channel_id=1, source_target_pairs={{0,24},{1,25},{2,26},{3,27},{4,28},{5,29},{6,30},{7,31},{8,16},{9,... | collective-permute-start | bytes 1572872 | tf_op jit(solution)/shard_map/ppermute | solution.py:454
  331.4 20.9 %collective-permute-start.46 = (bf16[4,128,512]{2,1,0:T(8,128)(2,1)S(1)}, bf16[4,128,512]{2,1,0:T(8,128)(2,1)}, u32[]{:S(2)}, u32[]{:S(2)}) collective-permute-start(bf16[4,128,512]{2,1,0:T(8,128)(2,1)S(1)} %get-tuple-element.270), channel_id=1, source_target_pairs={{0,16},{1,17},{2,18},{3,19},{4,20},{5,21},{6,22},{7,23},{8,24},{9,... | collective-permute-start | bytes 1572872 | tf_op jit(solution)/shard_map/ppermute | solution.py:454
  354.3 6.4 %collective-permute-start.48 = (bf16[128,512]{1,0:T(8,128)(2,1)S(1)}, bf16[128,512]{1,0:T(8,128)(2,1)S(1)}, u32[]{:S(2)}, u32[]{:S(2)}) collective-permute-start(bf16[128,512]{1,0:T(8,128)(2,1)S(1)} %get-tuple-element.285), channel_id=1, source_target_pairs={{0,2},{1,3},{2,0},{3,1},{4,6},{5,7},{6,4},{7,5},{8,10},{9,11},{10,... | collective-permute-start | bytes 393224 | tf_op jit(solution)/shard_map/ppermute | solution.py:454
  356.5 7.1 %collective-permute-start.50 = (bf16[128,512]{1,0:T(8,128)(2,1)S(1)}, bf16[128,512]{1,0:T(8,128)(2,1)S(1)}, u32[]{:S(2)}, u32[]{:S(2)}) collective-permute-start(bf16[128,512]{1,0:T(8,128)(2,1)S(1)} %get-tuple-element.286), channel_id=1, source_target_pairs={{0,6},{1,7},{2,4},{3,5},{4,2},{5,3},{6,0},{7,1},{8,14},{9,15},{10,... | collective-permute-start | bytes 393224 | tf_op jit(solution)/shard_map/ppermute | solution.py:454
  359.1 8.8 %collective-permute-start.49 = (bf16[128,512]{1,0:T(8,128)(2,1)S(1)}, bf16[128,512]{1,0:T(8,128)(2,1)S(1)}, u32[]{:S(2)}, u32[]{:S(2)}) collective-permute-start(bf16[128,512]{1,0:T(8,128)(2,1)S(1)} %get-tuple-element.287), channel_id=1, source_target_pairs={{0,4},{1,5},{2,6},{3,7},{4,0},{5,1},{6,2},{7,3},{8,12},{9,13},{10,... | collective-permute-start | bytes 393224 | tf_op jit(solution)/shard_map/ppermute | solution.py:454
  (51 other events, 500.5 us)

commit v3 on v2

v3 whole, which is shorter than its diff:
```python
import functools
import math

import jax
import jax.numpy as jnp
from jax import lax
from jax.experimental import pallas as pl
from jax.experimental.pallas import tpu as pltpu
from jax.sharding import PartitionSpec as P

HEADS = 8
STEP = 5
SEGMENTS = 10
norm_eps = 1e-05
beta_first = 0.5
beta_second = 0.5
adam_eps = 1e-08
weight_decay = 0.01
mask_fill = -1000000000.0
LOW = jnp.bfloat16
FULL = jnp.float32


def dot_nn(left, right):
    return lax.dot_general(left, right, (((1,), (0,)), ((), ())), preferred_element_type=FULL)


def dot_nt(left, right):
    return lax.dot_general(left, right, (((1,), (1,)), ((), ())), preferred_element_type=FULL)


def dot_tn(left, right):
    return lax.dot_general(left, right, (((0,), (0,)), ((), ())), preferred_element_type=FULL)


def head_masks(width, group, factor):
    lane = lax.broadcasted_iota(jnp.int32, (1, group * width), 1) // width
    return [jnp.where(lane == h, factor, 0.0).astype(LOW) for h in range(group)]


def window(start, size, total):
    return pl.multiple_of(jnp.minimum(start // 16 * 16, total - size), 16)


def inside(base, size, begin, end):
    place = lax.broadcasted_iota(jnp.int32, (size, 1), 0) + base
    return (place >= begin) & (place < end)


def attend_forward(row_starts, col_starts, q_ref, k_ref, v_ref, out_ref, sums_ref):
    total, model = q_ref.shape
    width = model // HEADS
    group = 256 // width
    span = 256
    scales = head_masks(width, group, 1.0 / math.sqrt(width))

    def segment(s, carry):
        row_begin, row_end = row_starts[s], row_starts[s + 1]
        col_begin, col_end = col_starts[s], col_starts[s + 1]
        row_base, col_base = window(row_begin, span, total), window(col_begin, span, total)
        rows, cols = pl.ds(row_base, span), pl.ds(col_base, span)
        row_mask = inside(row_base, span, row_begin, row_end)
        col_mask = inside(col_base, span, col_begin, col_end)
        for g in range(HEADS // group):
            lanes = slice(g * 256, (g + 1) * 256)
            query, keys, values = q_ref[rows, lanes], k_ref[cols, lanes], v_ref[cols, lanes]
            stacked = jnp.concatenate([query * scale for scale in scales], axis=0)
            scores = jnp.where(col_mask, dot_nt(keys, stacked), mask_fill)
            largest = jnp.max(scores, axis=0, keepdims=True)
            expo = jnp.exp(scores - largest)
            totals = jnp.sum(expo, axis=0, keepdims=True)
            sums_ref[s, g] = largest + jnp.log(totals)
            probs = (expo * (1.0 / totals)).astype(LOW)
            turned = values.T
            parts = [
                dot_nn(turned[h * width : (h + 1) * width], probs[:, h * span : (h + 1) * span])
                for h in range(group)
            ]
            mixed = jnp.concatenate(parts, axis=0).T
            old = out_ref[rows, lanes].astype(FULL)
            out_ref[rows, lanes] = jnp.where(row_mask, mixed, old).astype(LOW)
        return carry

    lax.fori_loop(0, SEGMENTS, segment, 0)


def attend_backward(
    row_starts, col_starts, q_ref, k_ref, v_ref, grad_ref, sums_ref, dq_ref, dk_ref, dv_ref
):
    total, model = q_ref.shape
    width = model // HEADS
    group = 256 // width
    span = 256
    factor = 1.0 / math.sqrt(width)
    scales = head_masks(width, group, factor)
    picks = head_masks(width, group, 1.0)

    def segment(s, carry):
        row_begin, row_end = row_starts[s], row_starts[s + 1]
        col_begin, col_end = col_starts[s], col_starts[s + 1]
        row_base, col_base = window(row_begin, span, total), window(col_begin, span, total)
        rows, cols = pl.ds(row_base, span), pl.ds(col_base, span)
        row_mask = inside(row_base, span, row_begin, row_end)
        col_mask = inside(col_base, span, col_begin, col_end)
        for g in range(HEADS // group):
            lanes = slice(g * 256, (g + 1) * 256)
            query, keys, values = q_ref[rows, lanes], k_ref[cols, lanes], v_ref[cols, lanes]
            grad = jnp.where(row_mask, grad_ref[rows, lanes].astype(FULL), 0.0).astype(LOW)
            stacked = jnp.concatenate([query * scale for scale in scales], axis=0)
            grads = jnp.concatenate([grad * item for item in picks], axis=0)
            scores = jnp.where(col_mask, dot_nt(keys, stacked), mask_fill)
            probs = jnp.exp(scores - sums_ref[s, g])
            grad_values = dot_nn(probs.astype(LOW), grads)
            weighted = probs * dot_nt(values, grads)
            inner = jnp.sum(weighted, axis=0, keepdims=True)
            grad_scores = (weighted - probs * inner).astype(LOW)
            grad_keys = dot_nn(grad_scores, stacked)
            turned = keys.T
            parts = [
                dot_nn(
                    turned[h * width : (h + 1) * width], grad_scores[:, h * span : (h + 1) * span]
                )
                for h in range(group)
            ]
            grad_query = jnp.concatenate(parts, axis=0).T * factor
            for ref, place, mask, value in (
                (dq_ref, rows, row_mask, grad_query),
                (dk_ref, cols, col_mask, grad_keys),
                (dv_ref, cols, col_mask, grad_values),
            ):
                old = ref[place, lanes].astype(FULL)
                ref[place, lanes] = jnp.where(mask, value, old).astype(LOW)
        return carry

    lax.fori_loop(0, SEGMENTS, segment, 0)


def normalize(values):
    center = values - jnp.mean(values, axis=-1, keepdims=True)
    inverse = lax.rsqrt(jnp.mean(center * center, axis=-1, keepdims=True) + norm_eps)
    return center * inverse, inverse


def normalize_back(grad, gain, unit, inverse):
    scaled = grad * (1.0 + gain)
    mean = jnp.mean(scaled, axis=-1, keepdims=True)
    along = jnp.mean(scaled * unit, axis=-1, keepdims=True)
    return (scaled - mean - unit * along) * inverse


def column_sum(values):
    return jnp.sum(values.astype(FULL), axis=0, keepdims=True)


STEP_ROWS = 256


def row_steps(total, step):
    def run(i, carry):
        step(pl.ds(pl.multiple_of(i * STEP_ROWS, STEP_ROWS), STEP_ROWS))
        return carry

    lax.fori_loop(0, total // STEP_ROWS, run, 0)


def load_weights(place, depth, sources, targets, semaphores):
    if len(sources) == 1:
        offset = 0
        for target, semaphore in zip(targets, semaphores):
            source = sources[0].at[:, offset : offset + target.shape[1]]
            offset += target.shape[1]
            pltpu.make_async_copy(source, target, semaphore).start()
        return
    half = len(sources) // 2
    for k, source in enumerate(sources):
        base = (k % half) * 2 * depth + k // half
        for layer in range(depth):
            other = place ^ (base + 2 * layer)
            offset = 0
            for target, semaphore in zip(targets, semaphores):
                rows = source.shape[1]
                span = target.shape[1]
                to_rows = pl.ds(pl.multiple_of(other * rows, rows), rows)
                pltpu.make_async_copy(
                    source.at[layer, :, offset : offset + span], target.at[to_rows, :], semaphore
                ).start()
                offset += span


def await_weights(target, semaphore):
    pltpu.make_async_copy(target, target, semaphore).wait()


def store_grad(refs, core, lanes, value):
    value = value.astype(LOW)
    if len(refs) == 1:
        refs[0][:, lanes] = value
        return
    sent, kept = refs
    chips, rows = kept.shape[0], kept.shape[1]
    parts = value.reshape(chips, 2, rows, value.shape[1])
    first = core == 0
    kept[:, :, lanes] = jnp.where(first, parts[:, 0], parts[:, 1])
    sent[:, :, lanes] = jnp.where(first, parts[:, 1], parts[:, 0])


def self_forward_kernel(count, depth, place, row_starts, tokens, *rest):
    sources = rest[:count]
    weights, vectors, queries, keys, values, mixed, sums, semaphores = rest[count:]
    model = tokens.shape[1]
    load_weights(place[0], depth, sources, [weights], [semaphores.at[0]])
    await_weights(weights, semaphores.at[0])
    turned = weights[:, 3 * model : 3 * model + 128].astype(FULL).T
    vectors[...] = turned[: vectors.shape[0]]

    def project(rows):
        block = tokens[rows, :]
        queries[rows, :] = (dot_nn(block, weights[:, :model]) + vectors[0:1, :]).astype(LOW)
        keys[rows, :] = dot_nn(block, weights[:, model : 2 * model]).astype(LOW)
        values[rows, :] = (
            dot_nn(block, weights[:, 2 * model : 3 * model]) + vectors[1:2, :]
        ).astype(LOW)

    row_steps(tokens.shape[0], project)
    attend_forward(row_starts, row_starts, queries, keys, values, mixed, sums)


def cross_forward_kernel(
    count, depth, place, row_starts, col_starts, tokens, encoded, mixed, vectors, *rest
):
    sources = rest[:count]
    (
        weights, unit_one, inverse_one, first_low, queries, keys, values, cross_mixed, sums, semaphores,
    ) = rest[count:]
    model = tokens.shape[1]
    load_weights(place[0], depth, sources, [weights], [semaphores.at[0]])
    await_weights(weights, semaphores.at[0])

    def project(rows):
        block = encoded[rows, :]
        keys[rows, :] = dot_nn(block, weights[:, 2 * model : 3 * model]).astype(LOW)
        values[rows, :] = (
            dot_nn(block, weights[:, 3 * model : 4 * model]) + vectors[4:5, :]
        ).astype(LOW)
        summed = tokens[rows, :].astype(FULL) + dot_nn(mixed[rows, :], weights[:, :model])
        unit, inverse = normalize(summed + vectors[2:3, :])
        unit_one[rows, :] = unit
        inverse_one[rows, :] = inverse
        low = (unit * (1.0 + vectors[7:8, :]) + vectors[10:11, :]).astype(LOW)
        first_low[rows, :] = low
        queries[rows, :] = (dot_nn(low, weights[:, model : 2 * model]) + vectors[3:4, :]).astype(LOW)

    row_steps(tokens.shape[0], project)
    attend_forward(row_starts, col_starts, queries, keys, values, cross_mixed, sums)


def cross_finish_kernel(unit_one, cross_mixed, weights, vectors, unit_two, inverse_two):
    first = unit_one[...] * (1.0 + vectors[7:8, :]) + vectors[10:11, :]
    summed = first + dot_nn(cross_mixed[...], weights[...]) + vectors[5:6, :]
    unit, inverse = normalize(summed)
    unit_two[...] = unit
    inverse_two[...] = inverse


gelu_scale = math.sqrt(2.0 / math.pi)
gelu_cubic = 0.044715


def ffn_kernel(count, depth, place, unit_two, inverse_two, cotangent, cross_out, vectors, *rest):
    sources = rest[:count]
    (
        layer_out, grad_sum, grad_out, grad_mixed, sums, bias_sums, *grads,
        first_weights, second_weights, second_low, hidden, grad_ffn, grad_pre, slopes, semaphores,
    ) = rest[count:]
    step = pl.program_id(0)
    model = unit_two.shape[1]
    pieces = first_weights.shape[1] // model
    rows = pl.ds(pl.multiple_of(step * STEP_ROWS, STEP_ROWS), STEP_ROWS)

    @pl.when(step == 0)
    def _():
        sums[...] = jnp.zeros_like(sums)
        bias_sums[...] = jnp.zeros_like(bias_sums)
        load_ffn(place[0], depth, sources, first_weights, second_weights, semaphores)
        await_weights(first_weights, semaphores.at[0])
        await_weights(second_weights, semaphores.at[1])

    unit = unit_two[...]
    second = unit * (1.0 + vectors[8:9, :]) + vectors[11:12, :]
    low = second.astype(LOW)
    second_low[rows, :] = low
    total = second + vectors[6:7, :]
    for j in range(pieces):
        lanes = slice(j * model, (j + 1) * model)
        pre = dot_nn(low, first_weights[:, lanes]) + vectors[13 + j : 14 + j, :]
        square = pre * pre
        bend = jnp.tanh(gelu_scale * pre * (1.0 + gelu_cubic * square))
        half = 0.5 * (1.0 + bend)
        value = (pre * half).astype(LOW)
        hidden[rows, lanes] = value
        inner = gelu_scale * (1.0 + 3.0 * gelu_cubic * square)
        slopes[:, lanes] = half + 0.5 * pre * (1.0 - bend * bend) * inner
        total = total + dot_nn(value, second_weights[lanes, :])
    unit_three, inverse_three = normalize(total)
    layer_out[...] = (unit_three * (1.0 + vectors[9:10, :]) + vectors[12:13, :]).astype(LOW)
    upper = cotangent[...].astype(FULL)
    third = normalize_back(upper, vectors[9:10, :], unit_three, inverse_three)
    third_low = third.astype(LOW)
    grad_ffn[rows, :] = third_low
    sums[0:1, :] += column_sum(third_low)
    sums[1:2, :] += column_sum(upper * unit_three)
    sums[2:3, :] += column_sum(upper)
    below = third
    for j in range(pieces):
        lanes = slice(j * model, (j + 1) * model)
        pre = (dot_nt(third_low, second_weights[lanes, :]) * slopes[:, lanes]).astype(LOW)
        grad_pre[rows, lanes] = pre
        bias_sums[j : j + 1, :] += column_sum(pre)
        below = below + dot_nt(pre, first_weights[:, lanes])
    sums[3:4, :] += column_sum(below * unit)
    sums[4:5, :] += column_sum(below)
    second_sum = normalize_back(below, vectors[8:9, :], unit, inverse_two[...])
    grad_sum[...] = second_sum
    out_low = second_sum.astype(LOW)
    grad_out[...] = out_low
    sums[5:6, :] += column_sum(out_low)
    grad_mixed[...] = dot_nt(out_low, cross_out[...]).astype(LOW)

    @pl.when(step == pl.num_programs(0) - 1)
    def _():
        core = place[0] % 2
        for j in range(pieces):
            lanes = slice(j * model, (j + 1) * model)
            store_grad(grads, core, lanes, dot_tn(second_low[...], grad_pre[:, lanes]))
        span = second_weights.shape[0] // pieces
        for j in range(pieces):
            value = dot_tn(hidden[:, j * span : (j + 1) * span], grad_ffn[...])
            store_ffn_out(grads, core, j, pieces, value)


def load_ffn(place, depth, sources, first_weights, second_weights, semaphores):
    first_width = first_weights.shape[1]
    if len(sources) == 1:
        pltpu.make_async_copy(
            sources[0].at[:, :first_width], first_weights, semaphores.at[0]
        ).start()
        pieces = first_width // first_weights.shape[0]
        model = first_weights.shape[0]
        for j in range(pieces):
            pltpu.make_async_copy(
                sources[0].at[:, first_width + j * model : first_width + (j + 1) * model],
                second_weights.at[pl.ds(j * model, model), :],
                semaphores.at[1],
            ).start()
        return
    half = len(sources) // 2
    model = second_weights.shape[1]
    for k, source in enumerate(sources):
        base = (k % half) * 2 * depth + k // half
        rows = source.shape[1]
        for layer in range(depth):
            other = place ^ (base + 2 * layer)
            to_rows = pl.ds(pl.multiple_of(other * rows, rows), rows)
            pltpu.make_async_copy(
                source.at[layer, :, :first_width], first_weights.at[to_rows, :], semaphores.at[0]
            ).start()
            pieces = first_width // model
            for j in range(pieces):
                start = pl.multiple_of((other * pieces + j) * rows, rows)
                pltpu.make_async_copy(
                    source.at[layer, :, first_width + j * model : first_width + (j + 1) * model],
                    second_weights.at[pl.ds(start, rows), :],
                    semaphores.at[1],
                ).start()


def store_ffn_out(refs, core, block, pieces, value):
    value = value.astype(LOW)
    model = value.shape[1]
    if len(refs) == 1:
        offset = (pieces + block) * model
        refs[0][:, offset : offset + model] = value
        return
    sent, kept = refs
    rows = kept.shape[1]
    chips = kept.shape[0] // pieces
    parts = value.reshape(chips, 2, pieces, rows, model)
    first = core == 0
    for j in range(pieces):
        lanes = slice((pieces + j) * model, (pieces + j + 1) * model)
        place = slice(block * chips, (block + 1) * chips)
        kept[place, :, lanes] = jnp.where(first, parts[:, 0, j], parts[:, 1, j])
        sent[place, :, lanes] = jnp.where(first, parts[:, 1, j], parts[:, 0, j])


def cross_backward_kernel(
    row_starts, col_starts, queries, keys, values, grad_mixed, sums_in, dq, dk, dv
):
    attend_backward(row_starts, col_starts, queries, keys, values, grad_mixed, sums_in, dq, dk, dv)


def cross_grads_kernel(
    place, dq, dk, dv, weights, vectors, grad_sum, unit_one, inverse_one,
    first_low, encoded, cross_mixed, grad_out, first_sum, self_low, grad_mixed, sums, *grads,
):
    model = dq.shape[1]
    sums[...] = jnp.zeros_like(sums)

    def finish(rows):
        query, value = dq[rows, :], dv[rows, :]
        sums[0:1, :] += column_sum(query)
        sums[1:2, :] += column_sum(value)
        upper = grad_sum[rows, :] + dot_nt(query, weights[:, model : 2 * model])
        unit = unit_one[rows, :]
        sums[2:3, :] += column_sum(upper * unit)
        sums[3:4, :] += column_sum(upper)
        below = normalize_back(upper, vectors[7:8, :], unit, inverse_one[rows, :])
        first_sum[rows, :] = below
        low = below.astype(LOW)
        self_low[rows, :] = low
        sums[4:5, :] += column_sum(low)
        grad_mixed[rows, :] = dot_nt(low, weights[:, :model]).astype(LOW)

    row_steps(dq.shape[0], finish)
    core = place[0] % 2
    pairs = ((first_low, dq), (encoded, dk), (encoded, dv), (cross_mixed, grad_out))
    for j, (left, right) in enumerate(pairs):
        lanes = slice(j * model, (j + 1) * model)
        store_grad(grads, core, lanes, dot_tn(left[...], right[...]))


def encoded_grad_kernel(dk, dv, key_weights, value_weights, encoded_grad):
    encoded_grad[...] = dot_nt(dk[...], key_weights[...]) + dot_nt(dv[...], value_weights[...])


def self_backward_kernel(row_starts, queries, keys, values, grad_mixed, sums_in, dq, dk, dv):
    attend_backward(row_starts, row_starts, queries, keys, values, grad_mixed, sums_in, dq, dk, dv)


def self_grads_kernel(
    place, tokens, mixed, dq, dk, dv, self_low, cross_sums, ffn_sums, bias_sums, *rest
):
    *grads, stack = rest
    model = dq.shape[1]
    core = place[0] % 2
    pairs = ((tokens, dq), (tokens, dk), (tokens, dv), (mixed, self_low))
    for j, (left, right) in enumerate(pairs):
        lanes = slice(j * model, (j + 1) * model)
        store_grad(grads, core, lanes, dot_tn(left[...], right[...]))
    stack[...] = jnp.zeros_like(stack)
    stack[0:1, :] = column_sum(dq[...])
    stack[1:2, :] = column_sum(dv[...])
    order = (
        (2, cross_sums, 4), (3, cross_sums, 0), (4, cross_sums, 1), (5, ffn_sums, 5),
        (6, ffn_sums, 0), (7, cross_sums, 2), (8, ffn_sums, 3), (9, ffn_sums, 1),
        (10, cross_sums, 3), (11, ffn_sums, 4), (12, ffn_sums, 2),
    )
    for to, ref, at in order:
        stack[to : to + 1, :] = ref[at : at + 1, :]
    extra = bias_sums.shape[0]
    stack[13 : 13 + extra, :] = bias_sums[...]
    start = len(pairs) * model
    store_grad(grads, core, slice(start, start + 128), stack[...].T)


def tokens_grad_kernel(dq, dk, dv, first_sum, weights, tokens_grad):
    model = dq.shape[1]
    below = first_sum[...] + dot_nt(dq[...], weights[:, :model])
    below = below + dot_nt(dk[...], weights[:, model : 2 * model])
    tokens_grad[...] = below + dot_nt(dv[...], weights[:, 2 * model : 3 * model])


PARAMS = pltpu.CompilerParams(vmem_limit_bytes=58 << 20)
ANY = pl.BlockSpec(memory_space=pl.ANY)


def call(kernel, name, scalars, arrays, outs, flops, sources=(), scratch=()):
    specs = [pl.BlockSpec(memory_space=pltpu.SMEM)] * len(scalars)
    specs += [pl.BlockSpec(memory_space=pltpu.VMEM)] * len(arrays)
    specs += [ANY] * len(sources)
    shapes = [jax.ShapeDtypeStruct(*item) for item in outs]
    moved = sum(item.size * item.dtype.itemsize for item in [*arrays, *sources, *shapes])
    return pl.pallas_call(
        kernel,
        out_shape=shapes,
        in_specs=specs,
        out_specs=[pl.BlockSpec(memory_space=pltpu.VMEM)] * len(outs),
        scratch_shapes=list(scratch),
        compiler_params=PARAMS,
        cost_estimate=pl.CostEstimate(flops=flops, transcendentals=0, bytes_accessed=moved),
        name=name,
    )(*scalars, *arrays, *sources)


def blocked(kernel, name, arrays, fixed, outs, flops, scalars=(), sources=(), fixed_outs=(), scratch=()):
    total = arrays[0].shape[0]
    specs = [pl.BlockSpec(memory_space=pltpu.SMEM)] * len(scalars)
    specs += [pl.BlockSpec((STEP_ROWS, item.shape[1]), lambda i: (i, 0)) for item in arrays]
    for item, shape, index in fixed:
        specs.append(pl.BlockSpec(shape, lambda i, index=index: index))
    specs += [ANY] * len(sources)
    shapes = [jax.ShapeDtypeStruct(*item) for item in [*outs, *fixed_outs]]
    out_specs = [pl.BlockSpec((STEP_ROWS, item[0][1]), lambda i: (i, 0)) for item in outs]
    for item in fixed_outs:
        out_specs.append(pl.BlockSpec(item[0], lambda i, size=len(item[0]): (0,) * size))
    inputs = [*arrays, *[item[0] for item in fixed]]
    moved = sum(item.size * item.dtype.itemsize for item in [*arrays, *sources, *shapes])
    return pl.pallas_call(
        kernel,
        grid=(total // STEP_ROWS,),
        out_shape=shapes,
        in_specs=specs,
        out_specs=out_specs,
        scratch_shapes=list(scratch),
        compiler_params=PARAMS,
        cost_estimate=pl.CostEstimate(flops=flops, transcendentals=0, bytes_accessed=moved),
        name=name,
    )(*scalars, *inputs, *sources)


def segment_starts(ids):
    marks = jnp.arange(SEGMENTS + 1, dtype=ids.dtype)
    return jnp.sum((ids[None, :] < marks[:, None]).astype(jnp.int32), axis=1)


def adamw(master, grad, first, second, rate):
    first_new = beta_first * first + (1.0 - beta_first) * grad
    second_new = beta_second * second + (1.0 - beta_second) * grad * grad
    first_hat = first_new / (1.0 - beta_first**STEP)
    second_hat = second_new / (1.0 - beta_second**STEP)
    master_new = master - rate * (
        first_hat / (jnp.sqrt(second_hat) + adam_eps) + weight_decay * master
    )
    return (first_new, second_new, master_new, master_new.astype(jnp.bfloat16))


AXES = ("dp", "fsdp")


def exchange(values, offset):
    count = lax.axis_size("dp") * lax.axis_size("fsdp")
    return lax.ppermute(values, AXES, [(i, i ^ offset) for i in range(count)])


def after(value, *others):
    return lax.optimization_barrier((value, *others))[0]


def layer_stack(piece):
    depth = lax.axis_size("fsdp") // 2
    return jnp.stack([piece] + [exchange(piece, 2 * k) for k in range(1, depth)])


def square_list(stack):
    dp_count, fsdp_count = lax.axis_size("dp"), lax.axis_size("fsdp")
    return [stack] + [exchange(stack, fsdp_count * k) for k in range(1, dp_count)]


def core_list(near):
    return near + [exchange(item, 1) for item in near]


def ordered(parts, place):
    half = len(parts) // 2
    both = jnp.stack([jnp.stack(parts[:half]), jnp.stack(parts[half:])], axis=2)
    flat = both.reshape((-1,) + both.shape[3:])
    return flat[jnp.arange(flat.shape[0]) ^ place]


def pick(values, index, axis):
    return lax.dynamic_index_in_dim(values, index, axis, keepdims=False)


def split_core(grads):
    if len(grads) == 2:
        return grads
    dp_count, fsdp_count = lax.axis_size("dp"), lax.axis_size("fsdp")
    count = dp_count * fsdp_count
    core = lax.axis_index("fsdp") % 2
    parts = grads[0].reshape((count // 2, 2, -1) + grads[0].shape[1:])
    return pick(parts, 1 - core, 1), pick(parts, core, 1)


def sum_core(kept, received):
    dp_count = lax.axis_size("dp")
    shape = (dp_count, kept.shape[0] // dp_count) + kept.shape[1:]
    return kept.reshape(shape).astype(FULL) + received.reshape(shape).astype(FULL)


def sum_square(pair):
    dp_count, fsdp_count = lax.axis_size("dp"), lax.axis_size("fsdp")
    place = lax.axis_index("dp")
    moved = [
        exchange(pick(pair, place ^ k, 0).astype(LOW), fsdp_count * k) for k in range(1, dp_count)
    ]
    return pick(pair, place, 0), moved


def sum_layers(square):
    depth = lax.axis_size("fsdp") // 2
    place = lax.axis_index("fsdp") // 2
    moved = [exchange(pick(square, place ^ k, 0).astype(LOW), 2 * k) for k in range(1, depth)]
    return pick(square, place, 0), moved


def add_all(kept, moved):
    for item in moved:
        kept = kept + item.astype(FULL)
    return kept


def body(
    tokens,
    encoded,
    cotangent,
    target_ids,
    source_ids,
    qkv_master,
    qkv_first,
    qkv_second,
    out_master,
    out_first,
    out_second,
    ffn_in_master,
    ffn_in_first,
    ffn_in_second,
    ffn_out_master,
    ffn_out_first,
    ffn_out_second,
    vector_master,
    vector_first,
    vector_second,
):
    total, model = tokens.shape
    dp_count, fsdp_count = lax.axis_size("dp"), lax.axis_size("fsdp")
    count, depth = dp_count * fsdp_count, fsdp_count // 2
    rows = model // count
    aligned = rows % 16 == 0
    place = lax.axis_index("dp") * fsdp_count + lax.axis_index("fsdp")
    spot = place.reshape(1).astype(jnp.int32)
    low_qkv, low_out = qkv_master.astype(LOW), out_master.astype(LOW)
    low_vector = jnp.pad(vector_master.astype(LOW).T, ((0, 0), (0, 128 - vector_master.shape[0])))
    pieces = ffn_in_master.shape[1] // model

    def to_columns(values):
        return values.reshape(-1, rows, model).transpose(1, 0, 2).reshape(rows, -1)

    self_piece = jnp.concatenate([low_qkv[0], low_qkv[1], low_qkv[2], low_vector], axis=1)
    cross_piece = jnp.concatenate([low_out[0], low_qkv[3], low_qkv[4], low_qkv[5], low_out[1]], axis=1)
    ffn_piece = jnp.concatenate(
        [ffn_in_master.astype(LOW), to_columns(ffn_out_master.astype(LOW))], axis=1
    )
    row_starts, col_starts = segment_starts(target_ids[0]), segment_starts(source_ids[0])

    def sources_of(parts):
        if aligned:
            return parts
        flat = ordered(parts, place)
        return [flat.reshape(model, -1)]

    def ffn_sources_of(parts):
        if aligned:
            return parts
        flat = ordered(parts, place)
        width = pieces * model
        second = flat[:, :, width:].reshape(count, rows, pieces, model).transpose(0, 2, 1, 3)
        second = second.reshape(pieces, model, model).transpose(1, 0, 2).reshape(model, -1)
        return [jnp.concatenate([flat[:, :, :width].reshape(model, -1), second], axis=1)]

    wide, tall, thin = ((total, model), LOW), ((total, model), FULL), ((total, 1), FULL)
    log_sums = ((SEGMENTS, model // 256, 1, 1024), FULL)
    small = ((8, model), FULL)
    unit = 2 * total * model * model
    attend = 2 * SEGMENTS * HEADS * 256 * 256 * 256
    wait_one, wait_two = pltpu.SemaphoreType.DMA((1,)), pltpu.SemaphoreType.DMA((2,))

    def grad_outs(columns):
        if aligned:
            return [((count // 2, rows, columns), LOW)] * 2
        return [((model, columns), LOW)]

    self_stack = layer_stack(self_piece)
    later = after(jnp.concatenate([cross_piece, ffn_piece], axis=1), self_stack)
    self_near = square_list(self_stack)
    later_stack = layer_stack(later)
    self_parts = core_list(self_near)
    cross_columns = cross_piece.shape[1]
    cross_near = square_list(later_stack[:, :, :cross_columns])
    ffn_near = square_list(later_stack[:, :, cross_columns:])

    sources = sources_of(self_parts)
    (
        self_weights, vectors, queries, keys, values, mixed, self_sums,
    ) = call(
        functools.partial(self_forward_kernel, len(sources), depth), "self_forward",
        [spot, row_starts], [after(tokens, later_stack)],
        [((model, self_piece.shape[1]), LOW), ((24, model), FULL), wide, wide, wide, wide, log_sums],
        3 * unit + 2 * attend, sources, [wait_one],
    )
    sources = sources_of(core_list(cross_near))
    (
        cross_weights, unit_one, inverse_one, first_low, cross_queries, cross_keys, cross_values,
        cross_mixed, cross_log,
    ) = call(
        functools.partial(cross_forward_kernel, len(sources), depth), "cross_forward",
        [spot, row_starts, col_starts], [tokens, encoded, mixed, vectors],
        [((model, cross_columns), LOW), tall, thin, wide, wide, wide, wide, wide, log_sums],
        4 * unit + 2 * attend, sources, [wait_one],
    )

    def weight_block(weights, index):
        return (weights, (model, model), (0, index))

    whole_vectors = (vectors, vectors.shape, (0, 0))
    unit_two, inverse_two = blocked(
        cross_finish_kernel, "cross_finish", [unit_one, cross_mixed],
        [weight_block(cross_weights, 4), whole_vectors], [tall, thin], unit,
    )
    sources = ffn_sources_of(core_list(ffn_near))
    hidden = pieces * model
    (
        layer_out, grad_sum, grad_cross_out, grad_cross_mixed, ffn_sums, bias_sums, *ffn_grads
    ) = blocked(
        functools.partial(ffn_kernel, len(sources), depth), "ffn",
        [unit_two, inverse_two, cotangent], [weight_block(cross_weights, 4), whole_vectors],
        [wide, tall, wide, wide], (5 * pieces + 1) * unit, [spot], sources,
        [small, small, *grad_outs(2 * hidden)],
        [
            pltpu.VMEM((model, hidden), LOW), pltpu.VMEM((hidden, model), LOW),
            pltpu.VMEM((total, model), LOW), pltpu.VMEM((total, hidden), LOW),
            pltpu.VMEM((total, model), LOW), pltpu.VMEM((total, hidden), LOW),
            pltpu.VMEM((STEP_ROWS, hidden), FULL), wait_two,
        ],
    )
    if not aligned:
        first, second = ffn_grads[0][:, :hidden], ffn_grads[0][:, hidden:]
        second = second.reshape(model, pieces, model).transpose(1, 0, 2)
        second = second.reshape(count, pieces, rows, model).transpose(0, 2, 1, 3)
        ffn_grads = [jnp.concatenate([first, second.reshape(model, -1)], axis=1)]
    sent, kept = split_core(ffn_grads)
    ffn_moved = exchange(sent, 1)
    cross_dq, cross_dk, cross_dv = call(
        cross_backward_kernel, "cross_backward", [row_starts, col_starts],
        [cross_queries, cross_keys, cross_values, grad_cross_mixed, cross_log],
        [wide, wide, wide], 5 * attend,
    )
    ffn_kept, ffn_moved = sum_square(sum_core(kept, after(ffn_moved, cross_dq)))
    first_sum, self_low, grad_mixed, cross_vector, *cross_grads = call(
        cross_grads_kernel, "cross_grads", [spot],
        [
            cross_dq, cross_dk, cross_dv, cross_weights, vectors, grad_sum, unit_one, inverse_one,
            first_low, encoded, cross_mixed, grad_cross_out,
        ],
        [tall, wide, wide, small, *grad_outs(4 * model)], 6 * unit,
    )
    sent, kept = split_core(cross_grads)
    cross_moved = exchange(sent, 1)
    (encoded_grad,) = blocked(
        encoded_grad_kernel, "encoded_grad", [after(cross_dk, sent), cross_dv],
        [weight_block(cross_weights, 2), weight_block(cross_weights, 3)], [tall], 2 * unit,
    )
    cross_kept, cross_moved = sum_square(sum_core(kept, after(cross_moved, encoded_grad)))
    grad_mixed = after(grad_mixed, encoded_grad, cross_kept)
    self_dq, self_dk, self_dv = call(
        self_backward_kernel, "self_backward", [row_starts],
        [queries, keys, values, grad_mixed, self_sums], [wide, wide, wide], 5 * attend,
    )
    ffn_kept, ffn_moved = sum_layers(add_all(ffn_kept, ffn_moved))
    self_grads = call(
        self_grads_kernel, "self_grads", [spot],
        [tokens, mixed, self_dq, self_dk, self_dv, self_low, cross_vector, ffn_sums, bias_sums],
        grad_outs(4 * model + 128), 4 * unit, (), [pltpu.VMEM((128, model), FULL)],
    )
    sent, kept = split_core(self_grads)
    self_moved = exchange(sent, 1)
    (tokens_grad,) = blocked(
        tokens_grad_kernel, "tokens_grad", [after(self_dq, sent), self_dk, self_dv, first_sum],
        [(self_weights, self_weights.shape, (0, 0))], [tall], 3 * unit,
    )
    self_kept, self_moved = sum_square(sum_core(kept, after(self_moved, tokens_grad)))
    cross_kept, cross_moved = sum_layers(add_all(cross_kept, cross_moved))
    ffn_total = add_all(ffn_kept, ffn_moved)
    cross_total = add_all(cross_kept, cross_moved)
    self_kept, self_moved = sum_layers(add_all(self_kept, self_moved))
    self_total = add_all(self_kept, self_moved)

    def block(values, index):
        return values[:, index * model : (index + 1) * model]

    summed_qkv = jnp.stack(
        [block(self_total, i) for i in range(3)] + [block(cross_total, i) for i in range(3)]
    )
    summed_out = jnp.stack([block(self_total, 3), block(cross_total, 3)])
    summed_ffn_in = ffn_total[:, :hidden]
    summed_ffn_out = (
        ffn_total[:, hidden:].reshape(rows, pieces, model).transpose(1, 0, 2).reshape(-1, model)
    )
    summed_vector = self_total[:, 4 * model : 4 * model + vector_master.shape[0]].T
    grad_scale = 1.0 / math.sqrt(total * count)
    qkv_first_new, qkv_second_new, qkv_master_new, qkv_copy = adamw(
        qkv_master, summed_qkv * grad_scale, qkv_first, qkv_second, 0.04
    )
    out_first_new, out_second_new, out_master_new, out_copy = adamw(
        out_master, summed_out * grad_scale, out_first, out_second, 0.3
    )
    ffn_in_first_new, ffn_in_second_new, ffn_in_master_new, ffn_in_copy = adamw(
        ffn_in_master, summed_ffn_in * grad_scale, ffn_in_first, ffn_in_second, 0.04
    )
    ffn_out_first_new, ffn_out_second_new, ffn_out_master_new, ffn_out_copy = adamw(
        ffn_out_master, summed_ffn_out * grad_scale, ffn_out_first, ffn_out_second, 0.02
    )
    vector_first_new, vector_second_new, vector_master_new, vector_copy = adamw(
        vector_master, summed_vector * grad_scale, vector_first, vector_second, 0.35
    )
    return (
        layer_out,
        tokens_grad,
        encoded_grad,
        qkv_first_new,
        qkv_second_new,
        qkv_master_new,
        qkv_copy,
        out_first_new,
        out_second_new,
        out_master_new,
        out_copy,
        ffn_in_first_new,
        ffn_in_second_new,
        ffn_in_master_new,
        ffn_in_copy,
        ffn_out_first_new,
        ffn_out_second_new,
        ffn_out_master_new,
        ffn_out_copy,
        vector_first_new,
        vector_second_new,
        vector_master_new,
        vector_copy,
    )


def solution(mesh):
    return jax.shard_map(
        body,
        mesh=mesh,
        in_specs=(
            P(("dp", "fsdp"), None),
            P(("dp", "fsdp"), None),
            P(("dp", "fsdp"), None),
            P(("dp", "fsdp"), None),
            P(("dp", "fsdp"), None),
            P(None, ("dp", "fsdp"), None),
            P(None, ("dp", "fsdp"), None),
            P(None, ("dp", "fsdp"), None),
            P(None, ("dp", "fsdp"), None),
            P(None, ("dp", "fsdp"), None),
            P(None, ("dp", "fsdp"), None),
            P(("dp", "fsdp"), None),
            P(("dp", "fsdp"), None),
            P(("dp", "fsdp"), None),
            P(("dp", "fsdp"), None),
            P(("dp", "fsdp"), None),
            P(("dp", "fsdp"), None),
            P(None, ("dp", "fsdp")),
            P(None, ("dp", "fsdp")),
            P(None, ("dp", "fsdp")),
        ),
        out_specs=(
            P(("dp", "fsdp"), None),
            P(("dp", "fsdp"), None),
            P(("dp", "fsdp"), None),
            P(None, ("dp", "fsdp"), None),
            P(None, ("dp", "fsdp"), None),
            P(None, ("dp", "fsdp"), None),
            P(None, ("dp", "fsdp"), None),
            P(None, ("dp", "fsdp"), None),
            P(None, ("dp", "fsdp"), None),
            P(None, ("dp", "fsdp"), None),
            P(None, ("dp", "fsdp"), None),
            P(("dp", "fsdp"), None),
            P(("dp", "fsdp"), None),
            P(("dp", "fsdp"), None),
            P(("dp", "fsdp"), None),
            P(("dp", "fsdp"), None),
            P(("dp", "fsdp"), None),
            P(("dp", "fsdp"), None),
            P(("dp", "fsdp"), None),
            P(None, ("dp", "fsdp")),
            P(None, ("dp", "fsdp")),
            P(None, ("dp", "fsdp")),
            P(None, ("dp", "fsdp")),
        ),
        check_vma=False,
    )
```

time: 375 us -> 294 us (0.78); the launches traced: 370 us -> 293 us
  local copies, waits for them, and re-layouts: 60 us -> 3.41 us
  Pallas kernels: 122 us -> 154 us
  other arithmetic: 35.2 us -> 14.2 us
  matrix products: 17.5 us -> 0 us
  starting transfers between devices: 56.4 us -> 47.8 us
    pallas_call x1 -> x4, Pallas kernels: 21.9 us -> 44.6 us  [blocked(): pl.pallas_call(kernel, grid=(total // STEP_ROWS,), out_shape=shapes, in_s...]
    unnamed x116 -> x95, local copies, waits for them, and re-layouts: 20.4 us -> 2.72 us
    dot_general x10 -> x0, matrix products: 17.5 us -> none  [weight_grad(): lax.dot_general(left, right, (((0,), (0,)), ((), ())), preferred_element_...]
    another operation x17 -> x3, other arithmetic: 14.9 us -> 0.15 us  [layer_stack(): jnp.stack([piece] + [exchange(piece, 2 * k) for k in range(1, depth)])]
    reshape x6 -> x1, local copies, waits for them, and re-layouts: 12.9 us -> 0.05 us  [to_columns(): return values.reshape(-1, rows, model).transpose(1, 0, 2).reshape(rows, -1)]
    slice x18 -> x2, local copies, waits for them, and re-layouts: 10.9 us -> 0.06 us  [the longest x1 0.04 us: body(): ffn_near = square_list(later_stack[:, :, cross_columns:])]
    gather x3 -> x0, local copies, waits for them, and re-layouts: 9.23 us -> none  [ordered(): return flat[jnp.arange(count) ^ own_index()]]
    ppermute x51 -> x48, starting transfers between devices: 56.4 us -> 47.8 us  [exchange(): return lax.ppermute(values, AXES, [(i, i ^ offset) for i in range(count)])]
  transfers between devices with their start and end apart: 51 -> 48, of which waited for: 18 -> 14; matrix products, arithmetic and copies ran while one was open for 17% -> 4% of each run, Pallas kernels for 12% -> 31%
where the time goes in v3:
time: 294 us; the launch traced here: 293 us
  Pallas kernels  154 us (52%)
  waiting for transfers between devices  72.9 us (25%)
  starting transfers between devices  47.8 us (16%)
  other arithmetic  14.2 us (5%)
  local copies, waits for them, and re-layouts  3.41 us (1%)
    pallas_call x6, Pallas kernels, call(): pl.pallas_call(kernel, out_shape=shapes, in_specs=specs, out_specs=[pl.Bl...  109 us
    ppermute x48, waiting for transfers between devices, exchange(): return lax.ppermute(values, AXES, [(i, i ^ offset) for i in range(count)])  72.9 us
    ppermute x48, starting transfers between devices, exchange(): return lax.ppermute(values, AXES, [(i, i ^ offset) for i in range(count)])  47.8 us
    pallas_call x4, Pallas kernels, blocked(): pl.pallas_call(kernel, grid=(total // STEP_ROWS,), out_shape=shapes, in_s...  44.6 us
  transfers between devices with their start and end apart: 48, of which 14 were waited for; matrix products, arithmetic and copies ran while one was open for 4% of the time, Pallas kernels for 31%

profile of v3, /device:TPU:0, one launch (start us, length us, event | category | flops | bytes accessed | tf_op | source)
XLA Modules:
  0.0 293.3 jit_solution(17714920102395011290)
XLA Ops:
  2.3 3.0 %collective-permute-start = (bf16[16,1664]{1,0:T(8,128)(2,1)S(1)}, bf16[16,1664]{1,0:T(8,128)(2,1)S(1)}, u32[]{:S(2)}, u32[]{:S(2)}) collective-permute-start(bf16[16,1664]{1,0:T(8,128)(2,1)S(1)} %fusion.30), channel_id=1, source_target_pairs={{0,2},{1,3},{2,0},{3,1},{4,6},{5,7},{6,4},{7,5},{8,10},{9,11},{10,... | collective-permute-start | bytes 159752 | tf_op jit(solution)/shard_map/ppermute | solution.py:542
  5.4 2.6 collective-permute-start.1
  11.4 2.5 collective-permute-done.2
  14.0 1.5 collective-permute-start.4
  15.6 1.5 collective-permute-start.6
  17.0 1.5 collective-permute-start.7
  19.0 3.8 %collective-permute-done.3 = bf16[16,6656]{1,0:T(8,128)(2,1)S(1)} collective-permute-done((bf16[16,6656]{1,0:T(8,128)(2,1)S(1)}, bf16[16,6656]{1,0:T(8,128)(2,1)S(1)}, u32[]{:S(2)}, u32[]{:S(2)}) %collective-permute-start.3) | collective-permute-done | bytes 213024 | tf_op jit(solution)/shard_map/ppermute | solution.py:542
  22.8 2.1 collective-permute-start.5
  24.9 5.7 %collective-permute-done.4 = bf16[16,6656]{1,0:T(8,128)(2,1)S(1)} collective-permute-done((bf16[16,6656]{1,0:T(8,128)(2,1)S(1)}, bf16[16,6656]{1,0:T(8,128)(2,1)S(1)}, u32[]{:S(2)}, u32[]{:S(2)}) %collective-permute-start.4) | collective-permute-done | bytes 213024 | tf_op jit(solution)/shard_map/ppermute | solution.py:542
  31.8 1.6 collective-permute-start.20
  34.0 1.5 collective-permute-start.14
  35.5 1.4 collective-permute-start.15
  39.0 14.7 %collective-permute-done.13.rest_1_ = bf16[4,16,2560]{2,1,0:T(8,128)(2,1)S(1)} collective-permute-done((bf16[4,16,2560]{2,1,0:T(8,128)(2,1)S(1)}, bf16[4,16,2560]{2,1,0:T(8,128)(2,1)S(1)}, u32[]{:S(2)}, u32[]{:S(2)}) %collective-permute-start.13) | collective-permute-done | bytes 327712 | tf_op jit(solution)/shard_map/ppermute | solution.py:542
  53.7 1.5 collective-permute-start.21
  55.2 1.4 collective-permute-start.22
  56.6 5.1 %collective-permute-done.15.rest_3_ = bf16[4,16,2560]{2,1,0:T(8,128)(2,1)S(1)} collective-permute-done((bf16[4,16,2560]{2,1,0:T(8,128)(2,1)S(1)}, bf16[4,16,2560]{2,1,0:T(8,128)(2,1)S(1)}, u32[]{:S(2)}, u32[]{:S(2)}) %collective-permute-start.15) | collective-permute-done | bytes 327712 | tf_op jit(solution)/shard_map/ppermute | solution.py:542
  62.3 20.4 %self_forward.1 = (bf16[512,1664]{1,0:T(8,128)(2,1)}, f32[24,512]{1,0:T(8,128)}, bf16[1024,512]{1,0:T(8,128)(2,1)}, bf16[1024,512]{1,0:T(8,128)(2,1)}, bf16[1024...) custom-call(s32[1]{0:T(128)} %bitcast.place, s32[11]{0:T(128)} %convert_reduce_fusion.1.row_starts, ...), custom_call_target="tpu_custom_call" | custom-call | flops 6979321856 | bytes 8781824 | tf_op jit(solution)/shard_map/self_forward/pallas_call | solution.py:483
  84.7 25.2 %cross_forward.1 = (bf16[512,2560]{1,0:T(8,128)(2,1)}, f32[1024,512]{1,0:T(8,128)}, f32[1024,1]{1,0:T(8,128)}, bf16[1024,512]{1,0:T(8,128)(2,1)}, bf16[1024,512]...) custom-call(s32[1]{0:T(128)} %bitcast.place, ...), custom_call_target="tpu_custom_call" | custom-call | flops 7516192768 | bytes 15863808 | tf_op jit(solution)/shard_map/cross_forward/pallas_call | solution.py:483
  109.9 5.1 %cross_finish.1 = (f32[1024,512]{1,0:T(8,128)}, f32[1024,1]{1,0:T(8,128)}) custom-call(f32[1024,512]{1,0:T(8,128)} %get-tuple-element.75.unit_one, bf16[1024,512]{1,0:T(8,128)(2,1)} %get-tuple-element.76.cross_mixed, bf16[512,2560]{1,0:T(8,128)(2,1)} %get-tuple-element.77.weights.cross_out.key_weights.value_weights, f32[24,512]{1,0:T(8,128)} %get-tuple-element.74.vectors), custom_call_target="tpu_custom_call" | custom-call | flops 536870912 | bytes 5246976 | tf_op jit(solution)/shard_map/cross_finish/pallas_call | solution.py:508
  116.3 28.1 %ffn.1 = (bf16[1024,512]{1,0:T(8,128)(2,1)}, f32[1024,512]{1,0:T(8,128)}, bf16[1024,512]{1,0:T(8,128)(2,1)}, bf16[1024,512]{1,0:T(8,128)(2,1)}, f32[8,512]{1,0:T...) custom-call(s32[1]{0:T(128)} %bitcast.place, ...), custom_call_target="tpu_custom_call" | custom-call | flops 11274289152 | bytes 16814080 | tf_op jit(solution)/shard_map/ffn/pallas_call | solution.py:508
  144.4 22.0 %cross_backward.1 = (bf16[1024,512]{1,0:T(8,128)(2,1)}, bf16[1024,512]{1,0:T(8,128)(2,1)}, bf16[1024,512]{1,0:T(8,128)(2,1)}) custom-call(s32[11]{0:T(128)} %convert_reduce_fusion.1.row_starts, s32[11]{0:T(128)} %convert_reduce_fusion.col_starts, bf16[1024,512]{1,0:T(8,128)(2,1)} %get-tuple-element.84.queries, bf16[1024,512]{1,0:T(8,128)(2,1)} %get-tuple-element.85.keys, ...), custom_call_target="tpu_custom_call" | custom-call | flops 13421772800 | bytes 7421952 | tf_op jit(solution)/shard_map/cross_backward/pallas_call | solution.py:483
  166.5 12.5 %cross_grads.1 = (f32[1024,512]{1,0:T(8,128)}, bf16[1024,512]{1,0:T(8,128)(2,1)}, bf16[1024,512]{1,0:T(8,128)(2,1)}, f32[8,512]{1,0:T(8,128)}, bf16[16,16,2048]{...) custom-call(s32[1]{0:T(128)} %bitcast.place, bf16[1024,512]{1,0:T(8,128)(2,1)} %get-tuple-element.89.dq, ...), custom_call_target="tpu_custom_call" | custom-call | flops 3221225472 | bytes 20516864 | tf_op jit(solution)/shard_map/cross_grads/pallas_call | solution.py:483
  179.4 5.0 %encoded_grad.1 = f32[1024,512]{1,0:T(8,128)} custom-call(bf16[1024,512]{1,0:T(8,128)(2,1)} %get-tuple-element.98.dk, bf16[1024,512]{1,0:T(8,128)(2,1)} %get-tuple-element.91.dv, bf16[512,2560]{1,0:T(8,128)(2,1)} %get-tuple-element.77.weights.cross_out.key_weights.value_weights, bf16[512,2560]{1,0:T(8,128)(2,1)} %get-tuple-element.77.weights.cross_out.key_weights.value_weights), custom_call_target="tpu_custom_call" | custom-call | flops 1073741824 | bytes 4194304 | tf_op jit(solution)/shard_map/encoded_grad/pallas_call | solution.py:508
  184.9 1.5 collective-permute-start.35
  187.0 1.5 collective-permute-start.37
  188.5 5.7 %collective-permute-done.35 = bf16[4,16,2048]{2,1,0:T(8,128)(2,1)S(1)} collective-permute-done((bf16[4,16,2048]{2,1,0:T(8,128)(2,1)S(1)}, bf16[4,16,2048]{2,1,0:T(8,128)(2,1)S(1)}, u32[]{:S(2)}, u32[]{:S(2)}) %collective-permute-start.35) | collective-permute-done | bytes 262176 | tf_op jit(solution)/shard_map/ppermute | solution.py:542
  194.2 6.0 %collective-permute-done.36 = bf16[4,16,2048]{2,1,0:T(8,128)(2,1)S(1)} collective-permute-done((bf16[4,16,2048]{2,1,0:T(8,128)(2,1)S(1)}, bf16[4,16,2048]{2,1,0:T(8,128)(2,1)S(1)}, u32[]{:S(2)}, u32[]{:S(2)}) %collective-permute-start.36) | collective-permute-done | bytes 262176 | tf_op jit(solution)/shard_map/ppermute | solution.py:542
  200.1 1.1 convert_add_fusion.3
  201.2 22.2 %self_backward.1 = (bf16[1024,512]{1,0:T(8,128)(2,1)}, bf16[1024,512]{1,0:T(8,128)(2,1)}, bf16[1024,512]{1,0:T(8,128)(2,1)}) custom-call(s32[11]{0:T(128)} %convert_reduce_fusion.1.row_starts, bf16[1024,512]{1,0:T(8,128)(2,1)} %get-tuple-element.81.queries, bf16[1024,512]{1,0:T(8,128)(2,1)} %get-tuple-element.82.keys, ...), custom_call_target="tpu_custom_call" | custom-call | flops 13421772800 | bytes 7421952 | tf_op jit(solution)/shard_map/self_backward/pallas_call | solution.py:483
  223.4 6.7 %self_grads.1 = (bf16[16,16,2176]{2,1,0:T(8,128)(2,1)}, bf16[16,16,2176]{2,1,0:T(8,128)(2,1)}) custom-call(s32[1]{0:T(128)} %bitcast.place, bf16[1024,512]{1,0:T(8,128)(2,1)} %tokens.4, bf16[1024,512]{1,0:T(8,128)(2,1)} %get-tuple-element.73.mixed, bf16[1024,512]{1,0:T(8,128)(2,1)} %get-tuple-element.111.dq, bf16[1024,512]{1,0:T(8,128)(2,1)} %get-tuple-element.104.dk, ...), custom_call_target="tpu_custom_call" | custom-call | flops 2147483648 | bytes 8568832 | tf_op jit(solution)/shard_map/self_grads/pallas_call | solution.py:483
  230.1 3.0 %collective-permute-start.38 = (bf16[16,2048]{1,0:T(8,128)(2,1)S(1)}, bf16[16,2048]{1,0:T(8,128)(2,1)S(1)}, u32[]{:S(2)}, u32[]{:S(2)}) collective-permute-start(bf16[16,2048]{1,0:T(8,128)(2,1)S(1)} %get-tuple-element.156), channel_id=1, source_target_pairs={{0,2},{1,3},{2,0},{3,1},{4,6},{5,7},{6,4},{7,5},{8,10},{9,11},{10,... | collective-permute-start | bytes 196616 | tf_op jit(solution)/shard_map/ppermute | solution.py:542
  233.4 2.2 collective-permute-start.40
  235.5 6.4 %tokens_grad.1 = f32[1024,512]{1,0:T(8,128)} custom-call(bf16[1024,512]{1,0:T(8,128)(2,1)} %get-tuple-element.111.dq, bf16[1024,512]{1,0:T(8,128)(2,1)} %get-tuple-element.104.dk, bf16[1024,512]{1,0:T(8,128)(2,1)} %get-tuple-element.105.dv, f32[1024,512]{1,0:T(8,128)} %get-tuple-element.112.first_sum, bf16[512,1664]{1,0:T(8,128)(2,1)} %get-tuple-element.113.weights), custom_call_target="tpu_custom_call" | custom-call | flops 1610612736 | bytes 7340032 | tf_op jit(solution)/shard_map/tokens_grad/pallas_call | solution.py:508
  242.0 2.3 convert_add_fusion
  245.2 1.3 collective-permute-start.43
  246.5 1.6 collective-permute-start.44
  249.1 1.3 collective-permute-start.30
  250.4 9.0 %collective-permute-done.42 = bf16[4,16,4096]{2,1,0:T(8,128)(2,1)S(1)} collective-permute-done((bf16[4,16,4096]{2,1,0:T(8,128)(2,1)S(1)}, bf16[4,16,4096]{2,1,0:T(8,128)(2,1)S(1)}, u32[]{:S(2)}, u32[]{:S(2)}) %collective-permute-start.42) | collective-permute-done | bytes 524320 | tf_op jit(solution)/shard_map/ppermute | solution.py:542
  259.4 1.3 collective-permute-start.31
  260.7 10.5 %collective-permute-done.43 = bf16[4,16,4096]{2,1,0:T(8,128)(2,1)S(1)} collective-permute-done((bf16[4,16,4096]{2,1,0:T(8,128)(2,1)S(1)}, bf16[4,16,4096]{2,1,0:T(8,128)(2,1)S(1)}, u32[]{:S(2)}, u32[]{:S(2)}) %collective-permute-start.43) | collective-permute-done | bytes 524320 | tf_op jit(solution)/shard_map/ppermute | solution.py:542
  271.6 1.1 collective-permute-start.45
  272.8 1.1 collective-permute-start.46
  273.9 2.8 collective-permute-done.29
  276.7 1.7 collective-permute-start.47
  278.3 3.5 %collective-permute-done.30 = bf16[4,16,2176]{2,1,0:T(8,128)(2,1)S(1)} collective-permute-done((bf16[4,16,2176]{2,1,0:T(8,128)(2,1)S(1)}, bf16[4,16,2176]{2,1,0:T(8,128)(2,1)S(1)}, u32[]{:S(2)}, u32[]{:S(2)}) %collective-permute-start.30) | collective-permute-done | bytes 278560 | tf_op jit(solution)/shard_map/ppermute | solution.py:542
  283.0 1.3 collective-permute-start.33
  284.3 2.2 collective-permute-start.34
  288.4 2.5 collective-permute-done.33
  (193 shorter events, 22.4 us)
Async XLA Ops:
  2.3 8.5 %collective-permute-start = (bf16[16,1664]{1,0:T(8,128)(2,1)S(1)}, bf16[16,1664]{1,0:T(8,128)(2,1)S(1)}, u32[]{:S(2)}, u32[]{:S(2)}) collective-permute-start(bf16[16,1664]{1,0:T(8,128)(2,1)S(1)} %fusion.30), channel_id=1, source_target_pairs={{0,2},{1,3},{2,0},{3,1},{4,6},{5,7},{6,4},{7,5},{8,10},{9,11},{10,... | collective-permute-start | bytes 159752 | tf_op jit(solution)/shard_map/ppermute | solution.py:542
  5.4 6.1 %collective-permute-start.1 = (bf16[16,1664]{1,0:T(8,128)(2,1)S(1)}, bf16[16,1664]{1,0:T(8,128)(2,1)S(1)}, u32[]{:S(2)}, u32[]{:S(2)}) collective-permute-start(bf16[16,1664]{1,0:T(8,128)(2,1)S(1)} %fusion.30), channel_id=1, source_target_pairs={{0,4},{1,5},{2,6},{3,7},{4,0},{5,1},{6,2},{7,3},{8,12},{9,13},{10,... | collective-permute-start | bytes 159752 | tf_op jit(solution)/shard_map/ppermute | solution.py:542
  7.9 5.9 %collective-permute-start.2 = (bf16[16,1664]{1,0:T(8,128)(2,1)S(1)}, bf16[16,1664]{1,0:T(8,128)(2,1)S(1)}, u32[]{:S(2)}, u32[]{:S(2)}) collective-permute-start(bf16[16,1664]{1,0:T(8,128)(2,1)S(1)} %fusion.30), channel_id=1, source_target_pairs={{0,6},{1,7},{2,4},{3,5},{4,2},{5,3},{6,0},{7,1},{8,14},{9,15},{10,... | collective-permute-start | bytes 159752 | tf_op jit(solution)/shard_map/ppermute | solution.py:542
  13.9 8.9 %collective-permute-start.3 = (bf16[16,6656]{1,0:T(8,128)(2,1)S(1)}, bf16[16,6656]{1,0:T(8,128)(2,1)S(1)}, u32[]{:S(2)}, u32[]{:S(2)}) collective-permute-start(bf16[16,6656]{1,0:T(8,128)(2,1)S(1)} %constant_dynamic-update-slice_fusion), channel_id=1, source_target_pairs={{0,2},{1,3},{2,0},{3,1},{4,6},{5,7},{6,4},{7,5},{8,10},{9,11},{10,... | collective-permute-start | bytes 638984 | tf_op jit(solution)/shard_map/ppermute | solution.py:542
  14.0 16.6 %collective-permute-start.4 = (bf16[16,6656]{1,0:T(8,128)(2,1)S(1)}, bf16[16,6656]{1,0:T(8,128)(2,1)S(1)}, u32[]{:S(2)}, u32[]{:S(2)}) collective-permute-start(bf16[16,6656]{1,0:T(8,128)(2,1)S(1)} %constant_dynamic-update-slice_fusion), channel_id=1, source_target_pairs={{0,4},{1,5},{2,6},{3,7},{4,0},{5,1},{6,2},{7,3},{8,12},{9,13},{10,... | collective-permute-start | bytes 638984 | tf_op jit(solution)/shard_map/ppermute | solution.py:542
  15.6 15.0 %collective-permute-start.6 = (bf16[4,16,1664]{2,1,0:T(8,128)(2,1)S(1)}, bf16[4,16,1664]{2,1,0:T(8,128)(2,1)S(1)}, u32[]{:S(2)}, u32[]{:S(2)}) collective-permute-start(bf16[4,16,1664]{2,1,0:T(8,128)(2,1)S(1)} %pad_maximum_fusion.1.rest_0_), channel_id=1, source_target_pairs={{0,8},{1,9},{2,10},{3,11},{4,12},{5,13},{6,14},{7,15},{8,0},{9,1},... | collective-permute-start | bytes 638984 | tf_op jit(solution)/shard_map/ppermute | solution.py:542
  17.0 14.1 %collective-permute-start.7 = (bf16[4,16,1664]{2,1,0:T(8,128)(2,1)S(1)}, bf16[4,16,1664]{2,1,0:T(8,128)(2,1)S(1)}, u32[]{:S(2)}, u32[]{:S(2)}) collective-permute-start(bf16[4,16,1664]{2,1,0:T(8,128)(2,1)S(1)} %pad_maximum_fusion.1.rest_0_), channel_id=1, source_target_pairs={{0,16},{1,17},{2,18},{3,19},{4,20},{5,21},{6,22},{7,23},{8,24},{9,... | collective-permute-start | bytes 638984 | tf_op jit(solution)/shard_map/ppermute | solution.py:542
  18.6 12.6 %collective-permute-start.8 = (bf16[4,16,1664]{2,1,0:T(8,128)(2,1)S(1)}, bf16[4,16,1664]{2,1,0:T(8,128)(2,1)S(1)}, u32[]{:S(2)}, u32[]{:S(2)}) collective-permute-start(bf16[4,16,1664]{2,1,0:T(8,128)(2,1)S(1)} %pad_maximum_fusion.1.rest_0_), channel_id=1, source_target_pairs={{0,24},{1,25},{2,26},{3,27},{4,28},{5,29},{6,30},{7,31},{8,16},{9,... | collective-permute-start | bytes 638984 | tf_op jit(solution)/shard_map/ppermute | solution.py:542
  22.8 8.8 %collective-permute-start.5 = (bf16[16,6656]{1,0:T(8,128)(2,1)S(1)}, bf16[16,6656]{1,0:T(8,128)(2,1)S(1)}, u32[]{:S(2)}, u32[]{:S(2)}) collective-permute-start(bf16[16,6656]{1,0:T(8,128)(2,1)S(1)} %constant_dynamic-update-slice_fusion), channel_id=1, source_target_pairs={{0,6},{1,7},{2,4},{3,5},{4,2},{5,3},{6,0},{7,1},{8,14},{9,15},{10,... | collective-permute-start | bytes 638984 | tf_op jit(solution)/shard_map/ppermute | solution.py:542
  30.6 2.8 collective-permute-start.9
  30.6 3.4 %collective-permute-start.10 = (bf16[4,16,1664]{2,1,0:T(8,128)(2,1)S(1)}, bf16[4,16,1664]{2,1,0:T(8,128)(2,1)S(1)}, u32[]{:S(2)}, u32[]{:S(2)}) collective-permute-start(bf16[4,16,1664]{2,1,0:T(8,128)(2,1)S(1)} %collective-permute-done.6.rest_1_), channel_id=1, source_target_pairs={{0,1},{1,0},{2,3},{3,2},{4,5},{5,4},{6,7},{7,6},{8,9},{9,8},{10,11... | collective-permute-start | bytes 638984 | tf_op jit(solution)/shard_map/ppermute | solution.py:542
  31.1 4.4 %collective-permute-start.11 = (bf16[4,16,1664]{2,1,0:T(8,128)(2,1)S(1)}, bf16[4,16,1664]{2,1,0:T(8,128)(2,1)S(1)}, u32[]{:S(2)}, u32[]{:S(2)}) collective-permute-start(bf16[4,16,1664]{2,1,0:T(8,128)(2,1)S(1)} %collective-permute-done.7.rest_2_), channel_id=1, source_target_pairs={{0,1},{1,0},{2,3},{3,2},{4,5},{5,4},{6,7},{7,6},{8,9},{9,8},{10,11... | collective-permute-start | bytes 638984 | tf_op jit(solution)/shard_map/ppermute | solution.py:542
  31.2 5.8 %collective-permute-start.12 = (bf16[4,16,1664]{2,1,0:T(8,128)(2,1)S(1)}, bf16[4,16,1664]{2,1,0:T(8,128)(2,1)S(1)}, u32[]{:S(2)}, u32[]{:S(2)}) collective-permute-start(bf16[4,16,1664]{2,1,0:T(8,128)(2,1)S(1)} %collective-permute-done.8.rest_3_), channel_id=1, source_target_pairs={{0,1},{1,0},{2,3},{3,2},{4,5},{5,4},{6,7},{7,6},{8,9},{9,8},{10,11... | collective-permute-start | bytes 638984 | tf_op jit(solution)/shard_map/ppermute | solution.py:542
  31.8 30.5 %collective-permute-start.20 = (bf16[4,16,4096]{2,1,0:T(8,128)(2,1)S(1)}, bf16[4,16,4096]{2,1,0:T(8,128)(2,1)S(1)}, u32[]{:S(2)}, u32[]{:S(2)}) collective-permute-start(bf16[4,16,4096]{2,1,0:T(8,128)(2,1)S(1)} %slice.93.rest_0_), channel_id=1, source_target_pairs={{0,8},{1,9},{2,10},{3,11},{4,12},{5,13},{6,14},{7,15},{8,0},{9,1},... | collective-permute-start | bytes 1572872 | tf_op jit(solution)/shard_map/ppermute | solution.py:542
  33.4 20.3 %collective-permute-start.13 = (bf16[4,16,2560]{2,1,0:T(8,128)(2,1)S(1)}, bf16[4,16,2560]{2,1,0:T(8,128)(2,1)S(1)}, u32[]{:S(2)}, u32[]{:S(2)}) collective-permute-start(bf16[4,16,2560]{2,1,0:T(8,128)(2,1)S(1)} %slice.92.rest_0_), channel_id=1, source_target_pairs={{0,8},{1,9},{2,10},{3,11},{4,12},{5,13},{6,14},{7,15},{8,0},{9,1},... | collective-permute-start | bytes 983048 | tf_op jit(solution)/shard_map/ppermute | solution.py:542
  34.0 21.2 %collective-permute-start.14 = (bf16[4,16,2560]{2,1,0:T(8,128)(2,1)S(1)}, bf16[4,16,2560]{2,1,0:T(8,128)(2,1)S(1)}, u32[]{:S(2)}, u32[]{:S(2)}) collective-permute-start(bf16[4,16,2560]{2,1,0:T(8,128)(2,1)S(1)} %slice.92.rest_0_), channel_id=1, source_target_pairs={{0,16},{1,17},{2,18},{3,19},{4,20},{5,21},{6,22},{7,23},{8,24},{9,... | collective-permute-start | bytes 983048 | tf_op jit(solution)/shard_map/ppermute | solution.py:542
  35.5 26.2 %collective-permute-start.15 = (bf16[4,16,2560]{2,1,0:T(8,128)(2,1)S(1)}, bf16[4,16,2560]{2,1,0:T(8,128)(2,1)S(1)}, u32[]{:S(2)}, u32[]{:S(2)}) collective-permute-start(bf16[4,16,2560]{2,1,0:T(8,128)(2,1)S(1)} %slice.92.rest_0_), channel_id=1, source_target_pairs={{0,24},{1,25},{2,26},{3,27},{4,28},{5,29},{6,30},{7,31},{8,16},{9,... | collective-permute-start | bytes 983048 | tf_op jit(solution)/shard_map/ppermute | solution.py:542
  37.0 24.8 %collective-permute-start.16 = (bf16[4,16,2560]{2,1,0:T(8,128)(2,1)S(1)}, bf16[4,16,2560]{2,1,0:T(8,128)(2,1)S(1)}, u32[]{:S(2)}, u32[]{:S(2)}) collective-permute-start(bf16[4,16,2560]{2,1,0:T(8,128)(2,1)S(1)} %slice.92.rest_0_), channel_id=1, source_target_pairs={{0,1},{1,0},{2,3},{3,2},{4,5},{5,4},{6,7},{7,6},{8,9},{9,8},{10,11... | collective-permute-start | bytes 983048 | tf_op jit(solution)/shard_map/ppermute | solution.py:542
  53.7 29.6 %collective-permute-start.21 = (bf16[4,16,4096]{2,1,0:T(8,128)(2,1)S(1)}, bf16[4,16,4096]{2,1,0:T(8,128)(2,1)S(1)}, u32[]{:S(2)}, u32[]{:S(2)}) collective-permute-start(bf16[4,16,4096]{2,1,0:T(8,128)(2,1)S(1)} %slice.93.rest_0_), channel_id=1, source_target_pairs={{0,16},{1,17},{2,18},{3,19},{4,20},{5,21},{6,22},{7,23},{8,24},{9,... | collective-permute-start | bytes 1572872 | tf_op jit(solution)/shard_map/ppermute | solution.py:542
  55.2 28.1 %collective-permute-start.22 = (bf16[4,16,4096]{2,1,0:T(8,128)(2,1)S(1)}, bf16[4,16,4096]{2,1,0:T(8,128)(2,1)S(1)}, u32[]{:S(2)}, u32[]{:S(2)}) collective-permute-start(bf16[4,16,4096]{2,1,0:T(8,128)(2,1)S(1)} %slice.93.rest_0_), channel_id=1, source_target_pairs={{0,24},{1,25},{2,26},{3,27},{4,28},{5,29},{6,30},{7,31},{8,16},{9,... | collective-permute-start | bytes 1572872 | tf_op jit(solution)/shard_map/ppermute | solution.py:542
  61.7 22.1 %collective-permute-start.17 = (bf16[4,16,2560]{2,1,0:T(8,128)(2,1)S(1)}, bf16[4,16,2560]{2,1,0:T(8,128)(2,1)S(1)}, u32[]{:S(2)}, u32[]{:S(2)}) collective-permute-start(bf16[4,16,2560]{2,1,0:T(8,128)(2,1)S(1)} %collective-permute-done.13.rest_1_), channel_id=1, source_target_pairs={{0,1},{1,0},{2,3},{3,2},{4,5},{5,4},{6,7},{7,6},{8,9},{9,8},{10,11... | collective-permute-start | bytes 983048 | tf_op jit(solution)/shard_map/ppermute | solution.py:542
  61.8 22.8 %collective-permute-start.18 = (bf16[4,16,2560]{2,1,0:T(8,128)(2,1)S(1)}, bf16[4,16,2560]{2,1,0:T(8,128)(2,1)}, u32[]{:S(2)}, u32[]{:S(2)}) collective-permute-start(bf16[4,16,2560]{2,1,0:T(8,128)(2,1)S(1)} %collective-permute-done.14.rest_2_), channel_id=1, source_target_pairs={{0,1},{1,0},{2,3},{3,2},{4,5},{5,4},{6,7},{7,6},{8,9},{9,8},{10,11... | collective-permute-start | bytes 983048 | tf_op jit(solution)/shard_map/ppermute | solution.py:542
  62.3 22.4 %collective-permute-start.19 = (bf16[4,16,2560]{2,1,0:T(8,128)(2,1)S(1)}, bf16[4,16,2560]{2,1,0:T(8,128)(2,1)}, u32[]{:S(2)}, u32[]{:S(2)}) collective-permute-start(bf16[4,16,2560]{2,1,0:T(8,128)(2,1)S(1)} %collective-permute-done.15.rest_3_), channel_id=1, source_target_pairs={{0,1},{1,0},{2,3},{3,2},{4,5},{5,4},{6,7},{7,6},{8,9},{9,8},{10,11... | collective-permute-start | bytes 983048 | tf_op jit(solution)/shard_map/ppermute | solution.py:542
  83.2 31.8 %collective-permute-start.23 = (bf16[4,16,4096]{2,1,0:T(8,128)(2,1)S(1)}, bf16[4,16,4096]{2,1,0:T(8,128)(2,1)S(1)}, u32[]{:S(2)}, u32[]{:S(2)}) collective-permute-start(bf16[4,16,4096]{2,1,0:T(8,128)(2,1)S(1)} %slice.93.rest_0_), channel_id=1, source_target_pairs={{0,1},{1,0},{2,3},{3,2},{4,5},{5,4},{6,7},{7,6},{8,9},{9,8},{10,11... | collective-permute-start | bytes 1572872 | tf_op jit(solution)/shard_map/ppermute | solution.py:542
  83.3 31.7 %collective-permute-start.24 = (bf16[4,16,4096]{2,1,0:T(8,128)(2,1)S(1)}, bf16[4,16,4096]{2,1,0:T(8,128)(2,1)S(1)}, u32[]{:S(2)}, u32[]{:S(2)}) collective-permute-start(bf16[4,16,4096]{2,1,0:T(8,128)(2,1)S(1)} %collective-permute-done.20.rest_1_), channel_id=1, source_target_pairs={{0,1},{1,0},{2,3},{3,2},{4,5},{5,4},{6,7},{7,6},{8,9},{9,8},{10,11... | collective-permute-start | bytes 1572872 | tf_op jit(solution)/shard_map/ppermute | solution.py:542
  83.8 31.2 %collective-permute-start.25 = (bf16[4,16,4096]{2,1,0:T(8,128)(2,1)S(1)}, bf16[4,16,4096]{2,1,0:T(8,128)(2,1)S(1)}, u32[]{:S(2)}, u32[]{:S(2)}) collective-permute-start(bf16[4,16,4096]{2,1,0:T(8,128)(2,1)S(1)} %collective-permute-done.21.rest_2_), channel_id=1, source_target_pairs={{0,1},{1,0},{2,3},{3,2},{4,5},{5,4},{6,7},{7,6},{8,9},{9,8},{10,11... | collective-permute-start | bytes 1572872 | tf_op jit(solution)/shard_map/ppermute | solution.py:542
  84.6 30.5 %collective-permute-start.26 = (bf16[4,16,4096]{2,1,0:T(8,128)(2,1)S(1)}, bf16[4,16,4096]{2,1,0:T(8,128)(2,1)S(1)}, u32[]{:S(2)}, u32[]{:S(2)}) collective-permute-start(bf16[4,16,4096]{2,1,0:T(8,128)(2,1)S(1)} %collective-permute-done.22.rest_3_), channel_id=1, source_target_pairs={{0,1},{1,0},{2,3},{3,2},{4,5},{5,4},{6,7},{7,6},{8,9},{9,8},{10,11... | collective-permute-start | bytes 1572872 | tf_op jit(solution)/shard_map/ppermute | solution.py:542
  179.0 5.4 %collective-permute-start.27 = (bf16[16,16,2048]{2,1,0:T(8,128)(2,1)}, bf16[16,16,2048]{2,1,0:T(8,128)(2,1)S(1)}, u32[]{:S(2)}, u32[]{:S(2)}) collective-permute-start(bf16[16,16,2048]{2,1,0:T(8,128)(2,1)} %get-tuple-element.97), channel_id=1, source_target_pairs={{0,1},{1,0},{2,3},{3,2},{4,5},{5,4},{6,7},{7,6},{8,9},{9,8},{10,11... | collective-permute-start | bytes 3145736 | tf_op jit(solution)/shard_map/ppermute | solution.py:542
  184.9 9.2 %collective-permute-start.35 = (bf16[4,16,2048]{2,1,0:T(8,128)(2,1)S(1)}, bf16[4,16,2048]{2,1,0:T(8,128)(2,1)S(1)}, u32[]{:S(2)}, u32[]{:S(2)}) collective-permute-start(bf16[4,16,2048]{2,1,0:T(8,128)(2,1)S(1)} %get-tuple-element.147), channel_id=1, source_target_pairs={{0,8},{1,9},{2,10},{3,11},{4,12},{5,13},{6,14},{7,15},{8,0},{9,1},... | collective-permute-start | bytes 786440 | tf_op jit(solution)/shard_map/ppermute | solution.py:542
  186.5 13.7 %collective-permute-start.36 = (bf16[4,16,2048]{2,1,0:T(8,128)(2,1)S(1)}, bf16[4,16,2048]{2,1,0:T(8,128)(2,1)S(1)}, u32[]{:S(2)}, u32[]{:S(2)}) collective-permute-start(bf16[4,16,2048]{2,1,0:T(8,128)(2,1)S(1)} %get-tuple-element.149), channel_id=1, source_target_pairs={{0,16},{1,17},{2,18},{3,19},{4,20},{5,21},{6,22},{7,23},{8,24},{9,... | collective-permute-start | bytes 786440 | tf_op jit(solution)/shard_map/ppermute | solution.py:542
  187.0 13.2 %collective-permute-start.37 = (bf16[4,16,2048]{2,1,0:T(8,128)(2,1)S(1)}, bf16[4,16,2048]{2,1,0:T(8,128)(2,1)}, u32[]{:S(2)}, u32[]{:S(2)}) collective-permute-start(bf16[4,16,2048]{2,1,0:T(8,128)(2,1)S(1)} %get-tuple-element.148), channel_id=1, source_target_pairs={{0,24},{1,25},{2,26},{3,27},{4,28},{5,29},{6,30},{7,31},{8,16},{9,... | collective-permute-start | bytes 786440 | tf_op jit(solution)/shard_map/ppermute | solution.py:542
  188.5 53.5 %collective-permute-start.41 = (bf16[16,16,4096]{2,1,0:T(8,128)(2,1)}, bf16[16,16,4096]{2,1,0:T(8,128)(2,1)}, u32[]{:S(2)}, u32[]{:S(2)}) collective-permute-start(bf16[16,16,4096]{2,1,0:T(8,128)(2,1)} %get-tuple-element.117), channel_id=1, source_target_pairs={{0,1},{1,0},{2,3},{3,2},{4,5},{5,4},{6,7},{7,6},{8,9},{9,8},{10,11... | collective-permute-start | bytes 6291464 | tf_op jit(solution)/shard_map/ppermute | solution.py:542
  230.1 18.0 %collective-permute-start.28 = (bf16[16,16,2176]{2,1,0:T(8,128)(2,1)}, bf16[16,16,2176]{2,1,0:T(8,128)(2,1)S(1)}, u32[]{:S(2)}, u32[]{:S(2)}) collective-permute-start(bf16[16,16,2176]{2,1,0:T(8,128)(2,1)} %get-tuple-element.110), channel_id=1, source_target_pairs={{0,1},{1,0},{2,3},{3,2},{4,5},{5,4},{6,7},{7,6},{8,9},{9,8},{10,11... | collective-permute-start | bytes 3342344 | tf_op jit(solution)/shard_map/ppermute | solution.py:542
  230.1 11.8 %collective-permute-start.38 = (bf16[16,2048]{1,0:T(8,128)(2,1)S(1)}, bf16[16,2048]{1,0:T(8,128)(2,1)S(1)}, u32[]{:S(2)}, u32[]{:S(2)}) collective-permute-start(bf16[16,2048]{1,0:T(8,128)(2,1)S(1)} %get-tuple-element.156), channel_id=1, source_target_pairs={{0,2},{1,3},{2,0},{3,1},{4,6},{5,7},{6,4},{7,5},{8,10},{9,11},{10,... | collective-permute-start | bytes 196616 | tf_op jit(solution)/shard_map/ppermute | solution.py:542
  233.1 8.8 %collective-permute-start.39 = (bf16[16,2048]{1,0:T(8,128)(2,1)S(1)}, bf16[16,2048]{1,0:T(8,128)(2,1)S(1)}, u32[]{:S(2)}, u32[]{:S(2)}) collective-permute-start(bf16[16,2048]{1,0:T(8,128)(2,1)S(1)} %get-tuple-element.158), channel_id=1, source_target_pairs={{0,4},{1,5},{2,6},{3,7},{4,0},{5,1},{6,2},{7,3},{8,12},{9,13},{10,... | collective-permute-start | bytes 196616 | tf_op jit(solution)/shard_map/ppermute | solution.py:542
  233.4 8.6 %collective-permute-start.40 = (bf16[16,2048]{1,0:T(8,128)(2,1)S(1)}, bf16[16,2048]{1,0:T(8,128)(2,1)S(1)}, u32[]{:S(2)}, u32[]{:S(2)}) collective-permute-start(bf16[16,2048]{1,0:T(8,128)(2,1)S(1)} %get-tuple-element.157), channel_id=1, source_target_pairs={{0,6},{1,7},{2,4},{3,5},{4,2},{5,3},{6,0},{7,1},{8,14},{9,15},{10,... | collective-permute-start | bytes 196616 | tf_op jit(solution)/shard_map/ppermute | solution.py:542
  244.6 14.9 %collective-permute-start.42 = (bf16[4,16,4096]{2,1,0:T(8,128)(2,1)S(1)}, bf16[4,16,4096]{2,1,0:T(8,128)(2,1)S(1)}, u32[]{:S(2)}, u32[]{:S(2)}) collective-permute-start(bf16[4,16,4096]{2,1,0:T(8,128)(2,1)S(1)} %get-tuple-element.141), channel_id=1, source_target_pairs={{0,8},{1,9},{2,10},{3,11},{4,12},{5,13},{6,14},{7,15},{8,0},{9,1},... | collective-permute-start | bytes 1572872 | tf_op jit(solution)/shard_map/ppermute | solution.py:542
  245.2 26.1 %collective-permute-start.43 = (bf16[4,16,4096]{2,1,0:T(8,128)(2,1)S(1)}, bf16[4,16,4096]{2,1,0:T(8,128)(2,1)S(1)}, u32[]{:S(2)}, u32[]{:S(2)}) collective-permute-start(bf16[4,16,4096]{2,1,0:T(8,128)(2,1)S(1)} %get-tuple-element.143), channel_id=1, source_target_pairs={{0,16},{1,17},{2,18},{3,19},{4,20},{5,21},{6,22},{7,23},{8,24},{9,... | collective-permute-start | bytes 1572872 | tf_op jit(solution)/shard_map/ppermute | solution.py:542
  246.5 24.8 %collective-permute-start.44 = (bf16[4,16,4096]{2,1,0:T(8,128)(2,1)S(1)}, bf16[4,16,4096]{2,1,0:T(8,128)(2,1)S(1)}, u32[]{:S(2)}, u32[]{:S(2)}) collective-permute-start(bf16[4,16,4096]{2,1,0:T(8,128)(2,1)S(1)} %get-tuple-element.142), channel_id=1, source_target_pairs={{0,24},{1,25},{2,26},{3,27},{4,28},{5,29},{6,30},{7,31},{8,16},{9,... | collective-permute-start | bytes 1572872 | tf_op jit(solution)/shard_map/ppermute | solution.py:542
  248.5 28.2 %collective-permute-start.29 = (bf16[4,16,2176]{2,1,0:T(8,128)(2,1)S(1)}, bf16[4,16,2176]{2,1,0:T(8,128)(2,1)S(1)}, u32[]{:S(2)}, u32[]{:S(2)}) collective-permute-start(bf16[4,16,2176]{2,1,0:T(8,128)(2,1)S(1)} %get-tuple-element.144), channel_id=1, source_target_pairs={{0,8},{1,9},{2,10},{3,11},{4,12},{5,13},{6,14},{7,15},{8,0},{9,1},... | collective-permute-start | bytes 835592 | tf_op jit(solution)/shard_map/ppermute | solution.py:542
  249.1 32.7 %collective-permute-start.30 = (bf16[4,16,2176]{2,1,0:T(8,128)(2,1)S(1)}, bf16[4,16,2176]{2,1,0:T(8,128)(2,1)S(1)}, u32[]{:S(2)}, u32[]{:S(2)}) collective-permute-start(bf16[4,16,2176]{2,1,0:T(8,128)(2,1)S(1)} %get-tuple-element.146), channel_id=1, source_target_pairs={{0,16},{1,17},{2,18},{3,19},{4,20},{5,21},{6,22},{7,23},{8,24},{9,... | collective-permute-start | bytes 835592 | tf_op jit(solution)/shard_map/ppermute | solution.py:542
  259.4 22.4 %collective-permute-start.31 = (bf16[4,16,2176]{2,1,0:T(8,128)(2,1)S(1)}, bf16[4,16,2176]{2,1,0:T(8,128)(2,1)S(1)}, u32[]{:S(2)}, u32[]{:S(2)}) collective-permute-start(bf16[4,16,2176]{2,1,0:T(8,128)(2,1)S(1)} %get-tuple-element.145), channel_id=1, source_target_pairs={{0,24},{1,25},{2,26},{3,27},{4,28},{5,29},{6,30},{7,31},{8,16},{9,... | collective-permute-start | bytes 835592 | tf_op jit(solution)/shard_map/ppermute | solution.py:542
  271.6 12.7 %collective-permute-start.45 = (bf16[16,4096]{1,0:T(8,128)(2,1)S(1)}, bf16[16,4096]{1,0:T(8,128)(2,1)S(1)}, u32[]{:S(2)}, u32[]{:S(2)}) collective-permute-start(bf16[16,4096]{1,0:T(8,128)(2,1)S(1)} %get-tuple-element.150), channel_id=1, source_target_pairs={{0,2},{1,3},{2,0},{3,1},{4,6},{5,7},{6,4},{7,5},{8,10},{9,11},{10,... | collective-permute-start | bytes 393224 | tf_op jit(solution)/shard_map/ppermute | solution.py:542
  272.8 13.7 %collective-permute-start.46 = (bf16[16,4096]{1,0:T(8,128)(2,1)S(1)}, bf16[16,4096]{1,0:T(8,128)(2,1)S(1)}, u32[]{:S(2)}, u32[]{:S(2)}) collective-permute-start(bf16[16,4096]{1,0:T(8,128)(2,1)S(1)} %get-tuple-element.152), channel_id=1, source_target_pairs={{0,4},{1,5},{2,6},{3,7},{4,0},{5,1},{6,2},{7,3},{8,12},{9,13},{10,... | collective-permute-start | bytes 393224 | tf_op jit(solution)/shard_map/ppermute | solution.py:542
  276.7 9.8 %collective-permute-start.47 = (bf16[16,4096]{1,0:T(8,128)(2,1)S(1)}, bf16[16,4096]{1,0:T(8,128)(2,1)S(1)}, u32[]{:S(2)}, u32[]{:S(2)}) collective-permute-start(bf16[16,4096]{1,0:T(8,128)(2,1)S(1)} %get-tuple-element.151), channel_id=1, source_target_pairs={{0,6},{1,7},{2,4},{3,5},{4,2},{5,3},{6,0},{7,1},{8,14},{9,15},{10,... | collective-permute-start | bytes 393224 | tf_op jit(solution)/shard_map/ppermute | solution.py:542
  282.0 6.3 %collective-permute-start.32 = (bf16[16,2176]{1,0:T(8,128)(2,1)S(1)}, bf16[16,2176]{1,0:T(8,128)(2,1)S(1)}, u32[]{:S(2)}, u32[]{:S(2)}) collective-permute-start(bf16[16,2176]{1,0:T(8,128)(2,1)S(1)} %get-tuple-element.153), channel_id=1, source_target_pairs={{0,2},{1,3},{2,0},{3,1},{4,6},{5,7},{6,4},{7,5},{8,10},{9,11},{10,... | collective-permute-start | bytes 208904 | tf_op jit(solution)/shard_map/ppermute | solution.py:542
  283.0 7.9 %collective-permute-start.33 = (bf16[16,2176]{1,0:T(8,128)(2,1)S(1)}, bf16[16,2176]{1,0:T(8,128)(2,1)S(1)}, u32[]{:S(2)}, u32[]{:S(2)}) collective-permute-start(bf16[16,2176]{1,0:T(8,128)(2,1)S(1)} %get-tuple-element.155), channel_id=1, source_target_pairs={{0,4},{1,5},{2,6},{3,7},{4,0},{5,1},{6,2},{7,3},{8,12},{9,13},{10,... | collective-permute-start | bytes 208904 | tf_op jit(solution)/shard_map/ppermute | solution.py:542
  284.3 6.6 %collective-permute-start.34 = (bf16[16,2176]{1,0:T(8,128)(2,1)S(1)}, bf16[16,2176]{1,0:T(8,128)(2,1)S(1)}, u32[]{:S(2)}, u32[]{:S(2)}) collective-permute-start(bf16[16,2176]{1,0:T(8,128)(2,1)S(1)} %get-tuple-element.154), channel_id=1, source_target_pairs={{0,6},{1,7},{2,4},{3,5},{4,2},{5,3},{6,0},{7,1},{8,14},{9,15},{10,... | collective-permute-start | bytes 208904 | tf_op jit(solution)/shard_map/ppermute | solution.py:542
  (42 other events, 570.3 us)

commit v4 on v3

--- a/solution.py
+++ b/solution.py
@@ -47,41 +47,74 @@
     return (place >= begin) & (place < end)
 
 
+def each_span(row_starts, col_starts, total, same, work):
+    def segment(s, carry):
+        row_begin, row_end = row_starts[s], row_starts[s + 1]
+        col_begin, col_end = col_starts[s], col_starts[s + 1]
+        row_short = row_end - window(row_begin, 128, total) <= 128
+        col_short = col_end - window(col_begin, 128, total) <= 128
+        for row_span in (128, 256):
+            for col_span in (128, 256):
+                if same and row_span != col_span:
+                    continue
+                wanted = row_short if row_span == 128 else jnp.logical_not(row_short)
+                if not same:
+                    other = col_short if col_span == 128 else jnp.logical_not(col_short)
+                    wanted = jnp.logical_and(wanted, other)
+
+                @pl.when(wanted)
+                def _(row_span=row_span, col_span=col_span):
+                    row_base = window(row_begin, row_span, total)
+                    col_base = window(col_begin, col_span, total)
+                    work(
+                        s,
+                        pl.ds(row_base, row_span),
+                        pl.ds(col_base, col_span),
+                        inside(row_base, row_span, row_begin, row_end),
+                        inside(col_base, col_span, col_begin, col_end),
+                        row_span,
+                    )
+
+        return carry
+
+    lax.fori_loop(0, SEGMENTS, segment, 0)
+
+
 def attend_forward(row_starts, col_starts, q_ref, k_ref, v_ref, out_ref, sums_ref):
     total, model = q_ref.shape
     width = model // HEADS
     group = 256 // width
-    span = 256
     scales = head_masks(width, group, 1.0 / math.sqrt(width))
-
-    def segment(s, carry):
-        row_begin, row_end = row_starts[s], row_starts[s + 1]
-        col_begin, col_end = col_starts[s], col_starts[s + 1]
-        row_base, col_base = window(row_begin, span, total), window(col_begin, span, total)
-        rows, cols = pl.ds(row_base, span), pl.ds(col_base, span)
-        row_mask = inside(row_base, span, row_begin, row_end)
-        col_mask = inside(col_base, span, col_begin, col_end)
-        for g in range(HEADS // group):
-            lanes = slice(g * 256, (g + 1) * 256)
-            query, keys, values = q_ref[rows, lanes], k_ref[cols, lanes], v_ref[cols, lanes]
+    parts = [slice(g * 256, (g + 1) * 256) for g in range(HEADS // group)]
+
+    def work(s, rows, cols, row_mask, col_mask, span):
+        raw = []
+        for lanes in parts:
+            query, keys = q_ref[rows, lanes], k_ref[cols, lanes]
             stacked = jnp.concatenate([query * scale for scale in scales], axis=0)
-            scores = jnp.where(col_mask, dot_nt(keys, stacked), mask_fill)
+            raw.append(dot_nt(keys, stacked))
+        turned = [v_ref[cols, lanes].T for lanes in parts]
+        probs = []
+        for g, item in enumerate(raw):
+            scores = jnp.where(col_mask, item, mask_fill)
             largest = jnp.max(scores, axis=0, keepdims=True)
             expo = jnp.exp(scores - largest)
             totals = jnp.sum(expo, axis=0, keepdims=True)
-            sums_ref[s, g] = largest + jnp.log(totals)
-            probs = (expo * (1.0 / totals)).astype(LOW)
-            turned = values.T
-            parts = [
-                dot_nn(turned[h * width : (h + 1) * width], probs[:, h * span : (h + 1) * span])
+            sums_ref[s, g, :, : group * span] = largest + jnp.log(totals)
+            probs.append((expo * (1.0 / totals)).astype(LOW))
+        mixed = [
+            [
+                dot_nn(side[h * width : (h + 1) * width], prob[:, h * span : (h + 1) * span])
                 for h in range(group)
             ]
-            mixed = jnp.concatenate(parts, axis=0).T
+            for side, prob in zip(turned, probs)
+        ]
+        for lanes, items in zip(parts, mixed):
+            value = jnp.concatenate(items, axis=0).T
             old = out_ref[rows, lanes].astype(FULL)
-            out_ref[rows, lanes] = jnp.where(row_mask, mixed, old).astype(LOW)
-        return carry
-
-    lax.fori_loop(0, SEGMENTS, segment, 0)
+            out_ref[rows, lanes] = jnp.where(row_mask, value, old).astype(LOW)
+
+    each_span(row_starts, col_starts, total, row_starts is col_starts, work)
 
 
 def attend_backward(
@@ -90,49 +123,49 @@
     total, model = q_ref.shape
     width = model // HEADS
     group = 256 // width
-    span = 256
     factor = 1.0 / math.sqrt(width)
     scales = head_masks(width, group, factor)
     picks = head_masks(width, group, 1.0)
-
-    def segment(s, carry):
-        row_begin, row_end = row_starts[s], row_starts[s + 1]
-        col_begin, col_end = col_starts[s], col_starts[s + 1]
-        row_base, col_base = window(row_begin, span, total), window(col_begin, span, total)
-        rows, cols = pl.ds(row_base, span), pl.ds(col_base, span)
-        row_mask = inside(row_base, span, row_begin, row_end)
-        col_mask = inside(col_base, span, col_begin, col_end)
-        for g in range(HEADS // group):
-            lanes = slice(g * 256, (g + 1) * 256)
+    parts = [slice(g * 256, (g + 1) * 256) for g in range(HEADS // group)]
+
+    def work(s, rows, cols, row_mask, col_mask, span):
+        stacks, grads, raw, grad_probs = [], [], [], []
+        for lanes in parts:
             query, keys, values = q_ref[rows, lanes], k_ref[cols, lanes], v_ref[cols, lanes]
             grad = jnp.where(row_mask, grad_ref[rows, lanes].astype(FULL), 0.0).astype(LOW)
-            stacked = jnp.concatenate([query * scale for scale in scales], axis=0)
-            grads = jnp.concatenate([grad * item for item in picks], axis=0)
-            scores = jnp.where(col_mask, dot_nt(keys, stacked), mask_fill)
-            probs = jnp.exp(scores - sums_ref[s, g])
-            grad_values = dot_nn(probs.astype(LOW), grads)
-            weighted = probs * dot_nt(values, grads)
+            stacks.append(jnp.concatenate([query * scale for scale in scales], axis=0))
+            grads.append(jnp.concatenate([grad * item for item in picks], axis=0))
+            raw.append(dot_nt(keys, stacks[-1]))
+            grad_probs.append(dot_nt(values, grads[-1]))
+        grad_values, grad_scores = [], []
+        for g, (item, grad_prob) in enumerate(zip(raw, grad_probs)):
+            scores = jnp.where(col_mask, item, mask_fill)
+            probs = jnp.exp(scores - sums_ref[s, g, :, : group * span])
+            grad_values.append(dot_nn(probs.astype(LOW), grads[g]))
+            weighted = probs * grad_prob
             inner = jnp.sum(weighted, axis=0, keepdims=True)
-            grad_scores = (weighted - probs * inner).astype(LOW)
-            grad_keys = dot_nn(grad_scores, stacked)
-            turned = keys.T
-            parts = [
-                dot_nn(
-                    turned[h * width : (h + 1) * width], grad_scores[:, h * span : (h + 1) * span]
-                )
-                for h in range(group)
-            ]
-            grad_query = jnp.concatenate(parts, axis=0).T * factor
+            grad_scores.append((weighted - probs * inner).astype(LOW))
+        grad_keys, grad_queries = [], []
+        for lanes, item, stacked in zip(parts, grad_scores, stacks):
+            grad_keys.append(dot_nn(item, stacked))
+            turned = k_ref[cols, lanes].T
+            grad_queries.append(
+                [
+                    dot_nn(turned[h * width : (h + 1) * width], item[:, h * span : (h + 1) * span])
+                    for h in range(group)
+                ]
+            )
+        for g, lanes in enumerate(parts):
+            grad_query = jnp.concatenate(grad_queries[g], axis=0).T * factor
             for ref, place, mask, value in (
                 (dq_ref, rows, row_mask, grad_query),
-                (dk_ref, cols, col_mask, grad_keys),
-                (dv_ref, cols, col_mask, grad_values),
+                (dk_ref, cols, col_mask, grad_keys[g]),
+                (dv_ref, cols, col_mask, grad_values[g]),
             ):
                 old = ref[place, lanes].astype(FULL)
                 ref[place, lanes] = jnp.where(mask, value, old).astype(LOW)
-        return carry
-
-    lax.fori_loop(0, SEGMENTS, segment, 0)
+
+    each_span(row_starts, col_starts, total, row_starts is col_starts, work)
 
 
 def normalize(values):
@@ -470,26 +503,83 @@
     tokens_grad[...] = below + dot_nt(dv[...], weights[:, 2 * model : 3 * model])
 
 
-PARAMS = pltpu.CompilerParams(vmem_limit_bytes=58 << 20)
-ANY = pl.BlockSpec(memory_space=pl.ANY)
+def fold_core_kernel(shape, place, kept, received, own, *sends):
+    dp_count, depth = shape
+    at = place[0] // (2 * depth)
+    for k, ref in enumerate((own, *sends)):
+        spot = pl.ds((at ^ k) * depth, depth)
+        value = kept[spot].astype(FULL) + received[spot].astype(FULL)
+        ref[...] = value.astype(ref.dtype)
+
+
+def fold_square_kernel(shape, place, kept, *rest):
+    dp_count, depth = shape
+    received, outs = rest[: dp_count - 1], rest[dp_count - 1 :]
+    at = place[0] // 2 % depth
+    for k, ref in enumerate(outs):
+        spot = pl.ds(at ^ k, 1)
+        value = kept[spot]
+        for item in received:
+            value = value + item[spot].astype(FULL)
+        ref[...] = value[0].astype(ref.dtype)
+
+
+LIMITS = {
+    "fold_core": 12,
+    "fold_square": 10,
+    "self_forward": 14,
+    "cross_forward": 16,
+    "cross_finish": 9,
+    "ffn": 27,
+    "cross_backward": 11,
+    "cross_grads": 16,
+    "encoded_grad": 9,
+    "self_backward": 11,
+    "self_grads": 14,
+    "tokens_grad": 11,
+}
+
+
+def out_kind(item):
+    if len(item) == 3:
+        return pltpu.VMEM(item[0], item[1])
+    return jax.ShapeDtypeStruct(*item)
+
+
+def keep(item):
+    return (item[0], item[1], True)
+
+
+def limit(name):
+    return pltpu.CompilerParams(vmem_limit_bytes=LIMITS[name] << 20)
+
+
+def pinned(sources):
+    if len(sources) == 1:
+        return sources
+    return [pltpu.with_memory_space_constraint(item, pltpu.VMEM) for item in sources]
+
+
+def source_spec(sources):
+    return pl.BlockSpec(memory_space=pltpu.VMEM if len(sources) > 1 else pl.ANY)
 
 
 def call(kernel, name, scalars, arrays, outs, flops, sources=(), scratch=()):
     specs = [pl.BlockSpec(memory_space=pltpu.SMEM)] * len(scalars)
     specs += [pl.BlockSpec(memory_space=pltpu.VMEM)] * len(arrays)
-    specs += [ANY] * len(sources)
-    shapes = [jax.ShapeDtypeStruct(*item) for item in outs]
-    moved = sum(item.size * item.dtype.itemsize for item in [*arrays, *sources, *shapes])
+    specs += [source_spec(sources)] * len(sources)
+    shapes = [out_kind(item) for item in outs]
+    moved = sum(item.size * item.dtype.itemsize for item in [*arrays, *sources])
     return pl.pallas_call(
         kernel,
         out_shape=shapes,
         in_specs=specs,
         out_specs=[pl.BlockSpec(memory_space=pltpu.VMEM)] * len(outs),
         scratch_shapes=list(scratch),
-        compiler_params=PARAMS,
+        compiler_params=limit(name),
         cost_estimate=pl.CostEstimate(flops=flops, transcendentals=0, bytes_accessed=moved),
         name=name,
-    )(*scalars, *arrays, *sources)
+    )(*scalars, *arrays, *pinned(sources))
 
 
 def blocked(kernel, name, arrays, fixed, outs, flops, scalars=(), sources=(), fixed_outs=(), scratch=()):
@@ -497,14 +587,19 @@
     specs = [pl.BlockSpec(memory_space=pltpu.SMEM)] * len(scalars)
     specs += [pl.BlockSpec((STEP_ROWS, item.shape[1]), lambda i: (i, 0)) for item in arrays]
     for item, shape, index in fixed:
-        specs.append(pl.BlockSpec(shape, lambda i, index=index: index))
-    specs += [ANY] * len(sources)
-    shapes = [jax.ShapeDtypeStruct(*item) for item in [*outs, *fixed_outs]]
+        specs.append(
+            pl.BlockSpec(shape, lambda i, index=index: index, pipeline_mode=pl.Buffered(1))
+        )
+    specs += [source_spec(sources)] * len(sources)
+    shapes = [out_kind(item) for item in [*outs, *fixed_outs]]
     out_specs = [pl.BlockSpec((STEP_ROWS, item[0][1]), lambda i: (i, 0)) for item in outs]
     for item in fixed_outs:
-        out_specs.append(pl.BlockSpec(item[0], lambda i, size=len(item[0]): (0,) * size))
+        index = (0,) * len(item[0])
+        out_specs.append(
+            pl.BlockSpec(item[0], lambda i, index=index: index, pipeline_mode=pl.Buffered(1))
+        )
     inputs = [*arrays, *[item[0] for item in fixed]]
-    moved = sum(item.size * item.dtype.itemsize for item in [*arrays, *sources, *shapes])
+    moved = sum(item.size * item.dtype.itemsize for item in [*arrays, *sources])
     return pl.pallas_call(
         kernel,
         grid=(total // STEP_ROWS,),
@@ -512,10 +607,10 @@
         in_specs=specs,
         out_specs=out_specs,
         scratch_shapes=list(scratch),
-        compiler_params=PARAMS,
+        compiler_params=limit(name),
         cost_estimate=pl.CostEstimate(flops=flops, transcendentals=0, bytes_accessed=moved),
         name=name,
-    )(*scalars, *inputs, *sources)
+    )(*scalars, *inputs, *pinned(sources))
 
 
 def segment_starts(ids):
@@ -574,33 +669,49 @@
 def split_core(grads):
     if len(grads) == 2:
         return grads
-    dp_count, fsdp_count = lax.axis_size("dp"), lax.axis_size("fsdp")
-    count = dp_count * fsdp_count
+    count = lax.axis_size("dp") * lax.axis_size("fsdp")
     core = lax.axis_index("fsdp") % 2
     parts = grads[0].reshape((count // 2, 2, -1) + grads[0].shape[1:])
     return pick(parts, 1 - core, 1), pick(parts, core, 1)
 
 
-def sum_core(kept, received):
-    dp_count = lax.axis_size("dp")
-    shape = (dp_count, kept.shape[0] // dp_count) + kept.shape[1:]
-    return kept.reshape(shape).astype(FULL) + received.reshape(shape).astype(FULL)
-
-
-def sum_square(pair):
-    dp_count, fsdp_count = lax.axis_size("dp"), lax.axis_size("fsdp")
-    place = lax.axis_index("dp")
-    moved = [
-        exchange(pick(pair, place ^ k, 0).astype(LOW), fsdp_count * k) for k in range(1, dp_count)
-    ]
-    return pick(pair, place, 0), moved
-
-
-def sum_layers(square):
-    depth = lax.axis_size("fsdp") // 2
-    place = lax.axis_index("fsdp") // 2
-    moved = [exchange(pick(square, place ^ k, 0).astype(LOW), 2 * k) for k in range(1, depth)]
-    return pick(square, place, 0), moved
+def fold_core(spot, kept, received):
+    dp_count, depth = lax.axis_size("dp"), lax.axis_size("fsdp") // 2
+    shape = (depth,) + kept.shape[1:]
+    if kept.shape[1] % 16:
+        place = lax.axis_index("dp")
+        pair = (kept.astype(FULL) + received.astype(FULL)).reshape((dp_count,) + shape)
+        sends = [pick(pair, place ^ k, 0).astype(LOW) for k in range(1, dp_count)]
+        return pick(pair, place, 0), sends
+    own, *sends = call(
+        functools.partial(fold_core_kernel, (dp_count, depth)), "fold_core", [spot],
+        [kept, received], [(shape, FULL)] + [(shape, LOW)] * (dp_count - 1), kept.size,
+    )
+    return own, sends
+
+
+def fold_square(spot, kept, received):
+    dp_count, depth = lax.axis_size("dp"), lax.axis_size("fsdp") // 2
+    shape = kept.shape[1:]
+    if kept.shape[1] % 16:
+        place = lax.axis_index("fsdp") // 2
+        square = add_all(kept, received)
+        sends = [pick(square, place ^ k, 0).astype(LOW) for k in range(1, depth)]
+        return pick(square, place, 0), sends
+    own, *sends = call(
+        functools.partial(fold_square_kernel, (dp_count, depth)), "fold_square", [spot],
+        [kept, *received], [(shape, FULL)] + [(shape, LOW)] * (depth - 1), kept.size,
+    )
+    return own, sends
+
+
+def move_square(sends):
+    stride = lax.axis_size("fsdp")
+    return [exchange(item, stride * (k + 1)) for k, item in enumerate(sends)]
+
+
+def move_layers(sends):
+    return [exchange(item, 2 * (k + 1)) for k, item in enumerate(sends)]
 
 
 def add_all(kept, moved):
@@ -638,7 +749,8 @@
     aligned = rows % 16 == 0
     place = lax.axis_index("dp") * fsdp_count + lax.axis_index("fsdp")
     spot = place.reshape(1).astype(jnp.int32)
-    low_qkv, low_out = qkv_master.astype(LOW), out_master.astype(LOW)
+    low_qkv = after(qkv_master, spot).astype(LOW)
+    low_out = out_master.astype(LOW)
     low_vector = jnp.pad(vector_master.astype(LOW).T, ((0, 0), (0, 128 - vector_master.shape[0])))
     pieces = ffn_in_master.shape[1] // model
 
@@ -694,7 +806,10 @@
     ) = call(
         functools.partial(self_forward_kernel, len(sources), depth), "self_forward",
         [spot, row_starts], [after(tokens, later_stack)],
-        [((model, self_piece.shape[1]), LOW), ((24, model), FULL), wide, wide, wide, wide, log_sums],
+        [
+            keep(((model, self_piece.shape[1]), LOW)), ((24, model), FULL),
+            keep(wide), keep(wide), keep(wide), keep(wide), keep(log_sums),
+        ],
         3 * unit + 2 * attend, sources, [wait_one],
     )
     sources = sources_of(core_list(cross_near))
@@ -704,7 +819,10 @@
     ) = call(
         functools.partial(cross_forward_kernel, len(sources), depth), "cross_forward",
         [spot, row_starts, col_starts], [tokens, encoded, mixed, vectors],
-        [((model, cross_columns), LOW), tall, thin, wide, wide, wide, wide, wide, log_sums],
+        [
+            keep(((model, cross_columns), LOW)), keep(tall), thin, keep(wide), keep(wide),
+            keep(wide), keep(wide), keep(wide), keep(log_sums),
+        ],
         4 * unit + 2 * attend, sources, [wait_one],
     )
 
@@ -741,17 +859,18 @@
     ffn_moved = exchange(sent, 1)
     cross_dq, cross_dk, cross_dv = call(
         cross_backward_kernel, "cross_backward", [row_starts, col_starts],
-        [cross_queries, cross_keys, cross_values, grad_cross_mixed, cross_log],
-        [wide, wide, wide], 5 * attend,
-    )
-    ffn_kept, ffn_moved = sum_square(sum_core(kept, after(ffn_moved, cross_dq)))
+        [cross_queries, cross_keys, cross_values, after(grad_cross_mixed, sent), cross_log],
+        [keep(wide), keep(wide), keep(wide)], 5 * attend,
+    )
+    ffn_kept, ffn_sends = fold_core(spot, kept, after(ffn_moved, cross_dq))
+    ffn_moved = move_square(ffn_sends)
     first_sum, self_low, grad_mixed, cross_vector, *cross_grads = call(
         cross_grads_kernel, "cross_grads", [spot],
         [
-            cross_dq, cross_dk, cross_dv, cross_weights, vectors, grad_sum, unit_one, inverse_one,
-            first_low, encoded, cross_mixed, grad_cross_out,
+            after(cross_dq, *ffn_sends), cross_dk, cross_dv, cross_weights, vectors, grad_sum,
+            unit_one, inverse_one, first_low, encoded, cross_mixed, grad_cross_out,
         ],
-        [tall, wide, wide, small, *grad_outs(4 * model)], 6 * unit,
+        [keep(tall), keep(wide), keep(wide), small, *grad_outs(4 * model)], 6 * unit,
     )
     sent, kept = split_core(cross_grads)
     cross_moved = exchange(sent, 1)
@@ -759,13 +878,13 @@
         encoded_grad_kernel, "encoded_grad", [after(cross_dk, sent), cross_dv],
         [weight_block(cross_weights, 2), weight_block(cross_weights, 3)], [tall], 2 * unit,
     )
-    cross_kept, cross_moved = sum_square(sum_core(kept, after(cross_moved, encoded_grad)))
-    grad_mixed = after(grad_mixed, encoded_grad, cross_kept)
+    cross_kept, cross_sends = fold_core(spot, kept, after(cross_moved, encoded_grad))
+    cross_moved = move_square(cross_sends)
     self_dq, self_dk, self_dv = call(
         self_backward_kernel, "self_backward", [row_starts],
-        [queries, keys, values, grad_mixed, self_sums], [wide, wide, wide], 5 * attend,
-    )
-    ffn_kept, ffn_moved = sum_layers(add_all(ffn_kept, ffn_moved))
+        [queries, keys, values, after(grad_mixed, *cross_sends), self_sums],
+        [keep(wide), keep(wide), keep(wide)], 5 * attend,
+    )
     self_grads = call(
         self_grads_kernel, "self_grads", [spot],
         [tokens, mixed, self_dq, self_dk, self_dv, self_low, cross_vector, ffn_sums, bias_sums],
@@ -773,15 +892,25 @@
     )
     sent, kept = split_core(self_grads)
     self_moved = exchange(sent, 1)
+    ffn_kept, ffn_sends = fold_square(spot, ffn_kept, [after(item, sent) for item in ffn_moved])
+    ffn_moved = move_layers(ffn_sends)
     (tokens_grad,) = blocked(
-        tokens_grad_kernel, "tokens_grad", [after(self_dq, sent), self_dk, self_dv, first_sum],
+        tokens_grad_kernel, "tokens_grad",
+        [after(self_dq, *ffn_sends), self_dk, self_dv, first_sum],
         [(self_weights, self_weights.shape, (0, 0))], [tall], 3 * unit,
     )
-    self_kept, self_moved = sum_square(sum_core(kept, after(self_moved, tokens_grad)))
-    cross_kept, cross_moved = sum_layers(add_all(cross_kept, cross_moved))
+    self_kept, self_sends = fold_core(spot, kept, after(self_moved, tokens_grad))
+    self_moved = move_square(self_sends)
+    cross_kept, cross_sends = fold_square(
+        spot, cross_kept, [after(item, *self_sends) for item in cross_moved]
+    )
+    cross_moved = move_layers(cross_sends)
     ffn_total = add_all(ffn_kept, ffn_moved)
     cross_total = add_all(cross_kept, cross_moved)
-    self_kept, self_moved = sum_layers(add_all(self_kept, self_moved))
+    self_kept, self_sends = fold_square(
+        spot, self_kept, [after(item, *cross_sends) for item in self_moved]
+    )
+    self_moved = move_layers(self_sends)
     self_total = add_all(self_kept, self_moved)
 
     def block(values, index):

time: 294 us -> 229 us (0.78)
  Pallas kernels: 154 us -> 108 us
  waiting for transfers between devices: 72.9 us -> 49.7 us
  other arithmetic: 14.2 us -> 8.9 us
  local copies, waits for them, and re-layouts: 3.41 us -> 7.98 us
  starting transfers between devices: 47.8 us -> 51.4 us
    pallas_call x6 -> x12, Pallas kernels: 109 us -> 73.6 us  [call(): pl.pallas_call(kernel, out_shape=shapes, in_specs=specs, out_specs=[pl.Bl...]
    ppermute x48, waiting for transfers between devices: 72.9 us -> 49.7 us  [exchange(): return lax.ppermute(values, AXES, [(i, i ^ offset) for i in range(count)])]
    pallas_call x4, Pallas kernels: 44.6 us -> 34.9 us  [blocked(): pl.pallas_call(kernel, grid=(total // STEP_ROWS,), out_shape=shapes, in_s...]
    ppermute x48, starting transfers between devices: 47.8 us -> 51.4 us  [exchange(): return lax.ppermute(values, AXES, [(i, i ^ offset) for i in range(count)])]
    mul x0 -> x2, local copies, waits for them, and re-layouts: none -> 3.25 us  [adamw(): first_new = beta_first * first + (1.0 - beta_first) * grad]
    add x3 -> x0, other arithmetic: 2.94 us -> none  [sum_core(): kept.reshape(shape).astype(FULL) + received.reshape(shape).astype(FULL)]
  transfers between devices with their start and end apart: 48 -> 48, of which waited for: 14 -> 13; matrix products, arithmetic and copies ran while one was open for 4% -> 5% of each run, Pallas kernels for 31% -> 33%
where the time goes in v4:
time: 229 us; the launch traced here: 228 us
  Pallas kernels  108 us (47%)
  starting transfers between devices  51.4 us (22%)
  waiting for transfers between devices  49.7 us (22%)
  other arithmetic  8.9 us (4%)
  local copies, waits for them, and re-layouts  7.98 us (3%)
    pallas_call x12, Pallas kernels, call(): pl.pallas_call(kernel, out_shape=shapes, in_specs=specs, out_specs=[pl.Bl...  73.6 us
    ppermute x48, starting transfers between devices, exchange(): return lax.ppermute(values, AXES, [(i, i ^ offset) for i in range(count)])  51.4 us
    ppermute x48, waiting for transfers between devices, exchange(): return lax.ppermute(values, AXES, [(i, i ^ offset) for i in range(count)])  49.7 us
    pallas_call x4, Pallas kernels, blocked(): pl.pallas_call(kernel, grid=(total // STEP_ROWS,), out_shape=shapes, in_s...  34.9 us
  transfers between devices with their start and end apart: 48, of which 13 were waited for; matrix products, arithmetic and copies ran while one was open for 5% of the time, Pallas kernels for 33%

profile of v4, /device:TPU:0, one launch (start us, length us, event | category | flops | bytes accessed | tf_op | source)
XLA Modules:
  0.0 227.8 jit_solution(12949965261863914951)
XLA Ops:
  2.3 4.1 %collective-permute-start.1 = (bf16[16,1664]{1,0:T(8,128)(2,1)S(1)}, bf16[16,1664]{1,0:T(8,128)(2,1)S(1)}, u32[]{:S(2)}, u32[]{:S(2)}) collective-permute-start(bf16[16,1664]{1,0:T(8,128)(2,1)S(1)} %fusion.2), channel_id=1, source_target_pairs={{0,4},{1,5},{2,6},{3,7},{4,0},{5,1},{6,2},{7,3},{8,12},{9,13},{10,... | collective-permute-start | bytes 159752 | tf_op jit(solution)/shard_map/ppermute | solution.py:637
  6.4 1.6 collective-permute-start
  10.0 1.0 convert_dynamic-update-slice_fusion
  11.0 2.9 %collective-permute-done.2 = bf16[16,1664]{1,0:T(8,128)(2,1)S(1)} collective-permute-done((bf16[16,1664]{1,0:T(8,128)(2,1)S(1)}, bf16[16,1664]{1,0:T(8,128)(2,1)S(1)}, u32[]{:S(2)}, u32[]{:S(2)}) %collective-permute-start.2) | collective-permute-done | bytes 53280 | tf_op jit(solution)/shard_map/ppermute | solution.py:637
  14.9 2.4 %collective-permute-start.8 = (bf16[4,16,1664]{2,1,0:T(8,128)(2,1)S(1)}, bf16[4,16,1664]{2,1,0:T(8,128)(2,1)S(1)}, u32[]{:S(2)}, u32[]{:S(2)}) collective-permute-start(bf16[4,16,1664]{2,1,0:T(8,128)(2,1)S(1)} %pad_maximum_fusion.1.rest_0_), channel_id=1, source_target_pairs={{0,24},{1,25},{2,26},{3,27},{4,28},{5,29},{6,30},{7,31},{8,16},{9,... | collective-permute-start | bytes 638984 | tf_op jit(solution)/shard_map/ppermute | solution.py:637
  18.4 5.2 %collective-permute-done.5 = bf16[16,6656]{1,0:T(8,128)(2,1)S(1)} collective-permute-done((bf16[16,6656]{1,0:T(8,128)(2,1)S(1)}, bf16[16,6656]{1,0:T(8,128)(2,1)S(1)}, u32[]{:S(2)}, u32[]{:S(2)}) %collective-permute-start.5) | collective-permute-done | bytes 213024 | tf_op jit(solution)/shard_map/ppermute | solution.py:637
  23.6 6.4 %collective-permute-start.3 = (bf16[16,6656]{1,0:T(8,128)(2,1)S(1)}, bf16[16,6656]{1,0:T(8,128)(2,1)S(1)}, u32[]{:S(2)}, u32[]{:S(2)}) collective-permute-start(bf16[16,6656]{1,0:T(8,128)(2,1)S(1)} %constant_dynamic-update-slice_fusion), channel_id=1, source_target_pairs={{0,2},{1,3},{2,0},{3,1},{4,6},{5,7},{6,4},{7,5},{8,10},{9,11},{10,... | collective-permute-start | bytes 638984 | tf_op jit(solution)/shard_map/ppermute | solution.py:637
  30.1 2.3 %collective-permute-done.4 = bf16[16,6656]{1,0:T(8,128)(2,1)S(1)} collective-permute-done((bf16[16,6656]{1,0:T(8,128)(2,1)S(1)}, bf16[16,6656]{1,0:T(8,128)(2,1)S(1)}, u32[]{:S(2)}, u32[]{:S(2)}) %collective-permute-start.4) | collective-permute-done | bytes 213024 | tf_op jit(solution)/shard_map/ppermute | solution.py:637
  33.4 1.8 collective-permute-done.3
  35.3 2.5 %collective-permute-start.22 = (bf16[4,16,4096]{2,1,0:T(8,128)(2,1)S(1)}, bf16[4,16,4096]{2,1,0:T(8,128)(2,1)S(1)}, u32[]{:S(2)}, u32[]{:S(2)}) collective-permute-start(bf16[4,16,4096]{2,1,0:T(8,128)(2,1)S(1)} %slice.93.rest_0_), channel_id=1, source_target_pairs={{0,24},{1,25},{2,26},{3,27},{4,28},{5,29},{6,30},{7,31},{8,16},{9,... | collective-permute-start | bytes 1572872 | tf_op jit(solution)/shard_map/ppermute | solution.py:637
  38.5 1.5 collective-permute-start.14
  40.0 1.5 collective-permute-start.13
  42.4 15.8 %collective-permute-done.15.rest_3_ = bf16[4,16,2560]{2,1,0:T(8,128)(2,1)S(1)} collective-permute-done((bf16[4,16,2560]{2,1,0:T(8,128)(2,1)S(1)}, bf16[4,16,2560]{2,1,0:T(8,128)(2,1)S(1)}, u32[]{:S(2)}, u32[]{:S(2)}) %collective-permute-start.15) | collective-permute-done | bytes 327712 | tf_op jit(solution)/shard_map/ppermute | solution.py:637
  58.2 1.5 collective-permute-start.20
  59.7 2.8 %collective-permute-done.14.rest_2_ = bf16[4,16,2560]{2,1,0:T(8,128)(2,1)S(1)} collective-permute-done((bf16[4,16,2560]{2,1,0:T(8,128)(2,1)S(1)}, bf16[4,16,2560]{2,1,0:T(8,128)(2,1)S(1)}, u32[]{:S(2)}, u32[]{:S(2)}) %collective-permute-start.14) | collective-permute-done | bytes 327712 | tf_op jit(solution)/shard_map/ppermute | solution.py:637
  62.5 2.8 %collective-permute-done.13.rest_1_ = bf16[4,16,2560]{2,1,0:T(8,128)(2,1)S(1)} collective-permute-done((bf16[4,16,2560]{2,1,0:T(8,128)(2,1)S(1)}, bf16[4,16,2560]{2,1,0:T(8,128)(2,1)S(1)}, u32[]{:S(2)}, u32[]{:S(2)}) %collective-permute-start.13) | collective-permute-done | bytes 327712 | tf_op jit(solution)/shard_map/ppermute | solution.py:637
  65.8 15.2 %self_forward.1 = (bf16[512,1664]{1,0:T(8,128)(2,1)S(1)}, f32[24,512]{1,0:T(8,128)S(1)}, bf16[1024,512]{1,0:T(8,128)(2,1)S(1)}, bf16[1024,512]{1,0:T(8,128)(2,1)...) custom-call(s32[1]{0:T(128)} %bitcast.place, ...), custom_call_target="tpu_custom_call" | custom-call | flops 6979321856 | bytes 2752512 | tf_op jit(solution)/shard_map/self_forward/pallas_call | solution.py:573
  81.0 1.0 copy-done.5
  83.0 17.3 %cross_forward.1 = (bf16[512,2560]{1,0:T(8,128)(2,1)S(1)}, f32[1024,512]{1,0:T(8,128)S(1)}, f32[1024,1]{1,0:T(8,128)S(1)}, bf16[1024,512]{1,0:T(8,128)(2,1)S(1)}...) custom-call(s32[1]{0:T(128)} %bitcast.place, ...), custom_call_target="tpu_custom_call" | custom-call | flops 7516192768 | bytes 5816320 | tf_op jit(solution)/shard_map/cross_forward/pallas_call | solution.py:573
  100.4 2.0 cross_finish.1
  102.5 26.4 %ffn.1 = (bf16[1024,512]{1,0:T(8,128)(2,1)}, f32[1024,512]{1,0:T(8,128)S(1)}, bf16[1024,512]{1,0:T(8,128)(2,1)S(1)}, bf16[1024,512]{1,0:T(8,128)(2,1)S(1)}, f32[...) custom-call(s32[1]{0:T(128)} %bitcast.place, ...), custom_call_target="tpu_custom_call" | custom-call | flops 11274289152 | bytes 7344128 | tf_op jit(solution)/shard_map/ffn/pallas_call | solution.py:603
  129.0 14.0 %cross_backward.1 = (bf16[1024,512]{1,0:T(8,128)(2,1)S(1)}, bf16[1024,512]{1,0:T(8,128)(2,1)S(1)}, bf16[1024,512]{1,0:T(8,128)(2,1)S(1)}) custom-call(s32[11]{0:T(128)S(1)} %convert_reduce_fusion.1.row_starts, s32[11]{0:T(128)S(1)} %convert_reduce_fusion.col_starts, bf16[1024,512]{1,0:T(8,128)(2,1)S(1)} %get-tuple-element.121.queries, ...), custom_call_target="tpu_custom_call" | custom-call | flops 13421772800 | bytes 4276224 | tf_op jit(solution)/shard_map/cross_backward/pallas_call | solution.py:573
  143.4 5.9 %cross_grads.1 = (f32[1024,512]{1,0:T(8,128)S(1)}, bf16[1024,512]{1,0:T(8,128)(2,1)S(1)}, bf16[1024,512]{1,0:T(8,128)(2,1)S(1)}, f32[8,512]{1,0:T(8,128)S(1)}, b...) custom-call(s32[1]{0:T(128)} %bitcast.place, bf16[1024,512]{1,0:T(8,128)(2,1)S(1)} %get-tuple-element.134.dq, ...), custom_call_target="tpu_custom_call" | custom-call | flops 3221225472 | bytes 14209024 | tf_op jit(solution)/shard_map/cross_grads/pallas_call | solution.py:573
  150.2 2.8 %collective-permute-start.31 = (bf16[4,16,4096]{2,1,0:T(8,128)(2,1)S(1)}, bf16[4,16,4096]{2,1,0:T(8,128)(2,1)S(1)}, u32[]{:S(2)}, u32[]{:S(2)}) collective-permute-start(bf16[4,16,4096]{2,1,0:T(8,128)(2,1)S(1)} %get-tuple-element.133), channel_id=1, source_target_pairs={{0,24},{1,25},{2,26},{3,27},{4,28},{5,29},{6,30},{7,31},{8,16},{9,... | collective-permute-start | bytes 1572872 | tf_op jit(solution)/shard_map/ppermute | solution.py:637
  153.0 3.1 %encoded_grad.1 = f32[1024,512]{1,0:T(8,128)} custom-call(bf16[1024,512]{1,0:T(8,128)(2,1)S(1)} %get-tuple-element.144.dk, bf16[1024,512]{1,0:T(8,128)(2,1)S(1)} %get-tuple-element.136.dv, bf16[512,2560]{1,0:T(8,128)(2,1)S(1)} %get-tuple-element.114.weights.cross_out.key_weights.value_weights, ...), custom_call_target="tpu_custom_call" | custom-call | flops 1073741824 | bytes 2097152 | tf_op jit(solution)/shard_map/encoded_grad/pallas_call | solution.py:603
  156.1 1.0 fold_core.4
  157.9 15.4 %self_backward.1 = (bf16[1024,512]{1,0:T(8,128)(2,1)S(1)}, bf16[1024,512]{1,0:T(8,128)(2,1)S(1)}, bf16[1024,512]{1,0:T(8,128)(2,1)S(1)}) custom-call(s32[11]{0:T(128)S(1)} %convert_reduce_fusion.1.row_starts, bf16[1024,512]{1,0:T(8,128)(2,1)S(1)} %copy-done.4, bf16[1024,512]{1,0:T(8,128)(2,1)S(1)} %copy-done.6, bf16[1024,512]{1,0:T(8,128)(2,1)S(1)} %copy-done.8, ...), custom_call_target="tpu_custom_call" | custom-call | flops 13421772800 | bytes 4276224 | tf_op jit(solution)/shard_map/self_backward/pallas_call | solution.py:573
  173.3 3.5 %self_grads.1 = (bf16[16,16,2176]{2,1,0:T(8,128)(2,1)}, bf16[16,16,2176]{2,1,0:T(8,128)(2,1)S(1)}) custom-call(s32[1]{0:T(128)} %bitcast.place, bf16[1024,512]{1,0:T(8,128)(2,1)S(1)} %copy-done.2, bf16[1024,512]{1,0:T(8,128)(2,1)S(1)} %get-tuple-element.110.mixed, bf16[1024,512]{1,0:T(8,128)(2,1)S(1)} %get-tuple-element.166.dq, ...), custom_call_target="tpu_custom_call" | custom-call | flops 2147483648 | bytes 6340608 | tf_op jit(solution)/shard_map/self_grads/pallas_call | solution.py:573
  177.2 2.0 collective-permute-start.46
  179.2 2.4 %collective-permute-start.47 = (bf16[16,4096]{1,0:T(8,128)(2,1)S(1)}, bf16[16,4096]{1,0:T(8,128)(2,1)S(1)}, u32[]{:S(2)}, u32[]{:S(2)}) collective-permute-start(bf16[16,4096]{1,0:T(8,128)(2,1)S(1)} %get-tuple-element.165), channel_id=1, source_target_pairs={{0,6},{1,7},{2,4},{3,5},{4,2},{5,3},{6,0},{7,1},{8,14},{9,15},{10,... | collective-permute-start | bytes 393224 | tf_op jit(solution)/shard_map/ppermute | solution.py:637
  181.8 3.4 %tokens_grad.1 = f32[1024,512]{1,0:T(8,128)} custom-call(bf16[1024,512]{1,0:T(8,128)(2,1)S(1)} %get-tuple-element.166.dq, bf16[1024,512]{1,0:T(8,128)(2,1)S(1)} %get-tuple-element.153.dk, bf16[1024,512]{1,0:T(8,128)(2,1)S(1)} %get-tuple-element.154.dv, f32[1024,512]{1,0:T(8,128)S(1)} %get-tuple-element.167.first_sum, ...), custom_call_target="tpu_custom_call" | custom-call | flops 1610612736 | bytes 5242880 | tf_op jit(solution)/shard_map/tokens_grad/pallas_call | solution.py:603
  185.2 3.3 %collective-permute-start.36 = (bf16[4,16,2048]{2,1,0:T(8,128)(2,1)}, bf16[4,16,2048]{2,1,0:T(8,128)(2,1)S(1)}, u32[]{:S(2)}, u32[]{:S(2)}) collective-permute-start(bf16[4,16,2048]{2,1,0:T(8,128)(2,1)} %get-tuple-element.148), channel_id=1, source_target_pairs={{0,24},{1,25},{2,26},{3,27},{4,28},{5,29},{6,30},{7,31},{8,16},{9,... | collective-permute-start | bytes 786440 | tf_op jit(solution)/shard_map/ppermute | solution.py:637
  189.7 1.6 mul.224
  191.4 1.6 copy.47
  193.0 1.6 mul.229
  194.6 1.0 copy.48
  196.2 2.0 collective-permute-start.42
  198.2 1.1 collective-permute-start.43
  199.3 1.4 collective-permute-start.44
  201.5 1.1 collective-permute-start.33
  202.6 1.0 collective-permute-start.37
  203.6 1.4 collective-permute-start.38
  205.7 5.4 %collective-permute-done.33.rest_0_ = bf16[4,16,2176]{2,1,0:T(8,128)(2,1)S(1)} collective-permute-done((bf16[4,16,2176]{2,1,0:T(8,128)(2,1)S(1)}, bf16[4,16,2176]{2,1,0:T(8,128)(2,1)S(1)}, u32[]{:S(2)}, u32[]{:S(2)}) %collective-permute-start.33) | collective-permute-done | bytes 278560 | tf_op jit(solution)/shard_map/ppermute | solution.py:637
  211.1 5.4 %collective-permute-done.37.rest_1_ = bf16[4,16,2176]{2,1,0:T(8,128)(2,1)S(1)} collective-permute-done((bf16[4,16,2176]{2,1,0:T(8,128)(2,1)S(1)}, bf16[4,16,2176]{2,1,0:T(8,128)(2,1)S(1)}, u32[]{:S(2)}, u32[]{:S(2)}) %collective-permute-start.37) | collective-permute-done | bytes 278560 | tf_op jit(solution)/shard_map/ppermute | solution.py:637
  216.7 2.5 %collective-permute-start.40 = (bf16[16,2176]{1,0:T(8,128)(2,1)S(1)}, bf16[16,2176]{1,0:T(8,128)(2,1)S(1)}, u32[]{:S(2)}, u32[]{:S(2)}) collective-permute-start(bf16[16,2176]{1,0:T(8,128)(2,1)S(1)} %get-tuple-element.187), channel_id=1, source_target_pairs={{0,4},{1,5},{2,6},{3,7},{4,0},{5,1},{6,2},{7,3},{8,12},{9,13},{10,... | collective-permute-start | bytes 208904 | tf_op jit(solution)/shard_map/ppermute | solution.py:637
  219.2 1.9 collective-permute-start.41
  221.1 2.4 %collective-permute-done.40 = bf16[16,2176]{1,0:T(8,128)(2,1)S(1)} collective-permute-done((bf16[16,2176]{1,0:T(8,128)(2,1)S(1)}, bf16[16,2176]{1,0:T(8,128)(2,1)S(1)}, u32[]{:S(2)}, u32[]{:S(2)}) %collective-permute-start.40) | collective-permute-done | bytes 69664 | tf_op jit(solution)/shard_map/ppermute | solution.py:637
  223.5 1.9 collective-permute-done.41
  (160 shorter events, 18.2 us)
Async XLA Ops:
  2.3 8.6 %collective-permute-start.1 = (bf16[16,1664]{1,0:T(8,128)(2,1)S(1)}, bf16[16,1664]{1,0:T(8,128)(2,1)S(1)}, u32[]{:S(2)}, u32[]{:S(2)}) collective-permute-start(bf16[16,1664]{1,0:T(8,128)(2,1)S(1)} %fusion.2), channel_id=1, source_target_pairs={{0,4},{1,5},{2,6},{3,7},{4,0},{5,1},{6,2},{7,3},{8,12},{9,13},{10,... | collective-permute-start | bytes 159752 | tf_op jit(solution)/shard_map/ppermute | solution.py:637
  6.4 4.6 %collective-permute-start = (bf16[16,1664]{1,0:T(8,128)(2,1)S(1)}, bf16[16,1664]{1,0:T(8,128)(2,1)S(1)}, u32[]{:S(2)}, u32[]{:S(2)}) collective-permute-start(bf16[16,1664]{1,0:T(8,128)(2,1)S(1)} %fusion.2), channel_id=1, source_target_pairs={{0,2},{1,3},{2,0},{3,1},{4,6},{5,7},{6,4},{7,5},{8,10},{9,11},{10,... | collective-permute-start | bytes 159752 | tf_op jit(solution)/shard_map/ppermute | solution.py:637
  8.0 5.9 %collective-permute-start.2 = (bf16[16,1664]{1,0:T(8,128)(2,1)S(1)}, bf16[16,1664]{1,0:T(8,128)(2,1)S(1)}, u32[]{:S(2)}, u32[]{:S(2)}) collective-permute-start(bf16[16,1664]{1,0:T(8,128)(2,1)S(1)} %fusion.2), channel_id=1, source_target_pairs={{0,6},{1,7},{2,4},{3,5},{4,2},{5,3},{6,0},{7,1},{8,14},{9,15},{10,... | collective-permute-start | bytes 159752 | tf_op jit(solution)/shard_map/ppermute | solution.py:637
  14.0 9.6 %collective-permute-start.5 = (bf16[16,6656]{1,0:T(8,128)(2,1)S(1)}, bf16[16,6656]{1,0:T(8,128)(2,1)S(1)}, u32[]{:S(2)}, u32[]{:S(2)}) collective-permute-start(bf16[16,6656]{1,0:T(8,128)(2,1)S(1)} %constant_dynamic-update-slice_fusion), channel_id=1, source_target_pairs={{0,6},{1,7},{2,4},{3,5},{4,2},{5,3},{6,0},{7,1},{8,14},{9,15},{10,... | collective-permute-start | bytes 638984 | tf_op jit(solution)/shard_map/ppermute | solution.py:637
  14.9 17.4 %collective-permute-start.4 = (bf16[16,6656]{1,0:T(8,128)(2,1)S(1)}, bf16[16,6656]{1,0:T(8,128)(2,1)S(1)}, u32[]{:S(2)}, u32[]{:S(2)}) collective-permute-start(bf16[16,6656]{1,0:T(8,128)(2,1)S(1)} %constant_dynamic-update-slice_fusion), channel_id=1, source_target_pairs={{0,4},{1,5},{2,6},{3,7},{4,0},{5,1},{6,2},{7,3},{8,12},{9,13},{10,... | collective-permute-start | bytes 638984 | tf_op jit(solution)/shard_map/ppermute | solution.py:637
  14.9 17.4 %collective-permute-start.8 = (bf16[4,16,1664]{2,1,0:T(8,128)(2,1)S(1)}, bf16[4,16,1664]{2,1,0:T(8,128)(2,1)S(1)}, u32[]{:S(2)}, u32[]{:S(2)}) collective-permute-start(bf16[4,16,1664]{2,1,0:T(8,128)(2,1)S(1)} %pad_maximum_fusion.1.rest_0_), channel_id=1, source_target_pairs={{0,24},{1,25},{2,26},{3,27},{4,28},{5,29},{6,30},{7,31},{8,16},{9,... | collective-permute-start | bytes 638984 | tf_op jit(solution)/shard_map/ppermute | solution.py:637
  17.4 15.5 %collective-permute-start.7 = (bf16[4,16,1664]{2,1,0:T(8,128)(2,1)S(1)}, bf16[4,16,1664]{2,1,0:T(8,128)(2,1)S(1)}, u32[]{:S(2)}, u32[]{:S(2)}) collective-permute-start(bf16[4,16,1664]{2,1,0:T(8,128)(2,1)S(1)} %pad_maximum_fusion.1.rest_0_), channel_id=1, source_target_pairs={{0,16},{1,17},{2,18},{3,19},{4,20},{5,21},{6,22},{7,23},{8,24},{9,... | collective-permute-start | bytes 638984 | tf_op jit(solution)/shard_map/ppermute | solution.py:637
  17.9 15.1 %collective-permute-start.6 = (bf16[4,16,1664]{2,1,0:T(8,128)(2,1)S(1)}, bf16[4,16,1664]{2,1,0:T(8,128)(2,1)S(1)}, u32[]{:S(2)}, u32[]{:S(2)}) collective-permute-start(bf16[4,16,1664]{2,1,0:T(8,128)(2,1)S(1)} %pad_maximum_fusion.1.rest_0_), channel_id=1, source_target_pairs={{0,8},{1,9},{2,10},{3,11},{4,12},{5,13},{6,14},{7,15},{8,0},{9,1},... | collective-permute-start | bytes 638984 | tf_op jit(solution)/shard_map/ppermute | solution.py:637
  23.6 11.5 %collective-permute-start.3 = (bf16[16,6656]{1,0:T(8,128)(2,1)S(1)}, bf16[16,6656]{1,0:T(8,128)(2,1)S(1)}, u32[]{:S(2)}, u32[]{:S(2)}) collective-permute-start(bf16[16,6656]{1,0:T(8,128)(2,1)S(1)} %constant_dynamic-update-slice_fusion), channel_id=1, source_target_pairs={{0,2},{1,3},{2,0},{3,1},{4,6},{5,7},{6,4},{7,5},{8,10},{9,11},{10,... | collective-permute-start | bytes 638984 | tf_op jit(solution)/shard_map/ppermute | solution.py:637
  32.4 5.5 %collective-permute-start.9 = (bf16[4,16,1664]{2,1,0:T(8,128)(2,1)S(1)}, bf16[4,16,1664]{2,1,0:T(8,128)(2,1)S(1)}, u32[]{:S(2)}, u32[]{:S(2)}) collective-permute-start(bf16[4,16,1664]{2,1,0:T(8,128)(2,1)S(1)} %pad_maximum_fusion.1.rest_0_), channel_id=1, source_target_pairs={{0,1},{1,0},{2,3},{3,2},{4,5},{5,4},{6,7},{7,6},{8,9},{9,8},{10,11... | collective-permute-start | bytes 638984 | tf_op jit(solution)/shard_map/ppermute | solution.py:637
  32.4 5.6 %collective-permute-start.12 = (bf16[4,16,1664]{2,1,0:T(8,128)(2,1)S(1)}, bf16[4,16,1664]{2,1,0:T(8,128)(2,1)S(1)}, u32[]{:S(2)}, u32[]{:S(2)}) collective-permute-start(bf16[4,16,1664]{2,1,0:T(8,128)(2,1)S(1)} %collective-permute-done.8.rest_3_), channel_id=1, source_target_pairs={{0,1},{1,0},{2,3},{3,2},{4,5},{5,4},{6,7},{7,6},{8,9},{9,8},{10,11... | collective-permute-start | bytes 638984 | tf_op jit(solution)/shard_map/ppermute | solution.py:637
  32.9 5.6 %collective-permute-start.11 = (bf16[4,16,1664]{2,1,0:T(8,128)(2,1)S(1)}, bf16[4,16,1664]{2,1,0:T(8,128)(2,1)S(1)}, u32[]{:S(2)}, u32[]{:S(2)}) collective-permute-start(bf16[4,16,1664]{2,1,0:T(8,128)(2,1)S(1)} %collective-permute-done.7.rest_2_), channel_id=1, source_target_pairs={{0,1},{1,0},{2,3},{3,2},{4,5},{5,4},{6,7},{7,6},{8,9},{9,8},{10,11... | collective-permute-start | bytes 638984 | tf_op jit(solution)/shard_map/ppermute | solution.py:637
  32.9 7.1 %collective-permute-start.10 = (bf16[4,16,1664]{2,1,0:T(8,128)(2,1)S(1)}, bf16[4,16,1664]{2,1,0:T(8,128)(2,1)S(1)}, u32[]{:S(2)}, u32[]{:S(2)}) collective-permute-start(bf16[4,16,1664]{2,1,0:T(8,128)(2,1)S(1)} %collective-permute-done.6.rest_1_), channel_id=1, source_target_pairs={{0,1},{1,0},{2,3},{3,2},{4,5},{5,4},{6,7},{7,6},{8,9},{9,8},{10,11... | collective-permute-start | bytes 638984 | tf_op jit(solution)/shard_map/ppermute | solution.py:637
  35.3 30.0 %collective-permute-start.22 = (bf16[4,16,4096]{2,1,0:T(8,128)(2,1)S(1)}, bf16[4,16,4096]{2,1,0:T(8,128)(2,1)S(1)}, u32[]{:S(2)}, u32[]{:S(2)}) collective-permute-start(bf16[4,16,4096]{2,1,0:T(8,128)(2,1)S(1)} %slice.93.rest_0_), channel_id=1, source_target_pairs={{0,24},{1,25},{2,26},{3,27},{4,28},{5,29},{6,30},{7,31},{8,16},{9,... | collective-permute-start | bytes 1572872 | tf_op jit(solution)/shard_map/ppermute | solution.py:637
  37.9 3.9 %collective-permute-start.16 = (bf16[4,16,2560]{2,1,0:T(8,128)(2,1)S(1)}, bf16[4,16,2560]{2,1,0:T(8,128)(2,1)S(1)}, u32[]{:S(2)}, u32[]{:S(2)}) collective-permute-start(bf16[4,16,2560]{2,1,0:T(8,128)(2,1)S(1)} %slice.92.rest_0_), channel_id=1, source_target_pairs={{0,1},{1,0},{2,3},{3,2},{4,5},{5,4},{6,7},{7,6},{8,9},{9,8},{10,11... | collective-permute-start | bytes 983048 | tf_op jit(solution)/shard_map/ppermute | solution.py:637
  38.0 20.3 %collective-permute-start.15 = (bf16[4,16,2560]{2,1,0:T(8,128)(2,1)S(1)}, bf16[4,16,2560]{2,1,0:T(8,128)(2,1)S(1)}, u32[]{:S(2)}, u32[]{:S(2)}) collective-permute-start(bf16[4,16,2560]{2,1,0:T(8,128)(2,1)S(1)} %slice.92.rest_0_), channel_id=1, source_target_pairs={{0,24},{1,25},{2,26},{3,27},{4,28},{5,29},{6,30},{7,31},{8,16},{9,... | collective-permute-start | bytes 983048 | tf_op jit(solution)/shard_map/ppermute | solution.py:637
  38.5 24.0 %collective-permute-start.14 = (bf16[4,16,2560]{2,1,0:T(8,128)(2,1)S(1)}, bf16[4,16,2560]{2,1,0:T(8,128)(2,1)S(1)}, u32[]{:S(2)}, u32[]{:S(2)}) collective-permute-start(bf16[4,16,2560]{2,1,0:T(8,128)(2,1)S(1)} %slice.92.rest_0_), channel_id=1, source_target_pairs={{0,16},{1,17},{2,18},{3,19},{4,20},{5,21},{6,22},{7,23},{8,24},{9,... | collective-permute-start | bytes 983048 | tf_op jit(solution)/shard_map/ppermute | solution.py:637
  40.0 25.3 %collective-permute-start.13 = (bf16[4,16,2560]{2,1,0:T(8,128)(2,1)S(1)}, bf16[4,16,2560]{2,1,0:T(8,128)(2,1)S(1)}, u32[]{:S(2)}, u32[]{:S(2)}) collective-permute-start(bf16[4,16,2560]{2,1,0:T(8,128)(2,1)S(1)} %slice.92.rest_0_), channel_id=1, source_target_pairs={{0,8},{1,9},{2,10},{3,11},{4,12},{5,13},{6,14},{7,15},{8,0},{9,1},... | collective-permute-start | bytes 983048 | tf_op jit(solution)/shard_map/ppermute | solution.py:637
  41.8 40.2 %collective-permute-start.21 = (bf16[4,16,4096]{2,1,0:T(8,128)(2,1)S(1)}, bf16[4,16,4096]{2,1,0:T(8,128)(2,1)S(1)}, u32[]{:S(2)}, u32[]{:S(2)}) collective-permute-start(bf16[4,16,4096]{2,1,0:T(8,128)(2,1)S(1)} %slice.93.rest_0_), channel_id=1, source_target_pairs={{0,16},{1,17},{2,18},{3,19},{4,20},{5,21},{6,22},{7,23},{8,24},{9,... | collective-permute-start | bytes 1572872 | tf_op jit(solution)/shard_map/ppermute | solution.py:637
  58.2 23.8 %collective-permute-start.20 = (bf16[4,16,4096]{2,1,0:T(8,128)(2,1)S(1)}, bf16[4,16,4096]{2,1,0:T(8,128)(2,1)S(1)}, u32[]{:S(2)}, u32[]{:S(2)}) collective-permute-start(bf16[4,16,4096]{2,1,0:T(8,128)(2,1)S(1)} %slice.93.rest_0_), channel_id=1, source_target_pairs={{0,8},{1,9},{2,10},{3,11},{4,12},{5,13},{6,14},{7,15},{8,0},{9,1},... | collective-permute-start | bytes 1572872 | tf_op jit(solution)/shard_map/ppermute | solution.py:637
  62.5 20.0 %collective-permute-start.19 = (bf16[4,16,2560]{2,1,0:T(8,128)(2,1)S(1)}, bf16[4,16,2560]{2,1,0:T(8,128)(2,1)S(1)}, u32[]{:S(2)}, u32[]{:S(2)}) collective-permute-start(bf16[4,16,2560]{2,1,0:T(8,128)(2,1)S(1)} %collective-permute-done.15.rest_3_), channel_id=1, source_target_pairs={{0,1},{1,0},{2,3},{3,2},{4,5},{5,4},{6,7},{7,6},{8,9},{9,8},{10,11... | collective-permute-start | bytes 983048 | tf_op jit(solution)/shard_map/ppermute | solution.py:637
  65.3 17.3 %collective-permute-start.18 = (bf16[4,16,2560]{2,1,0:T(8,128)(2,1)S(1)}, bf16[4,16,2560]{2,1,0:T(8,128)(2,1)S(1)}, u32[]{:S(2)}, u32[]{:S(2)}) collective-permute-start(bf16[4,16,2560]{2,1,0:T(8,128)(2,1)S(1)} %collective-permute-done.14.rest_2_), channel_id=1, source_target_pairs={{0,1},{1,0},{2,3},{3,2},{4,5},{5,4},{6,7},{7,6},{8,9},{9,8},{10,11... | collective-permute-start | bytes 983048 | tf_op jit(solution)/shard_map/ppermute | solution.py:637
  65.3 17.7 %collective-permute-start.17 = (bf16[4,16,2560]{2,1,0:T(8,128)(2,1)S(1)}, bf16[4,16,2560]{2,1,0:T(8,128)(2,1)S(1)}, u32[]{:S(2)}, u32[]{:S(2)}) collective-permute-start(bf16[4,16,2560]{2,1,0:T(8,128)(2,1)S(1)} %collective-permute-done.13.rest_1_), channel_id=1, source_target_pairs={{0,1},{1,0},{2,3},{3,2},{4,5},{5,4},{6,7},{7,6},{8,9},{9,8},{10,11... | collective-permute-start | bytes 983048 | tf_op jit(solution)/shard_map/ppermute | solution.py:637
  82.0 20.4 %collective-permute-start.23 = (bf16[4,16,4096]{2,1,0:T(8,128)(2,1)S(1)}, bf16[4,16,4096]{2,1,0:T(8,128)(2,1)S(1)}, u32[]{:S(2)}, u32[]{:S(2)}) collective-permute-start(bf16[4,16,4096]{2,1,0:T(8,128)(2,1)S(1)} %slice.93.rest_0_), channel_id=1, source_target_pairs={{0,1},{1,0},{2,3},{3,2},{4,5},{5,4},{6,7},{7,6},{8,9},{9,8},{10,11... | collective-permute-start | bytes 1572872 | tf_op jit(solution)/shard_map/ppermute | solution.py:637
  82.0 20.4 %collective-permute-start.26 = (bf16[4,16,4096]{2,1,0:T(8,128)(2,1)S(1)}, bf16[4,16,4096]{2,1,0:T(8,128)(2,1)S(1)}, u32[]{:S(2)}, u32[]{:S(2)}) collective-permute-start(bf16[4,16,4096]{2,1,0:T(8,128)(2,1)S(1)} %collective-permute-done.22.rest_3_), channel_id=1, source_target_pairs={{0,1},{1,0},{2,3},{3,2},{4,5},{5,4},{6,7},{7,6},{8,9},{9,8},{10,11... | collective-permute-start | bytes 1572872 | tf_op jit(solution)/shard_map/ppermute | solution.py:637
  82.5 19.9 %collective-permute-start.25 = (bf16[4,16,4096]{2,1,0:T(8,128)(2,1)S(1)}, bf16[4,16,4096]{2,1,0:T(8,128)(2,1)S(1)}, u32[]{:S(2)}, u32[]{:S(2)}) collective-permute-start(bf16[4,16,4096]{2,1,0:T(8,128)(2,1)S(1)} %collective-permute-done.21.rest_2_), channel_id=1, source_target_pairs={{0,1},{1,0},{2,3},{3,2},{4,5},{5,4},{6,7},{7,6},{8,9},{9,8},{10,11... | collective-permute-start | bytes 1572872 | tf_op jit(solution)/shard_map/ppermute | solution.py:637
  82.6 19.9 %collective-permute-start.24 = (bf16[4,16,4096]{2,1,0:T(8,128)(2,1)S(1)}, bf16[4,16,4096]{2,1,0:T(8,128)(2,1)S(1)}, u32[]{:S(2)}, u32[]{:S(2)}) collective-permute-start(bf16[4,16,4096]{2,1,0:T(8,128)(2,1)S(1)} %collective-permute-done.20.rest_1_), channel_id=1, source_target_pairs={{0,1},{1,0},{2,3},{3,2},{4,5},{5,4},{6,7},{7,6},{8,9},{9,8},{10,11... | collective-permute-start | bytes 1572872 | tf_op jit(solution)/shard_map/ppermute | solution.py:637
  128.9 14.1 %collective-permute-start.27 = (bf16[16,16,4096]{2,1,0:T(8,128)(2,1)S(1)}, bf16[16,16,4096]{2,1,0:T(8,128)(2,1)S(1)}, u32[]{:S(2)}, u32[]{:S(2)}) collective-permute-start(bf16[16,16,4096]{2,1,0:T(8,128)(2,1)S(1)} %get-tuple-element.125), channel_id=1, source_target_pairs={{0,1},{1,0},{2,3},{3,2},{4,5},{5,4},{6,7},{7,6},{8,9},{9,8},{10,11... | collective-permute-start | bytes 6291464 | tf_op jit(solution)/shard_map/ppermute | solution.py:637
  149.4 6.7 %collective-permute-start.28 = (bf16[16,16,2048]{2,1,0:T(8,128)(2,1)S(1)}, bf16[16,16,2048]{2,1,0:T(8,128)(2,1)S(1)}, u32[]{:S(2)}, u32[]{:S(2)}) collective-permute-start(bf16[16,16,2048]{2,1,0:T(8,128)(2,1)S(1)} %get-tuple-element.143), channel_id=1, source_target_pairs={{0,1},{1,0},{2,3},{3,2},{4,5},{5,4},{6,7},{7,6},{8,9},{9,8},{10,11... | collective-permute-start | bytes 3145736 | tf_op jit(solution)/shard_map/ppermute | solution.py:637
  149.4 27.4 %collective-permute-start.29 = (bf16[4,16,4096]{2,1,0:T(8,128)(2,1)S(1)}, bf16[4,16,4096]{2,1,0:T(8,128)(2,1)S(1)}, u32[]{:S(2)}, u32[]{:S(2)}) collective-permute-start(bf16[4,16,4096]{2,1,0:T(8,128)(2,1)S(1)} %get-tuple-element.131), channel_id=1, source_target_pairs={{0,8},{1,9},{2,10},{3,11},{4,12},{5,13},{6,14},{7,15},{8,0},{9,1},... | collective-permute-start | bytes 1572872 | tf_op jit(solution)/shard_map/ppermute | solution.py:637
  149.5 27.3 %collective-permute-start.30 = (bf16[4,16,4096]{2,1,0:T(8,128)(2,1)S(1)}, bf16[4,16,4096]{2,1,0:T(8,128)(2,1)S(1)}, u32[]{:S(2)}, u32[]{:S(2)}) collective-permute-start(bf16[4,16,4096]{2,1,0:T(8,128)(2,1)S(1)} %get-tuple-element.132), channel_id=1, source_target_pairs={{0,16},{1,17},{2,18},{3,19},{4,20},{5,21},{6,22},{7,23},{8,24},{9,... | collective-permute-start | bytes 1572872 | tf_op jit(solution)/shard_map/ppermute | solution.py:637
  150.2 26.7 %collective-permute-start.31 = (bf16[4,16,4096]{2,1,0:T(8,128)(2,1)S(1)}, bf16[4,16,4096]{2,1,0:T(8,128)(2,1)S(1)}, u32[]{:S(2)}, u32[]{:S(2)}) collective-permute-start(bf16[4,16,4096]{2,1,0:T(8,128)(2,1)S(1)} %get-tuple-element.133), channel_id=1, source_target_pairs={{0,24},{1,25},{2,26},{3,27},{4,28},{5,29},{6,30},{7,31},{8,16},{9,... | collective-permute-start | bytes 1572872 | tf_op jit(solution)/shard_map/ppermute | solution.py:637
  177.1 8.1 %collective-permute-start.45 = (bf16[16,4096]{1,0:T(8,128)(2,1)S(1)}, bf16[16,4096]{1,0:T(8,128)(2,1)S(1)}, u32[]{:S(2)}, u32[]{:S(2)}) collective-permute-start(bf16[16,4096]{1,0:T(8,128)(2,1)S(1)} %get-tuple-element.163), channel_id=1, source_target_pairs={{0,2},{1,3},{2,0},{3,1},{4,6},{5,7},{6,4},{7,5},{8,10},{9,11},{10,... | collective-permute-start | bytes 393224 | tf_op jit(solution)/shard_map/ppermute | solution.py:637
  177.2 11.6 %collective-permute-start.46 = (bf16[16,4096]{1,0:T(8,128)(2,1)S(1)}, bf16[16,4096]{1,0:T(8,128)(2,1)S(1)}, u32[]{:S(2)}, u32[]{:S(2)}) collective-permute-start(bf16[16,4096]{1,0:T(8,128)(2,1)S(1)} %get-tuple-element.164), channel_id=1, source_target_pairs={{0,4},{1,5},{2,6},{3,7},{4,0},{5,1},{6,2},{7,3},{8,12},{9,13},{10,... | collective-permute-start | bytes 393224 | tf_op jit(solution)/shard_map/ppermute | solution.py:637
  179.2 9.6 %collective-permute-start.47 = (bf16[16,4096]{1,0:T(8,128)(2,1)S(1)}, bf16[16,4096]{1,0:T(8,128)(2,1)S(1)}, u32[]{:S(2)}, u32[]{:S(2)}) collective-permute-start(bf16[16,4096]{1,0:T(8,128)(2,1)S(1)} %get-tuple-element.165), channel_id=1, source_target_pairs={{0,6},{1,7},{2,4},{3,5},{4,2},{5,3},{6,0},{7,1},{8,14},{9,15},{10,... | collective-permute-start | bytes 393224 | tf_op jit(solution)/shard_map/ppermute | solution.py:637
  181.5 14.4 %collective-permute-start.34 = (bf16[4,16,2048]{2,1,0:T(8,128)(2,1)}, bf16[4,16,2048]{2,1,0:T(8,128)(2,1)S(1)}, u32[]{:S(2)}, u32[]{:S(2)}) collective-permute-start(bf16[4,16,2048]{2,1,0:T(8,128)(2,1)} %get-tuple-element.146), channel_id=1, source_target_pairs={{0,8},{1,9},{2,10},{3,11},{4,12},{5,13},{6,14},{7,15},{8,0},{9,1},... | collective-permute-start | bytes 786440 | tf_op jit(solution)/shard_map/ppermute | solution.py:637
  181.6 14.4 %collective-permute-start.35 = (bf16[4,16,2048]{2,1,0:T(8,128)(2,1)}, bf16[4,16,2048]{2,1,0:T(8,128)(2,1)S(1)}, u32[]{:S(2)}, u32[]{:S(2)}) collective-permute-start(bf16[4,16,2048]{2,1,0:T(8,128)(2,1)} %get-tuple-element.147), channel_id=1, source_target_pairs={{0,16},{1,17},{2,18},{3,19},{4,20},{5,21},{6,22},{7,23},{8,24},{9,... | collective-permute-start | bytes 786440 | tf_op jit(solution)/shard_map/ppermute | solution.py:637
  185.2 10.8 %collective-permute-start.36 = (bf16[4,16,2048]{2,1,0:T(8,128)(2,1)}, bf16[4,16,2048]{2,1,0:T(8,128)(2,1)S(1)}, u32[]{:S(2)}, u32[]{:S(2)}) collective-permute-start(bf16[4,16,2048]{2,1,0:T(8,128)(2,1)} %get-tuple-element.148), channel_id=1, source_target_pairs={{0,24},{1,25},{2,26},{3,27},{4,28},{5,29},{6,30},{7,31},{8,16},{9,... | collective-permute-start | bytes 786440 | tf_op jit(solution)/shard_map/ppermute | solution.py:637
  188.8 6.9 %collective-permute-start.32 = (bf16[16,16,2176]{2,1,0:T(8,128)(2,1)}, bf16[16,16,2176]{2,1,0:T(8,128)(2,1)S(1)}, u32[]{:S(2)}, u32[]{:S(2)}) collective-permute-start(bf16[16,16,2176]{2,1,0:T(8,128)(2,1)} %get-tuple-element.159), channel_id=1, source_target_pairs={{0,1},{1,0},{2,3},{3,2},{4,5},{5,4},{6,7},{7,6},{8,9},{9,8},{10,11... | collective-permute-start | bytes 3342344 | tf_op jit(solution)/shard_map/ppermute | solution.py:637
  196.2 7.4 %collective-permute-start.42 = (bf16[16,2048]{1,0:T(8,128)(2,1)S(1)}, bf16[16,2048]{1,0:T(8,128)(2,1)S(1)}, u32[]{:S(2)}, u32[]{:S(2)}) collective-permute-start(bf16[16,2048]{1,0:T(8,128)(2,1)S(1)} %get-tuple-element.179), channel_id=1, source_target_pairs={{0,2},{1,3},{2,0},{3,1},{4,6},{5,7},{6,4},{7,5},{8,10},{9,11},{10,... | collective-permute-start | bytes 196616 | tf_op jit(solution)/shard_map/ppermute | solution.py:637
  198.2 7.4 %collective-permute-start.43 = (bf16[16,2048]{1,0:T(8,128)(2,1)S(1)}, bf16[16,2048]{1,0:T(8,128)(2,1)S(1)}, u32[]{:S(2)}, u32[]{:S(2)}) collective-permute-start(bf16[16,2048]{1,0:T(8,128)(2,1)S(1)} %get-tuple-element.180), channel_id=1, source_target_pairs={{0,4},{1,5},{2,6},{3,7},{4,0},{5,1},{6,2},{7,3},{8,12},{9,13},{10,... | collective-permute-start | bytes 196616 | tf_op jit(solution)/shard_map/ppermute | solution.py:637
  199.3 6.3 %collective-permute-start.44 = (bf16[16,2048]{1,0:T(8,128)(2,1)S(1)}, bf16[16,2048]{1,0:T(8,128)(2,1)S(1)}, u32[]{:S(2)}, u32[]{:S(2)}) collective-permute-start(bf16[16,2048]{1,0:T(8,128)(2,1)S(1)} %get-tuple-element.181), channel_id=1, source_target_pairs={{0,6},{1,7},{2,4},{3,5},{4,2},{5,3},{6,0},{7,1},{8,14},{9,15},{10,... | collective-permute-start | bytes 196616 | tf_op jit(solution)/shard_map/ppermute | solution.py:637
  201.5 9.6 %collective-permute-start.33 = (bf16[4,16,2176]{2,1,0:T(8,128)(2,1)S(1)}, bf16[4,16,2176]{2,1,0:T(8,128)(2,1)S(1)}, u32[]{:S(2)}, u32[]{:S(2)}) collective-permute-start(bf16[4,16,2176]{2,1,0:T(8,128)(2,1)S(1)} %get-tuple-element.172), channel_id=1, source_target_pairs={{0,8},{1,9},{2,10},{3,11},{4,12},{5,13},{6,14},{7,15},{8,0},{9,1},... | collective-permute-start | bytes 835592 | tf_op jit(solution)/shard_map/ppermute | solution.py:637
  202.6 13.9 %collective-permute-start.37 = (bf16[4,16,2176]{2,1,0:T(8,128)(2,1)S(1)}, bf16[4,16,2176]{2,1,0:T(8,128)(2,1)S(1)}, u32[]{:S(2)}, u32[]{:S(2)}) collective-permute-start(bf16[4,16,2176]{2,1,0:T(8,128)(2,1)S(1)} %get-tuple-element.174), channel_id=1, source_target_pairs={{0,16},{1,17},{2,18},{3,19},{4,20},{5,21},{6,22},{7,23},{8,24},{9,... | collective-permute-start | bytes 835592 | tf_op jit(solution)/shard_map/ppermute | solution.py:637
  203.6 12.9 %collective-permute-start.38 = (bf16[4,16,2176]{2,1,0:T(8,128)(2,1)S(1)}, bf16[4,16,2176]{2,1,0:T(8,128)(2,1)S(1)}, u32[]{:S(2)}, u32[]{:S(2)}) collective-permute-start(bf16[4,16,2176]{2,1,0:T(8,128)(2,1)S(1)} %get-tuple-element.175), channel_id=1, source_target_pairs={{0,24},{1,25},{2,26},{3,27},{4,28},{5,29},{6,30},{7,31},{8,16},{9,... | collective-permute-start | bytes 835592 | tf_op jit(solution)/shard_map/ppermute | solution.py:637
  216.6 4.5 %collective-permute-start.39 = (bf16[16,2176]{1,0:T(8,128)(2,1)S(1)}, bf16[16,2176]{1,0:T(8,128)(2,1)S(1)}, u32[]{:S(2)}, u32[]{:S(2)}) collective-permute-start(bf16[16,2176]{1,0:T(8,128)(2,1)S(1)} %get-tuple-element.186), channel_id=1, source_target_pairs={{0,2},{1,3},{2,0},{3,1},{4,6},{5,7},{6,4},{7,5},{8,10},{9,11},{10,... | collective-permute-start | bytes 208904 | tf_op jit(solution)/shard_map/ppermute | solution.py:637
  216.7 6.8 %collective-permute-start.40 = (bf16[16,2176]{1,0:T(8,128)(2,1)S(1)}, bf16[16,2176]{1,0:T(8,128)(2,1)S(1)}, u32[]{:S(2)}, u32[]{:S(2)}) collective-permute-start(bf16[16,2176]{1,0:T(8,128)(2,1)S(1)} %get-tuple-element.187), channel_id=1, source_target_pairs={{0,4},{1,5},{2,6},{3,7},{4,0},{5,1},{6,2},{7,3},{8,12},{9,13},{10,... | collective-permute-start | bytes 208904 | tf_op jit(solution)/shard_map/ppermute | solution.py:637
  219.2 6.1 %collective-permute-start.41 = (bf16[16,2176]{1,0:T(8,128)(2,1)S(1)}, bf16[16,2176]{1,0:T(8,128)(2,1)S(1)}, u32[]{:S(2)}, u32[]{:S(2)}) collective-permute-start(bf16[16,2176]{1,0:T(8,128)(2,1)S(1)} %get-tuple-element.188), channel_id=1, source_target_pairs={{0,6},{1,7},{2,4},{3,5},{4,2},{5,3},{6,0},{7,1},{8,14},{9,15},{10,... | collective-permute-start | bytes 208904 | tf_op jit(solution)/shard_map/ppermute | solution.py:637
  (27 other events, 495.5 us)

commit v5 on v4

--- a/solution.py
+++ b/solution.py
@@ -434,15 +434,19 @@
 
 def cross_grads_kernel(
     place, dq, dk, dv, weights, vectors, grad_sum, unit_one, inverse_one,
-    first_low, encoded, cross_mixed, grad_out, first_sum, self_low, grad_mixed, sums, *grads,
+    first_low, encoded, cross_mixed, grad_out,
+    first_sum, self_low, grad_mixed, sums, encoded_grad, *grads,
 ):
     model = dq.shape[1]
     sums[...] = jnp.zeros_like(sums)
 
     def finish(rows):
-        query, value = dq[rows, :], dv[rows, :]
+        query, key, value = dq[rows, :], dk[rows, :], dv[rows, :]
         sums[0:1, :] += column_sum(query)
         sums[1:2, :] += column_sum(value)
+        encoded_grad[rows, :] = dot_nt(key, weights[:, 2 * model : 3 * model]) + dot_nt(
+            value, weights[:, 3 * model : 4 * model]
+        )
         upper = grad_sum[rows, :] + dot_nt(query, weights[:, model : 2 * model])
         unit = unit_one[rows, :]
         sums[2:3, :] += column_sum(upper * unit)
@@ -462,18 +466,12 @@
         store_grad(grads, core, lanes, dot_tn(left[...], right[...]))
 
 
-def encoded_grad_kernel(dk, dv, key_weights, value_weights, encoded_grad):
-    encoded_grad[...] = dot_nt(dk[...], key_weights[...]) + dot_nt(dv[...], value_weights[...])
-
-
-def self_backward_kernel(row_starts, queries, keys, values, grad_mixed, sums_in, dq, dk, dv):
-    attend_backward(row_starts, row_starts, queries, keys, values, grad_mixed, sums_in, dq, dk, dv)
-
-
-def self_grads_kernel(
-    place, tokens, mixed, dq, dk, dv, self_low, cross_sums, ffn_sums, bias_sums, *rest
+def self_backward_kernel(
+    place, row_starts, queries, keys, values, grad_mixed, sums_in, tokens, mixed, self_low,
+    cross_sums, ffn_sums, bias_sums, dq, dk, dv, *rest,
 ):
     *grads, stack = rest
+    attend_backward(row_starts, row_starts, queries, keys, values, grad_mixed, sums_in, dq, dk, dv)
     model = dq.shape[1]
     core = place[0] % 2
     pairs = ((tokens, dq), (tokens, dk), (tokens, dv), (mixed, self_low))
@@ -524,7 +522,104 @@
         ref[...] = value[0].astype(ref.dtype)
 
 
+def fold_halves_kernel(depth, place, kept, received, keep_first, send_first, keep_second, send_second):
+    at = place[0] // (2 * depth)
+    half = kept.shape[2] // 2
+    low, high = slice(0, half), slice(half, 2 * half)
+    for ref, lanes, offsets in (
+        (keep_first, low, (0, 1)),
+        (send_first, low, (2, 3)),
+        (keep_second, high, (0, 2)),
+        (send_second, high, (1, 3)),
+    ):
+        for slot, k in enumerate(offsets):
+            spot = pl.ds((at ^ k) * depth, depth)
+            value = kept[spot, :, lanes].astype(FULL) + received[spot, :, lanes].astype(FULL)
+            ref[slot] = value.astype(ref.dtype)
+
+
+def fold_pairs_kernel(keep_first, got_first, keep_second, got_second, *outs):
+    own_first, send_first, own_second, send_second = outs
+    own_first[...] = keep_first[0] + got_first[0].astype(FULL)
+    send_first[...] = (keep_first[1] + got_first[1].astype(FULL)).astype(LOW)
+    own_second[...] = keep_second[0] + got_second[0].astype(FULL)
+    send_second[...] = (keep_second[1] + got_second[1].astype(FULL)).astype(LOW)
+
+
+def fold_layers_kernel(depth, place, first, got_first, second, got_second, cross, *rest):
+    *got_cross, keep, send = rest
+    at = place[0] // 2 % depth
+    half = first.shape[2]
+    for ref, offsets in ((keep, (0, 1)), (send, (2, 3))):
+        for slot, k in enumerate(offsets):
+            spot = pl.ds(at ^ k, 1)
+            value = first[spot] + got_first[spot].astype(FULL)
+            ref[slot, :, :half] = value[0].astype(ref.dtype)
+            value = second[spot] + got_second[spot].astype(FULL)
+            ref[slot, :, half : 2 * half] = value[0].astype(ref.dtype)
+            value = cross[spot]
+            for item in got_cross:
+                value = value + item[spot].astype(FULL)
+            ref[slot, :, 2 * half :] = value[0].astype(ref.dtype)
+
+
+def fold_last_kernel(keep, got, own, send):
+    own[...] = keep[0] + got[0].astype(FULL)
+    send[...] = (keep[1] + got[1].astype(FULL)).astype(LOW)
+
+
+def update_into(outs, index, state, grad, rate):
+    for ref, value in zip(outs, adamw(state[0][index], grad, state[1][index], state[2][index], rate)):
+        ref[index] = value
+
+
+def ffn_update_kernel(grad_scale, own, got, *rest):
+    first_state, second_state, outs = rest[:3], rest[3:6], rest[6:]
+    rows, width = first_state[0].shape
+    model = second_state[0].shape[1]
+    grad = (own[:, :width] + got[:, :width].astype(FULL)) * grad_scale
+    update_into(outs[:4], (slice(None), slice(None)), first_state, grad, 0.04)
+    for j in range(second_state[0].shape[0] // rows):
+        lanes = slice(width + j * model, width + (j + 1) * model)
+        grad = (own[:, lanes] + got[:, lanes].astype(FULL)) * grad_scale
+        index = (slice(j * rows, (j + 1) * rows), slice(None))
+        update_into(outs[4:], index, second_state, grad, 0.02)
+
+
+def final_update_kernel(grad_scale, start, own, got, kept, *rest):
+    moved, states, outs = rest[:-21], rest[-21:-12], rest[-12:]
+    qkv_state, out_state, vector_state = states[:3], states[3:6], states[6:]
+    model = qkv_state[0].shape[2]
+
+    def self_grad(lanes):
+        value = kept[:, lanes]
+        for item in moved:
+            value = value + item[:, lanes].astype(FULL)
+        return value * grad_scale
+
+    def cross_grad(index):
+        lanes = slice(start + index * model, start + (index + 1) * model)
+        return (own[:, lanes] + got[:, lanes].astype(FULL)) * grad_scale
+
+    for j in range(4):
+        grad = self_grad(slice(j * model, (j + 1) * model))
+        if j < 3:
+            update_into(outs[:4], j, qkv_state, grad, 0.04)
+            update_into(outs[:4], 3 + j, qkv_state, cross_grad(j), 0.04)
+        else:
+            update_into(outs[4:8], 0, out_state, grad, 0.3)
+            update_into(outs[4:8], 1, out_state, cross_grad(j), 0.3)
+    grad = self_grad(slice(4 * model, 4 * model + vector_state[0].shape[1]))
+    update_into(outs[8:], (slice(None), slice(None)), vector_state, grad, 0.35)
+
+
 LIMITS = {
+    "fold_halves": 16,
+    "fold_pairs": 14,
+    "fold_layers": 12,
+    "fold_last": 8,
+    "ffn_update": 8,
+    "final_update": 10,
     "fold_core": 12,
     "fold_square": 10,
     "self_forward": 14,
@@ -532,10 +627,8 @@
     "cross_finish": 9,
     "ffn": 27,
     "cross_backward": 11,
-    "cross_grads": 16,
-    "encoded_grad": 9,
-    "self_backward": 11,
-    "self_grads": 14,
+    "cross_grads": 20,
+    "self_backward": 16,
     "tokens_grad": 11,
 }
 
@@ -649,6 +742,22 @@
 def square_list(stack):
     dp_count, fsdp_count = lax.axis_size("dp"), lax.axis_size("fsdp")
     return [stack] + [exchange(stack, fsdp_count * k) for k in range(1, dp_count)]
+
+
+def forward_list(stack):
+    stride, near = lax.axis_size("fsdp"), [stack]
+    for k in range(1, lax.axis_size("dp")):
+        near.append(None if k & (k - 1) else exchange(stack, stride * k))
+    return near
+
+
+def forward_rest(near, gate):
+    stride = lax.axis_size("fsdp")
+    for k, item in enumerate(near):
+        if item is None:
+            high = 1 << (k.bit_length() - 1)
+            near[k] = exchange(after(near[k - high], gate), stride * high)
+    return near
 
 
 def core_list(near):
@@ -797,22 +906,24 @@
     later_stack = layer_stack(later)
     self_parts = core_list(self_near)
     cross_columns = cross_piece.shape[1]
-    cross_near = square_list(later_stack[:, :, :cross_columns])
-    ffn_near = square_list(later_stack[:, :, cross_columns:])
+    cross_own, ffn_own = later_stack[:, :, :cross_columns], later_stack[:, :, cross_columns:]
+    cross_near = square_list(cross_own)
+    ffn_near = forward_list(ffn_own)
 
     sources = sources_of(self_parts)
     (
         self_weights, vectors, queries, keys, values, mixed, self_sums,
     ) = call(
         functools.partial(self_forward_kernel, len(sources), depth), "self_forward",
-        [spot, row_starts], [after(tokens, later_stack)],
+        [spot, row_starts], [after(tokens, cross_own, ffn_own)],
         [
             keep(((model, self_piece.shape[1]), LOW)), ((24, model), FULL),
             keep(wide), keep(wide), keep(wide), keep(wide), keep(log_sums),
         ],
         3 * unit + 2 * attend, sources, [wait_one],
     )
-    sources = sources_of(core_list(cross_near))
+    ffn_near = forward_rest(ffn_near, mixed)
+    sources = sources_of(core_list([after(item, mixed) for item in cross_near]))
     (
         cross_weights, unit_one, inverse_one, first_low, cross_queries, cross_keys, cross_values,
         cross_mixed, cross_log,
@@ -834,7 +945,8 @@
         cross_finish_kernel, "cross_finish", [unit_one, cross_mixed],
         [weight_block(cross_weights, 4), whole_vectors], [tall, thin], unit,
     )
-    sources = ffn_sources_of(core_list(ffn_near))
+    gates = [mixed] * (dp_count // 2) + [cross_mixed] * (dp_count // 2)
+    sources = ffn_sources_of(core_list([after(*pair) for pair in zip(ffn_near, gates)]))
     hidden = pieces * model
     (
         layer_out, grad_sum, grad_cross_out, grad_cross_mixed, ffn_sums, bias_sums, *ffn_grads
@@ -862,38 +974,67 @@
         [cross_queries, cross_keys, cross_values, after(grad_cross_mixed, sent), cross_log],
         [keep(wide), keep(wide), keep(wide)], 5 * attend,
     )
-    ffn_kept, ffn_sends = fold_core(spot, kept, after(ffn_moved, cross_dq))
-    ffn_moved = move_square(ffn_sends)
-    first_sum, self_low, grad_mixed, cross_vector, *cross_grads = call(
+    fast = aligned and dp_count == 4 and depth == 4
+    ffn_moved = after(ffn_moved, cross_dq)
+    if fast:
+        pair = (2, depth, rows, hidden)
+        keep_first, send_first, keep_second, send_second = call(
+            functools.partial(fold_halves_kernel, depth), "fold_halves", [spot], [kept, ffn_moved],
+            [(pair, FULL), (pair, LOW), (pair, FULL), (pair, LOW)], 1,
+        )
+        ffn_sends = [send_first, send_second]
+        got_first = exchange(send_first, 2 * fsdp_count)
+        got_second = exchange(send_second, fsdp_count)
+    else:
+        ffn_kept, ffn_sends = fold_core(spot, kept, ffn_moved)
+        ffn_moved = move_square(ffn_sends)
+    first_sum, self_low, grad_mixed, cross_vector, encoded_grad, *cross_grads = call(
         cross_grads_kernel, "cross_grads", [spot],
         [
             after(cross_dq, *ffn_sends), cross_dk, cross_dv, cross_weights, vectors, grad_sum,
             unit_one, inverse_one, first_low, encoded, cross_mixed, grad_cross_out,
         ],
-        [keep(tall), keep(wide), keep(wide), small, *grad_outs(4 * model)], 6 * unit,
+        [keep(tall), keep(wide), keep(wide), small, tall, *grad_outs(4 * model)], 8 * unit,
     )
     sent, kept = split_core(cross_grads)
-    cross_moved = exchange(sent, 1)
-    (encoded_grad,) = blocked(
-        encoded_grad_kernel, "encoded_grad", [after(cross_dk, sent), cross_dv],
-        [weight_block(cross_weights, 2), weight_block(cross_weights, 3)], [tall], 2 * unit,
-    )
-    cross_kept, cross_sends = fold_core(spot, kept, after(cross_moved, encoded_grad))
+    ffn_sends = [sent]
+    if fast:
+        half = (depth, rows, hidden)
+        own_first, send_first, own_second, send_second = call(
+            fold_pairs_kernel, "fold_pairs", [],
+            [keep_first, after(got_first, sent), keep_second, got_second],
+            [(half, FULL), (half, LOW), (half, FULL), (half, LOW)], 1,
+        )
+        ffn_sends = [send_first, send_second]
+        got_first = exchange(send_first, fsdp_count)
+        got_second = exchange(send_second, 2 * fsdp_count)
+    cross_moved = exchange(after(sent, *ffn_sends), 1)
+    cross_kept, cross_sends = fold_core(spot, kept, cross_moved)
     cross_moved = move_square(cross_sends)
-    self_dq, self_dk, self_dv = call(
-        self_backward_kernel, "self_backward", [row_starts],
-        [queries, keys, values, after(grad_mixed, *cross_sends), self_sums],
-        [keep(wide), keep(wide), keep(wide)], 5 * attend,
-    )
-    self_grads = call(
-        self_grads_kernel, "self_grads", [spot],
-        [tokens, mixed, self_dq, self_dk, self_dv, self_low, cross_vector, ffn_sums, bias_sums],
-        grad_outs(4 * model + 128), 4 * unit, (), [pltpu.VMEM((128, model), FULL)],
+    self_dq, self_dk, self_dv, *self_grads = call(
+        self_backward_kernel, "self_backward", [spot, row_starts],
+        [
+            queries, keys, values, after(grad_mixed, *cross_sends, *ffn_sends), self_sums,
+            tokens, mixed, self_low, cross_vector, ffn_sums, bias_sums,
+        ],
+        [keep(wide), keep(wide), keep(wide), *grad_outs(4 * model + 128)],
+        5 * attend + 4 * unit, (), [pltpu.VMEM((128, model), FULL)],
     )
     sent, kept = split_core(self_grads)
-    self_moved = exchange(sent, 1)
-    ffn_kept, ffn_sends = fold_square(spot, ffn_kept, [after(item, sent) for item in ffn_moved])
-    ffn_moved = move_layers(ffn_sends)
+    if fast:
+        wide_pair = (2, rows, 2 * hidden + 4 * model)
+        layer_keep, layer_send = call(
+            functools.partial(fold_layers_kernel, depth), "fold_layers", [spot],
+            [own_first, after(got_first, sent), own_second, got_second, cross_kept, *cross_moved],
+            [(wide_pair, FULL), (wide_pair, LOW)], 1,
+        )
+        ffn_sends = [layer_send]
+        layer_got = exchange(layer_send, 4)
+        self_moved = exchange(after(sent, layer_send), 1)
+    else:
+        self_moved = exchange(sent, 1)
+        ffn_kept, ffn_sends = fold_square(spot, ffn_kept, [after(item, sent) for item in ffn_moved])
+        ffn_moved = move_layers(ffn_sends)
     (tokens_grad,) = blocked(
         tokens_grad_kernel, "tokens_grad",
         [after(self_dq, *ffn_sends), self_dk, self_dv, first_sum],
@@ -901,6 +1042,40 @@
     )
     self_kept, self_sends = fold_core(spot, kept, after(self_moved, tokens_grad))
     self_moved = move_square(self_sends)
+    grad_scale = 1.0 / math.sqrt(total * count)
+    if fast:
+        wide_row = wide_pair[1:]
+        layer_own, layer_send = call(
+            fold_last_kernel, "fold_last", [], [layer_keep, after(layer_got, *self_sends)],
+            [(wide_row, FULL), (wide_row, LOW)], 1,
+        )
+        layer_got = exchange(layer_send, 2)
+        kinds = [FULL, FULL, FULL, LOW]
+        ffn_out_state = (ffn_out_master, ffn_out_first, ffn_out_second)
+        ffn_in_state = (ffn_in_master, ffn_in_first, ffn_in_second)
+        ffn_new = call(
+            functools.partial(ffn_update_kernel, grad_scale), "ffn_update", [],
+            [layer_own, layer_got, *ffn_in_state, *ffn_out_state],
+            [(ffn_in_master.shape, kind) for kind in kinds]
+            + [(ffn_out_master.shape, kind) for kind in kinds], 1,
+        )
+        self_kept, self_sends = fold_square(
+            spot, self_kept, [after(item, layer_send) for item in self_moved]
+        )
+        self_moved = move_layers(self_sends)
+        states = [
+            qkv_master, qkv_first, qkv_second, out_master, out_first, out_second,
+            vector_master.T, vector_first.T, vector_second.T,
+        ]
+        final_new = call(
+            functools.partial(final_update_kernel, grad_scale, 2 * hidden), "final_update", [],
+            [layer_own, layer_got, self_kept, *self_moved, *states],
+            [(item.shape, kind) for item in states[::3] for kind in kinds], 1,
+        )
+        return (
+            layer_out, tokens_grad, encoded_grad, *final_new[:8], *ffn_new,
+            *[item.T for item in final_new[8:]],
+        )
     cross_kept, cross_sends = fold_square(
         spot, cross_kept, [after(item, *self_sends) for item in cross_moved]
     )
@@ -925,7 +1100,6 @@
         ffn_total[:, hidden:].reshape(rows, pieces, model).transpose(1, 0, 2).reshape(-1, model)
     )
     summed_vector = self_total[:, 4 * model : 4 * model + vector_master.shape[0]].T
-    grad_scale = 1.0 / math.sqrt(total * count)
     qkv_first_new, qkv_second_new, qkv_master_new, qkv_copy = adamw(
         qkv_master, summed_qkv * grad_scale, qkv_first, qkv_second, 0.04
     )

time: 229 us -> 206 us (0.90)
  Pallas kernels: 108 us -> 99.4 us
  local copies, waits for them, and re-layouts: 7.98 us -> 0.21 us
  starting transfers between devices: 51.4 us -> 44.2 us
  waiting for transfers between devices: 49.7 us -> 55.6 us
  other arithmetic: 8.9 us -> 4.68 us
    ppermute x48 -> x45, starting transfers between devices: 51.4 us -> 44.2 us  [exchange(): return lax.ppermute(values, AXES, [(i, i ^ offset) for i in range(count)])]
    pallas_call x12 -> x14, Pallas kernels: 73.6 us -> 67.6 us  [call(): pl.pallas_call(kernel, out_shape=shapes, in_specs=specs, out_specs=[pl.Bl...]
    mul x4 -> x0, local copies, waits for them, and re-layouts: 5.91 us -> none  [the longest x2 3.25 us: adamw(): first_new = beta_first * first + (1.0 - beta_first) * grad]
    ppermute x48 -> x45, waiting for transfers between devices: 49.7 us -> 55.6 us  [exchange(): return lax.ppermute(values, AXES, [(i, i ^ offset) for i in range(count)])]
    pallas_call x4 -> x3, Pallas kernels: 34.9 us -> 31.8 us  [blocked(): pl.pallas_call(kernel, grid=(total // STEP_ROWS,), out_shape=shapes, in_s...]
    convert_element_type x4 -> x0, other arithmetic: 3.09 us -> none  [adamw(): return (first_new, second_new, master_new, master_new.astype(jnp.bfloat16))]
  transfers between devices with their start and end apart: 48 -> 45, of which waited for: 13 -> 14; matrix products, arithmetic and copies ran while one was open for 5% -> 2% of each run, Pallas kernels for 33% -> 35%
where the time goes in v5:
time: 206 us
  Pallas kernels  99.4 us (48%)
  waiting for transfers between devices  55.6 us (27%)
  starting transfers between devices  44.2 us (21%)
  other arithmetic  4.68 us (2%)
    pallas_call x14, Pallas kernels, call(): pl.pallas_call(kernel, out_shape=shapes, in_specs=specs, out_specs=[pl.Bl...  67.6 us
    ppermute x45, waiting for transfers between devices, exchange(): return lax.ppermute(values, AXES, [(i, i ^ offset) for i in range(count)])  55.6 us
    ppermute x45, starting transfers between devices, exchange(): return lax.ppermute(values, AXES, [(i, i ^ offset) for i in range(count)])  44.2 us
    pallas_call x3, Pallas kernels, blocked(): pl.pallas_call(kernel, grid=(total // STEP_ROWS,), out_shape=shapes, in_s...  31.8 us
  transfers between devices with their start and end apart: 45, of which 14 were waited for; matrix products, arithmetic and copies ran while one was open for 2% of the time, Pallas kernels for 35%

profile of v5, /device:TPU:0, one launch (start us, length us, event | category | flops | bytes accessed | tf_op | source)
XLA Modules:
  0.0 205.6 jit_solution(9720047705342383379)
XLA Ops:
  0.7 0.7 convert_bitcast_fusion
  1.4 0.9 convert_element_type.26
  2.4 4.1 %collective-permute-start.1 = (bf16[16,1664]{1,0:T(8,128)(2,1)S(1)}, bf16[16,1664]{1,0:T(8,128)(2,1)S(1)}, u32[]{:S(2)}, u32[]{:S(2)}) collective-permute-start(bf16[16,1664]{1,0:T(8,128)(2,1)S(1)} %fusion.1), channel_id=1, source_target_pairs={{0,4},{1,5},{2,6},{3,7},{4,0},{5,1},{6,2},{7,3},{8,12},{9,13},{10,... | collective-permute-start | bytes 159752 | tf_op jit(solution)/shard_map/ppermute | solution.py:730
  6.5 1.6 collective-permute-start
  8.1 0.8 convert_element_type.25
  8.9 0.9 convert_element_type.28
  10.0 0.9 convert_dynamic-update-slice_fusion
  10.9 3.1 %collective-permute-done.2 = bf16[16,1664]{1,0:T(8,128)(2,1)S(1)} collective-permute-done((bf16[16,1664]{1,0:T(8,128)(2,1)S(1)}, bf16[16,1664]{1,0:T(8,128)(2,1)S(1)}, u32[]{:S(2)}, u32[]{:S(2)}) %collective-permute-start.2) | collective-permute-done | bytes 53280 | tf_op jit(solution)/shard_map/ppermute | solution.py:730
  14.0 0.9 collective-permute-start.5
  14.9 3.6 %collective-permute-start.3 = (bf16[16,6656]{1,0:T(8,128)(2,1)S(1)}, bf16[16,6656]{1,0:T(8,128)(2,1)S(1)}, u32[]{:S(2)}, u32[]{:S(2)}) collective-permute-start(bf16[16,6656]{1,0:T(8,128)(2,1)S(1)} %constant_dynamic-update-slice_fusion), channel_id=1, source_target_pairs={{0,2},{1,3},{2,0},{3,1},{4,6},{5,7},{6,4},{7,5},{8,10},{9,11},{10,... | collective-permute-start | bytes 638984 | tf_op jit(solution)/shard_map/ppermute | solution.py:730
  18.7 2.5 %collective-permute-start.8 = (bf16[4,16,1664]{2,1,0:T(8,128)(2,1)S(1)}, bf16[4,16,1664]{2,1,0:T(8,128)(2,1)S(1)}, u32[]{:S(2)}, u32[]{:S(2)}) collective-permute-start(bf16[4,16,1664]{2,1,0:T(8,128)(2,1)S(1)} %pad_maximum_fusion.4.rest_0_), channel_id=1, source_target_pairs={{0,24},{1,25},{2,26},{3,27},{4,28},{5,29},{6,30},{7,31},{8,16},{9,... | collective-permute-start | bytes 638984 | tf_op jit(solution)/shard_map/ppermute | solution.py:730
  21.2 2.9 %collective-permute-done.5 = bf16[16,6656]{1,0:T(8,128)(2,1)S(1)} collective-permute-done((bf16[16,6656]{1,0:T(8,128)(2,1)S(1)}, bf16[16,6656]{1,0:T(8,128)(2,1)S(1)}, u32[]{:S(2)}, u32[]{:S(2)}) %collective-permute-start.5) | collective-permute-done | bytes 213024 | tf_op jit(solution)/shard_map/ppermute | solution.py:730
  24.1 1.5 collective-permute-start.7
  25.6 6.7 %collective-permute-done.4 = bf16[16,6656]{1,0:T(8,128)(2,1)S(1)} collective-permute-done((bf16[16,6656]{1,0:T(8,128)(2,1)S(1)}, bf16[16,6656]{1,0:T(8,128)(2,1)S(1)}, u32[]{:S(2)}, u32[]{:S(2)}) %collective-permute-start.4) | collective-permute-done | bytes 213024 | tf_op jit(solution)/shard_map/ppermute | solution.py:730
  32.3 1.5 collective-permute-start.6
  34.4 3.7 %collective-permute-done.6.rest_1_ = bf16[4,16,1664]{2,1,0:T(8,128)(2,1)S(1)} collective-permute-done((bf16[4,16,1664]{2,1,0:T(8,128)(2,1)S(1)}, bf16[4,16,1664]{2,1,0:T(8,128)(2,1)S(1)}, u32[]{:S(2)}, u32[]{:S(2)}) %collective-permute-start.6) | collective-permute-done | bytes 213024 | tf_op jit(solution)/shard_map/ppermute | solution.py:730
  38.2 2.5 %collective-permute-start.15 = (bf16[4,16,2560]{2,1,0:T(8,128)(2,1)S(1)}, bf16[4,16,2560]{2,1,0:T(8,128)(2,1)S(1)}, u32[]{:S(2)}, u32[]{:S(2)}) collective-permute-start(bf16[4,16,2560]{2,1,0:T(8,128)(2,1)S(1)} %pad_maximum_fusion.3.rest_0_), channel_id=1, source_target_pairs={{0,24},{1,25},{2,26},{3,27},{4,28},{5,29},{6,30},{7,31},{8,16},{9,... | collective-permute-start | bytes 983048 | tf_op jit(solution)/shard_map/ppermute | solution.py:730
  41.2 0.5 collective-permute-start.13
  41.8 1.5 collective-permute-start.20
  43.3 13.5 %self_forward.1 = (bf16[512,1664]{1,0:T(8,128)(2,1)S(1)}, f32[24,512]{1,0:T(8,128)S(1)}, bf16[1024,512]{1,0:T(8,128)(2,1)S(1)}, bf16[1024,512]{1,0:T(8,128)(2,1)...) custom-call(s32[1]{0:T(128)} %bitcast.place, ...), custom_call_target="tpu_custom_call" | custom-call | flops 6979321856 | bytes 2752512 | tf_op jit(solution)/shard_map/self_forward/pallas_call | solution.py:666
  58.0 9.7 %collective-permute-done.20.rest_1_ = bf16[4,16,4096]{2,1,0:T(8,128)(2,1)S(1)} collective-permute-done((bf16[4,16,4096]{2,1,0:T(8,128)(2,1)S(1)}, bf16[4,16,4096]{2,1,0:T(8,128)(2,1)S(1)}, u32[]{:S(2)}, u32[]{:S(2)}) %collective-permute-start.20) | collective-permute-done | bytes 524320 | tf_op jit(solution)/shard_map/ppermute | solution.py:730
  68.7 1.5 collective-permute-start.22
  70.2 16.7 %cross_forward.1 = (bf16[512,2560]{1,0:T(8,128)(2,1)S(1)}, f32[1024,512]{1,0:T(8,128)S(1)}, f32[1024,1]{1,0:T(8,128)S(1)}, bf16[1024,512]{1,0:T(8,128)(2,1)S(1)}...) custom-call(s32[1]{0:T(128)} %bitcast.place, ...), custom_call_target="tpu_custom_call" | custom-call | flops 7516192768 | bytes 5816320 | tf_op jit(solution)/shard_map/cross_forward/pallas_call | solution.py:666
  87.1 5.4 %collective-permute-done.22.rest_3_ = bf16[4,16,4096]{2,1,0:T(8,128)(2,1)S(1)} collective-permute-done((bf16[4,16,4096]{2,1,0:T(8,128)(2,1)S(1)}, bf16[4,16,4096]{2,1,0:T(8,128)(2,1)S(1)}, u32[]{:S(2)}, u32[]{:S(2)}) %collective-permute-start.22) | collective-permute-done | bytes 524320 | tf_op jit(solution)/shard_map/ppermute | solution.py:730
  92.5 2.0 cross_finish.1
  94.5 26.4 %ffn.1 = (bf16[1024,512]{1,0:T(8,128)(2,1)}, f32[1024,512]{1,0:T(8,128)S(1)}, bf16[1024,512]{1,0:T(8,128)(2,1)S(1)}, bf16[1024,512]{1,0:T(8,128)(2,1)S(1)}, f32[...) custom-call(s32[1]{0:T(128)} %bitcast.place, ...), custom_call_target="tpu_custom_call" | custom-call | flops 11274289152 | bytes 7344128 | tf_op jit(solution)/shard_map/ffn/pallas_call | solution.py:696
  120.9 0.6 collective-permute-start.27
  121.5 12.4 %cross_backward.1 = (bf16[1024,512]{1,0:T(8,128)(2,1)S(1)}, bf16[1024,512]{1,0:T(8,128)(2,1)S(1)}, bf16[1024,512]{1,0:T(8,128)(2,1)S(1)}) custom-call(s32[11]{0:T(128)S(1)} %convert_reduce_fusion.1.row_starts, s32[11]{0:T(128)S(1)} %convert_reduce_fusion.col_starts, bf16[1024,512]{1,0:T(8,128)(2,1)S(1)} %get-tuple-element.155.queries, ...), custom_call_target="tpu_custom_call" | custom-call | flops 13421772800 | bytes 4276224 | tf_op jit(solution)/shard_map/cross_backward/pallas_call | solution.py:666
  134.9 1.9 collective-permute-start.29
  136.8 6.5 %cross_grads.1 = (f32[1024,512]{1,0:T(8,128)S(1)}, bf16[1024,512]{1,0:T(8,128)(2,1)S(1)}, bf16[1024,512]{1,0:T(8,128)(2,1)S(1)}, f32[8,512]{1,0:T(8,128)S(1)}, f...) custom-call(s32[1]{0:T(128)} %bitcast.place, ...), custom_call_target="tpu_custom_call" | custom-call | flops 4294967296 | bytes 14209024 | tf_op jit(solution)/shard_map/cross_grads/pallas_call | solution.py:666
  143.4 4.9 %collective-permute-done.28.got_first = bf16[2,4,16,2048]{3,2,1,0:T(8,128)(2,1)S(1)} collective-permute-done((bf16[2,4,16,2048]{3,2,1,0:T(8,128)(2,1)S(1)}, bf16[2,4,16,2048]{3,2,1,0:T(8,128)(2,1)S(1)}, u32[]{:S(2)}, u32[]{:S(2)}) %collective-permute-start.28) | collective-permute-done | bytes 524320 | tf_op jit(solution)/shard_map/ppermute | solution.py:730
  148.3 1.1 collective-permute-done.29.got_second
  149.6 1.8 collective-permute-start.31
  152.5 1.8 collective-permute-start.33
  154.6 1.4 collective-permute-start.35
  156.0 14.7 %self_backward.1 = (bf16[1024,512]{1,0:T(8,128)(2,1)S(1)}, bf16[1024,512]{1,0:T(8,128)(2,1)S(1)}, bf16[1024,512]{1,0:T(8,128)(2,1)S(1)}, bf16[16,16,2176]{2,1,0:T(8,128)(2,1)S(1)}, bf16[16,16,2176]{2,1,0:T(8,128)(2,1)S(1)}) custom-call(s32[1]{0:T(128)} %bitcast.place, s32[11]{0:T(128)S(1)} %convert_reduce_fusion.1.row_starts, ...), custom_call_target="tpu_custom_call" | custom-call | flops 15569256448 | bytes 7471104 | tf_op jit(solution)/shard_map/self_backward/pallas_call | solution.py:666
  171.5 1.3 collective-permute-start.36
  172.8 3.4 %tokens_grad.1 = f32[1024,512]{1,0:T(8,128)} custom-call(bf16[1024,512]{1,0:T(8,128)(2,1)S(1)} %get-tuple-element.199.dq, bf16[1024,512]{1,0:T(8,128)(2,1)S(1)} %get-tuple-element.200.dk, bf16[1024,512]{1,0:T(8,128)(2,1)S(1)} %get-tuple-element.201.dv, f32[1024,512]{1,0:T(8,128)S(1)} %get-tuple-element.202.first_sum, ...), custom_call_target="tpu_custom_call" | custom-call | flops 1610612736 | bytes 5242880 | tf_op jit(solution)/shard_map/tokens_grad/pallas_call | solution.py:696
  176.7 2.3 %collective-permute-start.39 = (bf16[4,16,2176]{2,1,0:T(8,128)(2,1)S(1)}, bf16[4,16,2176]{2,1,0:T(8,128)(2,1)S(1)}, u32[]{:S(2)}, u32[]{:S(2)}) collective-permute-start(bf16[4,16,2176]{2,1,0:T(8,128)(2,1)S(1)} %get-tuple-element.209), channel_id=1, source_target_pairs={{0,8},{1,9},{2,10},{3,11},{4,12},{5,13},{6,14},{7,15},{8,0},{9,1},... | collective-permute-start | bytes 835592 | tf_op jit(solution)/shard_map/ppermute | solution.py:730
  179.2 1.2 collective-permute-start.41
  180.5 11.7 %collective-permute-done.36.got = bf16[2,16,6144]{2,1,0:T(8,128)(2,1)S(1)} collective-permute-done((bf16[2,16,6144]{2,1,0:T(8,128)(2,1)S(1)}, bf16[2,16,6144]{2,1,0:T(8,128)(2,1)S(1)}, u32[]{:S(2)}, u32[]{:S(2)}) %collective-permute-start.36) | collective-permute-done | bytes 393248 | tf_op jit(solution)/shard_map/ppermute | solution.py:730
  192.3 1.3 collective-permute-done.40.rest_1_
  193.8 2.5 %collective-permute-start.42 = (bf16[16,2176]{1,0:T(8,128)(2,1)S(1)}, bf16[16,2176]{1,0:T(8,128)(2,1)S(1)}, u32[]{:S(2)}, u32[]{:S(2)}) collective-permute-start(bf16[16,2176]{1,0:T(8,128)(2,1)S(1)} %get-tuple-element.220), channel_id=1, source_target_pairs={{0,2},{1,3},{2,0},{3,1},{4,6},{5,7},{6,4},{7,5},{8,10},{9,11},{10,... | collective-permute-start | bytes 208904 | tf_op jit(solution)/shard_map/ppermute | solution.py:730
  196.6 2.1 %collective-permute-start.44 = (bf16[16,2176]{1,0:T(8,128)(2,1)S(1)}, bf16[16,2176]{1,0:T(8,128)(2,1)S(1)}, u32[]{:S(2)}, u32[]{:S(2)}) collective-permute-start(bf16[16,2176]{1,0:T(8,128)(2,1)S(1)} %get-tuple-element.222), channel_id=1, source_target_pairs={{0,6},{1,7},{2,4},{3,5},{4,2},{5,3},{6,0},{7,1},{8,14},{9,15},{10,... | collective-permute-start | bytes 208904 | tf_op jit(solution)/shard_map/ppermute | solution.py:730
  198.7 1.4 collective-permute-done.38.got
  200.2 1.1 ffn_update.1
  201.3 3.0 %collective-permute-done.43.rest_1_ = bf16[16,2176]{1,0:T(8,128)(2,1)S(1)} collective-permute-done((bf16[16,2176]{1,0:T(8,128)(2,1)S(1)}, bf16[16,2176]{1,0:T(8,128)(2,1)S(1)}, u32[]{:S(2)}, u32[]{:S(2)}) %collective-permute-start.43) | collective-permute-done | bytes 69664 | tf_op jit(solution)/shard_map/ppermute | solution.py:730
  204.3 1.1 final_update.1
  (120 shorter events, 8.5 us)
Async XLA Ops:
  2.3 40.9 %copy-start.17 = (bf16[1024,512]{1,0:T(8,128)(2,1)S(1)}, bf16[1024,512]{1,0:T(8,128)(2,1)}, u32[]{:S(2)}) copy-start(bf16[1024,512]{1,0:T(8,128)(2,1)} %tokens.4) | copy-start | bytes 3145732
  2.4 8.5 %collective-permute-start.1 = (bf16[16,1664]{1,0:T(8,128)(2,1)S(1)}, bf16[16,1664]{1,0:T(8,128)(2,1)S(1)}, u32[]{:S(2)}, u32[]{:S(2)}) collective-permute-start(bf16[16,1664]{1,0:T(8,128)(2,1)S(1)} %fusion.1), channel_id=1, source_target_pairs={{0,4},{1,5},{2,6},{3,7},{4,0},{5,1},{6,2},{7,3},{8,12},{9,13},{10,... | collective-permute-start | bytes 159752 | tf_op jit(solution)/shard_map/ppermute | solution.py:730
  6.5 4.4 %collective-permute-start = (bf16[16,1664]{1,0:T(8,128)(2,1)S(1)}, bf16[16,1664]{1,0:T(8,128)(2,1)S(1)}, u32[]{:S(2)}, u32[]{:S(2)}) collective-permute-start(bf16[16,1664]{1,0:T(8,128)(2,1)S(1)} %fusion.1), channel_id=1, source_target_pairs={{0,2},{1,3},{2,0},{3,1},{4,6},{5,7},{6,4},{7,5},{8,10},{9,11},{10,... | collective-permute-start | bytes 159752 | tf_op jit(solution)/shard_map/ppermute | solution.py:730
  8.0 5.9 %collective-permute-start.2 = (bf16[16,1664]{1,0:T(8,128)(2,1)S(1)}, bf16[16,1664]{1,0:T(8,128)(2,1)S(1)}, u32[]{:S(2)}, u32[]{:S(2)}) collective-permute-start(bf16[16,1664]{1,0:T(8,128)(2,1)S(1)} %fusion.1), channel_id=1, source_target_pairs={{0,6},{1,7},{2,4},{3,5},{4,2},{5,3},{6,0},{7,1},{8,14},{9,15},{10,... | collective-permute-start | bytes 159752 | tf_op jit(solution)/shard_map/ppermute | solution.py:730
  14.0 10.1 %collective-permute-start.5 = (bf16[16,6656]{1,0:T(8,128)(2,1)S(1)}, bf16[16,6656]{1,0:T(8,128)(2,1)S(1)}, u32[]{:S(2)}, u32[]{:S(2)}) collective-permute-start(bf16[16,6656]{1,0:T(8,128)(2,1)S(1)} %constant_dynamic-update-slice_fusion), channel_id=1, source_target_pairs={{0,6},{1,7},{2,4},{3,5},{4,2},{5,3},{6,0},{7,1},{8,14},{9,15},{10,... | collective-permute-start | bytes 638984 | tf_op jit(solution)/shard_map/ppermute | solution.py:730
  14.9 17.4 %collective-permute-start.4 = (bf16[16,6656]{1,0:T(8,128)(2,1)S(1)}, bf16[16,6656]{1,0:T(8,128)(2,1)S(1)}, u32[]{:S(2)}, u32[]{:S(2)}) collective-permute-start(bf16[16,6656]{1,0:T(8,128)(2,1)S(1)} %constant_dynamic-update-slice_fusion), channel_id=1, source_target_pairs={{0,4},{1,5},{2,6},{3,7},{4,0},{5,1},{6,2},{7,3},{8,12},{9,13},{10,... | collective-permute-start | bytes 638984 | tf_op jit(solution)/shard_map/ppermute | solution.py:730
  14.9 18.9 %collective-permute-start.3 = (bf16[16,6656]{1,0:T(8,128)(2,1)S(1)}, bf16[16,6656]{1,0:T(8,128)(2,1)S(1)}, u32[]{:S(2)}, u32[]{:S(2)}) collective-permute-start(bf16[16,6656]{1,0:T(8,128)(2,1)S(1)} %constant_dynamic-update-slice_fusion), channel_id=1, source_target_pairs={{0,2},{1,3},{2,0},{3,1},{4,6},{5,7},{6,4},{7,5},{8,10},{9,11},{10,... | collective-permute-start | bytes 638984 | tf_op jit(solution)/shard_map/ppermute | solution.py:730
  18.6 22.1 %collective-permute-start.9 = (bf16[4,16,1664]{2,1,0:T(8,128)(2,1)S(1)}, bf16[4,16,1664]{2,1,0:T(8,128)(2,1)S(1)}, u32[]{:S(2)}, u32[]{:S(2)}) collective-permute-start(bf16[4,16,1664]{2,1,0:T(8,128)(2,1)S(1)} %pad_maximum_fusion.4.rest_0_), channel_id=1, source_target_pairs={{0,1},{1,0},{2,3},{3,2},{4,5},{5,4},{6,7},{7,6},{8,9},{9,8},{10,11... | collective-permute-start | bytes 638984 | tf_op jit(solution)/shard_map/ppermute | solution.py:730
  18.7 15.2 %collective-permute-start.8 = (bf16[4,16,1664]{2,1,0:T(8,128)(2,1)S(1)}, bf16[4,16,1664]{2,1,0:T(8,128)(2,1)S(1)}, u32[]{:S(2)}, u32[]{:S(2)}) collective-permute-start(bf16[4,16,1664]{2,1,0:T(8,128)(2,1)S(1)} %pad_maximum_fusion.4.rest_0_), channel_id=1, source_target_pairs={{0,24},{1,25},{2,26},{3,27},{4,28},{5,29},{6,30},{7,31},{8,16},{9,... | collective-permute-start | bytes 638984 | tf_op jit(solution)/shard_map/ppermute | solution.py:730
  24.1 9.8 %collective-permute-start.7 = (bf16[4,16,1664]{2,1,0:T(8,128)(2,1)S(1)}, bf16[4,16,1664]{2,1,0:T(8,128)(2,1)S(1)}, u32[]{:S(2)}, u32[]{:S(2)}) collective-permute-start(bf16[4,16,1664]{2,1,0:T(8,128)(2,1)S(1)} %pad_maximum_fusion.4.rest_0_), channel_id=1, source_target_pairs={{0,16},{1,17},{2,18},{3,19},{4,20},{5,21},{6,22},{7,23},{8,24},{9,... | collective-permute-start | bytes 638984 | tf_op jit(solution)/shard_map/ppermute | solution.py:730
  32.3 5.8 %collective-permute-start.6 = (bf16[4,16,1664]{2,1,0:T(8,128)(2,1)S(1)}, bf16[4,16,1664]{2,1,0:T(8,128)(2,1)S(1)}, u32[]{:S(2)}, u32[]{:S(2)}) collective-permute-start(bf16[4,16,1664]{2,1,0:T(8,128)(2,1)S(1)} %pad_maximum_fusion.4.rest_0_), channel_id=1, source_target_pairs={{0,8},{1,9},{2,10},{3,11},{4,12},{5,13},{6,14},{7,15},{8,0},{9,1},... | collective-permute-start | bytes 638984 | tf_op jit(solution)/shard_map/ppermute | solution.py:730
  33.9 7.4 %collective-permute-start.12 = (bf16[4,16,1664]{2,1,0:T(8,128)(2,1)S(1)}, bf16[4,16,1664]{2,1,0:T(8,128)(2,1)S(1)}, u32[]{:S(2)}, u32[]{:S(2)}) collective-permute-start(bf16[4,16,1664]{2,1,0:T(8,128)(2,1)S(1)} %collective-permute-done.8.rest_3_), channel_id=1, source_target_pairs={{0,1},{1,0},{2,3},{3,2},{4,5},{5,4},{6,7},{7,6},{8,9},{9,8},{10,11... | collective-permute-start | bytes 638984 | tf_op jit(solution)/shard_map/ppermute | solution.py:730
  34.0 7.8 %collective-permute-start.11 = (bf16[4,16,1664]{2,1,0:T(8,128)(2,1)S(1)}, bf16[4,16,1664]{2,1,0:T(8,128)(2,1)S(1)}, u32[]{:S(2)}, u32[]{:S(2)}) collective-permute-start(bf16[4,16,1664]{2,1,0:T(8,128)(2,1)S(1)} %collective-permute-done.7.rest_2_), channel_id=1, source_target_pairs={{0,1},{1,0},{2,3},{3,2},{4,5},{5,4},{6,7},{7,6},{8,9},{9,8},{10,11... | collective-permute-start | bytes 638984 | tf_op jit(solution)/shard_map/ppermute | solution.py:730
  38.2 5.1 %collective-permute-start.10 = (bf16[4,16,1664]{2,1,0:T(8,128)(2,1)S(1)}, bf16[4,16,1664]{2,1,0:T(8,128)(2,1)S(1)}, u32[]{:S(2)}, u32[]{:S(2)}) collective-permute-start(bf16[4,16,1664]{2,1,0:T(8,128)(2,1)S(1)} %collective-permute-done.6.rest_1_), channel_id=1, source_target_pairs={{0,1},{1,0},{2,3},{3,2},{4,5},{5,4},{6,7},{7,6},{8,9},{9,8},{10,11... | collective-permute-start | bytes 638984 | tf_op jit(solution)/shard_map/ppermute | solution.py:730
  38.2 32.0 %copy-start.16 = (bf16[1024,512]{1,0:T(8,128)(2,1)S(1)}, bf16[1024,512]{1,0:T(8,128)(2,1)}, u32[]{:S(2)}) copy-start(bf16[1024,512]{1,0:T(8,128)(2,1)} %encoded.3) | copy-start | bytes 3145732
  38.2 18.6 %collective-permute-start.15 = (bf16[4,16,2560]{2,1,0:T(8,128)(2,1)S(1)}, bf16[4,16,2560]{2,1,0:T(8,128)(2,1)S(1)}, u32[]{:S(2)}, u32[]{:S(2)}) collective-permute-start(bf16[4,16,2560]{2,1,0:T(8,128)(2,1)S(1)} %pad_maximum_fusion.3.rest_0_), channel_id=1, source_target_pairs={{0,24},{1,25},{2,26},{3,27},{4,28},{5,29},{6,30},{7,31},{8,16},{9,... | collective-permute-start | bytes 983048 | tf_op jit(solution)/shard_map/ppermute | solution.py:730
  40.7 16.6 %collective-permute-start.14 = (bf16[4,16,2560]{2,1,0:T(8,128)(2,1)S(1)}, bf16[4,16,2560]{2,1,0:T(8,128)(2,1)S(1)}, u32[]{:S(2)}, u32[]{:S(2)}) collective-permute-start(bf16[4,16,2560]{2,1,0:T(8,128)(2,1)S(1)} %pad_maximum_fusion.3.rest_0_), channel_id=1, source_target_pairs={{0,16},{1,17},{2,18},{3,19},{4,20},{5,21},{6,22},{7,23},{8,24},{9,... | collective-permute-start | bytes 983048 | tf_op jit(solution)/shard_map/ppermute | solution.py:730
  41.2 15.6 %collective-permute-start.13 = (bf16[4,16,2560]{2,1,0:T(8,128)(2,1)S(1)}, bf16[4,16,2560]{2,1,0:T(8,128)(2,1)S(1)}, u32[]{:S(2)}, u32[]{:S(2)}) collective-permute-start(bf16[4,16,2560]{2,1,0:T(8,128)(2,1)S(1)} %pad_maximum_fusion.3.rest_0_), channel_id=1, source_target_pairs={{0,8},{1,9},{2,10},{3,11},{4,12},{5,13},{6,14},{7,15},{8,0},{9,1},... | collective-permute-start | bytes 983048 | tf_op jit(solution)/shard_map/ppermute | solution.py:730
  41.8 25.9 %collective-permute-start.20 = (bf16[4,16,4096]{2,1,0:T(8,128)(2,1)S(1)}, bf16[4,16,4096]{2,1,0:T(8,128)(2,1)S(1)}, u32[]{:S(2)}, u32[]{:S(2)}) collective-permute-start(bf16[4,16,4096]{2,1,0:T(8,128)(2,1)S(1)} %pad_maximum_fusion.rest_0_), channel_id=1, source_target_pairs={{0,8},{1,9},{2,10},{3,11},{4,12},{5,13},{6,14},{7,15},{8,0},{9,1},... | collective-permute-start | bytes 1572872 | tf_op jit(solution)/shard_map/ppermute | solution.py:730
  56.8 11.4 %collective-permute-start.16 = (bf16[4,16,2560]{2,1,0:T(8,128)(2,1)S(1)}, bf16[4,16,2560]{2,1,0:T(8,128)(2,1)S(1)}, u32[]{:S(2)}, u32[]{:S(2)}) collective-permute-start(bf16[4,16,2560]{2,1,0:T(8,128)(2,1)S(1)} %pad_maximum_fusion.3.rest_0_), channel_id=1, source_target_pairs={{0,1},{1,0},{2,3},{3,2},{4,5},{5,4},{6,7},{7,6},{8,9},{9,8},{10,11... | collective-permute-start | bytes 983048 | tf_op jit(solution)/shard_map/ppermute | solution.py:730
  56.9 11.3 %collective-permute-start.17 = (bf16[4,16,2560]{2,1,0:T(8,128)(2,1)S(1)}, bf16[4,16,2560]{2,1,0:T(8,128)(2,1)S(1)}, u32[]{:S(2)}, u32[]{:S(2)}) collective-permute-start(bf16[4,16,2560]{2,1,0:T(8,128)(2,1)S(1)} %collective-permute-done.13.rest_1_), channel_id=1, source_target_pairs={{0,1},{1,0},{2,3},{3,2},{4,5},{5,4},{6,7},{7,6},{8,9},{9,8},{10,11... | collective-permute-start | bytes 983048 | tf_op jit(solution)/shard_map/ppermute | solution.py:730
  57.3 11.3 %collective-permute-start.18 = (bf16[4,16,2560]{2,1,0:T(8,128)(2,1)S(1)}, bf16[4,16,2560]{2,1,0:T(8,128)(2,1)S(1)}, u32[]{:S(2)}, u32[]{:S(2)}) collective-permute-start(bf16[4,16,2560]{2,1,0:T(8,128)(2,1)S(1)} %collective-permute-done.14.rest_2_), channel_id=1, source_target_pairs={{0,1},{1,0},{2,3},{3,2},{4,5},{5,4},{6,7},{7,6},{8,9},{9,8},{10,11... | collective-permute-start | bytes 983048 | tf_op jit(solution)/shard_map/ppermute | solution.py:730
  57.4 12.8 %collective-permute-start.19 = (bf16[4,16,2560]{2,1,0:T(8,128)(2,1)S(1)}, bf16[4,16,2560]{2,1,0:T(8,128)(2,1)S(1)}, u32[]{:S(2)}, u32[]{:S(2)}) collective-permute-start(bf16[4,16,2560]{2,1,0:T(8,128)(2,1)S(1)} %collective-permute-done.15.rest_3_), channel_id=1, source_target_pairs={{0,1},{1,0},{2,3},{3,2},{4,5},{5,4},{6,7},{7,6},{8,9},{9,8},{10,11... | collective-permute-start | bytes 983048 | tf_op jit(solution)/shard_map/ppermute | solution.py:730
  67.7 19.3 %collective-permute-start.21 = (bf16[4,16,4096]{2,1,0:T(8,128)(2,1)S(1)}, bf16[4,16,4096]{2,1,0:T(8,128)(2,1)S(1)}, u32[]{:S(2)}, u32[]{:S(2)}) collective-permute-start(bf16[4,16,4096]{2,1,0:T(8,128)(2,1)S(1)} %pad_maximum_fusion.rest_0_), channel_id=1, source_target_pairs={{0,16},{1,17},{2,18},{3,19},{4,20},{5,21},{6,22},{7,23},{8,24},{9,... | collective-permute-start | bytes 1572872 | tf_op jit(solution)/shard_map/ppermute | solution.py:730
  68.2 26.3 %collective-permute-start.23 = (bf16[4,16,4096]{2,1,0:T(8,128)(2,1)S(1)}, bf16[4,16,4096]{2,1,0:T(8,128)(2,1)S(1)}, u32[]{:S(2)}, u32[]{:S(2)}) collective-permute-start(bf16[4,16,4096]{2,1,0:T(8,128)(2,1)S(1)} %pad_maximum_fusion.rest_0_), channel_id=1, source_target_pairs={{0,1},{1,0},{2,3},{3,2},{4,5},{5,4},{6,7},{7,6},{8,9},{9,8},{10,11... | collective-permute-start | bytes 1572872 | tf_op jit(solution)/shard_map/ppermute | solution.py:730
  68.2 26.3 %collective-permute-start.24 = (bf16[4,16,4096]{2,1,0:T(8,128)(2,1)S(1)}, bf16[4,16,4096]{2,1,0:T(8,128)(2,1)S(1)}, u32[]{:S(2)}, u32[]{:S(2)}) collective-permute-start(bf16[4,16,4096]{2,1,0:T(8,128)(2,1)S(1)} %collective-permute-done.20.rest_1_), channel_id=1, source_target_pairs={{0,1},{1,0},{2,3},{3,2},{4,5},{5,4},{6,7},{7,6},{8,9},{9,8},{10,11... | collective-permute-start | bytes 1572872 | tf_op jit(solution)/shard_map/ppermute | solution.py:730
  68.7 23.8 %collective-permute-start.22 = (bf16[4,16,4096]{2,1,0:T(8,128)(2,1)S(1)}, bf16[4,16,4096]{2,1,0:T(8,128)(2,1)S(1)}, u32[]{:S(2)}, u32[]{:S(2)}) collective-permute-start(bf16[4,16,4096]{2,1,0:T(8,128)(2,1)S(1)} %collective-permute-done.20.rest_1_), channel_id=1, source_target_pairs={{0,16},{1,17},{2,18},{3,19},{4,20},{5,21},{6,22},{7,23},{8,24},{9,... | collective-permute-start | bytes 1572872 | tf_op jit(solution)/shard_map/ppermute | solution.py:730
  87.0 7.5 %collective-permute-start.25 = (bf16[4,16,4096]{2,1,0:T(8,128)(2,1)S(1)}, bf16[4,16,4096]{2,1,0:T(8,128)(2,1)S(1)}, u32[]{:S(2)}, u32[]{:S(2)}) collective-permute-start(bf16[4,16,4096]{2,1,0:T(8,128)(2,1)S(1)} %collective-permute-done.21.rest_2_), channel_id=1, source_target_pairs={{0,1},{1,0},{2,3},{3,2},{4,5},{5,4},{6,7},{7,6},{8,9},{9,8},{10,11... | collective-permute-start | bytes 1572872 | tf_op jit(solution)/shard_map/ppermute | solution.py:730
  92.5 2.0 collective-permute-start.26
  120.9 13.0 %collective-permute-start.27 = (bf16[16,16,4096]{2,1,0:T(8,128)(2,1)S(1)}, bf16[16,16,4096]{2,1,0:T(8,128)(2,1)S(1)}, u32[]{:S(2)}, u32[]{:S(2)}) collective-permute-start(bf16[16,16,4096]{2,1,0:T(8,128)(2,1)S(1)} %get-tuple-element.159), channel_id=1, source_target_pairs={{0,1},{1,0},{2,3},{3,2},{4,5},{5,4},{6,7},{7,6},{8,9},{9,8},{10,11... | collective-permute-start | bytes 6291464 | tf_op jit(solution)/shard_map/ppermute | solution.py:730
  134.4 13.9 %collective-permute-start.28 = (bf16[2,4,16,2048]{3,2,1,0:T(8,128)(2,1)S(1)}, bf16[2,4,16,2048]{3,2,1,0:T(8,128)(2,1)S(1)}, u32[]{:S(2)}, u32[]{:S(2)}) collective-permute-start(bf16[2,4,16,2048]{3,2,1,0:T(8,128)(2,1)S(1)} %get-tuple-element.165), channel_id=1, source_target_pairs={{0,16},{1,17},{2,18},{3,19},{4,20},{5,21},{6,22},{7,23},{8,24},{9,... | collective-permute-start | bytes 1572872 | tf_op jit(solution)/shard_map/ppermute | solution.py:730
  134.9 14.4 %collective-permute-start.29 = (bf16[2,4,16,2048]{3,2,1,0:T(8,128)(2,1)S(1)}, bf16[2,4,16,2048]{3,2,1,0:T(8,128)(2,1)S(1)}, u32[]{:S(2)}, u32[]{:S(2)}) collective-permute-start(bf16[2,4,16,2048]{3,2,1,0:T(8,128)(2,1)S(1)} %get-tuple-element.166), channel_id=1, source_target_pairs={{0,8},{1,9},{2,10},{3,11},{4,12},{5,13},{6,14},{7,15},{8,0},{9,1},... | collective-permute-start | bytes 1572872 | tf_op jit(solution)/shard_map/ppermute | solution.py:730
  149.5 2.7 %collective-permute-start.30 = (bf16[16,16,2048]{2,1,0:T(8,128)(2,1)S(1)}, bf16[16,16,2048]{2,1,0:T(8,128)(2,1)S(1)}, u32[]{:S(2)}, u32[]{:S(2)}) collective-permute-start(bf16[16,16,2048]{2,1,0:T(8,128)(2,1)S(1)} %get-tuple-element.182), channel_id=1, source_target_pairs={{0,1},{1,0},{2,3},{3,2},{4,5},{5,4},{6,7},{7,6},{8,9},{9,8},{10,11... | collective-permute-start | bytes 3145736 | tf_op jit(solution)/shard_map/ppermute | solution.py:730
  149.6 21.1 %collective-permute-start.31 = (bf16[4,16,2048]{2,1,0:T(8,128)(2,1)S(1)}, bf16[4,16,2048]{2,1,0:T(8,128)(2,1)S(1)}, u32[]{:S(2)}, u32[]{:S(2)}) collective-permute-start(bf16[4,16,2048]{2,1,0:T(8,128)(2,1)S(1)} %get-tuple-element.180), channel_id=1, source_target_pairs={{0,8},{1,9},{2,10},{3,11},{4,12},{5,13},{6,14},{7,15},{8,0},{9,1},... | collective-permute-start | bytes 786440 | tf_op jit(solution)/shard_map/ppermute | solution.py:730
  151.4 19.3 %collective-permute-start.32 = (bf16[4,16,2048]{2,1,0:T(8,128)(2,1)S(1)}, bf16[4,16,2048]{2,1,0:T(8,128)(2,1)S(1)}, u32[]{:S(2)}, u32[]{:S(2)}) collective-permute-start(bf16[4,16,2048]{2,1,0:T(8,128)(2,1)S(1)} %get-tuple-element.181), channel_id=1, source_target_pairs={{0,16},{1,17},{2,18},{3,19},{4,20},{5,21},{6,22},{7,23},{8,24},{9,... | collective-permute-start | bytes 786440 | tf_op jit(solution)/shard_map/ppermute | solution.py:730
  152.5 18.3 %collective-permute-start.33 = (bf16[4,16,2048]{2,1,0:T(8,128)(2,1)S(1)}, bf16[4,16,2048]{2,1,0:T(8,128)(2,1)S(1)}, u32[]{:S(2)}, u32[]{:S(2)}) collective-permute-start(bf16[4,16,2048]{2,1,0:T(8,128)(2,1)S(1)} %get-tuple-element.183), channel_id=1, source_target_pairs={{0,8},{1,9},{2,10},{3,11},{4,12},{5,13},{6,14},{7,15},{8,0},{9,1},... | collective-permute-start | bytes 786440 | tf_op jit(solution)/shard_map/ppermute | solution.py:730
  154.3 16.7 %collective-permute-start.34 = (bf16[4,16,2048]{2,1,0:T(8,128)(2,1)S(1)}, bf16[4,16,2048]{2,1,0:T(8,128)(2,1)S(1)}, u32[]{:S(2)}, u32[]{:S(2)}) collective-permute-start(bf16[4,16,2048]{2,1,0:T(8,128)(2,1)S(1)} %get-tuple-element.184), channel_id=1, source_target_pairs={{0,16},{1,17},{2,18},{3,19},{4,20},{5,21},{6,22},{7,23},{8,24},{9,... | collective-permute-start | bytes 786440 | tf_op jit(solution)/shard_map/ppermute | solution.py:730
  154.6 16.4 %collective-permute-start.35 = (bf16[4,16,2048]{2,1,0:T(8,128)(2,1)S(1)}, bf16[4,16,2048]{2,1,0:T(8,128)(2,1)S(1)}, u32[]{:S(2)}, u32[]{:S(2)}) collective-permute-start(bf16[4,16,2048]{2,1,0:T(8,128)(2,1)S(1)} %get-tuple-element.185), channel_id=1, source_target_pairs={{0,24},{1,25},{2,26},{3,27},{4,28},{5,29},{6,30},{7,31},{8,16},{9,... | collective-permute-start | bytes 786440 | tf_op jit(solution)/shard_map/ppermute | solution.py:730
  171.2 5.0 %collective-permute-start.37 = (bf16[16,16,2176]{2,1,0:T(8,128)(2,1)S(1)}, bf16[16,16,2176]{2,1,0:T(8,128)(2,1)S(1)}, u32[]{:S(2)}, u32[]{:S(2)}) collective-permute-start(bf16[16,16,2176]{2,1,0:T(8,128)(2,1)S(1)} %get-tuple-element.207), channel_id=1, source_target_pairs={{0,1},{1,0},{2,3},{3,2},{4,5},{5,4},{6,7},{7,6},{8,9},{9,8},{10,11... | collective-permute-start | bytes 3342344 | tf_op jit(solution)/shard_map/ppermute | solution.py:730
  171.5 20.7 %collective-permute-start.36 = (bf16[2,16,6144]{2,1,0:T(8,128)(2,1)S(1)}, bf16[2,16,6144]{2,1,0:T(8,128)(2,1)S(1)}, u32[]{:S(2)}, u32[]{:S(2)}) collective-permute-start(bf16[2,16,6144]{2,1,0:T(8,128)(2,1)S(1)} %get-tuple-element.198), channel_id=1, source_target_pairs={{0,4},{1,5},{2,6},{3,7},{4,0},{5,1},{6,2},{7,3},{8,12},{9,13},{10,... | collective-permute-start | bytes 1179656 | tf_op jit(solution)/shard_map/ppermute | solution.py:730
  176.5 27.7 %copy-start = (f32[6,16,512]{2,1,0:T(8,128)S(1)}, f32[6,16,512]{2,1,0:T(8,128)}, u32[]{:S(2)}) copy-start(f32[6,16,512]{2,1,0:T(8,128)} %rest_3_.2) | copy-start | bytes 589828
  176.7 15.7 %collective-permute-start.39 = (bf16[4,16,2176]{2,1,0:T(8,128)(2,1)S(1)}, bf16[4,16,2176]{2,1,0:T(8,128)(2,1)S(1)}, u32[]{:S(2)}, u32[]{:S(2)}) collective-permute-start(bf16[4,16,2176]{2,1,0:T(8,128)(2,1)S(1)} %get-tuple-element.209), channel_id=1, source_target_pairs={{0,8},{1,9},{2,10},{3,11},{4,12},{5,13},{6,14},{7,15},{8,0},{9,1},... | collective-permute-start | bytes 835592 | tf_op jit(solution)/shard_map/ppermute | solution.py:730
  178.9 14.7 %collective-permute-start.40 = (bf16[4,16,2176]{2,1,0:T(8,128)(2,1)S(1)}, bf16[4,16,2176]{2,1,0:T(8,128)(2,1)S(1)}, u32[]{:S(2)}, u32[]{:S(2)}) collective-permute-start(bf16[4,16,2176]{2,1,0:T(8,128)(2,1)S(1)} %get-tuple-element.210), channel_id=1, source_target_pairs={{0,16},{1,17},{2,18},{3,19},{4,20},{5,21},{6,22},{7,23},{8,24},{9,... | collective-permute-start | bytes 835592 | tf_op jit(solution)/shard_map/ppermute | solution.py:730
  179.2 14.4 %collective-permute-start.41 = (bf16[4,16,2176]{2,1,0:T(8,128)(2,1)S(1)}, bf16[4,16,2176]{2,1,0:T(8,128)(2,1)S(1)}, u32[]{:S(2)}, u32[]{:S(2)}) collective-permute-start(bf16[4,16,2176]{2,1,0:T(8,128)(2,1)S(1)} %get-tuple-element.211), channel_id=1, source_target_pairs={{0,24},{1,25},{2,26},{3,27},{4,28},{5,29},{6,30},{7,31},{8,16},{9,... | collective-permute-start | bytes 835592 | tf_op jit(solution)/shard_map/ppermute | solution.py:730
  192.2 7.9 %collective-permute-start.38 = (bf16[16,6144]{1,0:T(8,128)(2,1)S(1)}, bf16[16,6144]{1,0:T(8,128)(2,1)S(1)}, u32[]{:S(2)}, u32[]{:S(2)}) collective-permute-start(bf16[16,6144]{1,0:T(8,128)(2,1)S(1)} %get-tuple-element.214), channel_id=1, source_target_pairs={{0,2},{1,3},{2,0},{3,1},{4,6},{5,7},{6,4},{7,5},{8,10},{9,11},{10,... | collective-permute-start | bytes 589832 | tf_op jit(solution)/shard_map/ppermute | solution.py:730
  193.8 7.5 %collective-permute-start.42 = (bf16[16,2176]{1,0:T(8,128)(2,1)S(1)}, bf16[16,2176]{1,0:T(8,128)(2,1)S(1)}, u32[]{:S(2)}, u32[]{:S(2)}) collective-permute-start(bf16[16,2176]{1,0:T(8,128)(2,1)S(1)} %get-tuple-element.220), channel_id=1, source_target_pairs={{0,2},{1,3},{2,0},{3,1},{4,6},{5,7},{6,4},{7,5},{8,10},{9,11},{10,... | collective-permute-start | bytes 208904 | tf_op jit(solution)/shard_map/ppermute | solution.py:730
  196.3 8.0 %collective-permute-start.43 = (bf16[16,2176]{1,0:T(8,128)(2,1)S(1)}, bf16[16,2176]{1,0:T(8,128)(2,1)S(1)}, u32[]{:S(2)}, u32[]{:S(2)}) collective-permute-start(bf16[16,2176]{1,0:T(8,128)(2,1)S(1)} %get-tuple-element.221), channel_id=1, source_target_pairs={{0,4},{1,5},{2,6},{3,7},{4,0},{5,1},{6,2},{7,3},{8,12},{9,13},{10,... | collective-permute-start | bytes 208904 | tf_op jit(solution)/shard_map/ppermute | solution.py:730
  196.6 7.7 %collective-permute-start.44 = (bf16[16,2176]{1,0:T(8,128)(2,1)S(1)}, bf16[16,2176]{1,0:T(8,128)(2,1)S(1)}, u32[]{:S(2)}, u32[]{:S(2)}) collective-permute-start(bf16[16,2176]{1,0:T(8,128)(2,1)S(1)} %get-tuple-element.222), channel_id=1, source_target_pairs={{0,6},{1,7},{2,4},{3,5},{4,2},{5,3},{6,0},{7,1},{8,14},{9,15},{10,... | collective-permute-start | bytes 208904 | tf_op jit(solution)/shard_map/ppermute | solution.py:730
  (17 other events, 404.5 us)
